TPU v7x, 256 devices: a whole 4x4x8 slice. The times are simulated.
256 devices in a mesh: req: 64 (over x, z, core), tp: 4 (over y).
Axes of the slice: x: 4, y: 4, z: 8, core: 2. Of those that a mesh axis runs over, the one named last changes fastest.
Arguments:
- tokens: bfloat16 [65536, 2048], P('req'), may hold values from -6 to 6
- input_norm_gain: float32 [2048], replicated, may hold values from 0.1 to 1.9
- query_matrix: bfloat16 [2048, 2048], P(None, 'tp')
- key_matrix: bfloat16 [2048, 1024], P(None, 'tp')
- value_matrix: bfloat16 [2048, 1024], P(None, 'tp'), may hold values from -0.125 to 0.125
- output_matrix: bfloat16 [2048, 2048], P('tp'), may hold values from -0.125 to 0.125
- adapter_down_maps: bfloat16 [1024, 2048, 16], P('req', 'tp'), may hold values from -0.125 to 0.125
- adapter_up_maps: bfloat16 [1024, 16, 2048], P('req', None, 'tp'), may hold values from -1.5 to 1.5
- request_row_counts: int32 [64, 32], P('req'), may hold values from 1 to 40, 1024 in all within a row
- prompt_group_per_request: int32 [64, 32], P('req'), may hold values from 0 to 2, as said below
- adapter_per_request: int32 [64, 32], P('req'), may hold values from 0 to 1023, as said below
- adapter_table_slot: int32 [1024], replicated, may hold values from 0 to 1023, as said below
Outputs:
- mixed: bfloat16 [65536, 2048], P('req', 'tp')
Inputs may be any that keep to these rules, and one draw needn't show every extreme that they name: `prompt_group_per_request`: on each device the requests form 3 consecutive groups numbered 0, 1, 2, each of 8 to 16 requests. `adapter_per_request`: the slots adapter_table_slot[a] of one device's 32 requests lie on 32 different indices of req, so a device sends at most 40 rows to one index of req, and some device sends exactly 40. `request_row_counts`: each device's requests fill its 1024 rows in order; each device has a request of exactly 40 rows. `adapter_table_slot`: every adapter has its own slot.
All inputs are finite; a program needn't handle non-finite values.
Results may differ from a plain program's by a relative error of at most 0.034.
Values may be sent and summed in bfloat16 or wider, within the bound.
A program may use at most 128 MiB of HBM per device.

v0:
```python
import jax
import jax.numpy as jnp
from jax import lax
from jax.sharding import PartitionSpec as P

HEAD_WIDTH = 128
REQ_DEV = 32
LMAX = 40


def apply_rotary(vectors, token_positions):
    head_size = vectors.shape[-1]
    half_dim = head_size // 2
    inverse = 1000000.0 ** (-(jnp.arange(half_dim, dtype=jnp.float32) * 2.0 / head_size))
    angles = token_positions[:, None] * inverse[None, :]
    cosine = jnp.cos(angles)[:, None, :]
    sine_part = jnp.sin(angles)[:, None, :]
    first_half = vectors[..., :half_dim]
    second = vectors[..., half_dim:]
    return jnp.concatenate(
        [first_half * cosine - second * sine_part, second * cosine + first_half * sine_part], -1
    )


def layout(lengths, groups, tok_rows):
    req_slots = lengths.shape[0]
    row_ids = jnp.arange(tok_rows, dtype=jnp.int32)
    row_ends = jnp.cumsum(lengths)
    starts = row_ends - lengths
    request_row = jnp.sum((row_ids[:, None] >= row_ends[None, :]).astype(jnp.int32), 1)
    request_hot = (request_row[:, None] == jnp.arange(req_slots, dtype=jnp.int32)[None, :]).astype(
        jnp.int32
    )
    previous = jnp.concatenate([jnp.full((1,), -1, jnp.int32), groups[:-1]])
    is_prompt = (groups != previous).astype(jnp.int32)
    prompt_len = jnp.sum(
        lengths[None, :]
        * is_prompt[None, :]
        * (groups[None, :] == groups[:, None]).astype(jnp.int32),
        1,
    )
    offset_req = (1 - is_prompt) * prompt_len - starts
    group_row = jnp.sum(request_hot * groups[None, :], 1)
    prompt_row = jnp.sum(request_hot * is_prompt[None, :], 1)
    offset_row = jnp.sum(request_hot * offset_req[None, :], 1)
    token_positions = (row_ids + offset_row).astype(jnp.float32)
    visible = (group_row[:, None] == group_row[None, :]) & (row_ids[None, :] <= row_ids[:, None])
    visible = visible & (
        (request_row[:, None] == request_row[None, :]) | (prompt_row[None, :] == 1)
    )
    return (request_hot, starts, visible, token_positions, row_ids)


def per_device(
    tokens,
    input_norm_gain,
    query_matrix,
    key_matrix,
    value_matrix,
    output_matrix,
    adapter_down_maps,
    adapter_up_maps,
    request_row_counts,
    prompt_group_per_request,
    adapter_per_request,
    adapter_table_slot,
):
    tp_count = lax.axis_size("tp")
    req_count = lax.axis_size("req")
    tp_index = lax.axis_index("tp")
    tok_rows, width = tokens.shape
    piece_width = width // tp_count
    lengths = request_row_counts[0]
    groups = prompt_group_per_request[0]
    adapters = adapter_per_request[0]
    req_slots = lengths.shape[0]
    request_hot, starts, visible, token_positions, row_ids = layout(lengths, groups, tok_rows)
    adapter_count = adapter_table_slot.shape[0]
    adapters_per_part = adapter_down_maps.shape[0]
    rank_extent = adapter_down_maps.shape[2]
    query_total_width = adapter_up_maps.shape[2]
    slots = jnp.sum(
        (adapters[:, None] == jnp.arange(adapter_count, dtype=jnp.int32)[None, :]).astype(jnp.int32)
        * adapter_table_slot[None, :],
        1,
    )
    holder = slots // adapters_per_part
    local_slot = slots % adapters_per_part
    slot_ids = jnp.arange(req_slots, dtype=jnp.int32)
    earlier_same = (
        (holder[:, None] == holder[None, :]) & (slot_ids[None, :] < slot_ids[:, None])
    ).astype(jnp.int32)
    per_holder = max(1, REQ_DEV // req_count)
    float_tok = tokens.astype(jnp.float32)
    normalized_input = (
        float_tok
        * lax.rsqrt(jnp.mean(float_tok * float_tok, -1, keepdims=True) + 1e-06)
        * input_norm_gain
    ).astype(jnp.bfloat16)
    normed_slice = lax.dynamic_slice_in_dim(
        normalized_input, tp_index * piece_width, piece_width, 1
    )
    down_matrix_flat = jnp.transpose(adapter_down_maps, (1, 0, 2)).reshape(
        piece_width, adapters_per_part * rank_extent
    )
    up_matrix_flat = adapter_up_maps.reshape(adapters_per_part * rank_extent, query_total_width)
    capacity = LMAX * per_holder
    base_slot = jnp.sum(lengths[None, :] * earlier_same, 1)
    slot_request = holder * capacity + base_slot - starts
    slot_row = jnp.sum(request_hot * slot_request[None, :], 1) + row_ids
    local_row = jnp.sum(request_hot * local_slot[None, :], 1)
    outgoing = (
        jnp.zeros((req_count * capacity, piece_width), jnp.bfloat16).at[slot_row].set(normed_slice)
    )
    outgoing = outgoing.reshape(req_count, capacity, piece_width)
    out_ids = (
        jnp.zeros((req_count * capacity,), jnp.int32)
        .at[slot_row]
        .set(local_row)
        .reshape(req_count, capacity)
    )
    rows_in = lax.all_to_all(outgoing, "req", split_axis=0, concat_axis=0, tiled=True)
    ids_in = lax.all_to_all(out_ids, "req", split_axis=0, concat_axis=0, tiled=True)
    wide_rank = jnp.einsum(
        "sid,dk->sik", rows_in, down_matrix_flat, preferred_element_type=jnp.float32
    )
    wide_rank = wide_rank.reshape(
        rows_in.shape[0], rows_in.shape[1], adapters_per_part, rank_extent
    )
    pick = ids_in[:, :, None] == jnp.arange(adapters_per_part, dtype=jnp.int32)[None, None, :]
    partial_rank = jnp.sum(jnp.where(pick[..., None], wide_rank, jnp.float32(0.0)), 2)
    rank_sum = lax.psum(partial_rank.astype(jnp.bfloat16), "tp")
    spread = jnp.where(pick[..., None], rank_sum[:, :, None, :], jnp.zeros((), jnp.bfloat16))
    spread = spread.reshape(rows_in.shape[0], rows_in.shape[1], adapters_per_part * rank_extent)
    update = (
        2.0 * jnp.einsum("sik,kq->siq", spread, up_matrix_flat, preferred_element_type=jnp.float32)
    ).astype(jnp.bfloat16)
    returned = lax.all_to_all(update, "req", split_axis=0, concat_axis=0, tiled=True)
    query_delta = returned.reshape(req_count * capacity, returned.shape[2])[slot_row]
    heads_local = query_matrix.shape[1] // HEAD_WIDTH
    kv_local = key_matrix.shape[1] // HEAD_WIDTH
    query_full = jnp.dot(
        normalized_input, query_matrix, preferred_element_type=jnp.float32
    ) + query_delta.astype(jnp.float32)
    query_heads = apply_rotary(
        query_full.reshape(tok_rows, heads_local, HEAD_WIDTH), token_positions
    ).astype(jnp.bfloat16)
    key_complete = jnp.dot(normalized_input, key_matrix, preferred_element_type=jnp.float32)
    key_head_rows = apply_rotary(
        key_complete.reshape(tok_rows, kv_local, HEAD_WIDTH), token_positions
    ).astype(jnp.bfloat16)
    value_head_rows = (
        jnp.dot(normalized_input, value_matrix, preferred_element_type=jnp.float32)
        .astype(jnp.bfloat16)
        .reshape(tok_rows, kv_local, HEAD_WIDTH)
    )
    key_head_rows = jnp.repeat(key_head_rows, heads_local // kv_local, axis=1)
    value_head_rows = jnp.repeat(value_head_rows, heads_local // kv_local, axis=1)
    scores = (
        jnp.einsum("qhd,khd->hqk", query_heads, key_head_rows, preferred_element_type=jnp.float32)
        / HEAD_WIDTH**0.5
    )
    scores = jnp.where(visible[None], scores, jnp.float32(-1e30))
    row_max = jnp.max(scores, -1, keepdims=True)
    weights = jnp.exp(scores - row_max)
    probabilities = (weights / jnp.sum(weights, -1, keepdims=True)).astype(jnp.bfloat16)
    attended = jnp.einsum(
        "hqk,khd->qhd", probabilities, value_head_rows, preferred_element_type=jnp.float32
    ).astype(jnp.bfloat16)
    head_term = jnp.dot(
        attended.reshape(tok_rows, heads_local * HEAD_WIDTH),
        output_matrix,
        preferred_element_type=jnp.float32,
    )
    summed = lax.psum_scatter(
        head_term.astype(jnp.bfloat16), "tp", scatter_dimension=1, tiled=True
    ).astype(jnp.float32)
    residual = lax.dynamic_slice_in_dim(tokens, tp_index * piece_width, piece_width, 1)
    return (residual.astype(jnp.float32) + summed).astype(jnp.bfloat16)


def solution(mesh):
    return jax.shard_map(
        per_device,
        mesh=mesh,
        in_specs=(
            P("req", None),
            P(),
            P(None, "tp"),
            P(None, "tp"),
            P(None, "tp"),
            P("tp", None),
            P("req", "tp", None),
            P("req", None, "tp"),
            P("req", None),
            P("req", None),
            P("req", None),
            P(),
        ),
        out_specs=P("req", "tp"),
        check_vma=False,
    )
```

profile of v0, /device:TPU:2, one launch (start us, length us, event | category | flops | bytes accessed | tf_op | source)
XLA Modules:
  0.0 346.8 jit_solution(15694868531542384394)
XLA Ops:
  6.5 1.0 select_reduce_fusion.4
  7.6 0.8 convert_bitcast_fusion
  8.4 0.7 select_bitcast_fusion
  9.1 0.7 copy.47
  9.8 0.1 reduce-window.4
  9.9 0.1 reduce
  10.0 0.1 convert_reduce_fusion
  10.1 0.9 select_reduce_fusion.7
  11.0 0.7 fusion.35
  11.7 0.8 select_reduce_fusion.2
  12.5 4.3 %scatter_custom_fusion = s32[2560]{0:T(1024)S(1)} fusion(s32[1024]{0:T(1024)S(1)} %bitcast.99, s32[1024]{0:T(1024)S(1)} %get-tuple-element.5, s32[]{:T(128)} %constant.65.clone.1), kind=kCustom, calls=%fused_computation.65 | custom fusion | bytes 10244 | tf_op jit(solution)/shard_map/scatter | solution.py:119
  16.8 0.7 all_to_all.12
  17.5 12.0 %all-to-all-start = ((s32[64,1,40]{2,1,0:T(1,128)}), s32[64,1,40]{2,1,0:T(1,128)S(1)}, u32[]{:S(2)}, u32[]{:S(2)}) async-start(s32[64,1,40]{2,1,0:T(1,128)} %bitcast.12), calls=%async_computation | async-start | bytes 65536 | tf_op jit(solution)/shard_map/all_to_all | solution.py:123
  29.6 3.2 fusion.2
  32.8 0.2 copy-done.1
  33.0 3.0 fusion.4
  36.0 7.5 %scatter_custom_fusion.1 = bf16[2560,512]{1,0:T(8,128)(2,1)} fusion(s32[1024]{0:T(1024)S(1)} %bitcast.100, bf16[]{:T(256)} %constant.80.clone.1, bf16[1024,2048]{1,0:T(8,128)(2,1)} %fusion.4, s32[]{:T(128)} %constant.65.clone.1, s32[]{:T(128)S(6)} %select_n.60), kind=kCustom, calls=%fused_computation.36 | custom fusion | bytes 3671044 | tf_op jit(solution)/shard_map/scatter | solution.py:113
  43.5 10.5 %all-to-all-start.1 = ((bf16[64,40,512]{2,1,0:T(8,128)(2,1)}), bf16[64,40,512]{2,1,0:T(8,128)(2,1)}, u32[]{:S(2)}, u32[]{:S(2)}) async-start(bf16[64,40,512]{2,1,0:T(8,128)(2,1)} %bitcast.92), calls=%async_computation.1 | async-start | bytes 5242880 | tf_op jit(solution)/shard_map/all_to_all | solution.py:122
  54.0 0.2 all-reduce.2.cloned.1.call-start
  54.2 0.1 iota_compare_fusion.1
  54.3 60.5 %all-to-all-done.1 = bf16[64,40,512]{2,1,0:T(8,128)(2,1)} async-done(((bf16[64,40,512]{2,1,0:T(8,128)(2,1)}), bf16[64,40,512]{2,1,0:T(8,128)(2,1)}, u32[]{:S(2)}, u32[]{:S(2)}) %all-to-all-start.1) | async-done | bytes 2621472 | tf_op jit(solution)/shard_map/all_to_all | solution.py:122
  114.8 6.4 %select_reduce_fusion = bf16[64,40,16]{1,2,0:T(8,128)(2,1)} fusion(pred[64,40,16]{1,2,0:T(8,128)(4,1)S(1)} %iota_compare_fusion.1, bf16[64,40,512]{2,1,0:T(8,128)(2,1)} %all-to-all-done.1, bf16[16,512,16]{1,2,0:T(8,128)(2,1)S(1)} %copy-done.4), kind=kOutput, calls=%fused_computation.15 | convolution fusion | flops 672358400 | bytes 3006464 | tf_op jit(solution)/shard_map/sid,dk->sik/dot_general | solution.py:124
  121.2 45.1 %all-reduce.2.cloned.1.call-done = bf16[64,40,16]{1,2,0:T(8,128)(2,1)} async-done(((bf16[64,40,16]{1,2,0:T(8,128)(2,1)}), bf16[64,40,16]{1,2,0:T(8,128)(2,1)}) %all-reduce.2.cloned.1.call-update) | async-done | bytes 81936 | tf_op jit(solution)/shard_map/psum | solution.py:132
  166.3 3.9 %fusion.9 = bf16[64,40,512]{2,1,0:T(8,128)(2,1)} fusion(pred[64,40,16]{1,2,0:T(8,128)(4,1)S(1)} %iota_compare_fusion.1, bf16[64,40,16]{1,2,0:T(8,128)(2,1)} %all-reduce.2.cloned.1.call-done, bf16[16,16,512]{2,1,0:T(8,128)(2,1)S(1)} %copy-done.5), kind=kOutput, calls=%fused_computation.19 | convolution fusion | flops 674365440 | bytes 3006464 | tf_op jit(solution)/shard_map/sik,kq->siq/dot_general | solution.py:136
  170.2 10.7 %all-to-all-start.2 = ((bf16[64,40,512]{2,1,0:T(8,128)(2,1)}), bf16[64,40,512]{2,1,0:T(8,128)(2,1)}, u32[]{:S(2)}, u32[]{:S(2)}) async-start(bf16[64,40,512]{2,1,0:T(8,128)(2,1)} %fusion.9), calls=%async_computation.2 | async-start | bytes 5242880 | tf_op jit(solution)/shard_map/all_to_all | solution.py:138
  181.0 1.0 multiply_cosine_fusion
  182.0 1.0 copy.51
  183.0 1.0 copy.53
  184.0 3.8 %fusion.45 = f32[1024,256]{0,1:T(8,128)S(1)} fusion(bf16[1024,2048]{1,0:T(8,128)(2,1)} %fusion.4, bf16[2048,256]{1,0:T(8,128)(2,1)} %param.15), kind=kOutput, calls=%fused_computation.99 | convolution fusion | flops 1073741824 | bytes 6291456 | tf_op jit(solution)/shard_map/dot_general | solution.py:148
  187.8 0.2 subtract_convert_fusion.1
  188.0 1.0 copy.54
  189.0 2.7 fusion.13
  191.8 4.6 %convolution_convert_fusion.1 = bf16[1024,256]{0,1:T(8,128)(2,1)} fusion(bf16[1024,2048]{1,0:T(8,128)(2,1)} %fusion.4, bf16[2048,256]{1,0:T(8,128)(2,1)} %param.16), kind=kOutput, calls=%fused_computation.38 | convolution fusion | flops 1074003968 | bytes 5767168 | tf_op jit(solution)/shard_map/dot_general | solution.py:153
  196.3 45.4 %all-to-all-done.2 = bf16[64,40,512]{2,1,0:T(8,128)(2,1)} async-done(((bf16[64,40,512]{2,1,0:T(8,128)(2,1)}), bf16[64,40,512]{2,1,0:T(8,128)(2,1)}, u32[]{:S(2)}, u32[]{:S(2)}) %all-to-all-start.2) | async-done | bytes 2621472 | tf_op jit(solution)/shard_map/all_to_all | solution.py:138
  241.7 6.1 %gather_fusion = bf16[1024,512]{1,0:T(8,128)(2,1)S(1)} fusion(bf16[2560,512]{1,0:T(8,128)(2,1)} %bitcast.25, s32[1024]{0:T(1024)S(1)} %broadcast_clamp_fusion), kind=kCustom, calls=%fused_computation | custom fusion | bytes 2101248 | tf_op jit(solution)/shard_map/gather | solution.py:139
  247.8 1.3 copy.49
  249.1 5.4 %convert_add_fusion = f32[1024,512]{0,1:T(8,128)S(1)} fusion(bf16[1024,512]{0,1:T(8,128)(2,1)} %copy.49, bf16[1024,2048]{1,0:T(8,128)(2,1)} %fusion.4, bf16[2048,512]{1,0:T(8,128)(2,1)} %param.14), kind=kOutput, calls=%fused_computation.31 | convolution fusion | flops 2148532224 | bytes 9437184 | tf_op jit(solution)/shard_map/dot_general | solution.py:142
  254.6 1.2 fusion.43
  255.7 3.2 copy.60
  258.9 1.9 copy.59
  260.8 4.1 %subtract_convert_fusion = (bf16[1024,4,64]{2,0,1:T(8,128)(2,1)S(1)}, bf16[1024,4,64]{2,0,1:T(8,128)(2,1)}) fusion(f32[1024,4,64]{2,0,1:T(8,128)} %copy.60, f32[1024,4,64]{2,0,1:T(8,128)} %copy.59, f32[1024,64]{1,0:T(8,128)} %copy.53, f32[1024,64]{1,0:T(8,128)} %copy.51), kind=kLoop, calls=%fused_computation.30 | loop fusion | flops 2097152 | bytes 3670016 | tf_op jit(solution)/shard_map/convert.2
  264.9 1.2 broadcast_in_dim.47
  266.1 11.7 %fusion.44 = (f32[4,1024]{1,0:T(4,128)S(1)}, f32[4,1024,1024]{1,2,0:T(8,128)}) fusion(pred[1024,1024]{0,1:T(8,128)(4,1)} %fusion.13, bf16[1024,4,128]{2,0,1:T(8,128)(2,1)} %bitcast.94, bf16[1024,4,64]{2,0,1:T(8,128)(2,1)} %get-tuple-element.13, bf16[1024,4,64]{2,0,1:T(8,128)(2,1)S(1)} %get-tuple-element.12), kind=kOutput, calls=%fused_computation.98 | convolution fusion | flops 1092617216 | bytes 19939328 | tf_op jit(solution)/shard_map/sub | solution.py:165
  277.8 1.2 broadcast_in_dim.39
  279.0 7.1 %fusion.22 = bf16[4,128,1024]{2,1,0:T(8,128)(2,1)S(1)} fusion(bf16[1024,4,128]{0,2,1:T(8,128)(2,1)S(1)} %bitcast.95, f32[4,1024,1024]{1,2,0:T(8,128)} %get-tuple-element.25, f32[4,1024]{1,0:T(4,128)S(1)} %get-tuple-element.24), kind=kOutput, calls=%fused_computation.35 | convolution fusion | flops 1082654720 | bytes 18890752 | tf_op jit(solution)/shard_map/hqk,khd->qhd/dot_general | solution.py:167
  286.1 4.3 %convolution_convert_fusion = bf16[1024,2048]{1,0:T(8,128)(2,1)} fusion(bf16[1024,512]{0,1:T(8,128)(2,1)S(1)} %bitcast.109, bf16[512,2048]{1,0:T(8,128)(2,1)S(1)} %copy-done), kind=kOutput, calls=%fused_computation.26 | convolution fusion | flops 2149580800 | bytes 7340032 | tf_op jit(solution)/shard_map/dot_general | solution.py:170
  290.4 46.7 %reduce-scatter.2.cloned.1.call-done = bf16[1024,512]{1,0:T(8,128)(2,1)} async-done(((bf16[1024,2048]{1,0:T(8,128)(2,1)}), bf16[1024,512]{1,0:T(8,128)(2,1)}) %reduce-scatter.2.cloned.1.call-update) | async-done | bytes 1048592 | tf_op jit(solution)/shard_map/reduce_scatter | solution.py:175
  337.1 2.8 add_convert_fusion
  (23 shorter events, 0.2 us)
Async XLA Ops:
  6.5 279.5 %copy-start = (bf16[512,2048]{1,0:T(8,128)(2,1)S(1)}, bf16[512,2048]{1,0:T(8,128)(2,1)}, u32[]{:S(2)}) copy-start(bf16[512,2048]{1,0:T(8,128)(2,1)} %param.17) | copy-start | bytes 6291460
  6.5 26.3 %copy-start.3 = (f32[2048]{0:T(1024)S(1)}, f32[2048]{0:T(1024)}, u32[]{:S(2)}) copy-start(f32[2048]{0:T(1024)} %param.13) | copy-start | bytes 24580
  17.5 25.9 %all-to-all-start = ((s32[64,1,40]{2,1,0:T(1,128)}), s32[64,1,40]{2,1,0:T(1,128)S(1)}, u32[]{:S(2)}, u32[]{:S(2)}) async-start(s32[64,1,40]{2,1,0:T(1,128)} %bitcast.12), calls=%async_computation | async-start | bytes 65536 | tf_op jit(solution)/shard_map/all_to_all | solution.py:123
  29.6 3.5 copy-start.1
  36.0 78.8 %copy-start.4 = (bf16[16,512,16]{1,2,0:T(8,128)(2,1)S(1)}, bf16[16,512,16]{1,2,0:T(8,128)(2,1)}, u32[]{:S(2)}) copy-start(bf16[16,512,16]{1,2,0:T(8,128)(2,1)} %param.18) | copy-start | bytes 786436
  43.5 71.3 %all-to-all-start.1 = ((bf16[64,40,512]{2,1,0:T(8,128)(2,1)}), bf16[64,40,512]{2,1,0:T(8,128)(2,1)}, u32[]{:S(2)}, u32[]{:S(2)}) async-start(bf16[64,40,512]{2,1,0:T(8,128)(2,1)} %bitcast.92), calls=%async_computation.1 | async-start | bytes 5242880 | tf_op jit(solution)/shard_map/all_to_all | solution.py:122
  54.0 112.3 %all-reduce.2.cloned.1.call-start = ((), (), s32[]{:S(2)}) async-start(), calls=%async_computation.4 | async-start | bytes 524288 | tf_op jit(solution)/shard_map/psum | solution.py:132
  54.3 112.0 %copy-start.5 = (bf16[16,16,512]{2,1,0:T(8,128)(2,1)S(1)}, bf16[16,16,512]{2,1,0:T(8,128)(2,1)}, u32[]{:S(2)}) copy-start(bf16[16,16,512]{2,1,0:T(8,128)(2,1)} %param.19) | copy-start | bytes 786436
  170.2 71.5 %all-to-all-start.2 = ((bf16[64,40,512]{2,1,0:T(8,128)(2,1)}), bf16[64,40,512]{2,1,0:T(8,128)(2,1)}, u32[]{:S(2)}, u32[]{:S(2)}) async-start(bf16[64,40,512]{2,1,0:T(8,128)(2,1)} %fusion.9), calls=%async_computation.2 | async-start | bytes 5242880 | tf_op jit(solution)/shard_map/all_to_all | solution.py:138
  180.9 156.2 %reduce-scatter.2.cloned.1.call-start = ((), (), s32[]{:S(2)}) async-start(), calls=%async_computation.5 | async-start | bytes 5242880 | tf_op jit(solution)/shard_map/reduce_scatter | solution.py:175
  260.8 4.1 %copy-start.2 = (bf16[1024,2,128]{2,0,1:T(8,128)(2,1)S(1)}, bf16[1024,2,128]{2,0,1:T(8,128)(2,1)}, u32[]{:S(2)}) copy-start(bf16[1024,2,128]{2,0,1:T(8,128)(2,1)} %copy.54) | copy-start | bytes 1572868
Sparse Core Ops, SparseCore 0:
  121.3 44.9 all-reduce.1
  290.5 46.5 reduce-scatter.1
where the time goes:
time: 348 us; the launch traced here: 347 us
  waiting for transfers between devices  198 us (57%)
  matrix products  47.1 us (14%)
  starting transfers between devices  33.5 us (10%)
  local copies, waits for them, and re-layouts  32.5 us (9%)
  other arithmetic  22.3 us (6%)
  between operations  13.6 us (4%)
    all_to_all x1, waiting for transfers between devices, per_device(): lax.all_to_all(outgoing, 'req', split_axis=0, concat_axis=0, tiled=True)  60.5 us
    reduce_scatter x1, waiting for transfers between devices, per_device(): lax.psum_scatter(head_term.astype(jnp.bfloat16), 'tp', scatter_dimension=...  46.7 us
    all_to_all x1, waiting for transfers between devices, per_device(): lax.all_to_all(update, 'req', split_axis=0, concat_axis=0, tiled=True)  45.4 us
    psum x1, waiting for transfers between devices, per_device(): rank_sum = lax.psum(partial_rank.astype(jnp.bfloat16), 'tp')  45.1 us
    all_to_all x1, starting transfers between devices, per_device(): lax.all_to_all(out_ids, 'req', split_axis=0, concat_axis=0, tiled=True)  12 us
    sub x1, matrix products, per_device(): weights = jnp.exp(scores - row_max)  11.7 us
    all_to_all x1, starting transfers between devices, per_device(): lax.all_to_all(update, 'req', split_axis=0, concat_axis=0, tiled=True)  10.7 us
    all_to_all x1, starting transfers between devices, per_device(): lax.all_to_all(outgoing, 'req', split_axis=0, concat_axis=0, tiled=True)  10.5 us
  transfers between devices with their start and end apart: 5, of which 4 were waited for; matrix products, arithmetic and copies ran while one was open for 8% of the time, Pallas kernels for 0%

commit v1 on v0

--- a/solution.py
+++ b/solution.py
@@ -75,22 +75,23 @@
     adapters = adapter_per_request[0]
     req_slots = lengths.shape[0]
     request_hot, starts, visible, token_positions, row_ids = layout(lengths, groups, tok_rows)
-    adapter_count = adapter_table_slot.shape[0]
     adapters_per_part = adapter_down_maps.shape[0]
     rank_extent = adapter_down_maps.shape[2]
-    query_total_width = adapter_up_maps.shape[2]
-    slots = jnp.sum(
-        (adapters[:, None] == jnp.arange(adapter_count, dtype=jnp.int32)[None, :]).astype(jnp.int32)
-        * adapter_table_slot[None, :],
-        1,
-    )
+    slots = adapter_table_slot[adapters]
     holder = slots // adapters_per_part
     local_slot = slots % adapters_per_part
-    slot_ids = jnp.arange(req_slots, dtype=jnp.int32)
-    earlier_same = (
-        (holder[:, None] == holder[None, :]) & (slot_ids[None, :] < slot_ids[:, None])
-    ).astype(jnp.int32)
-    per_holder = max(1, REQ_DEV // req_count)
+    holder_ids = jnp.arange(req_count, dtype=jnp.int32)
+    holder_hot = (holder[None, :] == holder_ids[:, None]).astype(jnp.int32)
+    wanted = jnp.sum(holder_hot * local_slot[None, :], 1)
+    wanted_in = lax.all_to_all(
+        wanted.reshape(req_count, 1), "req", split_axis=0, concat_axis=0, tiled=True
+    ).reshape(req_count)
+    down_sel = jnp.transpose(adapter_down_maps[wanted_in], (0, 2, 1))
+    up_sel = adapter_up_maps[wanted_in]
+    maps_out = jnp.concatenate([down_sel, up_sel], 1)
+    maps_in = lax.all_to_all(maps_out, "req", split_axis=0, concat_axis=0, tiled=True)
+    down_in = maps_in[:, :rank_extent, :].reshape(req_count * rank_extent, piece_width)
+    up_in = maps_in[:, rank_extent:, :].reshape(req_count * rank_extent, piece_width)
     float_tok = tokens.astype(jnp.float32)
     normalized_input = (
         float_tok
@@ -100,43 +101,22 @@
     normed_slice = lax.dynamic_slice_in_dim(
         normalized_input, tp_index * piece_width, piece_width, 1
     )
-    down_matrix_flat = jnp.transpose(adapter_down_maps, (1, 0, 2)).reshape(
-        piece_width, adapters_per_part * rank_extent
+    holder_row = jnp.sum(request_hot * holder[None, :], 1)
+    pick = (holder_row[:, None] == holder_ids[None, :])[:, :, None]
+    wide_rank = jnp.dot(
+        normed_slice, down_in.T, preferred_element_type=jnp.float32
+    ).reshape(tok_rows, req_count, rank_extent)
+    partial_rank = jnp.sum(jnp.where(pick, wide_rank, jnp.float32(0.0)), 1)
+    for step in (1, 2):
+        pairs = [(i, i ^ step) for i in range(tp_count)]
+        partial_rank = partial_rank + lax.ppermute(partial_rank, "tp", pairs)
+    rank = partial_rank.astype(jnp.bfloat16)
+    spread = jnp.where(pick, rank[:, None, :], jnp.zeros((), jnp.bfloat16)).reshape(
+        tok_rows, req_count * rank_extent
     )
-    up_matrix_flat = adapter_up_maps.reshape(adapters_per_part * rank_extent, query_total_width)
-    capacity = LMAX * per_holder
-    base_slot = jnp.sum(lengths[None, :] * earlier_same, 1)
-    slot_request = holder * capacity + base_slot - starts
-    slot_row = jnp.sum(request_hot * slot_request[None, :], 1) + row_ids
-    local_row = jnp.sum(request_hot * local_slot[None, :], 1)
-    outgoing = (
-        jnp.zeros((req_count * capacity, piece_width), jnp.bfloat16).at[slot_row].set(normed_slice)
-    )
-    outgoing = outgoing.reshape(req_count, capacity, piece_width)
-    out_ids = (
-        jnp.zeros((req_count * capacity,), jnp.int32)
-        .at[slot_row]
-        .set(local_row)
-        .reshape(req_count, capacity)
-    )
-    rows_in = lax.all_to_all(outgoing, "req", split_axis=0, concat_axis=0, tiled=True)
-    ids_in = lax.all_to_all(out_ids, "req", split_axis=0, concat_axis=0, tiled=True)
-    wide_rank = jnp.einsum(
-        "sid,dk->sik", rows_in, down_matrix_flat, preferred_element_type=jnp.float32
-    )
-    wide_rank = wide_rank.reshape(
-        rows_in.shape[0], rows_in.shape[1], adapters_per_part, rank_extent
-    )
-    pick = ids_in[:, :, None] == jnp.arange(adapters_per_part, dtype=jnp.int32)[None, None, :]
-    partial_rank = jnp.sum(jnp.where(pick[..., None], wide_rank, jnp.float32(0.0)), 2)
-    rank_sum = lax.psum(partial_rank.astype(jnp.bfloat16), "tp")
-    spread = jnp.where(pick[..., None], rank_sum[:, :, None, :], jnp.zeros((), jnp.bfloat16))
-    spread = spread.reshape(rows_in.shape[0], rows_in.shape[1], adapters_per_part * rank_extent)
-    update = (
-        2.0 * jnp.einsum("sik,kq->siq", spread, up_matrix_flat, preferred_element_type=jnp.float32)
+    query_delta = (
+        2.0 * jnp.dot(spread, up_in, preferred_element_type=jnp.float32)
     ).astype(jnp.bfloat16)
-    returned = lax.all_to_all(update, "req", split_axis=0, concat_axis=0, tiled=True)
-    query_delta = returned.reshape(req_count * capacity, returned.shape[2])[slot_row]
     heads_local = query_matrix.shape[1] // HEAD_WIDTH
     kv_local = key_matrix.shape[1] // HEAD_WIDTH
     query_full = jnp.dot(

time: 348 us -> 208 us (0.60)
  waiting for transfers between devices: 198 us -> 86.6 us
  local copies, waits for them, and re-layouts: 32.5 us -> 20.6 us
  matrix products: 47.1 us -> 37.5 us
  starting transfers between devices: 33.5 us -> 24.4 us
    all_to_all x3 -> x2, waiting for transfers between devices: 106 us -> 36.6 us  [the longest x1 32.9 us: per_device(): lax.all_to_all(maps_out, 'req', split_axis=0, concat_axis=0, tiled=True)]
    psum x1 -> x0, waiting for transfers between devices: 45.1 us -> none  [per_device(): rank_sum = lax.psum(partial_rank.astype(jnp.bfloat16), 'tp')]
    all_to_all x3 -> x2, starting transfers between devices: 33.2 us -> 19 us  [the longest x1 12 us: per_device(): lax.all_to_all(wanted.reshape(req_count, 1), 'req', split_axis=0, concat_...]
    scatter x2 -> x0, local copies, waits for them, and re-layouts: 11.8 us -> none  [the longest x1 7.5 us: per_device(): jnp.zeros((req_count * capacity, piece_width), jnp.bfloat16).at[slot_row]]
    ppermute x0 -> x2, starting transfers between devices: none -> 5.17 us  [per_device(): partial_rank = partial_rank + lax.ppermute(partial_rank, 'tp', pairs)]
    dot_general x2, matrix products: 10.2 us -> 6.22 us  [the longest x1 3.31 us: per_device(): jnp.dot(spread, up_in, preferred_element_type=jnp.float32)]
    gather x2 -> x3, local copies, waits for them, and re-layouts: 7.41 us -> 4.53 us  [the longest x1 2.53 us: per_device(): up_sel = adapter_up_maps[wanted_in]]
  transfers between devices with their start and end apart: 5 -> 5, of which waited for: 4 -> 5; matrix products, arithmetic and copies ran while one was open for 8% -> 12% of each run, Pallas kernels for 0% -> 0%
where the time goes in v1:
time: 208 us; the launch traced here: 207 us
  waiting for transfers between devices  86.6 us (42%)
  matrix products  37.5 us (18%)
  starting transfers between devices  24.4 us (12%)
  other arithmetic  24 us (12%)
  local copies, waits for them, and re-layouts  20.6 us (10%)
  between operations  13.6 us (7%)
    reduce_scatter x1, waiting for transfers between devices, per_device(): lax.psum_scatter(head_term.astype(jnp.bfloat16), 'tp', scatter_dimension=...  47.5 us
    all_to_all x1, waiting for transfers between devices, per_device(): lax.all_to_all(maps_out, 'req', split_axis=0, concat_axis=0, tiled=True)  32.9 us
    all_to_all x1, starting transfers between devices, per_device(): lax.all_to_all(wanted.reshape(req_count, 1), 'req', split_axis=0, concat_...  12 us
    sub x1, matrix products, per_device(): weights = jnp.exp(scores - row_max)  11.7 us
    dot_general x1, matrix products, per_device(): jnp.einsum('hqk,khd->qhd', probabilities, value_head_rows, preferred_elem...  7.06 us
    all_to_all x1, starting transfers between devices, per_device(): lax.all_to_all(maps_out, 'req', split_axis=0, concat_axis=0, tiled=True)  6.98 us
    unnamed x22, local copies, waits for them, and re-layouts  5.31 us
    ppermute x2, starting transfers between devices, per_device(): partial_rank = partial_rank + lax.ppermute(partial_rank, 'tp', pairs)  5.17 us
  transfers between devices with their start and end apart: 5, of which 5 were waited for; matrix products, arithmetic and copies ran while one was open for 12% of the time, Pallas kernels for 0%

profile of v1, /device:TPU:2, one launch (start us, length us, event | category | flops | bytes accessed | tf_op | source)
XLA Modules:
  0.0 206.7 jit_solution(6115400074369117992)
XLA Ops:
  6.5 0.8 fusion.29
  7.4 1.4 gather_fusion
  8.9 0.7 copy.60
  9.6 12.0 %all-to-all-start = ((s32[64,1,1]{2,1,0:T(1,128)}), s32[64,1,1]{2,1,0:T(1,128)S(1)}, u32[]{:S(2)}, u32[]{:S(2)}) async-start(s32[64,1,1]{2,1,0:T(1,128)} %copy.60), calls=%async_computation | async-start | bytes 65536 | tf_op jit(solution)/shard_map/all_to_all | solution.py:86
  21.6 0.8 convert_bitcast_fusion
  22.4 0.7 select_bitcast_fusion
  23.1 0.7 copy.59
  24.1 0.9 select_reduce_fusion.5
  25.0 0.7 fusion.32
  25.7 0.8 select_reduce_fusion.2
  26.5 3.7 %all-to-all-done = s32[64,1,1]{2,1,0:T(1,128)S(1)} async-done(((s32[64,1,1]{2,1,0:T(1,128)}), s32[64,1,1]{2,1,0:T(1,128)S(1)}, u32[]{:S(2)}, u32[]{:S(2)}) %all-to-all-start) | async-done | bytes 288 | tf_op jit(solution)/shard_map/all_to_all | solution.py:86
  30.1 1.2 reduce.1
  31.4 2.5 %gather_fusion.2 = bf16[64,16,512]{2,1,0:T(8,128)(2,1)} fusion(bf16[16,16,512]{2,1,0:T(8,128)(2,1)} %param.19, s32[1024]{0:T(1024)S(1)} %pad_clamp_fusion), kind=kCustom, calls=%fused_computation.2 | custom fusion | bytes 2097408 | tf_op jit(solution)/shard_map/gather | solution.py:90
  33.9 0.6 gather_fusion.1
  34.5 2.8 %pad_maximum_fusion = bf16[64,32,512]{2,1,0:T(8,128)(2,1)} fusion(bf16[64,16,512]{2,1,0:T(8,128)(2,1)} %gather_fusion.2, bf16[64,16,512]{2,1,0:T(8,128)(2,1)S(1)} %bitcast.57), kind=kLoop, calls=%fused_computation.22 | loop fusion | flops 4194304 | bytes 4194304 | tf_op jit(solution)/shard_map/concatenate | solution.py:91
  37.4 7.0 %all-to-all-start.1 = ((bf16[64,32,512]{2,1,0:T(8,128)(2,1)}), bf16[64,32,512]{2,1,0:T(8,128)(2,1)}, u32[]{:S(2)}, u32[]{:S(2)}) async-start(bf16[64,32,512]{2,1,0:T(8,128)(2,1)} %pad_maximum_fusion), calls=%async_computation.1 | async-start | bytes 4194304 | tf_op jit(solution)/shard_map/all_to_all | solution.py:92
  44.4 0.2 reduce-scatter.2.cloned.1.call-start
  44.6 3.2 %fusion.2 = f32[1024]{0:T(1024)S(1)} fusion(bf16[1024,2048]{1,0:T(8,128)(2,1)} %param.12), kind=kLoop, calls=%fused_computation.10 | loop fusion | flops 6290432 | bytes 4198400 | tf_op jit(solution)/shard_map/reduce_sum | solution.py:98
  47.9 1.0 multiply_cosine_fusion
  48.9 2.5 %fusion.10 = pred[1024,1024]{0,1:T(8,128)(4,1)} fusion(s32[1024]{0:T(1024)S(1)} %convert_reduce_fusion, s32[1024]{0:T(1024)S(1)} %get-tuple-element.8, pred[1024]{0:T(1024)(128)(4,1)S(1)} %broadcast_compare_fusion), kind=kLoop, calls=%fused_computation.20 | loop fusion | flops 6291456 | bytes 1057792 | tf_op jit(solution)/shard_map/and | solution.py:48
  51.4 1.0 fusion.4
  52.5 0.2 copy-done.8
  52.7 2.1 %convolution_convert_fusion.1 = bf16[1024,256]{0,1:T(8,128)(2,1)} fusion(bf16[1024,2048]{1,0:T(8,128)(2,1)S(1)} %fusion.4, bf16[2048,256]{1,0:T(8,128)(2,1)S(1)} %copy-done.8), kind=kOutput, calls=%fused_computation.34 | convolution fusion | flops 1074003968 | bytes 5767168 | tf_op jit(solution)/shard_map/dot_general | solution.py:133
  54.8 2.3 %fusion.45 = f32[1024,256]{0,1:T(8,128)} fusion(bf16[1024,2048]{1,0:T(8,128)(2,1)S(1)} %fusion.4, bf16[2048,256]{1,0:T(8,128)(2,1)S(1)} %copy-done.9), kind=kOutput, calls=%fused_computation.92 | convolution fusion | flops 1073741824 | bytes 6291456 | tf_op jit(solution)/shard_map/dot_general | solution.py:128
  57.1 3.8 %fusion.44 = f32[1024,512]{0,1:T(8,128)} fusion(bf16[1024,2048]{1,0:T(8,128)(2,1)S(1)} %fusion.4, bf16[2048,512]{1,0:T(8,128)(2,1)S(1)} %copy-done.7), kind=kOutput, calls=%fused_computation.91 | convolution fusion | flops 2147483648 | bytes 8388608 | tf_op jit(solution)/shard_map/dot_general | solution.py:122
  60.9 32.9 %all-to-all-done.1 = bf16[64,32,512]{2,1,0:T(8,128)(2,1)} async-done(((bf16[64,32,512]{2,1,0:T(8,128)(2,1)}), bf16[64,32,512]{2,1,0:T(8,128)(2,1)}, u32[]{:S(2)}, u32[]{:S(2)}) %all-to-all-start.1) | async-done | bytes 2097184 | tf_op jit(solution)/shard_map/all_to_all | solution.py:92
  93.8 2.8 %fusion.42 = (bf16[64,16,512]{2,1,0:T(8,128)(2,1)S(1)}, bf16[64,16,512]{2,1,0:T(8,128)(2,1)}) fusion(bf16[64,32,512]{2,1,0:T(8,128)(2,1)} %all-to-all-done.1), kind=kLoop, calls=%fused_computation.89 | loop fusion | bytes 4194304 | tf_op jit(solution)/shard_map/slice | solution.py:93
  96.6 2.9 %select_reduce_fusion = f32[1024,16]{0,1:T(8,128)S(1)} fusion(pred[1024,64]{0,1:T(8,128)(4,1)S(1)} %iota_compare_fusion.1, bf16[64,16,512]{2,1,0:T(8,128)(2,1)S(1)} %get-tuple-element.15, bf16[1024,2048]{1,0:T(8,128)(2,1)} %copy-done.3, s32[]{:T(128)S(6)} %select_n.57), kind=kOutput, calls=%fused_computation.17 | convolution fusion | flops 1075822592 | bytes 2228228 | tf_op jit(solution)/shard_map/dot_general | solution.py:106
  99.5 1.7 collective-permute-start
  101.2 0.2 subtract_convert_fusion.1
  101.4 1.0 copy.64
  102.4 1.0 copy.66
  103.4 0.7 collective-permute-done
  104.2 3.5 %collective-permute-start.1 = (f32[1024,16]{0,1:T(8,128)S(1)}, f32[1024,16]{0,1:T(8,128)S(1)}, u32[]{:S(2)}, u32[]{:S(2)}) collective-permute-start(f32[1024,16]{0,1:T(8,128)S(1)} %add.88), channel_id=1, source_target_pairs={{0,2},{1,3},{2,0},{3,1},{4,6},{5,7},{6,4},{7,5},{8,10},{9,11},{10,... | collective-permute-start | bytes 196616 | tf_op jit(solution)/shard_map/ppermute | solution.py:112
  107.7 1.0 copy.67
  108.7 1.7 collective-permute-done.1
  110.4 3.3 %convert_add_fusion = f32[1024,512]{0,1:T(8,128)S(1)} fusion(f32[1024,512]{0,1:T(8,128)} %fusion.44, pred[1024,64]{0,1:T(8,128)(4,1)S(1)} %iota_compare_fusion.1, bf16[64,16,512]{2,1,0:T(8,128)(2,1)} %get-tuple-element.16, bf16[1024,16]{0,1:T(8,128)(2,1)S(1)} %add_convert_fusion.3), kind=kOutput, calls=%fused_computation.28 | convolution fusion | flops 1076887552 | bytes 5341184 | tf_op jit(solution)/shard_map/dot_general | solution.py:118
  113.8 1.1 fusion.41
  114.9 3.2 %copy.73 = f32[1024,4,64]{2,0,1:T(8,128)} copy(f32[1024,4,64]{0,2,1:T(8,128)} %get-tuple-element.13) | data formatting | bytes 2097152
  118.1 1.9 copy.72
  120.0 4.1 %subtract_convert_fusion = (bf16[1024,4,64]{2,0,1:T(8,128)(2,1)S(1)}, bf16[1024,4,64]{2,0,1:T(8,128)(2,1)}) fusion(f32[1024,4,64]{2,0,1:T(8,128)} %copy.73, f32[1024,4,64]{2,0,1:T(8,128)} %copy.72, f32[1024,64]{1,0:T(8,128)} %copy.66, f32[1024,64]{1,0:T(8,128)} %copy.64), kind=kLoop, calls=%fused_computation.27 | loop fusion | flops 2097152 | bytes 3670016 | tf_op jit(solution)/shard_map/convert.2
  124.0 1.2 broadcast_in_dim.41
  125.2 11.7 %fusion.43 = (f32[4,1024]{1,0:T(4,128)S(1)}, f32[4,1024,1024]{1,2,0:T(8,128)}) fusion(pred[1024,1024]{0,1:T(8,128)(4,1)} %fusion.10, bf16[1024,4,128]{2,0,1:T(8,128)(2,1)} %bitcast.59, bf16[1024,4,64]{2,0,1:T(8,128)(2,1)} %get-tuple-element.12, bf16[1024,4,64]{2,0,1:T(8,128)(2,1)S(1)} %get-tuple-element.11), kind=kOutput, calls=%fused_computation.90 | convolution fusion | flops 1092617216 | bytes 19939328 | tf_op jit(solution)/shard_map/sub | solution.py:145
  136.9 1.2 broadcast_in_dim.35
  138.1 7.1 %fusion.17 = bf16[4,128,1024]{2,1,0:T(8,128)(2,1)S(1)} fusion(bf16[1024,4,128]{0,2,1:T(8,128)(2,1)S(1)} %bitcast.60, f32[4,1024,1024]{1,2,0:T(8,128)} %get-tuple-element.24, f32[4,1024]{1,0:T(4,128)S(1)} %get-tuple-element.23), kind=kOutput, calls=%fused_computation.33 | convolution fusion | flops 1082654720 | bytes 18890752 | tf_op jit(solution)/shard_map/hqk,khd->qhd/dot_general | solution.py:147
  145.2 4.3 %convolution_convert_fusion = bf16[1024,2048]{1,0:T(8,128)(2,1)} fusion(bf16[1024,512]{0,1:T(8,128)(2,1)S(1)} %bitcast.68, bf16[512,2048]{1,0:T(8,128)(2,1)S(1)} %copy-done), kind=kOutput, calls=%fused_computation.21 | convolution fusion | flops 2149580800 | bytes 7340032 | tf_op jit(solution)/shard_map/dot_general | solution.py:150
  149.5 47.5 %reduce-scatter.2.cloned.1.call-done = bf16[1024,512]{1,0:T(8,128)(2,1)} async-done(((bf16[1024,2048]{1,0:T(8,128)(2,1)}), bf16[1024,512]{1,0:T(8,128)(2,1)}) %reduce-scatter.2.cloned.1.call-update) | async-done | bytes 1048592 | tf_op jit(solution)/shard_map/reduce_scatter | solution.py:155
  197.0 2.8 %add_convert_fusion = bf16[1024,512]{1,0:T(8,128)(2,1)} fusion(bf16[1024,512]{1,0:T(8,128)(2,1)} %reduce-scatter.2.cloned.1.call-done, bf16[1024,2048]{1,0:T(8,128)(2,1)} %param.12, s32[]{:T(128)S(6)} %select_n.57), kind=kLoop, calls=%fused_computation.25 | loop fusion | flops 2097152 | bytes 3145732 | tf_op jit(solution)/shard_map/convert_element_type | solution.py:159
  (36 shorter events, 0.6 us)
Async XLA Ops:
  6.5 138.6 %copy-start = (bf16[512,2048]{1,0:T(8,128)(2,1)S(1)}, bf16[512,2048]{1,0:T(8,128)(2,1)}, u32[]{:S(2)}) copy-start(bf16[512,2048]{1,0:T(8,128)(2,1)} %param.17) | copy-start | bytes 6291460
  6.5 27.4 %copy-start.1 = (bf16[16,512,16]{1,2,0:T(8,128)(2,1)S(1)}, bf16[16,512,16]{1,2,0:T(8,128)(2,1)}, u32[]{:S(2)}) copy-start(bf16[16,512,16]{1,2,0:T(8,128)(2,1)} %param.18) | copy-start | bytes 786436
  9.6 20.5 %all-to-all-start = ((s32[64,1,1]{2,1,0:T(1,128)}), s32[64,1,1]{2,1,0:T(1,128)S(1)}, u32[]{:S(2)}, u32[]{:S(2)}) async-start(s32[64,1,1]{2,1,0:T(1,128)} %copy.60), calls=%async_computation | async-start | bytes 65536 | tf_op jit(solution)/shard_map/all_to_all | solution.py:86
  37.4 14.1 %copy-start.6 = (f32[2048]{0:T(1024)S(1)}, f32[2048]{0:T(1024)}, u32[]{:S(2)}) copy-start(f32[2048]{0:T(1024)} %param.13) | copy-start | bytes 24580
  37.4 56.4 %all-to-all-start.1 = ((bf16[64,32,512]{2,1,0:T(8,128)(2,1)}), bf16[64,32,512]{2,1,0:T(8,128)(2,1)}, u32[]{:S(2)}, u32[]{:S(2)}) async-start(bf16[64,32,512]{2,1,0:T(8,128)(2,1)} %pad_maximum_fusion), calls=%async_computation.1 | async-start | bytes 4194304 | tf_op jit(solution)/shard_map/all_to_all | solution.py:92
  44.4 152.7 %reduce-scatter.2.cloned.1.call-start = ((), (), s32[]{:S(2)}) async-start(), calls=%async_computation.3 | async-start | bytes 5242880 | tf_op jit(solution)/shard_map/reduce_scatter | solution.py:155
  44.6 6.8 %copy-start.2 = (bf16[1024,2048]{1,0:T(8,128)(2,1)S(1)}, bf16[1024,2048]{1,0:T(8,128)(2,1)}, u32[]{:S(2)}) copy-start(bf16[1024,2048]{1,0:T(8,128)(2,1)} %param.12) | copy-start | bytes 12582916
  51.4 1.2 copy-start.8
  52.7 4.4 %copy-start.3 = (bf16[1024,2048]{1,0:T(8,128)(2,1)}, bf16[1024,2048]{1,0:T(8,128)(2,1)S(1)}, u32[]{:S(2)}) copy-start(bf16[1024,2048]{1,0:T(8,128)(2,1)S(1)} %fusion.4) | copy-start | bytes 12582916
  52.7 2.1 %copy-start.9 = (bf16[2048,256]{1,0:T(8,128)(2,1)S(1)}, bf16[2048,256]{1,0:T(8,128)(2,1)}, u32[]{:S(2)}) copy-start(bf16[2048,256]{1,0:T(8,128)(2,1)} %param.15) | copy-start | bytes 3145732
  54.8 2.3 %copy-start.7 = (bf16[2048,512]{1,0:T(8,128)(2,1)S(1)}, bf16[2048,512]{1,0:T(8,128)(2,1)}, u32[]{:S(2)}) copy-start(bf16[2048,512]{1,0:T(8,128)(2,1)} %param.14) | copy-start | bytes 6291460
  96.6 4.6 %copy-start.5 = (f32[1024,256]{0,1:T(8,128)S(1)}, f32[1024,256]{0,1:T(8,128)}, u32[]{:S(2)}) copy-start(f32[1024,256]{0,1:T(8,128)} %fusion.45) | copy-start | bytes 3145732
  99.5 4.6 %collective-permute-start = (f32[1024,16]{0,1:T(8,128)S(1)}, f32[1024,16]{0,1:T(8,128)S(1)}, u32[]{:S(2)}, u32[]{:S(2)}) collective-permute-start(f32[1024,16]{0,1:T(8,128)S(1)} %select_reduce_fusion), channel_id=1, source_target_pairs={{0,1},{1,0},{2,3},{3,2},{4,5},{5,4},{6,7},{7,6},{8,9},{9,8},{10,11... | collective-permute-start | bytes 196616 | tf_op jit(solution)/shard_map/ppermute | solution.py:112
  104.2 6.3 %collective-permute-start.1 = (f32[1024,16]{0,1:T(8,128)S(1)}, f32[1024,16]{0,1:T(8,128)S(1)}, u32[]{:S(2)}, u32[]{:S(2)}) collective-permute-start(f32[1024,16]{0,1:T(8,128)S(1)} %add.88), channel_id=1, source_target_pairs={{0,2},{1,3},{2,0},{3,1},{4,6},{5,7},{6,4},{7,5},{8,10},{9,11},{10,... | collective-permute-start | bytes 196616 | tf_op jit(solution)/shard_map/ppermute | solution.py:112
  120.0 4.1 %copy-start.4 = (bf16[1024,2,128]{2,0,1:T(8,128)(2,1)S(1)}, bf16[1024,2,128]{2,0,1:T(8,128)(2,1)}, u32[]{:S(2)}) copy-start(bf16[1024,2,128]{2,0,1:T(8,128)(2,1)} %copy.67) | copy-start | bytes 1572868
Sparse Core Ops, SparseCore 0:
  149.6 47.3 reduce-scatter.1

commit v2 on v1

--- a/solution.py
+++ b/solution.py
@@ -1,6 +1,9 @@
 import jax
 import jax.numpy as jnp
+import functools
 from jax import lax
+from jax.experimental import pallas as pl
+from jax.experimental.pallas import tpu as pltpu
 from jax.sharding import PartitionSpec as P
 
 HEAD_WIDTH = 128
@@ -44,11 +47,129 @@
     prompt_row = jnp.sum(request_hot * is_prompt[None, :], 1)
     offset_row = jnp.sum(request_hot * offset_req[None, :], 1)
     token_positions = (row_ids + offset_row).astype(jnp.float32)
-    visible = (group_row[:, None] == group_row[None, :]) & (row_ids[None, :] <= row_ids[:, None])
-    visible = visible & (
-        (request_row[:, None] == request_row[None, :]) | (prompt_row[None, :] == 1)
-    )
-    return (request_hot, starts, visible, token_positions, row_ids)
+    group_ids = jnp.arange(3, dtype=jnp.int32)
+    group_hot = (groups[None, :] == group_ids[:, None]).astype(jnp.int32)
+    prompt_start = jnp.sum((starts * is_prompt)[None, :] * group_hot, 1)
+    prompt_len = jnp.sum((lengths * is_prompt)[None, :] * group_hot, 1)
+    rows = (request_row, group_row, prompt_row, prompt_start, prompt_len)
+    return (request_hot, starts, rows, token_positions, row_ids)
+
+
+BLOCK = 128
+
+
+def attend_kernel(
+    q_ref, k_ref, v_ref, kp_ref, vp_ref, bias_ref, wo_ref, res_ref, out_ref,
+    send_buf, recv_buf, send_sems, recv_sems, *, tp_count, heads, kv_heads, n_blocks
+):
+    me = lax.axis_index("tp")
+    row_dev = lax.axis_index("req")
+    piece = out_ref.shape[1]
+    barrier = pltpu.get_barrier_semaphore()
+    for k in range(1, tp_count):
+        peer = lax.rem(me + k, tp_count)
+        pl.semaphore_signal(
+            barrier, inc=1, device_id=(row_dev, peer), device_id_type=pl.DeviceIdType.MESH
+        )
+    pl.semaphore_wait(barrier, tp_count - 1)
+    rep = heads // kv_heads
+
+    def copy_of(b, k, source):
+        peer = lax.rem(me + k, tp_count)
+        col = pl.multiple_of(peer * piece, piece)
+        row = pl.multiple_of(b * BLOCK, BLOCK)
+        return pltpu.make_async_remote_copy(
+            src_ref=send_buf.at[b, :, pl.ds(col, piece)],
+            dst_ref=recv_buf.at[source, pl.ds(row, BLOCK)],
+            send_sem=send_sems.at[b * tp_count + k],
+            recv_sem=recv_sems.at[source * n_blocks + b],
+            device_id=(row_dev, peer),
+            device_id_type=pl.DeviceIdType.MESH,
+        )
+
+    def block_body(b, carry):
+        row = pl.multiple_of(b * BLOCK, BLOCK)
+        bias = bias_ref[b]
+        outs = []
+        for h in range(heads):
+            g = h // rep
+            qh = q_ref[pl.ds(row, BLOCK), pl.ds(h * 128, 128)]
+            kw = k_ref[pl.ds(row, 2 * BLOCK), pl.ds(g * 128, 128)]
+            vw = v_ref[pl.ds(row, 2 * BLOCK), pl.ds(g * 128, 128)]
+            kp = kp_ref[:, pl.ds(g * 128, 128)]
+            vp = vp_ref[:, pl.ds(g * 128, 128)]
+            keys = jnp.concatenate([kw, kp], 0)
+            vals = jnp.concatenate([vw, vp], 0)
+            s = lax.dot_general(
+                qh, keys, (((1,), (1,)), ((), ())), preferred_element_type=jnp.float32
+            ) / HEAD_WIDTH**0.5
+            s = s + bias
+            m = jnp.max(s, -1, keepdims=True)
+            w = jnp.exp(s - m)
+            p = (w / jnp.sum(w, -1, keepdims=True)).astype(jnp.bfloat16)
+            outs.append(
+                jnp.dot(p, vals, preferred_element_type=jnp.float32).astype(jnp.bfloat16)
+            )
+        att = jnp.concatenate(outs, 1)
+        part = jnp.dot(att, wo_ref[...], preferred_element_type=jnp.float32)
+        send_buf[b] = part.astype(jnp.bfloat16)
+        for k in range(1, tp_count):
+            copy_of(b, k, me).start()
+        return carry
+
+    lax.fori_loop(0, n_blocks, block_body, 0)
+
+    def wait_body(b, carry):
+        for k in range(1, tp_count):
+            copy_of(b, k, me).wait_send()
+            source = lax.rem(me + tp_count - k, tp_count)
+            copy_of(b, k, source).wait_recv()
+        return carry
+
+    lax.fori_loop(0, n_blocks, wait_body, 0)
+    own = pl.multiple_of(me * piece, piece)
+
+    def finish_body(b, carry):
+        row = pl.multiple_of(b * BLOCK, BLOCK)
+        total = res_ref[pl.ds(row, BLOCK), :].astype(jnp.float32)
+        total = total + send_buf[b, :, pl.ds(own, piece)].astype(jnp.float32)
+        for k in range(1, tp_count):
+            source = lax.rem(me + tp_count - k, tp_count)
+            total = total + recv_buf[source, pl.ds(row, BLOCK), :].astype(jnp.float32)
+        out_ref[pl.ds(row, BLOCK), :] = total.astype(out_ref.dtype)
+        return carry
+
+    lax.fori_loop(0, n_blocks, finish_body, 0)
+
+
+def attend_and_reduce(q, k_pad, v_pad, k_prompt, v_prompt, bias, wo, residual, tp_count):
+    rows, q_width = q.shape
+    n_blocks = rows // BLOCK
+    piece = residual.shape[1]
+    width = wo.shape[1]
+    kernel = functools.partial(
+        attend_kernel,
+        tp_count=tp_count,
+        heads=q_width // HEAD_WIDTH,
+        kv_heads=k_pad.shape[1] // HEAD_WIDTH,
+        n_blocks=n_blocks,
+    )
+    vmem = pltpu.MemorySpace.VMEM
+    return pl.pallas_call(
+        kernel,
+        out_shape=jax.ShapeDtypeStruct((rows, piece), jnp.bfloat16),
+        in_specs=[pl.BlockSpec(memory_space=vmem)] * 8,
+        out_specs=pl.BlockSpec(memory_space=vmem),
+        scratch_shapes=[
+            pltpu.VMEM((n_blocks, BLOCK, width), jnp.bfloat16),
+            pltpu.VMEM((tp_count, rows, piece), jnp.bfloat16),
+            pltpu.SemaphoreType.DMA((n_blocks * tp_count,)),
+            pltpu.SemaphoreType.DMA((tp_count * n_blocks,)),
+        ],
+        compiler_params=pltpu.CompilerParams(
+            collective_id=0, has_side_effects=True, vmem_limit_bytes=48 * 1024 * 1024
+        ),
+    )(q, k_pad, v_pad, k_prompt, v_prompt, bias, wo, residual)
 
 
 def per_device(
@@ -74,7 +195,7 @@
     groups = prompt_group_per_request[0]
     adapters = adapter_per_request[0]
     req_slots = lengths.shape[0]
-    request_hot, starts, visible, token_positions, row_ids = layout(lengths, groups, tok_rows)
+    request_hot, starts, row_info, token_positions, row_ids = layout(lengths, groups, tok_rows)
     adapters_per_part = adapter_down_maps.shape[0]
     rank_extent = adapter_down_maps.shape[2]
     slots = adapter_table_slot[adapters]
@@ -134,29 +255,76 @@
         .astype(jnp.bfloat16)
         .reshape(tok_rows, kv_local, HEAD_WIDTH)
     )
-    key_head_rows = jnp.repeat(key_head_rows, heads_local // kv_local, axis=1)
-    value_head_rows = jnp.repeat(value_head_rows, heads_local // kv_local, axis=1)
-    scores = (
-        jnp.einsum("qhd,khd->hqk", query_heads, key_head_rows, preferred_element_type=jnp.float32)
-        / HEAD_WIDTH**0.5
-    )
-    scores = jnp.where(visible[None], scores, jnp.float32(-1e30))
-    row_max = jnp.max(scores, -1, keepdims=True)
-    weights = jnp.exp(scores - row_max)
-    probabilities = (weights / jnp.sum(weights, -1, keepdims=True)).astype(jnp.bfloat16)
-    attended = jnp.einsum(
-        "hqk,khd->qhd", probabilities, value_head_rows, preferred_element_type=jnp.float32
-    ).astype(jnp.bfloat16)
-    head_term = jnp.dot(
-        attended.reshape(tok_rows, heads_local * HEAD_WIDTH),
+    request_row, group_row, prompt_row, prompt_start, prompt_len = row_info
+    n_blocks = tok_rows // BLOCK
+    group_count = prompt_start.shape[0]
+    kv_width = kv_local * HEAD_WIDTH
+    key_flat = key_head_rows.reshape(tok_rows, kv_width)
+    value_flat = value_head_rows.reshape(tok_rows, kv_width)
+    front = jnp.zeros((BLOCK, kv_width), jnp.bfloat16)
+    k_pad = jnp.concatenate([front, key_flat], 0)
+    v_pad = jnp.concatenate([front, value_flat], 0)
+    clamp_start = jnp.clip(prompt_start, 0, tok_rows - LMAX)
+    extra = BLOCK - group_count * LMAX
+    k_prompt = jnp.concatenate(
+        [lax.dynamic_slice_in_dim(key_flat, clamp_start[g], LMAX, 0) for g in range(group_count)]
+        + [jnp.zeros((extra, kv_width), jnp.bfloat16)],
+        0,
+    )
+    v_prompt = jnp.concatenate(
+        [lax.dynamic_slice_in_dim(value_flat, clamp_start[g], LMAX, 0) for g in range(group_count)]
+        + [jnp.zeros((extra, kv_width), jnp.bfloat16)],
+        0,
+    )
+    def windows(values, fill):
+        padded = jnp.concatenate([jnp.full((BLOCK,), fill, values.dtype), values]).reshape(
+            n_blocks + 1, BLOCK
+        )
+        return jnp.concatenate([padded[:-1], padded[1:]], 1)
+
+    win_row = windows(row_ids, -1)
+    win_req = windows(request_row, -1)
+    win_grp = windows(group_row, -1)
+    win_prm = windows(prompt_row, 0)
+    q_row = row_ids.reshape(n_blocks, BLOCK)[:, :, None]
+    q_req = request_row.reshape(n_blocks, BLOCK)[:, :, None]
+    q_grp = group_row.reshape(n_blocks, BLOCK)[:, :, None]
+    win_vis = (
+        (win_row[:, None, :] >= 0)
+        & (win_grp[:, None, :] == q_grp)
+        & (win_row[:, None, :] <= q_row)
+        & ((win_req[:, None, :] == q_req) | (win_prm[:, None, :] == 1))
+    )
+    p_row = (clamp_start[:, None] + jnp.arange(LMAX, dtype=jnp.int32)[None, :]).reshape(-1)
+    p_lo = jnp.repeat(prompt_start, LMAX)
+    p_hi = jnp.repeat(prompt_start + prompt_len, LMAX)
+    p_grp = jnp.repeat(jnp.arange(group_count, dtype=jnp.int32), LMAX)
+    p_row = jnp.concatenate([p_row, jnp.zeros((extra,), jnp.int32)])
+    p_lo = jnp.concatenate([p_lo, jnp.ones((extra,), jnp.int32)])
+    p_hi = jnp.concatenate([p_hi, jnp.zeros((extra,), jnp.int32)])
+    p_grp = jnp.concatenate([p_grp, jnp.full((extra,), -1, jnp.int32)])
+    win_first = q_row[:, :1, :] - BLOCK
+    prompt_vis = (
+        (p_grp[None, None, :] == q_grp)
+        & (p_row[None, None, :] >= p_lo[None, None, :])
+        & (p_row[None, None, :] < p_hi[None, None, :])
+        & (p_row[None, None, :] < win_first)
+        & (p_row[None, None, :] <= q_row)
+    )
+    vis = jnp.concatenate([win_vis, prompt_vis], 2)
+    bias = jnp.where(vis, jnp.float32(0.0), jnp.float32(-1e30))
+    residual = lax.dynamic_slice_in_dim(tokens, tp_index * piece_width, piece_width, 1)
+    return attend_and_reduce(
+        query_heads.reshape(tok_rows, heads_local * HEAD_WIDTH),
+        k_pad,
+        v_pad,
+        k_prompt,
+        v_prompt,
+        bias,
         output_matrix,
-        preferred_element_type=jnp.float32,
-    )
-    summed = lax.psum_scatter(
-        head_term.astype(jnp.bfloat16), "tp", scatter_dimension=1, tiled=True
-    ).astype(jnp.float32)
-    residual = lax.dynamic_slice_in_dim(tokens, tp_index * piece_width, piece_width, 1)
-    return (residual.astype(jnp.float32) + summed).astype(jnp.bfloat16)
+        residual,
+        tp_count,
+    )
 
 
 def solution(mesh):

time: 208 us -> 190 us (0.913)
  Pallas kernels: 0 us -> 53.8 us
  waiting for transfers between devices: 86.6 us -> 35.3 us
  matrix products: 37.5 us -> 13.2 us
  between operations: 13.6 us -> 6.19 us
  local copies, waits for them, and re-layouts: 20.6 us -> 24.7 us
  starting transfers between devices: 24.4 us -> 27.8 us
  other arithmetic: 24 us -> 27.3 us
    pallas_call x0 -> x1, Pallas kernels: none -> 53.8 us  [attend_and_reduce(): pl.pallas_call(kernel, out_shape=jax.ShapeDtypeStruct((rows, piece), jnp....]
    reduce_scatter x1 -> x0, waiting for transfers between devices: 47.5 us -> none  [per_device(): lax.psum_scatter(head_term.astype(jnp.bfloat16), 'tp', scatter_dimension=...]
    sub x1 -> x0, matrix products: 11.7 us -> none  [per_device(): weights = jnp.exp(scores - row_max)]
    dot_general x2 -> x0, matrix products: 11.4 us -> none  [the longest x1 7.06 us: per_device(): jnp.einsum('hqk,khd->qhd', probabilities, value_head_rows, preferred_elem...]
    unnamed x22 -> x45, local copies, waits for them, and re-layouts: 5.31 us -> 11.1 us
    all_to_all x1, starting transfers between devices: 6.98 us -> 10.7 us  [per_device(): lax.all_to_all(maps_out, 'req', split_axis=0, concat_axis=0, tiled=True)]
    all_to_all x1, waiting for transfers between devices: 3.67 us -> 0.01 us  [per_device(): lax.all_to_all(wanted.reshape(req_count, 1), 'req', split_axis=0, concat_...]
    concatenate x1 -> x2, other arithmetic: 0.03 us -> 2.84 us  [apply_rotary(): jnp.concatenate([first_half * cosine - second * sine_part, second * cosin...]
  transfers between devices with their start and end apart: 5 -> 4, of which waited for: 5 -> 2; matrix products, arithmetic and copies ran while one was open for 12% -> 18% of each run, Pallas kernels for 0% -> 0%
where the time goes in v2:
time: 190 us; the launch traced here: 188 us
  Pallas kernels  53.8 us (28%)
  waiting for transfers between devices  35.3 us (19%)
  starting transfers between devices  27.8 us (15%)
  other arithmetic  27.3 us (14%)
  local copies, waits for them, and re-layouts  24.7 us (13%)
  matrix products  13.2 us (7%)
  between operations  6.19 us (3%)
    pallas_call x1, Pallas kernels, attend_and_reduce(): pl.pallas_call(kernel, out_shape=jax.ShapeDtypeStruct((rows, piece), jnp....  53.8 us
    all_to_all x1, waiting for transfers between devices, per_device(): lax.all_to_all(maps_out, 'req', split_axis=0, concat_axis=0, tiled=True)  33.7 us
    all_to_all x1, starting transfers between devices, per_device(): lax.all_to_all(wanted.reshape(req_count, 1), 'req', split_axis=0, concat_...  12 us
    unnamed x45, local copies, waits for them, and re-layouts  11.1 us
    all_to_all x1, starting transfers between devices, per_device(): lax.all_to_all(maps_out, 'req', split_axis=0, concat_axis=0, tiled=True)  10.7 us
    another operation x4, other arithmetic  5.51 us
    ppermute x2, starting transfers between devices, per_device(): partial_rank = partial_rank + lax.ppermute(partial_rank, 'tp', pairs)  5.15 us
    dot_general x1, matrix products, per_device(): jnp.dot(normalized_input, value_matrix, preferred_element_type=jnp.float32)  3.88 us
  transfers between devices with their start and end apart: 4, of which 2 were waited for; matrix products, arithmetic and copies ran while one was open for 18% of the time, Pallas kernels for 0%

profile of v2, /device:TPU:2, one launch (start us, length us, event | category | flops | bytes accessed | tf_op | source)
XLA Modules:
  0.0 188.4 jit_solution(12340122850842613919)
XLA Ops:
  0.0 0.8 fusion.21
  0.8 1.4 gather_fusion
  2.3 0.7 copy.42
  3.0 12.0 %all-to-all-start = ((s32[64,1,1]{2,1,0:T(1,128)}), s32[64,1,1]{2,1,0:T(1,128)S(1)}, u32[]{:S(2)}, u32[]{:S(2)}) async-start(s32[64,1,1]{2,1,0:T(1,128)} %copy.42), calls=%async_computation | async-start | bytes 65536 | tf_op jit(solution)/shard_map/all_to_all | solution.py:207
  15.1 0.7 copy.41
  16.0 0.8 select_bitcast_fusion
  16.8 0.7 select_bitcast_fusion.1
  17.6 0.9 select_reduce_fusion.5
  18.5 0.7 fusion.26
  19.1 0.8 select_reduce_fusion.1
  20.0 3.2 %fusion = f32[1024]{0:T(1024)S(1)} fusion(bf16[1024,2048]{1,0:T(8,128)(2,1)} %param.12), kind=kLoop, calls=%fused_computation.5 | loop fusion | flops 6290432 | bytes 4198400 | tf_op jit(solution)/shard_map/reduce_sum | solution.py:219
  23.4 1.0 fusion.2
  24.6 1.3 fusion.34
  25.9 0.6 copy-done.8
  26.7 0.5 copy-done.14
  27.4 0.7 fusion.32
  29.9 3.1 %multiply_cosine_fusion = (f32[1024,64]{1,0:T(8,128)}, f32[1024,64]{1,0:T(8,128)}) fusion(f32[64]{0:T(128)S(1)} %negate_power_fusion, f32[1024]{0:T(1024)S(1)} %add_convert_fusion.3), kind=kLoop, calls=%fused_computation.32 | loop fusion | flops 65536 | bytes 528640 | tf_op jit(solution)/shard_map/cos | solution.py:19
  34.9 1.3 copy.53
  36.1 1.3 copy.54
  37.5 1.2 reduce.1
  38.7 0.6 gather_fusion.1
  39.3 2.5 %gather_fusion.2 = bf16[64,16,512]{2,1,0:T(8,128)(2,1)} fusion(bf16[16,16,512]{2,1,0:T(8,128)(2,1)} %param.19, s32[1024]{0:T(1024)S(1)} %pad_clamp_fusion), kind=kCustom, calls=%fused_computation.2 | custom fusion | bytes 2097408 | tf_op jit(solution)/shard_map/gather | solution.py:211
  41.9 2.8 %pad_maximum_fusion = bf16[64,32,512]{2,1,0:T(8,128)(2,1)} fusion(bf16[64,16,512]{2,1,0:T(8,128)(2,1)} %gather_fusion.2, bf16[64,16,512]{2,1,0:T(8,128)(2,1)S(1)} %bitcast.73), kind=kLoop, calls=%fused_computation.9 | loop fusion | flops 4194304 | bytes 4194304 | tf_op jit(solution)/shard_map/concatenate | solution.py:212
  44.7 10.7 %all-to-all-start.1 = ((bf16[64,32,512]{2,1,0:T(8,128)(2,1)}), bf16[64,32,512]{2,1,0:T(8,128)(2,1)}, u32[]{:S(2)}, u32[]{:S(2)}) async-start(bf16[64,32,512]{2,1,0:T(8,128)(2,1)} %pad_maximum_fusion), calls=%async_computation.1 | async-start | bytes 4194304 | tf_op jit(solution)/shard_map/all_to_all | solution.py:213
  55.3 2.3 %subtract_convert_fusion.1 = (bf16[1024,2,64]{2,1,0:T(2,128)(2,1)S(1)}, bf16[1024,2,64]{2,1,0:T(2,128)(2,1)S(1)}) fusion(f32[1024,2,64]{2,1,0:T(2,128)} %copy.54, f32[1024,2,64]{2,1,0:T(2,128)} %copy.53, f32[1024,64]{1,0:T(8,128)S(1)} %copy-done.7, f32[1024,64]{1,0:T(8,128)S(1)} %copy-done.6), kind=kLoop, calls=%fused_computation.26 | loop fusion | flops 1048576 | bytes 2097152 | tf_op jit(solution)/shard_map/convert
  57.7 1.4 pad_maximum_fusion.2
  61.9 3.9 %convolution_convert_fusion = bf16[1024,256]{1,0:T(8,128)(2,1)S(1)} fusion(bf16[1024,2048]{1,0:T(8,128)(2,1)} %copy-done.8, bf16[2048,256]{1,0:T(8,128)(2,1)} %param.16), kind=kOutput, calls=%fused_computation.19 | convolution fusion | flops 1074003968 | bytes 5767168 | tf_op jit(solution)/shard_map/dot_general | solution.py:254
  66.1 0.3 compare_and_fusion
  66.6 0.6 or_and_fusion
  67.3 3.8 %fusion.33 = f32[1024,512]{0,1:T(8,128)} fusion(bf16[1024,2048]{1,0:T(8,128)(2,1)S(1)} %copy-done.9, bf16[2048,512]{1,0:T(8,128)(2,1)S(1)} %copy-done), kind=kOutput, calls=%fused_computation.110 | convolution fusion | flops 2147483648 | bytes 8388608 | tf_op jit(solution)/shard_map/dot_general | solution.py:243
  71.1 33.7 %all-to-all-done.1 = bf16[64,32,512]{2,1,0:T(8,128)(2,1)} async-done(((bf16[64,32,512]{2,1,0:T(8,128)(2,1)}), bf16[64,32,512]{2,1,0:T(8,128)(2,1)}, u32[]{:S(2)}, u32[]{:S(2)}) %all-to-all-start.1) | async-done | bytes 2097184 | tf_op jit(solution)/shard_map/all_to_all | solution.py:213
  104.8 1.7 fusion.29
  106.5 2.8 %select_reduce_fusion = f32[1024,16]{0,1:T(8,128)S(1)} fusion(pred[1024,64]{0,1:T(8,128)(4,1)S(1)} %iota_compare_fusion, bf16[64,16,512]{2,1,0:T(8,128)(2,1)S(1)} %get-tuple-element.19, bf16[1024,2048]{1,0:T(8,128)(2,1)} %copy-done.8, s32[]{:T(128)S(6)} %select_n.71), kind=kOutput, calls=%fused_computation.8 | convolution fusion | flops 1075822592 | bytes 2228228 | tf_op jit(solution)/shard_map/dot_general | solution.py:227
  109.3 1.7 collective-permute-start
  111.0 1.4 add_select_fusion.bias_ref
  112.3 1.6 collective-permute-done
  114.0 3.5 %collective-permute-start.1 = (f32[1024,16]{0,1:T(8,128)S(1)}, f32[1024,16]{0,1:T(8,128)S(1)}, u32[]{:S(2)}, u32[]{:S(2)}) collective-permute-start(f32[1024,16]{0,1:T(8,128)S(1)} %add.150), channel_id=1, source_target_pairs={{0,2},{1,3},{2,0},{3,1},{4,6},{5,7},{6,4},{7,5},{8,10},{9,11},{10,... | collective-permute-start | bytes 196616 | tf_op jit(solution)/shard_map/ppermute | solution.py:233
  117.5 1.3 constant_dynamic-slice_fusion.res_ref
  118.8 0.9 concatenate.95.k_ref
  119.6 0.9 concatenate.96.v_ref
  120.5 1.4 convert_add_fusion
  122.0 1.5 fusion.28
  123.5 2.8 %copy.51 = f32[1024,4,64]{2,1,0:T(4,128)} copy(f32[1024,4,64]{0,2,1:T(8,128)} %get-tuple-element.18) | data formatting | bytes 2097152
  126.2 2.7 %copy.52 = f32[1024,4,64]{2,1,0:T(4,128)} copy(f32[1024,4,64]{0,2,1:T(8,128)} %get-tuple-element.17) | data formatting | bytes 2097152
  128.9 3.0 %subtract_convert_fusion = (bf16[1024,4,64]{2,1,0:T(4,128)(2,1)S(1)}, bf16[1024,4,64]{2,1,0:T(4,128)(2,1)S(1)}) fusion(f32[1024,4,64]{2,1,0:T(4,128)} %copy.52, f32[1024,4,64]{2,1,0:T(4,128)} %copy.51, f32[1024,64]{1,0:T(8,128)} %get-tuple-element.30, f32[1024,64]{1,0:T(8,128)} %get-tuple-element.29), kind=kLoop, calls=%fused_computation.13 | loop fusion | flops 2097152 | bytes 3670016 | tf_op jit(solution)/shard_map/convert.2
  132.0 1.4 pad_maximum_fusion.1
  133.7 53.8 %shard_map.118 = bf16[1024,512]{1,0:T(8,128)(2,1)S(1)} custom-call(bf16[1024,512]{1,0:T(8,128)(2,1)S(1)} %bitcast.72, bf16[1152,256]{1,0:T(8,128)(2,1)S(1)} %copy-done.2, bf16[1152,256]{1,0:T(8,128)(2,1)S(1)} %copy-done.3, bf16[128,256]{1,0:T(8,128)(2,1)S(1)} %get-tuple-element.36.kp_ref, bf16[128,256]{1,0:T(8,128)(2,1)S(1)} %get-tuple-element.35.vp_ref, ...), custom_call_target="tpu_custom_call" | custom-call | tf_op jit(solution)/shard_map/pallas_call | solution.py:158
  187.5 1.0 copy.66
  (83 shorter events, 2.6 us)
Async XLA Ops:
  0.0 67.2 %copy-start = (bf16[2048,512]{1,0:T(8,128)(2,1)S(1)}, bf16[2048,512]{1,0:T(8,128)(2,1)}, u32[]{:S(2)}) copy-start(bf16[2048,512]{1,0:T(8,128)(2,1)} %param.14) | copy-start | bytes 6291460
  3.0 34.4 %all-to-all-start = ((s32[64,1,1]{2,1,0:T(1,128)}), s32[64,1,1]{2,1,0:T(1,128)S(1)}, u32[]{:S(2)}, u32[]{:S(2)}) async-start(s32[64,1,1]{2,1,0:T(1,128)} %copy.42), calls=%async_computation | async-start | bytes 65536 | tf_op jit(solution)/shard_map/all_to_all | solution.py:207
  19.9 3.5 %copy-start.5 = (bf16[1024,2048]{1,0:T(8,128)(2,1)S(1)}, bf16[1024,2048]{1,0:T(8,128)(2,1)}, u32[]{:S(2)}) copy-start(bf16[1024,2048]{1,0:T(8,128)(2,1)} %param.12) | copy-start | bytes 12582916
  19.9 3.4 %copy-start.16 = (f32[2048]{0:T(1024)S(1)}, f32[2048]{0:T(1024)}, u32[]{:S(2)}) copy-start(f32[2048]{0:T(1024)} %param.13) | copy-start | bytes 24580
  23.4 1.2 copy-start.17
  24.6 1.9 %copy-start.8 = (bf16[1024,2048]{1,0:T(8,128)(2,1)}, bf16[1024,2048]{1,0:T(8,128)(2,1)S(1)}, u32[]{:S(2)}) copy-start(bf16[1024,2048]{1,0:T(8,128)(2,1)S(1)} %fusion.2) | copy-start | bytes 12582916
  26.5 0.7 copy-start.14
  29.9 8.8 %copy-start.4 = (bf16[16,512,16]{1,2,0:T(8,128)(2,1)S(1)}, bf16[16,512,16]{1,2,0:T(8,128)(2,1)}, u32[]{:S(2)}) copy-start(bf16[16,512,16]{1,2,0:T(8,128)(2,1)} %param.18) | copy-start | bytes 786436
  44.7 10.7 %copy-start.6 = (f32[1024,64]{1,0:T(8,128)S(1)}, f32[1024,64]{1,0:T(8,128)}, u32[]{:S(2)}) copy-start(f32[1024,64]{1,0:T(8,128)} %get-tuple-element.29) | copy-start | bytes 786436
  44.7 10.7 %copy-start.7 = (f32[1024,64]{1,0:T(8,128)S(1)}, f32[1024,64]{1,0:T(8,128)}, u32[]{:S(2)}) copy-start(f32[1024,64]{1,0:T(8,128)} %get-tuple-element.30) | copy-start | bytes 786436
  44.7 60.1 %all-to-all-start.1 = ((bf16[64,32,512]{2,1,0:T(8,128)(2,1)}), bf16[64,32,512]{2,1,0:T(8,128)(2,1)}, u32[]{:S(2)}, u32[]{:S(2)}) async-start(bf16[64,32,512]{2,1,0:T(8,128)(2,1)} %pad_maximum_fusion), calls=%async_computation.1 | async-start | bytes 4194304 | tf_op jit(solution)/shard_map/all_to_all | solution.py:213
  57.7 4.2 %copy-start.15 = (s32[8,128]{1,0:T(8,128)S(1)}, s32[8,128]{1,0:T(8,128)}, u32[]{:S(2)}) copy-start(s32[8,128]{1,0:T(8,128)} %constant.106.clone.1) | copy-start | bytes 12292
  59.2 6.6 %copy-start.10 = (bf16[128,8,2,128]{3,1,2,0:T(8,128)(2,1)}, bf16[128,8,2,128]{3,1,2,0:T(8,128)(2,1)S(1)}, u32[]{:S(2)}) copy-start(bf16[128,8,2,128]{3,1,2,0:T(8,128)(2,1)S(1)} %copy.64) | copy-start | bytes 1572868
  61.9 5.3 %copy-start.9 = (bf16[1024,2048]{1,0:T(8,128)(2,1)S(1)}, bf16[1024,2048]{1,0:T(8,128)(2,1)}, u32[]{:S(2)}) copy-start(bf16[1024,2048]{1,0:T(8,128)(2,1)} %copy-done.8) | copy-start | bytes 12582916
  65.8 0.8 copy-start.12
  109.3 9.5 %copy-start.11 = (bf16[128,8,2,128]{3,1,2,0:T(8,128)(2,1)S(1)}, bf16[128,8,2,128]{3,1,2,0:T(8,128)(2,1)}, u32[]{:S(2)}) copy-start(bf16[128,8,2,128]{3,1,2,0:T(8,128)(2,1)} %copy-done.10) | copy-start | bytes 1572868
  109.3 4.6 %collective-permute-start = (f32[1024,16]{0,1:T(8,128)S(1)}, f32[1024,16]{0,1:T(8,128)S(1)}, u32[]{:S(2)}, u32[]{:S(2)}) collective-permute-start(f32[1024,16]{0,1:T(8,128)S(1)} %select_reduce_fusion), channel_id=1, source_target_pairs={{0,1},{1,0},{2,3},{3,2},{4,5},{5,4},{6,7},{7,6},{8,9},{9,8},{10,11... | collective-permute-start | bytes 196616 | tf_op jit(solution)/shard_map/ppermute | solution.py:233
  112.3 7.3 %copy-start.13 = (bf16[1024,256]{1,0:T(8,128)(2,1)S(1)}, bf16[1024,256]{1,0:T(8,128)(2,1)}, u32[]{:S(2)}) copy-start(bf16[1024,256]{1,0:T(8,128)(2,1)} %copy-done.12) | copy-start | bytes 1572868
  114.0 6.6 %copy-start.18 = (f32[1024,512]{0,1:T(8,128)S(1)}, f32[1024,512]{0,1:T(8,128)}, u32[]{:S(2)}) copy-start(f32[1024,512]{0,1:T(8,128)} %fusion.33) | copy-start | bytes 6291460
  114.0 6.5 %collective-permute-start.1 = (f32[1024,16]{0,1:T(8,128)S(1)}, f32[1024,16]{0,1:T(8,128)S(1)}, u32[]{:S(2)}, u32[]{:S(2)}) collective-permute-start(f32[1024,16]{0,1:T(8,128)S(1)} %add.150), channel_id=1, source_target_pairs={{0,2},{1,3},{2,0},{3,1},{4,6},{5,7},{6,4},{7,5},{8,10},{9,11},{10,... | collective-permute-start | bytes 196616 | tf_op jit(solution)/shard_map/ppermute | solution.py:233
  131.9 1.6 copy-start.1
  131.9 1.6 copy-start.2
  132.0 1.7 copy-start.3

commit v3 on v2

--- a/solution.py
+++ b/solution.py
@@ -170,6 +170,87 @@
             collective_id=0, has_side_effects=True, vmem_limit_bytes=48 * 1024 * 1024
         ),
     )(q, k_pad, v_pad, k_prompt, v_prompt, bias, wo, residual)
+
+
+def exchange_kernel(wanted_ref, table_ref, out_ref, staging, landing, send_sems, recv_sems):
+    me = lax.axis_index("req")
+    col = lax.axis_index("tp")
+    count = lax.axis_size("req")
+    barrier = pltpu.get_barrier_semaphore()
+
+    def greet(k, carry):
+        peer = lax.rem(me + k, count)
+        pl.semaphore_signal(
+            barrier, inc=1, device_id=(peer, col), device_id_type=pl.DeviceIdType.MESH
+        )
+        return carry
+
+    lax.fori_loop(1, count, greet, 0)
+    pl.semaphore_wait(barrier, count - 1)
+
+    def send(k, carry):
+        dest = lax.rem(me + k, count)
+        staging[dest] = table_ref[wanted_ref[dest]]
+        pltpu.make_async_remote_copy(
+            src_ref=staging.at[dest],
+            dst_ref=landing.at[me],
+            send_sem=send_sems.at[k],
+            recv_sem=recv_sems.at[k],
+            device_id=(dest, col),
+            device_id_type=pl.DeviceIdType.MESH,
+        ).start()
+        return carry
+
+    lax.fori_loop(1, count, send, 0)
+    out_ref[me] = table_ref[wanted_ref[me]]
+
+    def finish(k, carry):
+        dest = lax.rem(me + k, count)
+        source = lax.rem(me + count - k, count)
+        pltpu.make_async_remote_copy(
+            src_ref=staging.at[dest],
+            dst_ref=landing.at[me],
+            send_sem=send_sems.at[k],
+            recv_sem=recv_sems.at[k],
+            device_id=(dest, col),
+            device_id_type=pl.DeviceIdType.MESH,
+        ).wait_send()
+        pltpu.make_async_remote_copy(
+            src_ref=staging.at[source],
+            dst_ref=landing.at[source],
+            send_sem=send_sems.at[k],
+            recv_sem=recv_sems.at[k],
+            device_id=(source, col),
+            device_id_type=pl.DeviceIdType.MESH,
+        ).wait_recv()
+        out_ref[source] = landing[source]
+        return carry
+
+    lax.fori_loop(1, count, finish, 0)
+
+
+def exchange_maps(wanted, table):
+    count = wanted.shape[0]
+    slab = table.shape[1:]
+    vmem = pltpu.MemorySpace.VMEM
+    return pl.pallas_call(
+        exchange_kernel,
+        out_shape=jax.ShapeDtypeStruct((count,) + slab, table.dtype),
+        in_specs=[
+            pl.BlockSpec(memory_space=pltpu.MemorySpace.SMEM),
+            pl.BlockSpec(memory_space=vmem),
+        ],
+        out_specs=pl.BlockSpec(memory_space=vmem),
+        scratch_shapes=[
+            pltpu.VMEM((count,) + slab, table.dtype),
+            pltpu.VMEM((count,) + slab, table.dtype),
+            pltpu.SemaphoreType.DMA((count,)),
+            pltpu.SemaphoreType.DMA((count,)),
+        ],
+        compiler_params=pltpu.CompilerParams(
+            collective_id=1, has_side_effects=True, vmem_limit_bytes=32 * 1024 * 1024
+        ),
+    )(wanted, table)
 
 
 def per_device(
@@ -207,10 +288,8 @@
     wanted_in = lax.all_to_all(
         wanted.reshape(req_count, 1), "req", split_axis=0, concat_axis=0, tiled=True
     ).reshape(req_count)
-    down_sel = jnp.transpose(adapter_down_maps[wanted_in], (0, 2, 1))
-    up_sel = adapter_up_maps[wanted_in]
-    maps_out = jnp.concatenate([down_sel, up_sel], 1)
-    maps_in = lax.all_to_all(maps_out, "req", split_axis=0, concat_axis=0, tiled=True)
+    table = jnp.concatenate([jnp.transpose(adapter_down_maps, (0, 2, 1)), adapter_up_maps], 1)
+    maps_in = exchange_maps(wanted_in, table)
     down_in = maps_in[:, :rank_extent, :].reshape(req_count * rank_extent, piece_width)
     up_in = maps_in[:, rank_extent:, :].reshape(req_count * rank_extent, piece_width)
     float_tok = tokens.astype(jnp.float32)

time: 190 us -> 200 us (1.053)
  Pallas kernels: 53.8 us -> 110 us
  waiting for transfers between devices: 35.3 us -> 1.76 us
  starting transfers between devices: 27.8 us -> 16.6 us
    pallas_call x0 -> x1, Pallas kernels: none -> 56.5 us  [exchange_maps(): pl.pallas_call(exchange_kernel, out_shape=jax.ShapeDtypeStruct((count,) +...]
    all_to_all x1 -> x0, waiting for transfers between devices: 33.7 us -> none  [per_device(): lax.all_to_all(maps_out, 'req', split_axis=0, concat_axis=0, tiled=True)]
    all_to_all x1 -> x0, starting transfers between devices: 10.7 us -> none  [per_device(): lax.all_to_all(maps_out, 'req', split_axis=0, concat_axis=0, tiled=True)]
    gather x2 -> x0, local copies, waits for them, and re-layouts: 3.15 us -> none  [the longest x1 2.53 us: per_device(): up_sel = adapter_up_maps[wanted_in]]
    dot_general x1, matrix products: 3.88 us -> 1.26 us  [per_device(): jnp.dot(normalized_input, value_matrix, preferred_element_type=jnp.float32)]
    dot_general x1, matrix products: 3.81 us -> 5.91 us  [per_device(): jnp.dot(normalized_input, query_matrix, preferred_element_type=jnp.float32)]
    unnamed x45 -> x61, local copies, waits for them, and re-layouts: 11.1 us -> 12.2 us
  transfers between devices with their start and end apart: 4 -> 3, of which waited for: 2 -> 1; matrix products, arithmetic and copies ran while one was open for 18% -> 21% of each run, Pallas kernels for 0% -> 0%
where the time goes in v3:
time: 200 us
  Pallas kernels  110 us (55%)
  other arithmetic  29.2 us (15%)
  local copies, waits for them, and re-layouts  23.1 us (12%)
  starting transfers between devices  16.6 us (8%)
  matrix products  12.7 us (6%)
  between operations  6.02 us (3%)
    pallas_call x1, Pallas kernels, exchange_maps(): pl.pallas_call(exchange_kernel, out_shape=jax.ShapeDtypeStruct((count,) +...  56.5 us
    pallas_call x1, Pallas kernels, attend_and_reduce(): pl.pallas_call(kernel, out_shape=jax.ShapeDtypeStruct((rows, piece), jnp....  53.7 us
    unnamed x61, local copies, waits for them, and re-layouts  12.2 us
    all_to_all x1, starting transfers between devices, per_device(): lax.all_to_all(wanted.reshape(req_count, 1), 'req', split_axis=0, concat_...  12 us
    another operation x4, other arithmetic  6.01 us
    dot_general x1, matrix products, per_device(): jnp.dot(normalized_input, query_matrix, preferred_element_type=jnp.float32)  5.91 us
    ppermute x2, starting transfers between devices, per_device(): partial_rank = partial_rank + lax.ppermute(partial_rank, 'tp', pairs)  4.63 us
  transfers between devices with their start and end apart: 3, of which 1 were waited for; matrix products, arithmetic and copies ran while one was open for 21% of the time, Pallas kernels for 0%

profile of v3, /device:TPU:2, one launch (start us, length us, event | category | flops | bytes accessed | tf_op | source)
XLA Modules:
  0.0 199.6 jit_solution(15784498234349536622)
XLA Ops:
  0.0 0.8 fusion.21
  0.8 1.4 gather_fusion
  2.3 0.7 copy.44
  3.0 12.0 %all-to-all-start = ((s32[64,1,1]{2,1,0:T(1,128)}), s32[64,1,1]{2,1,0:T(1,128)S(1)}, u32[]{:S(2)}, u32[]{:S(2)}) async-start(s32[64,1,1]{2,1,0:T(1,128)} %copy.44), calls=%async_computation | async-start | bytes 65536 | tf_op jit(solution)/shard_map/all_to_all | solution.py:288
  15.0 0.7 copy.43
  16.0 0.8 select_bitcast_fusion
  16.8 0.7 select_bitcast_fusion.1
  17.5 0.9 select_reduce_fusion.5
  18.4 0.8 select_reduce_fusion.7
  24.1 0.7 iota_add_fusion
  25.4 0.7 fusion.25
  26.6 1.4 select_reduce_fusion.1
  28.0 3.2 %fusion = f32[1024]{0:T(1024)S(1)} fusion(bf16[1024,2048]{1,0:T(8,128)(2,1)} %param.12), kind=kLoop, calls=%fused_computation.3 | loop fusion | flops 6290432 | bytes 4198400 | tf_op jit(solution)/shard_map/reduce_sum | solution.py:298
  31.4 1.0 fusion.2
  32.7 1.3 fusion.33
  34.0 0.7 copy-done.7
  34.6 1.0 fusion.29
  35.7 1.4 copy.53
  37.1 2.2 %copy.54 = f32[1024,2,64]{2,1,0:T(2,128)} copy(f32[1024,2,64]{0,2,1:T(8,128)} %get-tuple-element.21) | data formatting | bytes 1048576
  39.3 1.9 multiply_cosine_fusion
  41.2 2.8 %subtract_convert_fusion.1 = (bf16[1024,2,64]{2,1,0:T(2,128)(2,1)S(1)}, bf16[1024,2,64]{2,1,0:T(2,128)(2,1)S(1)}) fusion(f32[1024,2,64]{2,1,0:T(2,128)} %copy.54, f32[1024,2,64]{2,1,0:T(2,128)S(1)} %copy.53, f32[1024,64]{1,0:T(8,128)S(1)} %get-tuple-element.30, f32[1024,64]{1,0:T(8,128)S(1)} %get-tuple-element.29), kind=kLoop, calls=%fused_computation.23 | loop fusion | flops 1048576 | bytes 2097152 | tf_op jit(solution)/shard_map/convert
  44.1 1.4 pad_maximum_fusion.2
  45.6 1.3 convolution_convert_fusion
  48.8 0.6 constant_dynamic-slice_fusion.3
  49.4 0.7 iota_compare_fusion
  50.1 5.9 %fusion.32 = f32[1024,512]{0,1:T(8,128)} fusion(bf16[1024,2048]{1,0:T(8,128)(2,1)} %copy-done.7, bf16[2048,512]{1,0:T(8,128)(2,1)S(1)} %copy-done), kind=kOutput, calls=%fused_computation.105 | convolution fusion | flops 2147483648 | bytes 8388608 | tf_op jit(solution)/shard_map/dot_general | solution.py:322
  56.6 1.0 pad_maximum_fusion.1.table_ref
  58.2 0.6 or_and_fusion
  58.8 0.8 maximum_maximum_fusion.1
  59.6 1.2 reduce.1.wanted_ref
  60.9 56.5 %shard_map.118 = bf16[64,32,512]{2,1,0:T(8,128)(2,1)S(1)} custom-call(s32[64]{0:T(128)S(1)} %reduce.1.wanted_ref, bf16[16,32,512]{2,1,0:T(8,128)(2,1)S(1)} %pad_maximum_fusion.1.table_ref), custom_call_target="tpu_custom_call" | custom-call | tf_op jit(solution)/shard_map/pallas_call | solution.py:236
  117.6 0.6 copy-done.14
  118.2 2.8 %select_reduce_fusion = f32[1024,16]{0,1:T(8,128)S(1)} fusion(pred[1024,64]{0,1:T(8,128)(4,1)S(1)} %copy-done.14, bf16[64,16,512]{2,1,0:T(8,128)(2,1)S(1)} %get-tuple-element.19, bf16[1024,2048]{1,0:T(8,128)(2,1)} %copy-done.7, s32[]{:T(128)S(6)} %select_n.60), kind=kOutput, calls=%fused_computation.6 | convolution fusion | flops 1075822592 | bytes 2228228 | tf_op jit(solution)/shard_map/dot_general | solution.py:306
  121.0 1.4 collective-permute-start
  122.4 1.4 add_select_fusion.bias_ref
  123.8 1.8 collective-permute-done
  125.5 3.3 %collective-permute-start.1 = (f32[1024,16]{0,1:T(8,128)S(1)}, f32[1024,16]{0,1:T(8,128)S(1)}, u32[]{:S(2)}, u32[]{:S(2)}) collective-permute-start(f32[1024,16]{0,1:T(8,128)S(1)} %add.138), channel_id=1, source_target_pairs={{0,2},{1,3},{2,0},{3,1},{4,6},{5,7},{6,4},{7,5},{8,10},{9,11},{10,... | collective-permute-start | bytes 196616 | tf_op jit(solution)/shard_map/ppermute | solution.py:312
  128.8 1.3 constant_dynamic-slice_fusion.res_ref
  130.1 0.9 concatenate.95.k_ref
  131.0 0.9 concatenate.96.v_ref
  131.9 1.4 convert_add_fusion
  133.3 1.5 fusion.27
  134.8 2.7 %copy.51 = f32[1024,4,64]{2,1,0:T(4,128)} copy(f32[1024,4,64]{0,2,1:T(8,128)} %get-tuple-element.18) | data formatting | bytes 2097152
  137.5 2.7 %copy.52 = f32[1024,4,64]{2,1,0:T(4,128)} copy(f32[1024,4,64]{0,2,1:T(8,128)} %get-tuple-element.17) | data formatting | bytes 2097152
  140.2 3.0 %subtract_convert_fusion = (bf16[1024,4,64]{2,1,0:T(4,128)(2,1)S(1)}, bf16[1024,4,64]{2,1,0:T(4,128)(2,1)S(1)}) fusion(f32[1024,4,64]{2,1,0:T(4,128)} %copy.52, f32[1024,4,64]{2,1,0:T(4,128)} %copy.51, f32[1024,64]{1,0:T(8,128)} %copy-done.6, f32[1024,64]{1,0:T(8,128)} %copy-done.5), kind=kLoop, calls=%fused_computation.10 | loop fusion | flops 2097152 | bytes 3670016 | tf_op jit(solution)/shard_map/convert.2
  143.2 1.4 pad_maximum_fusion
  144.9 53.7 %shard_map.119 = bf16[1024,512]{1,0:T(8,128)(2,1)S(1)} custom-call(bf16[1024,512]{1,0:T(8,128)(2,1)S(1)} %bitcast.68, bf16[1152,256]{1,0:T(8,128)(2,1)S(1)} %copy-done.2, bf16[1152,256]{1,0:T(8,128)(2,1)S(1)} %copy-done.3, bf16[128,256]{1,0:T(8,128)(2,1)S(1)} %get-tuple-element.36.kp_ref, bf16[128,256]{1,0:T(8,128)(2,1)S(1)} %get-tuple-element.35.vp_ref, ...), custom_call_target="tpu_custom_call" | custom-call | tf_op jit(solution)/shard_map/pallas_call | solution.py:158
  198.6 1.0 copy.66
  (94 shorter events, 4.8 us)
Async XLA Ops:
  0.0 50.1 %copy-start = (bf16[2048,512]{1,0:T(8,128)(2,1)S(1)}, bf16[2048,512]{1,0:T(8,128)(2,1)}, u32[]{:S(2)}) copy-start(bf16[2048,512]{1,0:T(8,128)(2,1)} %param.14) | copy-start | bytes 6291460
  3.0 56.6 %all-to-all-start = ((s32[64,1,1]{2,1,0:T(1,128)}), s32[64,1,1]{2,1,0:T(1,128)S(1)}, u32[]{:S(2)}, u32[]{:S(2)}) async-start(s32[64,1,1]{2,1,0:T(1,128)} %copy.44), calls=%async_computation | async-start | bytes 65536 | tf_op jit(solution)/shard_map/all_to_all | solution.py:288
  19.3 4.2 %copy-start.20 = (s32[3]{0:T(128)}, s32[3]{0:T(128)S(1)}, u32[]{:S(2)}) copy-start(s32[3]{0:T(128)S(1)} %get-tuple-element.10) | copy-start | bytes 40
  28.0 3.4 %copy-start.4 = (bf16[1024,2048]{1,0:T(8,128)(2,1)S(1)}, bf16[1024,2048]{1,0:T(8,128)(2,1)}, u32[]{:S(2)}) copy-start(bf16[1024,2048]{1,0:T(8,128)(2,1)} %param.12) | copy-start | bytes 12582916
  28.0 3.4 %copy-start.18 = (f32[2048]{0:T(1024)S(1)}, f32[2048]{0:T(1024)}, u32[]{:S(2)}) copy-start(f32[2048]{0:T(1024)} %param.13) | copy-start | bytes 24580
  31.4 1.2 copy-start.24
  32.7 2.0 copy-start.7
  41.2 2.9 %copy-start.5 = (f32[1024,64]{1,0:T(8,128)}, f32[1024,64]{1,0:T(8,128)S(1)}, u32[]{:S(2)}) copy-start(f32[1024,64]{1,0:T(8,128)S(1)} %get-tuple-element.29) | copy-start | bytes 786436
  41.2 2.9 %copy-start.6 = (f32[1024,64]{1,0:T(8,128)}, f32[1024,64]{1,0:T(8,128)S(1)}, u32[]{:S(2)}) copy-start(f32[1024,64]{1,0:T(8,128)S(1)} %get-tuple-element.30) | copy-start | bytes 786436
  41.2 4.4 %copy-start.8 = (bf16[1024,2048]{1,0:T(8,128)(2,1)S(1)}, bf16[1024,2048]{1,0:T(8,128)(2,1)}, u32[]{:S(2)}) copy-start(bf16[1024,2048]{1,0:T(8,128)(2,1)} %copy-done.7) | copy-start | bytes 12582916
  44.1 1.5 copy-start.25
  45.6 3.1 %copy-start.9 = (bf16[128,8,2,128]{3,1,2,0:T(8,128)(2,1)}, bf16[128,8,2,128]{3,1,2,0:T(8,128)(2,1)S(1)}, u32[]{:S(2)}) copy-start(bf16[128,8,2,128]{3,1,2,0:T(8,128)(2,1)S(1)} %copy.64) | copy-start | bytes 1572868
  46.9 9.1 %copy-start.11 = (bf16[1024,256]{1,0:T(8,128)(2,1)}, bf16[1024,256]{1,0:T(8,128)(2,1)S(1)}, u32[]{:S(2)}) copy-start(bf16[1024,256]{1,0:T(8,128)(2,1)S(1)} %convolution_convert_fusion) | copy-start | bytes 1572868
  50.1 6.0 %copy-start.19 = (s32[3,40]{1,0:T(4,128)S(1)}, s32[3,40]{1,0:T(4,128)}, u32[]{:S(2)}) copy-start(s32[3,40]{1,0:T(4,128)} %iota_add_fusion) | copy-start | bytes 1444
  50.1 6.1 %copy-start.22 = (s32[3]{0:T(128)S(1)}, s32[3]{0:T(128)}, u32[]{:S(2)}) copy-start(s32[3]{0:T(128)} %get-tuple-element.33) | copy-start | bytes 40
  50.1 6.2 %copy-start.21 = (s32[3]{0:T(128)S(1)}, s32[3]{0:T(128)}, u32[]{:S(2)}) copy-start(s32[3]{0:T(128)} %copy-done.20) | copy-start | bytes 40
  50.1 6.5 %copy-start.13 = (bf16[16,16,512]{2,1,0:T(8,128)(2,1)S(1)}, bf16[16,16,512]{2,1,0:T(8,128)(2,1)}, u32[]{:S(2)}) copy-start(bf16[16,16,512]{2,1,0:T(8,128)(2,1)} %param.19) | copy-start | bytes 786436
  50.1 7.5 %copy-start.15 = (s32[1024]{0:T(1024)S(1)}, s32[1024]{0:T(1024)}, u32[]{:S(2)}) copy-start(s32[1024]{0:T(1024)} %get-tuple-element.5) | copy-start | bytes 12292
  50.1 7.6 %copy-start.16 = (s32[8,128]{1,0:T(8,128)S(1)}, s32[8,128]{1,0:T(8,128)}, u32[]{:S(2)}) copy-start(s32[8,128]{1,0:T(8,128)} %constant.104.clone.1) | copy-start | bytes 12292
  50.1 7.6 %copy-start.17 = (s32[8,128]{1,0:T(8,128)S(1)}, s32[8,128]{1,0:T(8,128)}, u32[]{:S(2)}) copy-start(s32[8,128]{1,0:T(8,128)} %fusion.18) | copy-start | bytes 12292
  50.1 7.6 %copy-start.23 = (s32[8]{0:T(128)S(1)}, s32[8]{0:T(128)}, u32[]{:S(2)}) copy-start(s32[8]{0:T(128)} %fusion.23) | copy-start | bytes 100
  117.4 0.8 copy-start.14
  121.0 9.1 %copy-start.10 = (bf16[128,8,2,128]{3,1,2,0:T(8,128)(2,1)S(1)}, bf16[128,8,2,128]{3,1,2,0:T(8,128)(2,1)}, u32[]{:S(2)}) copy-start(bf16[128,8,2,128]{3,1,2,0:T(8,128)(2,1)} %copy-done.9) | copy-start | bytes 1572868
  121.0 4.5 %collective-permute-start = (f32[1024,16]{0,1:T(8,128)S(1)}, f32[1024,16]{0,1:T(8,128)S(1)}, u32[]{:S(2)}, u32[]{:S(2)}) collective-permute-start(f32[1024,16]{0,1:T(8,128)S(1)} %select_reduce_fusion), channel_id=1, source_target_pairs={{0,1},{1,0},{2,3},{3,2},{4,5},{5,4},{6,7},{7,6},{8,9},{9,8},{10,11... | collective-permute-start | bytes 196616 | tf_op jit(solution)/shard_map/ppermute | solution.py:312
  123.8 7.2 %copy-start.12 = (bf16[1024,256]{1,0:T(8,128)(2,1)S(1)}, bf16[1024,256]{1,0:T(8,128)(2,1)}, u32[]{:S(2)}) copy-start(bf16[1024,256]{1,0:T(8,128)(2,1)} %copy-done.11) | copy-start | bytes 1572868
  125.5 6.3 %copy-start.26 = (f32[1024,512]{0,1:T(8,128)S(1)}, f32[1024,512]{0,1:T(8,128)}, u32[]{:S(2)}) copy-start(f32[1024,512]{0,1:T(8,128)} %fusion.32) | copy-start | bytes 6291460
  125.5 6.3 %collective-permute-start.1 = (f32[1024,16]{0,1:T(8,128)S(1)}, f32[1024,16]{0,1:T(8,128)S(1)}, u32[]{:S(2)}, u32[]{:S(2)}) collective-permute-start(f32[1024,16]{0,1:T(8,128)S(1)} %add.138), channel_id=1, source_target_pairs={{0,2},{1,3},{2,0},{3,1},{4,6},{5,7},{6,4},{7,5},{8,10},{9,11},{10,... | collective-permute-start | bytes 196616 | tf_op jit(solution)/shard_map/ppermute | solution.py:312
  143.2 1.6 copy-start.1
  143.2 1.6 copy-start.2
  143.2 1.7 copy-start.3

commit v4 on v2

--- a/solution.py
+++ b/solution.py
@@ -59,7 +59,8 @@
 
 
 def attend_kernel(
-    q_ref, k_ref, v_ref, kp_ref, vp_ref, bias_ref, wo_ref, res_ref, out_ref,
+    qb_ref, spread_ref, up_ref, cs_ref, sn_ref, k_ref, v_ref, kp_ref, vp_ref, bias_ref, wo_ref,
+    tok_ref, out_ref,
     send_buf, recv_buf, send_sems, recv_sems, *, tp_count, heads, kv_heads, n_blocks
 ):
     me = lax.axis_index("tp")
@@ -89,13 +90,26 @@
 
     def block_body(b, carry):
         row = pl.multiple_of(b * BLOCK, BLOCK)
+        first = pl.multiple_of(jnp.maximum(b - 1, 0) * BLOCK, BLOCK)
         bias = bias_ref[b]
+        delta = (
+            2.0
+            * jnp.dot(
+                spread_ref[pl.ds(row, BLOCK), :], up_ref[...], preferred_element_type=jnp.float32
+            )
+        ).astype(jnp.bfloat16).astype(jnp.float32)
+        cs = cs_ref[pl.ds(row, BLOCK), :]
+        sn = sn_ref[pl.ds(row, BLOCK), :]
         outs = []
         for h in range(heads):
             g = h // rep
-            qh = q_ref[pl.ds(row, BLOCK), pl.ds(h * 128, 128)]
-            kw = k_ref[pl.ds(row, 2 * BLOCK), pl.ds(g * 128, 128)]
-            vw = v_ref[pl.ds(row, 2 * BLOCK), pl.ds(g * 128, 128)]
+            dh = delta[:, h * 128 : (h + 1) * 128]
+            qh = (
+                qb_ref[pl.ds(row, BLOCK), pl.ds(h * 128, 128)]
+                + (dh * cs + pltpu.roll(dh, 64, 1) * sn)
+            ).astype(jnp.bfloat16)
+            kw = k_ref[pl.ds(first, 2 * BLOCK), pl.ds(g * 128, 128)]
+            vw = v_ref[pl.ds(first, 2 * BLOCK), pl.ds(g * 128, 128)]
             kp = kp_ref[:, pl.ds(g * 128, 128)]
             vp = vp_ref[:, pl.ds(g * 128, 128)]
             keys = jnp.concatenate([kw, kp], 0)
@@ -131,7 +145,7 @@
 
     def finish_body(b, carry):
         row = pl.multiple_of(b * BLOCK, BLOCK)
-        total = res_ref[pl.ds(row, BLOCK), :].astype(jnp.float32)
+        total = tok_ref[pl.ds(row, BLOCK), pl.ds(own, piece)].astype(jnp.float32)
         total = total + send_buf[b, :, pl.ds(own, piece)].astype(jnp.float32)
         for k in range(1, tp_count):
             source = lax.rem(me + tp_count - k, tp_count)
@@ -142,23 +156,23 @@
     lax.fori_loop(0, n_blocks, finish_body, 0)
 
 
-def attend_and_reduce(q, k_pad, v_pad, k_prompt, v_prompt, bias, wo, residual, tp_count):
-    rows, q_width = q.shape
+def attend_and_reduce(qb, spread, up, cs, sn, keys, values, k_prompt, v_prompt, bias, wo, tokens, tp_count):
+    rows, q_width = qb.shape
     n_blocks = rows // BLOCK
-    piece = residual.shape[1]
     width = wo.shape[1]
+    piece = width // tp_count
     kernel = functools.partial(
         attend_kernel,
         tp_count=tp_count,
         heads=q_width // HEAD_WIDTH,
-        kv_heads=k_pad.shape[1] // HEAD_WIDTH,
+        kv_heads=keys.shape[1] // HEAD_WIDTH,
         n_blocks=n_blocks,
     )
     vmem = pltpu.MemorySpace.VMEM
     return pl.pallas_call(
         kernel,
         out_shape=jax.ShapeDtypeStruct((rows, piece), jnp.bfloat16),
-        in_specs=[pl.BlockSpec(memory_space=vmem)] * 8,
+        in_specs=[pl.BlockSpec(memory_space=vmem)] * 12,
         out_specs=pl.BlockSpec(memory_space=vmem),
         scratch_shapes=[
             pltpu.VMEM((n_blocks, BLOCK, width), jnp.bfloat16),
@@ -169,7 +183,7 @@
         compiler_params=pltpu.CompilerParams(
             collective_id=0, has_side_effects=True, vmem_limit_bytes=48 * 1024 * 1024
         ),
-    )(q, k_pad, v_pad, k_prompt, v_prompt, bias, wo, residual)
+    )(qb, spread, up, cs, sn, keys, values, k_prompt, v_prompt, bias, wo, tokens)
 
 
 def per_device(
@@ -235,17 +249,19 @@
     spread = jnp.where(pick, rank[:, None, :], jnp.zeros((), jnp.bfloat16)).reshape(
         tok_rows, req_count * rank_extent
     )
-    query_delta = (
-        2.0 * jnp.dot(spread, up_in, preferred_element_type=jnp.float32)
-    ).astype(jnp.bfloat16)
     heads_local = query_matrix.shape[1] // HEAD_WIDTH
     kv_local = key_matrix.shape[1] // HEAD_WIDTH
-    query_full = jnp.dot(
-        normalized_input, query_matrix, preferred_element_type=jnp.float32
-    ) + query_delta.astype(jnp.float32)
-    query_heads = apply_rotary(
-        query_full.reshape(tok_rows, heads_local, HEAD_WIDTH), token_positions
-    ).astype(jnp.bfloat16)
+    query_base = jnp.dot(normalized_input, query_matrix, preferred_element_type=jnp.float32)
+    query_rot = apply_rotary(
+        query_base.reshape(tok_rows, heads_local, HEAD_WIDTH), token_positions
+    ).reshape(tok_rows, heads_local * HEAD_WIDTH)
+    half_dim = HEAD_WIDTH // 2
+    inverse = 1000000.0 ** (-(jnp.arange(half_dim, dtype=jnp.float32) * 2.0 / HEAD_WIDTH))
+    angles = token_positions[:, None] * inverse[None, :]
+    cosine = jnp.cos(angles)
+    sine = jnp.sin(angles)
+    cos_pair = jnp.concatenate([cosine, cosine], 1)
+    sin_pair = jnp.concatenate([-sine, sine], 1)
     key_complete = jnp.dot(normalized_input, key_matrix, preferred_element_type=jnp.float32)
     key_head_rows = apply_rotary(
         key_complete.reshape(tok_rows, kv_local, HEAD_WIDTH), token_positions
@@ -261,9 +277,6 @@
     kv_width = kv_local * HEAD_WIDTH
     key_flat = key_head_rows.reshape(tok_rows, kv_width)
     value_flat = value_head_rows.reshape(tok_rows, kv_width)
-    front = jnp.zeros((BLOCK, kv_width), jnp.bfloat16)
-    k_pad = jnp.concatenate([front, key_flat], 0)
-    v_pad = jnp.concatenate([front, value_flat], 0)
     clamp_start = jnp.clip(prompt_start, 0, tok_rows - LMAX)
     extra = BLOCK - group_count * LMAX
     k_prompt = jnp.concatenate(
@@ -276,22 +289,23 @@
         + [jnp.zeros((extra, kv_width), jnp.bfloat16)],
         0,
     )
-    def windows(values, fill):
-        padded = jnp.concatenate([jnp.full((BLOCK,), fill, values.dtype), values]).reshape(
-            n_blocks + 1, BLOCK
-        )
-        return jnp.concatenate([padded[:-1], padded[1:]], 1)
-
-    win_row = windows(row_ids, -1)
-    win_req = windows(request_row, -1)
-    win_grp = windows(group_row, -1)
-    win_prm = windows(prompt_row, 0)
+    firsts = [max(b - 1, 0) for b in range(n_blocks)]
+
+    def windows(values):
+        blocks = values.reshape(n_blocks, BLOCK)
+        lo = jnp.stack([blocks[f] for f in firsts])
+        hi = jnp.stack([blocks[f + 1] for f in firsts])
+        return jnp.concatenate([lo, hi], 1)
+
+    win_row = windows(row_ids)
+    win_req = windows(request_row)
+    win_grp = windows(group_row)
+    win_prm = windows(prompt_row)
     q_row = row_ids.reshape(n_blocks, BLOCK)[:, :, None]
     q_req = request_row.reshape(n_blocks, BLOCK)[:, :, None]
     q_grp = group_row.reshape(n_blocks, BLOCK)[:, :, None]
     win_vis = (
-        (win_row[:, None, :] >= 0)
-        & (win_grp[:, None, :] == q_grp)
+        (win_grp[:, None, :] == q_grp)
         & (win_row[:, None, :] <= q_row)
         & ((win_req[:, None, :] == q_req) | (win_prm[:, None, :] == 1))
     )
@@ -303,7 +317,7 @@
     p_lo = jnp.concatenate([p_lo, jnp.ones((extra,), jnp.int32)])
     p_hi = jnp.concatenate([p_hi, jnp.zeros((extra,), jnp.int32)])
     p_grp = jnp.concatenate([p_grp, jnp.full((extra,), -1, jnp.int32)])
-    win_first = q_row[:, :1, :] - BLOCK
+    win_first = win_row[:, :1][:, :, None]
     prompt_vis = (
         (p_grp[None, None, :] == q_grp)
         & (p_row[None, None, :] >= p_lo[None, None, :])
@@ -313,16 +327,19 @@
     )
     vis = jnp.concatenate([win_vis, prompt_vis], 2)
     bias = jnp.where(vis, jnp.float32(0.0), jnp.float32(-1e30))
-    residual = lax.dynamic_slice_in_dim(tokens, tp_index * piece_width, piece_width, 1)
     return attend_and_reduce(
-        query_heads.reshape(tok_rows, heads_local * HEAD_WIDTH),
-        k_pad,
-        v_pad,
+        query_rot,
+        spread,
+        up_in,
+        cos_pair,
+        sin_pair,
+        key_flat,
+        value_flat,
         k_prompt,
         v_prompt,
         bias,
         output_matrix,
-        residual,
+        tokens,
         tp_count,
     )
 

time: 190 us -> 199 us (1.047)
  local copies, waits for them, and re-layouts: 24.7 us -> 34.3 us
  waiting for transfers between devices: 35.3 us -> 31.2 us
  other arithmetic: 27.3 us -> 31 us
  Pallas kernels: 53.8 us -> 56.5 us
  matrix products: 13.2 us -> 10.6 us
    unnamed x45 -> x59, local copies, waits for them, and re-layouts: 11.1 us -> 17.9 us
    select_n x0 -> x2, local copies, waits for them, and re-layouts: none -> 6.4 us  [per_device(): jnp.where(pick, rank[:, None, :], jnp.zeros((), jnp.bfloat16))]
    all_to_all x1, waiting for transfers between devices: 33.7 us -> 29.5 us  [per_device(): lax.all_to_all(maps_out, 'req', split_axis=0, concat_axis=0, tiled=True)]
    neg x0 -> x1, other arithmetic: none -> 3.16 us  [per_device(): sin_pair = jnp.concatenate([-sine, sine], 1)]
    cos x1 -> x0, other arithmetic: 3.07 us -> none  [apply_rotary(): cosine = jnp.cos(angles)[:, None, :]]
    another operation x4, other arithmetic: 5.51 us -> 2.51 us
    pallas_call x1, Pallas kernels: 53.8 us -> 56.5 us  [attend_and_reduce(): pl.pallas_call(kernel, out_shape=jax.ShapeDtypeStruct((rows, piece), jnp....]
    convert_element_type x1, other arithmetic: 1.03 us -> 3.3 us  [per_device(): normalized_input = (float_tok * lax.rsqrt(jnp.mean(float_tok * float_tok,...]
  transfers between devices with their start and end apart: 4 -> 4, of which waited for: 2 -> 2; matrix products, arithmetic and copies ran while one was open for 18% -> 24% of each run, Pallas kernels for 0% -> 0%
where the time goes in v4:
time: 199 us; the launch traced here: 197 us
  Pallas kernels  56.5 us (28%)
  local copies, waits for them, and re-layouts  34.3 us (17%)
  waiting for transfers between devices  31.2 us (16%)
  other arithmetic  31 us (16%)
  starting transfers between devices  27.8 us (14%)
  matrix products  10.6 us (5%)
  between operations  5.99 us (3%)
    pallas_call x1, Pallas kernels, attend_and_reduce(): pl.pallas_call(kernel, out_shape=jax.ShapeDtypeStruct((rows, piece), jnp....  56.5 us
    all_to_all x1, waiting for transfers between devices, per_device(): lax.all_to_all(maps_out, 'req', split_axis=0, concat_axis=0, tiled=True)  29.5 us
    unnamed x59, local copies, waits for them, and re-layouts  17.9 us
    all_to_all x1, starting transfers between devices, per_device(): lax.all_to_all(wanted.reshape(req_count, 1), 'req', split_axis=0, concat_...  12 us
    all_to_all x1, starting transfers between devices, per_device(): lax.all_to_all(maps_out, 'req', split_axis=0, concat_axis=0, tiled=True)  10.7 us
    select_n x2, local copies, waits for them, and re-layouts, per_device(): jnp.where(pick, rank[:, None, :], jnp.zeros((), jnp.bfloat16))  6.4 us
    ppermute x2, starting transfers between devices, per_device(): partial_rank = partial_rank + lax.ppermute(partial_rank, 'tp', pairs)  5.16 us
  transfers between devices with their start and end apart: 4, of which 2 were waited for; matrix products, arithmetic and copies ran while one was open for 24% of the time, Pallas kernels for 0%

profile of v4, /device:TPU:2, one launch (start us, length us, event | category | flops | bytes accessed | tf_op | source)
XLA Modules:
  0.0 197.4 jit_solution(3401888565191605029)
XLA Ops:
  0.0 0.8 fusion.8
  0.8 1.4 gather_fusion
  2.3 0.7 copy.57
  3.0 12.0 %all-to-all-start = ((s32[64,1,1]{2,1,0:T(1,128)}), s32[64,1,1]{2,1,0:T(1,128)S(1)}, u32[]{:S(2)}, u32[]{:S(2)}) async-start(s32[64,1,1]{2,1,0:T(1,128)} %copy.57), calls=%async_computation | async-start | bytes 65536 | tf_op jit(solution)/shard_map/all_to_all | solution.py:221
  15.1 0.7 copy.55
  16.0 0.8 select_bitcast_fusion
  16.8 0.7 select_bitcast_fusion.1
  17.4 0.9 select_reduce_fusion.6
  18.4 0.8 select_reduce_fusion.7
  23.7 3.1 %fusion = f32[1024]{0:T(1024)S(1)} fusion(bf16[1024,2048]{1,0:T(8,128)(2,1)} %tok_ref.1), kind=kLoop, calls=%fused_computation.5 | loop fusion | flops 6290432 | bytes 4198400 | tf_op jit(solution)/shard_map/reduce_sum | solution.py:233
  27.6 3.3 %fusion.2 = bf16[1024,2048]{1,0:T(8,128)(2,1)S(1)} fusion(bf16[1024,2048]{1,0:T(8,128)(2,1)} %tok_ref.1, f32[2048]{0:T(1024)S(1)} %copy-done.23, f32[1024]{0:T(1024)S(1)} %add_rsqrt_fusion), kind=kLoop, calls=%fused_computation.7 | loop fusion | flops 8388608 | bytes 8400896 | tf_op jit(solution)/shard_map/convert_element_type | solution.py:235
  30.9 1.3 fusion.20
  32.8 2.4 %fusion.19 = f32[1024,512]{0,1:T(8,128)S(1)} fusion(bf16[1024,2048]{1,0:T(8,128)(2,1)S(1)} %fusion.2, bf16[2048,512]{1,0:T(8,128)(2,1)S(1)} %copy-done), kind=kOutput, calls=%fused_computation.120 | convolution fusion | flops 2147483648 | bytes 8388608 | tf_op jit(solution)/shard_map/dot_general | solution.py:254
  35.4 1.6 fusion.13
  37.0 3.2 %fusion.6 = (f32[1024,64]{1,0:T(8,128)}, f32[1024,64]{1,0:T(8,128)}, f32[1024,64]{1,0:T(8,128)}) fusion(f32[64]{0:T(128)S(1)} %negate_power_fusion, f32[1024]{0:T(1024)S(1)} %add_convert_fusion.2), kind=kLoop, calls=%fused_computation.31 | loop fusion | flops 131072 | bytes 790784 | tf_op jit(solution)/shard_map/neg | solution.py:264
  40.2 1.3 copy.67
  41.5 2.8 %copy.64 = f32[1024,4,64]{2,1,0:T(4,128)} copy(f32[1024,4,64]{0,2,1:T(8,128)} %get-tuple-element.19) | data formatting | bytes 2097152
  44.3 1.3 copy.66
  45.5 1.2 reduce.2
  46.8 1.6 gather_fusion.2
  49.0 2.8 %pad_maximum_fusion.1 = bf16[64,32,512]{2,1,0:T(8,128)(2,1)} fusion(bf16[64,16,512]{2,1,0:T(8,128)(2,1)} %gather_fusion.2, bf16[64,16,512]{2,1,0:T(8,128)(2,1)S(1)} %bitcast.110), kind=kLoop, calls=%fused_computation.11 | loop fusion | flops 4194304 | bytes 4194304 | tf_op jit(solution)/shard_map/concatenate | solution.py:226
  51.8 10.7 %all-to-all-start.1 = ((bf16[64,32,512]{2,1,0:T(8,128)(2,1)}), bf16[64,32,512]{2,1,0:T(8,128)(2,1)}, u32[]{:S(2)}, u32[]{:S(2)}) async-start(bf16[64,32,512]{2,1,0:T(8,128)(2,1)} %pad_maximum_fusion.1), calls=%async_computation.1 | async-start | bytes 4194304 | tf_op jit(solution)/shard_map/all_to_all | solution.py:227
  62.5 2.3 %subtract_convert_fusion = (bf16[1024,2,64]{2,1,0:T(2,128)(2,1)S(1)}, bf16[1024,2,64]{2,1,0:T(2,128)(2,1)S(1)}) fusion(f32[1024,2,64]{2,1,0:T(2,128)} %copy.67, f32[1024,2,64]{2,1,0:T(2,128)} %copy.66, f32[1024,64]{1,0:T(8,128)S(1)} %copy-done.10, f32[1024,64]{1,0:T(8,128)S(1)} %copy-done.12), kind=kLoop, calls=%fused_computation.20 | loop fusion | flops 1048576 | bytes 2097152 | tf_op jit(solution)/shard_map/convert
  64.8 1.4 pad_maximum_fusion.4
  66.3 2.9 %copy.63 = f32[1024,4,64]{2,1,0:T(4,128)} copy(f32[1024,4,64]{0,2,1:T(8,128)} %get-tuple-element.20) | data formatting | bytes 2097152
  71.4 3.9 %convolution_convert_fusion.v_ref = bf16[1024,256]{1,0:T(8,128)(2,1)S(1)} fusion(bf16[1024,2048]{1,0:T(8,128)(2,1)} %copy-done.18, bf16[2048,256]{1,0:T(8,128)(2,1)} %param.16), kind=kOutput, calls=%fused_computation.16 | convolution fusion | flops 1074003968 | bytes 5767168 | tf_op jit(solution)/shard_map/dot_general | solution.py:270
  75.4 0.8 copy-done.6
  76.2 1.2 multiply_subtract_fusion
  77.4 2.5 %pad_maximum_fusion = f32[1024,4,128]{2,1,0:T(4,128)} fusion(f32[1024,4,64]{2,1,0:T(4,128)S(1)} %get-tuple-element.14, f32[1024,4,64]{2,1,0:T(4,128)S(1)} %get-tuple-element.13), kind=kLoop, calls=%fused_computation.10 | loop fusion | flops 524288 | bytes 4194304 | tf_op jit(solution)/shard_map/concatenate | solution.py:23
  80.8 1.0 compare_and_fusion
  82.4 29.5 %all-to-all-done.1 = bf16[64,32,512]{2,1,0:T(8,128)(2,1)} async-done(((bf16[64,32,512]{2,1,0:T(8,128)(2,1)}), bf16[64,32,512]{2,1,0:T(8,128)(2,1)}, u32[]{:S(2)}, u32[]{:S(2)}) %all-to-all-start.1) | async-done | bytes 2097184 | tf_op jit(solution)/shard_map/all_to_all | solution.py:227
  111.9 1.8 fusion.12
  113.7 3.0 %select_reduce_fusion = f32[1024,16]{0,1:T(8,128)S(1)} fusion(pred[1024,64]{0,1:T(8,128)(4,1)S(1)} %copy-done.21, bf16[64,16,512]{2,1,0:T(8,128)(2,1)S(1)} %get-tuple-element.18, bf16[1024,2048]{1,0:T(8,128)(2,1)} %copy-done.18, s32[]{:T(128)S(6)} %select_n.74), kind=kOutput, calls=%fused_computation.8 | convolution fusion | flops 1075822592 | bytes 2228228 | tf_op jit(solution)/shard_map/dot_general | solution.py:241
  116.7 1.7 collective-permute-start
  118.4 1.3 add_select_fusion.bias_ref
  119.7 1.6 collective-permute-done
  121.3 3.5 %collective-permute-start.1 = (f32[1024,16]{0,1:T(8,128)S(1)}, f32[1024,16]{0,1:T(8,128)S(1)}, u32[]{:S(2)}, u32[]{:S(2)}) collective-permute-start(f32[1024,16]{0,1:T(8,128)S(1)} %add.128), channel_id=1, source_target_pairs={{0,2},{1,3},{2,0},{3,1},{4,6},{5,7},{6,4},{7,5},{8,10},{9,11},{10,... | collective-permute-start | bytes 196616 | tf_op jit(solution)/shard_map/ppermute | solution.py:247
  124.8 1.4 pad_maximum_fusion.2
  126.2 1.5 copy.74
  127.9 2.5 %copy.59 = bf16[1024,64,16]{0,2,1:T(8,128)(2,1)} copy(bf16[1024,64,16]{0,1,2:T(8,128)(2,1)S(1)} %broadcast_select_fusion) | data formatting | bytes 4194304 | tf_op jit(solution)/shard_map/jit(_where)/select_n | solution.py:249
  130.4 3.9 %copy.62.spread_ref = bf16[1024,1024]{1,0:T(8,128)(2,1)} copy(bf16[1024,1024]{0,1:T(8,128)(2,1)} %bitcast.112) | data formatting | bytes 4194304 | tf_op jit(solution)/shard_map/jit(_where)/select_n | solution.py:249
  134.3 1.4 copy-done.1
  135.7 1.0 copy-done.3
  136.7 1.0 copy-done.4
  137.8 1.0 copy-done.5
  138.8 1.0 copy-done.7
  139.9 56.5 %shard_map.118 = bf16[1024,512]{1,0:T(8,128)(2,1)S(1)} custom-call(f32[1024,512]{1,0:T(8,128)} %bitcast.113, bf16[1024,1024]{1,0:T(8,128)(2,1)} %copy.62.spread_ref, bf16[1024,512]{1,0:T(8,128)(2,1)S(1)} %bitcast.107, f32[1024,128]{1,0:T(8,128)S(1)} %copy-done.4, f32[1024,128]{1,0:T(8,128)S(1)} %copy-done.5, bf16[1024,256]{1,0:T(8,128)(2,1)S(1)} %bitcast.109, ...), custom_call_target="tpu_custom_call" | custom-call | tf_op jit(solution)/shard_map/pallas_call | solution.py:172
  196.4 1.0 copy.77
  (105 shorter events, 5.3 us)
Async XLA Ops:
  0.0 32.8 %copy-start = (bf16[2048,512]{1,0:T(8,128)(2,1)S(1)}, bf16[2048,512]{1,0:T(8,128)(2,1)}, u32[]{:S(2)}) copy-start(bf16[2048,512]{1,0:T(8,128)(2,1)} %param.14) | copy-start | bytes 6291460
  3.0 42.5 %all-to-all-start = ((s32[64,1,1]{2,1,0:T(1,128)}), s32[64,1,1]{2,1,0:T(1,128)S(1)}, u32[]{:S(2)}, u32[]{:S(2)}) async-start(s32[64,1,1]{2,1,0:T(1,128)} %copy.57), calls=%async_computation | async-start | bytes 65536 | tf_op jit(solution)/shard_map/all_to_all | solution.py:221
  23.7 3.1 %copy-start.24 = (s32[1,32]{1,0:T(1,128)S(1)}, s32[1,32]{1,0:T(1,128)}, u32[]{:S(2)}) copy-start(s32[1,32]{1,0:T(1,128)} %param.20) | copy-start | bytes 388
  23.7 3.6 %copy-start.22 = (s32[1,32]{1,0:T(1,128)S(1)}, s32[1,32]{1,0:T(1,128)}, u32[]{:S(2)}) copy-start(s32[1,32]{1,0:T(1,128)} %param.21) | copy-start | bytes 388
  23.7 3.9 %copy-start.23 = (f32[2048]{0:T(1024)S(1)}, f32[2048]{0:T(1024)}, u32[]{:S(2)}) copy-start(f32[2048]{0:T(1024)} %param.13) | copy-start | bytes 24580
  27.6 3.3 %copy-start.25 = (bf16[2048,256]{1,0:T(8,128)(2,1)S(1)}, bf16[2048,256]{1,0:T(8,128)(2,1)}, u32[]{:S(2)}) copy-start(bf16[2048,256]{1,0:T(8,128)(2,1)} %param.15) | copy-start | bytes 3145732
  30.9 1.9 copy-start.18
  41.5 5.3 %copy-start.17 = (bf16[16,16,512]{2,1,0:T(8,128)(2,1)S(1)}, bf16[16,16,512]{2,1,0:T(8,128)(2,1)}, u32[]{:S(2)}) copy-start(bf16[16,16,512]{2,1,0:T(8,128)(2,1)} %param.19) | copy-start | bytes 786436
  44.2 4.1 %copy-start.8 = (bf16[16,512,16]{1,2,0:T(8,128)(2,1)S(1)}, bf16[16,512,16]{1,2,0:T(8,128)(2,1)}, u32[]{:S(2)}) copy-start(bf16[16,512,16]{1,2,0:T(8,128)(2,1)} %param.18) | copy-start | bytes 786436
  51.8 10.7 %copy-start.10 = (f32[1024,64]{1,0:T(8,128)S(1)}, f32[1024,64]{1,0:T(8,128)}, u32[]{:S(2)}) copy-start(f32[1024,64]{1,0:T(8,128)} %get-tuple-element.30) | copy-start | bytes 786436
  51.8 10.7 %copy-start.12 = (f32[1024,64]{1,0:T(8,128)S(1)}, f32[1024,64]{1,0:T(8,128)}, u32[]{:S(2)}) copy-start(f32[1024,64]{1,0:T(8,128)} %get-tuple-element.31) | copy-start | bytes 786436
  51.8 60.1 %all-to-all-start.1 = ((bf16[64,32,512]{2,1,0:T(8,128)(2,1)}), bf16[64,32,512]{2,1,0:T(8,128)(2,1)}, u32[]{:S(2)}, u32[]{:S(2)}) async-start(bf16[64,32,512]{2,1,0:T(8,128)(2,1)} %pad_maximum_fusion.1), calls=%async_computation.1 | async-start | bytes 4194304 | tf_op jit(solution)/shard_map/all_to_all | solution.py:227
  66.3 9.9 %copy-start.2 = (bf16[128,8,2,128]{3,1,2,0:T(8,128)(2,1)}, bf16[128,8,2,128]{3,1,2,0:T(8,128)(2,1)S(1)}, u32[]{:S(2)}) copy-start(bf16[128,8,2,128]{3,1,2,0:T(8,128)(2,1)S(1)} %copy.75) | copy-start | bytes 1572868
  71.4 4.8 %copy-start.13 = (f32[1024,64]{1,0:T(8,128)S(1)}, f32[1024,64]{1,0:T(8,128)}, u32[]{:S(2)}) copy-start(f32[1024,64]{1,0:T(8,128)} %get-tuple-element.31) | copy-start | bytes 786436
  71.4 4.8 %copy-start.15 = (f32[1024,4,64]{2,1,0:T(4,128)S(1)}, f32[1024,4,64]{2,1,0:T(4,128)}, u32[]{:S(2)}) copy-start(f32[1024,4,64]{2,1,0:T(4,128)} %copy.64) | copy-start | bytes 3145732
  71.4 4.8 %copy-start.16 = (f32[1024,4,64]{2,1,0:T(4,128)S(1)}, f32[1024,4,64]{2,1,0:T(4,128)}, u32[]{:S(2)}) copy-start(f32[1024,4,64]{2,1,0:T(4,128)} %copy.63) | copy-start | bytes 3145732
  75.4 0.8 copy-start.6
  111.9 1.8 copy-start.21
  113.7 4.7 %copy-start.20 = (pred[8,128,128]{2,1,0:T(8,128)(4,1)S(1)}, pred[8,128,128]{2,1,0:T(8,128)(4,1)}, u32[]{:S(2)}) copy-start(pred[8,128,128]{2,1,0:T(8,128)(4,1)} %compare_and_fusion) | copy-start | bytes 393220
  113.7 11.2 %copy-start.11 = (f32[1024,64]{1,0:T(8,128)S(1)}, f32[1024,64]{1,0:T(8,128)}, u32[]{:S(2)}) copy-start(f32[1024,64]{1,0:T(8,128)} %get-tuple-element.30) | copy-start | bytes 786436
  113.7 11.2 %copy-start.14 = (f32[1024,64]{1,0:T(8,128)S(1)}, f32[1024,64]{1,0:T(8,128)}, u32[]{:S(2)}) copy-start(f32[1024,64]{1,0:T(8,128)} %get-tuple-element.31) | copy-start | bytes 786436
  113.7 11.2 %copy-start.19 = (f32[1024,64]{1,0:T(8,128)S(1)}, f32[1024,64]{1,0:T(8,128)}, u32[]{:S(2)}) copy-start(f32[1024,64]{1,0:T(8,128)} %get-tuple-element.29) | copy-start | bytes 786436
  116.7 9.5 %copy-start.9 = (f32[1024,4,128]{2,1,0:T(4,128)S(1)}, f32[1024,4,128]{2,1,0:T(4,128)}, u32[]{:S(2)}) copy-start(f32[1024,4,128]{2,1,0:T(4,128)} %pad_maximum_fusion) | copy-start | bytes 6291460
  116.7 4.6 %collective-permute-start = (f32[1024,16]{0,1:T(8,128)S(1)}, f32[1024,16]{0,1:T(8,128)S(1)}, u32[]{:S(2)}, u32[]{:S(2)}) collective-permute-start(f32[1024,16]{0,1:T(8,128)S(1)} %select_reduce_fusion), channel_id=1, source_target_pairs={{0,1},{1,0},{2,3},{3,2},{4,5},{5,4},{6,7},{7,6},{8,9},{9,8},{10,11... | collective-permute-start | bytes 196616 | tf_op jit(solution)/shard_map/ppermute | solution.py:247
  121.3 6.4 %collective-permute-start.1 = (f32[1024,16]{0,1:T(8,128)S(1)}, f32[1024,16]{0,1:T(8,128)S(1)}, u32[]{:S(2)}, u32[]{:S(2)}) collective-permute-start(f32[1024,16]{0,1:T(8,128)S(1)} %add.128), channel_id=1, source_target_pairs={{0,2},{1,3},{2,0},{3,1},{4,6},{5,7},{6,4},{7,5},{8,10},{9,11},{10,... | collective-permute-start | bytes 196616 | tf_op jit(solution)/shard_map/ppermute | solution.py:247
  134.3 1.4 copy-start.1
  135.7 1.0 copy-start.3
  136.7 1.0 copy-start.4
  137.8 1.0 copy-start.5
  138.8 1.0 copy-start.7

commit v5 on v2

--- a/solution.py
+++ b/solution.py
@@ -235,16 +235,34 @@
     spread = jnp.where(pick, rank[:, None, :], jnp.zeros((), jnp.bfloat16)).reshape(
         tok_rows, req_count * rank_extent
     )
-    query_delta = (
-        2.0 * jnp.dot(spread, up_in, preferred_element_type=jnp.float32)
-    ).astype(jnp.bfloat16)
     heads_local = query_matrix.shape[1] // HEAD_WIDTH
     kv_local = key_matrix.shape[1] // HEAD_WIDTH
-    query_full = jnp.dot(
-        normalized_input, query_matrix, preferred_element_type=jnp.float32
-    ) + query_delta.astype(jnp.float32)
-    query_heads = apply_rotary(
-        query_full.reshape(tok_rows, heads_local, HEAD_WIDTH), token_positions
+    half_dim = HEAD_WIDTH // 2
+    query_base = jnp.dot(normalized_input, query_matrix, preferred_element_type=jnp.float32)
+    query_rot = apply_rotary(
+        query_base.reshape(tok_rows, heads_local, HEAD_WIDTH), token_positions
+    ).reshape(tok_rows, heads_local * HEAD_WIDTH)
+    inverse = 1000000.0 ** (-(jnp.arange(half_dim, dtype=jnp.float32) * 2.0 / HEAD_WIDTH))
+    angles = token_positions[:, None] * inverse[None, :]
+    cosine = jnp.cos(angles)
+    sine = jnp.sin(angles)
+    cos_wide = jnp.tile(jnp.concatenate([cosine, cosine], 1), (1, heads_local))
+    sin_wide = jnp.tile(jnp.concatenate([sine, sine], 1), (1, heads_local))
+    up_halves = up_in.reshape(up_in.shape[0], heads_local, 2, half_dim)
+    up_turned = jnp.concatenate([-up_halves[:, :, 1:], up_halves[:, :, :1]], 2).reshape(
+        up_in.shape
+    )
+    both = (
+        2.0
+        * jnp.dot(
+            spread,
+            jnp.concatenate([up_in, up_turned], 1),
+            preferred_element_type=jnp.float32,
+        )
+    ).astype(jnp.bfloat16).astype(jnp.float32)
+    q_width = heads_local * HEAD_WIDTH
+    query_heads = (
+        query_rot + both[:, :q_width] * cos_wide + both[:, q_width:] * sin_wide
     ).astype(jnp.bfloat16)
     key_complete = jnp.dot(normalized_input, key_matrix, preferred_element_type=jnp.float32)
     key_head_rows = apply_rotary(
@@ -315,7 +333,7 @@
     bias = jnp.where(vis, jnp.float32(0.0), jnp.float32(-1e30))
     residual = lax.dynamic_slice_in_dim(tokens, tp_index * piece_width, piece_width, 1)
     return attend_and_reduce(
-        query_heads.reshape(tok_rows, heads_local * HEAD_WIDTH),
+        query_heads,
         k_pad,
         v_pad,
         k_prompt,

time: 190 us -> 203 us (1.068)
  waiting for transfers between devices: 35.3 us -> 16.5 us
  local copies, waits for them, and re-layouts: 24.7 us -> 42.8 us
  other arithmetic: 27.3 us -> 39.1 us
    all_to_all x1, waiting for transfers between devices: 33.7 us -> 16.5 us  [per_device(): lax.all_to_all(maps_out, 'req', split_axis=0, concat_axis=0, tiled=True)]
    concatenate x0 -> x2, other arithmetic: none -> 6.94 us  [the longest x1 5.63 us: per_device(): jnp.concatenate([-up_halves[:, :, 1:], up_halves[:, :, :1]], 2)]
    another operation x1 -> x4, local copies, waits for them, and re-layouts: 0.01 us -> 5.15 us  [the longest x1 4.42 us: per_device(): up_halves = up_in.reshape(up_in.shape[0], heads_local, 2, half_dim)]
    neg x0 -> x1, other arithmetic: none -> 4.67 us  [per_device(): -up_halves[:, :, 1:]]
    concatenate x0 -> x1, local copies, waits for them, and re-layouts: none -> 4.36 us  [per_device(): jnp.concatenate([-up_halves[:, :, 1:], up_halves[:, :, :1]], 2)]
    another operation x4 -> x3, other arithmetic: 5.51 us -> 1.34 us
    unnamed x45 -> x56, local copies, waits for them, and re-layouts: 11.1 us -> 14.9 us
    reshape x1 -> x2, local copies, waits for them, and re-layouts: 0.74 us -> 3 us  [the longest x1 2.27 us: per_device(): jnp.concatenate([-up_halves[:, :, 1:], up_halves[:, :, :1]], 2)]
  transfers between devices with their start and end apart: 4 -> 4, of which waited for: 2 -> 1; matrix products, arithmetic and copies ran while one was open for 18% -> 36% of each run, Pallas kernels for 0% -> 0%
where the time goes in v5:
time: 203 us; the launch traced here: 201 us
  Pallas kernels  55.1 us (27%)
  local copies, waits for them, and re-layouts  42.8 us (21%)
  other arithmetic  39.1 us (19%)
  starting transfers between devices  27.2 us (13%)
  waiting for transfers between devices  16.5 us (8%)
  matrix products  14.8 us (7%)
  between operations  5.86 us (3%)
    pallas_call x1, Pallas kernels, attend_and_reduce(): pl.pallas_call(kernel, out_shape=jax.ShapeDtypeStruct((rows, piece), jnp....  55.1 us
    all_to_all x1, waiting for transfers between devices, per_device(): lax.all_to_all(maps_out, 'req', split_axis=0, concat_axis=0, tiled=True)  16.5 us
    unnamed x56, local copies, waits for them, and re-layouts  14.9 us
    all_to_all x1, starting transfers between devices, per_device(): lax.all_to_all(wanted.reshape(req_count, 1), 'req', split_axis=0, concat_...  12 us
    all_to_all x1, starting transfers between devices, per_device(): lax.all_to_all(maps_out, 'req', split_axis=0, concat_axis=0, tiled=True)  10.3 us
    concatenate x1, other arithmetic, per_device(): jnp.concatenate([-up_halves[:, :, 1:], up_halves[:, :, :1]], 2)  5.63 us
    ppermute x2, starting transfers between devices, per_device(): partial_rank = partial_rank + lax.ppermute(partial_rank, 'tp', pairs)  4.87 us
    concatenate x2, other arithmetic, apply_rotary(): jnp.concatenate([first_half * cosine - second * sine_part, second * cosin...  4.71 us
  transfers between devices with their start and end apart: 4, of which 1 were waited for; matrix products, arithmetic and copies ran while one was open for 36% of the time, Pallas kernels for 0%

profile of v5, /device:TPU:2, one launch (start us, length us, event | category | flops | bytes accessed | tf_op | source)
XLA Modules:
  0.0 201.3 jit_solution(5596265170433085009)
XLA Ops:
  0.0 0.8 fusion.19
  0.8 1.4 gather_fusion
  3.0 12.0 %all-to-all-start = ((s32[64,1,1]{2,1,0:T(1,128)}), s32[64,1,1]{2,1,0:T(1,128)S(1)}, u32[]{:S(2)}, u32[]{:S(2)}) async-start(s32[64,1,1]{2,1,0:T(1,128)} %copy.53), calls=%async_computation | async-start | bytes 65536 | tf_op jit(solution)/shard_map/all_to_all | solution.py:207
  16.0 0.8 select_bitcast_fusion
  17.5 0.9 select_reduce_fusion.6
  19.1 0.8 select_reduce_fusion.1
  20.0 3.2 %fusion = f32[1024]{0:T(1024)S(1)} fusion(bf16[1024,2048]{1,0:T(8,128)(2,1)} %param.12), kind=kLoop, calls=%fused_computation.5 | loop fusion | flops 6290432 | bytes 4198400 | tf_op jit(solution)/shard_map/reduce_sum | solution.py:219
  23.4 1.0 fusion.2
  24.6 1.3 fusion.32
  26.7 1.3 copy.63
  27.9 1.3 copy.64
  29.4 4.6 %fusion.31 = f32[1024,512]{0,1:T(8,128)S(1)} fusion(bf16[1024,2048]{1,0:T(8,128)(2,1)} %copy-done.13, bf16[2048,512]{1,0:T(8,128)(2,1)S(1)} %copy-done), kind=kOutput, calls=%fused_computation.115 | convolution fusion | flops 2147483648 | bytes 8388608 | tf_op jit(solution)/shard_map/dot_general | solution.py:241
  33.9 1.6 fusion.27
  35.6 1.9 multiply_cosine_fusion
  37.5 1.2 subtract_convert_fusion
  38.7 2.2 %pad_maximum_fusion.5 = bf16[1024,2,128]{2,1,0:T(2,128)(2,1)} fusion(bf16[1024,2,64]{2,1,0:T(2,128)(2,1)S(1)} %get-tuple-element.16, bf16[1024,2,64]{2,1,0:T(2,128)(2,1)S(1)} %get-tuple-element.15), kind=kLoop, calls=%fused_computation.39 | loop fusion | flops 1048576 | bytes 1048576 | tf_op jit(solution)/shard_map/concatenate | solution.py:23
  40.9 1.2 reduce.2
  43.1 1.6 gather_fusion.2
  44.7 2.8 %pad_maximum_fusion.1 = bf16[64,32,512]{2,1,0:T(8,128)(2,1)} fusion(bf16[64,16,512]{2,1,0:T(8,128)(2,1)} %gather_fusion.2, bf16[64,16,512]{2,1,0:T(8,128)(2,1)S(1)} %bitcast.83), kind=kLoop, calls=%fused_computation.17 | loop fusion | flops 4194304 | bytes 4194304 | tf_op jit(solution)/shard_map/concatenate | solution.py:212
  47.5 10.3 %all-to-all-start.1 = ((bf16[64,32,512]{2,1,0:T(8,128)(2,1)}), bf16[64,32,512]{2,1,0:T(8,128)(2,1)S(1)}, u32[]{:S(2)}, u32[]{:S(2)}) async-start(bf16[64,32,512]{2,1,0:T(8,128)(2,1)} %pad_maximum_fusion.1), calls=%async_computation.1 | async-start | bytes 4194304 | tf_op jit(solution)/shard_map/all_to_all | solution.py:213
  62.0 1.9 copy.75
  63.9 2.7 %copy.60 = f32[1024,4,64]{2,1,0:T(4,128)} copy(f32[1024,4,64]{0,2,1:T(8,128)} %get-tuple-element.22) | data formatting | bytes 2097152
  66.7 2.7 %copy.61 = f32[1024,4,64]{2,1,0:T(4,128)} copy(f32[1024,4,64]{0,2,1:T(8,128)} %get-tuple-element.21) | data formatting | bytes 2097152
  70.0 1.9 concatenate.110.k_ref
  71.9 3.7 %convolution_convert_fusion = bf16[1024,256]{1,0:T(8,128)(2,1)S(1)} fusion(bf16[1024,2048]{1,0:T(8,128)(2,1)} %copy-done.13, bf16[2048,256]{1,0:T(8,128)(2,1)} %param.16), kind=kOutput, calls=%fused_computation.27 | convolution fusion | flops 1074003968 | bytes 5767168 | tf_op jit(solution)/shard_map/dot_general | solution.py:272
  76.4 0.9 concatenate.111.v_ref
  79.3 0.8 constant_dynamic-slice_fusion.6
  80.1 0.8 constant_dynamic-slice_fusion.3
  80.9 1.3 pad_maximum_fusion.3
  82.3 1.4 constant_dynamic-slice_fusion.res_ref
  84.8 1.3 add_select_fusion.bias_ref
  86.1 2.2 %multiply_subtract_fusion = (f32[1024,4,64]{2,1,0:T(4,128)S(1)}, f32[1024,4,64]{2,1,0:T(4,128)S(1)}) fusion(f32[1024,4,64]{2,1,0:T(4,128)S(1)} %copy-done.9, f32[1024,4,64]{2,1,0:T(4,128)S(1)} %copy-done.8, f32[1024,64]{1,0:T(8,128)} %copy-done.11, f32[1024,64]{1,0:T(8,128)} %copy-done.10), kind=kLoop, calls=%fused_computation.23 | loop fusion | flops 1572864 | bytes 4718592 | tf_op jit(solution)/shard_map/sub | solution.py:24
  88.3 2.5 %pad_maximum_fusion = f32[1024,4,128]{2,1,0:T(4,128)} fusion(f32[1024,4,64]{2,1,0:T(4,128)S(1)} %get-tuple-element.14, f32[1024,4,64]{2,1,0:T(4,128)S(1)} %get-tuple-element.13), kind=kLoop, calls=%fused_computation.16 | loop fusion | flops 524288 | bytes 4194304 | tf_op jit(solution)/shard_map/concatenate | solution.py:23
  90.9 16.5 %all-to-all-done.1 = bf16[64,32,512]{2,1,0:T(8,128)(2,1)S(1)} async-done(((bf16[64,32,512]{2,1,0:T(8,128)(2,1)}), bf16[64,32,512]{2,1,0:T(8,128)(2,1)S(1)}, u32[]{:S(2)}, u32[]{:S(2)}) %all-to-all-start.1) | async-done | bytes 2097184 | tf_op jit(solution)/shard_map/all_to_all | solution.py:213
  107.4 1.2 fusion.26
  108.5 2.8 %select_reduce_fusion = f32[1024,16]{0,1:T(8,128)S(1)} fusion(pred[1024,64]{0,1:T(8,128)(4,1)S(1)} %iota_compare_fusion, bf16[64,16,512]{2,1,0:T(8,128)(2,1)S(1)} %get-tuple-element.20, bf16[1024,2048]{1,0:T(8,128)(2,1)} %copy-done.13, s32[]{:T(128)S(6)} %select_n.75), kind=kOutput, calls=%fused_computation.9 | convolution fusion | flops 1075822592 | bytes 2228228 | tf_op jit(solution)/shard_map/dot_general | solution.py:227
  111.3 1.7 collective-permute-start
  113.0 4.4 %reshape_reshape.3 = bf16[1024,4,2,64]{3,2,1,0:T(2,128)(2,1)S(1)} reshape(bf16[64,16,512]{2,1,0:T(8,128)(2,1)} %get-tuple-element.19) | data formatting | bytes 2097152 | tf_op jit(solution)/shard_map/reshape;reshape | solution.py:251
  117.4 4.7 %slice_negate_fusion = (bf16[1024,4,1,64]{3,2,1,0:T(2,128)(2,1)S(1)}, bf16[1024,4,1,64]{3,2,1,0:T(2,128)(2,1)S(1)}) fusion(bf16[1024,4,2,64]{3,2,1,0:T(2,128)(2,1)S(1)} %reshape_reshape.3), kind=kLoop, calls=%fused_computation.15 | loop fusion | flops 262144 | bytes 2097152 | tf_op jit(solution)/shard_map/neg | solution.py:252
  122.1 3.2 %collective-permute-start.1 = (f32[1024,16]{0,1:T(8,128)S(1)}, f32[1024,16]{0,1:T(8,128)S(1)}, u32[]{:S(2)}, u32[]{:S(2)}) collective-permute-start(f32[1024,16]{0,1:T(8,128)S(1)} %add.155), channel_id=1, source_target_pairs={{0,2},{1,3},{2,0},{3,1},{4,6},{5,7},{6,4},{7,5},{8,10},{9,11},{10,... | collective-permute-start | bytes 196616 | tf_op jit(solution)/shard_map/ppermute | solution.py:233
  125.4 5.6 %pad_maximum_fusion.2 = bf16[1024,4,2,64]{3,2,1,0:T(2,128)(2,1)S(1)} fusion(bf16[1024,4,1,64]{3,2,1,0:T(2,128)(2,1)S(1)} %get-tuple-element.18, bf16[1024,4,1,64]{3,2,1,0:T(2,128)(2,1)S(1)} %get-tuple-element.17), kind=kLoop, calls=%fused_computation.18 | loop fusion | flops 2097152 | bytes 2097152 | tf_op jit(solution)/shard_map/concatenate | solution.py:252
  131.0 4.4 %copy.56 = bf16[1024,4,2,64]{0,3,2,1:T(8,128)(2,1)} copy(bf16[1024,4,2,64]{3,2,1,0:T(2,128)(2,1)S(1)} %pad_maximum_fusion.2) | data formatting | bytes 2097152 | tf_op jit(solution)/shard_map/concatenate | solution.py:252
  135.4 2.3 %copy.57 = bf16[1024,512]{1,0:T(8,128)(2,1)} copy(bf16[1024,512]{0,1:T(8,128)(2,1)} %bitcast.87) | data formatting | bytes 2097152 | tf_op jit(solution)/shard_map/reshape | solution.py:252
  137.8 1.2 copy.55
  139.3 2.4 %fusion.9 = f32[1024,1024]{1,0:T(8,128)S(1)} fusion(bf16[1024,1024]{0,1:T(8,128)(2,1)S(1)} %bitcast.92, bf16[1024,512]{1,0:T(8,128)(2,1)S(1)} %copy-done.19, bf16[1024,512]{1,0:T(8,128)(2,1)S(1)} %bitcast.88), kind=kOutput, calls=%fused_computation.25 | convolution fusion | flops 2154823680 | bytes 8388608 | tf_op jit(solution)/shard_map/dot_general | solution.py:257
  143.5 1.3 fusion.4.q_ref
  145.2 55.1 %shard_map.118 = bf16[1024,512]{1,0:T(8,128)(2,1)S(1)} custom-call(bf16[1024,512]{1,0:T(8,128)(2,1)S(1)} %fusion.4.q_ref, bf16[1152,256]{1,0:T(8,128)(2,1)S(1)} %copy-done.3, bf16[1152,256]{1,0:T(8,128)(2,1)S(1)} %copy-done.4, bf16[128,256]{1,0:T(8,128)(2,1)S(1)} %get-tuple-element.38.kp_ref, bf16[128,256]{1,0:T(8,128)(2,1)S(1)} %get-tuple-element.37.vp_ref, ...), custom_call_target="tpu_custom_call" | custom-call | tf_op jit(solution)/shard_map/pallas_call | solution.py:158
  200.4 1.0 copy.77
  (105 shorter events, 11.4 us)
Async XLA Ops:
  0.0 29.4 %copy-start = (bf16[2048,512]{1,0:T(8,128)(2,1)S(1)}, bf16[2048,512]{1,0:T(8,128)(2,1)}, u32[]{:S(2)}) copy-start(bf16[2048,512]{1,0:T(8,128)(2,1)} %param.14) | copy-start | bytes 6291460
  3.0 37.9 %all-to-all-start = ((s32[64,1,1]{2,1,0:T(1,128)}), s32[64,1,1]{2,1,0:T(1,128)S(1)}, u32[]{:S(2)}, u32[]{:S(2)}) async-start(s32[64,1,1]{2,1,0:T(1,128)} %copy.53), calls=%async_computation | async-start | bytes 65536 | tf_op jit(solution)/shard_map/all_to_all | solution.py:207
  19.9 3.5 %copy-start.6 = (bf16[1024,2048]{1,0:T(8,128)(2,1)S(1)}, bf16[1024,2048]{1,0:T(8,128)(2,1)}, u32[]{:S(2)}) copy-start(bf16[1024,2048]{1,0:T(8,128)(2,1)} %param.12) | copy-start | bytes 12582916
  19.9 3.4 %copy-start.23 = (f32[2048]{0:T(1024)S(1)}, f32[2048]{0:T(1024)}, u32[]{:S(2)}) copy-start(f32[2048]{0:T(1024)} %param.13) | copy-start | bytes 24580
  23.4 1.2 copy-start.24
  24.6 1.9 copy-start.13
  26.7 2.5 %copy-start.21 = (s32[1,32]{1,0:T(1,128)S(1)}, s32[1,32]{1,0:T(1,128)}, u32[]{:S(2)}) copy-start(s32[1,32]{1,0:T(1,128)} %param.21) | copy-start | bytes 388
  33.9 3.6 %copy-start.15 = (f32[1024,2,64]{2,1,0:T(2,128)S(1)}, f32[1024,2,64]{2,1,0:T(2,128)}, u32[]{:S(2)}) copy-start(f32[1024,2,64]{2,1,0:T(2,128)} %copy.63) | copy-start | bytes 1572868
  33.9 3.6 %copy-start.16 = (f32[1024,2,64]{2,1,0:T(2,128)S(1)}, f32[1024,2,64]{2,1,0:T(2,128)}, u32[]{:S(2)}) copy-start(f32[1024,2,64]{2,1,0:T(2,128)} %copy.64) | copy-start | bytes 1572868
  37.5 43.4 %copy-start.10 = (f32[1024,64]{1,0:T(8,128)}, f32[1024,64]{1,0:T(8,128)S(1)}, u32[]{:S(2)}) copy-start(f32[1024,64]{1,0:T(8,128)S(1)} %get-tuple-element.31) | copy-start | bytes 786436
  37.5 43.4 %copy-start.11 = (f32[1024,64]{1,0:T(8,128)}, f32[1024,64]{1,0:T(8,128)S(1)}, u32[]{:S(2)}) copy-start(f32[1024,64]{1,0:T(8,128)S(1)} %get-tuple-element.32) | copy-start | bytes 786436
  37.5 4.6 %copy-start.5 = (bf16[16,512,16]{1,2,0:T(8,128)(2,1)S(1)}, bf16[16,512,16]{1,2,0:T(8,128)(2,1)}, u32[]{:S(2)}) copy-start(bf16[16,512,16]{1,2,0:T(8,128)(2,1)} %param.18) | copy-start | bytes 786436
  42.2 1.0 copy-start.12
  47.5 59.9 %all-to-all-start.1 = ((bf16[64,32,512]{2,1,0:T(8,128)(2,1)}), bf16[64,32,512]{2,1,0:T(8,128)(2,1)S(1)}, u32[]{:S(2)}, u32[]{:S(2)}) async-start(bf16[64,32,512]{2,1,0:T(8,128)(2,1)} %pad_maximum_fusion.1), calls=%async_computation.1 | async-start | bytes 4194304 | tf_op jit(solution)/shard_map/all_to_all | solution.py:213
  71.9 7.4 %copy-start.22 = (s32[8,128]{1,0:T(8,128)S(1)}, s32[8,128]{1,0:T(8,128)}, u32[]{:S(2)}) copy-start(s32[8,128]{1,0:T(8,128)} %constant.106.clone.1) | copy-start | bytes 12292
  75.6 0.8 copy-start.20
  82.3 3.8 %copy-start.8 = (f32[1024,4,64]{2,1,0:T(4,128)S(1)}, f32[1024,4,64]{2,1,0:T(4,128)}, u32[]{:S(2)}) copy-start(f32[1024,4,64]{2,1,0:T(4,128)} %copy.60) | copy-start | bytes 3145732
  82.3 3.8 %copy-start.9 = (f32[1024,4,64]{2,1,0:T(4,128)S(1)}, f32[1024,4,64]{2,1,0:T(4,128)}, u32[]{:S(2)}) copy-start(f32[1024,4,64]{2,1,0:T(4,128)} %copy.61) | copy-start | bytes 3145732
  111.3 10.8 %collective-permute-start = (f32[1024,16]{0,1:T(8,128)S(1)}, f32[1024,16]{0,1:T(8,128)S(1)}, u32[]{:S(2)}, u32[]{:S(2)}) collective-permute-start(f32[1024,16]{0,1:T(8,128)S(1)} %select_reduce_fusion), channel_id=1, source_target_pairs={{0,1},{1,0},{2,3},{3,2},{4,5},{5,4},{6,7},{7,6},{8,9},{9,8},{10,11... | collective-permute-start | bytes 196616 | tf_op jit(solution)/shard_map/ppermute | solution.py:233
  122.1 15.5 %collective-permute-start.1 = (f32[1024,16]{0,1:T(8,128)S(1)}, f32[1024,16]{0,1:T(8,128)S(1)}, u32[]{:S(2)}, u32[]{:S(2)}) collective-permute-start(f32[1024,16]{0,1:T(8,128)S(1)} %add.155), channel_id=1, source_target_pairs={{0,2},{1,3},{2,0},{3,1},{4,6},{5,7},{6,4},{7,5},{8,10},{9,11},{10,... | collective-permute-start | bytes 196616 | tf_op jit(solution)/shard_map/ppermute | solution.py:233
  137.8 1.2 copy-start.14
  137.8 1.5 copy-start.19
  139.3 2.4 %copy-start.18 = (f32[1024,128]{1,0:T(8,128)S(1)}, f32[1024,128]{1,0:T(8,128)}, u32[]{:S(2)}) copy-start(f32[1024,128]{1,0:T(8,128)} %get-tuple-element.46) | copy-start | bytes 1572868
  141.8 1.0 copy-start.17
  141.8 1.8 copy-start.7
  143.5 1.4 copy-start.2
  143.5 1.5 copy-start.3
  143.5 1.7 copy-start.4
  145.2 56.1 %copy-start.1 = (bf16[2048,512]{1,0:T(8,128)(2,1)S(1)}, bf16[2048,512]{1,0:T(8,128)(2,1)}, u32[]{:S(2)}) copy-start(bf16[2048,512]{1,0:T(8,128)(2,1)} %param.14) | copy-start | bytes 6291460

commit v6 on v2

--- a/solution.py
+++ b/solution.py
@@ -59,7 +59,7 @@
 
 
 def attend_kernel(
-    q_ref, k_ref, v_ref, kp_ref, vp_ref, bias_ref, wo_ref, res_ref, out_ref,
+    q_ref, cs_ref, sn_ref, k_ref, v_ref, kp_ref, vp_ref, bias_ref, wo_ref, res_ref, out_ref,
     send_buf, recv_buf, send_sems, recv_sems, *, tp_count, heads, kv_heads, n_blocks
 ):
     me = lax.axis_index("tp")
@@ -90,10 +90,13 @@
     def block_body(b, carry):
         row = pl.multiple_of(b * BLOCK, BLOCK)
         bias = bias_ref[b]
+        cs = cs_ref[pl.ds(row, BLOCK), :]
+        sn = sn_ref[pl.ds(row, BLOCK), :]
         outs = []
         for h in range(heads):
             g = h // rep
-            qh = q_ref[pl.ds(row, BLOCK), pl.ds(h * 128, 128)]
+            qf = q_ref[pl.ds(row, BLOCK), pl.ds(h * 128, 128)]
+            qh = (qf * cs + pltpu.roll(qf, 64, 1) * sn).astype(jnp.bfloat16)
             kw = k_ref[pl.ds(row, 2 * BLOCK), pl.ds(g * 128, 128)]
             vw = v_ref[pl.ds(row, 2 * BLOCK), pl.ds(g * 128, 128)]
             kp = kp_ref[:, pl.ds(g * 128, 128)]
@@ -142,7 +145,7 @@
     lax.fori_loop(0, n_blocks, finish_body, 0)
 
 
-def attend_and_reduce(q, k_pad, v_pad, k_prompt, v_prompt, bias, wo, residual, tp_count):
+def attend_and_reduce(q, cs, sn, k_pad, v_pad, k_prompt, v_prompt, bias, wo, residual, tp_count):
     rows, q_width = q.shape
     n_blocks = rows // BLOCK
     piece = residual.shape[1]
@@ -158,7 +161,7 @@
     return pl.pallas_call(
         kernel,
         out_shape=jax.ShapeDtypeStruct((rows, piece), jnp.bfloat16),
-        in_specs=[pl.BlockSpec(memory_space=vmem)] * 8,
+        in_specs=[pl.BlockSpec(memory_space=vmem)] * 10,
         out_specs=pl.BlockSpec(memory_space=vmem),
         scratch_shapes=[
             pltpu.VMEM((n_blocks, BLOCK, width), jnp.bfloat16),
@@ -169,7 +172,7 @@
         compiler_params=pltpu.CompilerParams(
             collective_id=0, has_side_effects=True, vmem_limit_bytes=48 * 1024 * 1024
         ),
-    )(q, k_pad, v_pad, k_prompt, v_prompt, bias, wo, residual)
+    )(q, cs, sn, k_pad, v_pad, k_prompt, v_prompt, bias, wo, residual)
 
 
 def per_device(
@@ -243,9 +246,13 @@
     query_full = jnp.dot(
         normalized_input, query_matrix, preferred_element_type=jnp.float32
     ) + query_delta.astype(jnp.float32)
-    query_heads = apply_rotary(
-        query_full.reshape(tok_rows, heads_local, HEAD_WIDTH), token_positions
-    ).astype(jnp.bfloat16)
+    half_dim = HEAD_WIDTH // 2
+    inverse = 1000000.0 ** (-(jnp.arange(half_dim, dtype=jnp.float32) * 2.0 / HEAD_WIDTH))
+    angles = token_positions[:, None] * inverse[None, :]
+    cosine = jnp.cos(angles)
+    sine = jnp.sin(angles)
+    cos_pair = jnp.concatenate([cosine, cosine], 1)
+    sin_pair = jnp.concatenate([-sine, sine], 1)
     key_complete = jnp.dot(normalized_input, key_matrix, preferred_element_type=jnp.float32)
     key_head_rows = apply_rotary(
         key_complete.reshape(tok_rows, kv_local, HEAD_WIDTH), token_positions
@@ -315,7 +322,9 @@
     bias = jnp.where(vis, jnp.float32(0.0), jnp.float32(-1e30))
     residual = lax.dynamic_slice_in_dim(tokens, tp_index * piece_width, piece_width, 1)
     return attend_and_reduce(
-        query_heads.reshape(tok_rows, heads_local * HEAD_WIDTH),
+        query_full,
+        cos_pair,
+        sin_pair,
         k_pad,
         v_pad,
         k_prompt,

time: 190 us -> 181 us (0.953)
  local copies, waits for them, and re-layouts: 24.7 us -> 17.8 us
  other arithmetic: 27.3 us -> 24 us
    unnamed x45 -> x40, local copies, waits for them, and re-layouts: 11.1 us -> 6.43 us
    all_to_all x1, waiting for transfers between devices: 33.7 us -> 30.4 us  [per_device(): lax.all_to_all(maps_out, 'req', split_axis=0, concat_axis=0, tiled=True)]
    cos x1 -> x0, other arithmetic: 3.07 us -> none  [apply_rotary(): cosine = jnp.cos(angles)[:, None, :]]
    neg x0 -> x1, other arithmetic: none -> 2.95 us  [per_device(): sin_pair = jnp.concatenate([-sine, sine], 1)]
    another operation x4 -> x3, other arithmetic: 5.51 us -> 3.21 us
    ppermute x2, waiting for transfers between devices: 1.61 us -> 3.82 us  [per_device(): partial_rank = partial_rank + lax.ppermute(partial_rank, 'tp', pairs)]
  transfers between devices with their start and end apart: 4 -> 4, of which waited for: 2 -> 3; matrix products, arithmetic and copies ran while one was open for 18% -> 20% of each run, Pallas kernels for 0% -> 0%
where the time goes in v6:
time: 181 us; the launch traced here: 179 us
  Pallas kernels  54.5 us (30%)
  waiting for transfers between devices  34.2 us (19%)
  starting transfers between devices  27.6 us (15%)
  other arithmetic  24 us (13%)
  local copies, waits for them, and re-layouts  17.8 us (10%)
  matrix products  14.8 us (8%)
  between operations  6.31 us (3%)
    pallas_call x1, Pallas kernels, attend_and_reduce(): pl.pallas_call(kernel, out_shape=jax.ShapeDtypeStruct((rows, piece), jnp....  54.5 us
    all_to_all x1, waiting for transfers between devices, per_device(): lax.all_to_all(maps_out, 'req', split_axis=0, concat_axis=0, tiled=True)  30.4 us
    all_to_all x1, starting transfers between devices, per_device(): lax.all_to_all(wanted.reshape(req_count, 1), 'req', split_axis=0, concat_...  12 us
    all_to_all x1, starting transfers between devices, per_device(): lax.all_to_all(maps_out, 'req', split_axis=0, concat_axis=0, tiled=True)  10.7 us
    unnamed x40, local copies, waits for them, and re-layouts  6.43 us
    ppermute x2, starting transfers between devices, per_device(): partial_rank = partial_rank + lax.ppermute(partial_rank, 'tp', pairs)  4.93 us
    dot_general x1, matrix products, per_device(): jnp.dot(normalized_input, value_matrix, preferred_element_type=jnp.float32)  3.88 us
    ppermute x2, waiting for transfers between devices, per_device(): partial_rank = partial_rank + lax.ppermute(partial_rank, 'tp', pairs)  3.82 us
  transfers between devices with their start and end apart: 4, of which 3 were waited for; matrix products, arithmetic and copies ran while one was open for 20% of the time, Pallas kernels for 0%

profile of v6, /device:TPU:2, one launch (start us, length us, event | category | flops | bytes accessed | tf_op | source)
XLA Modules:
  0.0 179.3 jit_solution(2840818070095037368)
XLA Ops:
  0.0 0.8 fusion.22
  0.8 1.4 gather_fusion
  2.2 0.1 select_reduce_fusion.6
  2.3 0.7 copy.34
  3.0 12.0 %all-to-all-start = ((s32[64,1,1]{2,1,0:T(1,128)}), s32[64,1,1]{2,1,0:T(1,128)S(1)}, u32[]{:S(2)}, u32[]{:S(2)}) async-start(s32[64,1,1]{2,1,0:T(1,128)} %copy.34), calls=%async_computation | async-start | bytes 65536 | tf_op jit(solution)/shard_map/all_to_all | solution.py:210
  15.1 0.7 copy.33
  15.9 0.1 reduce
  16.0 0.9 select_bitcast_fusion
  16.9 0.9 select_bitcast_fusion.1
  17.9 0.9 select_reduce_fusion.5
  18.8 0.7 fusion.27
  19.5 0.8 select_reduce_fusion.1
  20.3 3.1 %fusion = f32[1024]{0:T(1024)S(1)} fusion(bf16[1024,2048]{1,0:T(8,128)(2,1)} %param.12), kind=kLoop, calls=%fused_computation.5 | loop fusion | flops 6290432 | bytes 4198400 | tf_op jit(solution)/shard_map/reduce_sum | solution.py:222
  23.4 1.0 fusion.2
  24.4 0.2 copy-done.16
  24.6 1.3 fusion.34
  25.9 0.6 copy-done.8
  26.5 1.0 fusion.30
  27.6 1.5 copy.41
  29.1 2.2 %copy.42 = f32[1024,2,64]{2,1,0:T(2,128)} copy(f32[1024,2,64]{0,2,1:T(8,128)} %get-tuple-element.17) | data formatting | bytes 1048576
  31.2 3.0 %fusion.17 = (f32[1024,64]{1,0:T(8,128)}, f32[1024,64]{1,0:T(8,128)S(1)}, f32[1024,64]{1,0:T(8,128)S(1)}) fusion(f32[64]{0:T(128)S(1)} %negate_power_fusion, f32[1024]{0:T(1024)S(1)} %add_convert_fusion.2), kind=kLoop, calls=%fused_computation.35 | loop fusion | flops 131072 | bytes 790784 | tf_op jit(solution)/shard_map/neg | solution.py:255
  34.2 0.8 copy-done.4
  35.0 3.0 %subtract_convert_fusion = (bf16[1024,2,64]{2,1,0:T(2,128)(2,1)}, bf16[1024,2,64]{2,1,0:T(2,128)(2,1)}) fusion(f32[1024,2,64]{2,1,0:T(2,128)} %copy.42, f32[1024,2,64]{2,1,0:T(2,128)S(1)} %copy.41, f32[1024,64]{1,0:T(8,128)S(1)} %get-tuple-element.26, f32[1024,64]{1,0:T(8,128)S(1)} %get-tuple-element.27), kind=kLoop, calls=%fused_computation.22 | loop fusion | flops 1048576 | bytes 2097152 | tf_op jit(solution)/shard_map/convert
  38.1 0.1 select_reduce_fusion.7
  38.2 1.2 reduce.1
  39.5 0.6 gather_fusion.1
  40.1 2.5 %gather_fusion.2 = bf16[64,16,512]{2,1,0:T(8,128)(2,1)} fusion(bf16[16,16,512]{2,1,0:T(8,128)(2,1)} %param.19, s32[1024]{0:T(1024)S(1)} %pad_clamp_fusion), kind=kCustom, calls=%fused_computation.2 | custom fusion | bytes 2097408 | tf_op jit(solution)/shard_map/gather | solution.py:214
  42.6 2.8 %pad_maximum_fusion = bf16[64,32,512]{2,1,0:T(8,128)(2,1)} fusion(bf16[64,16,512]{2,1,0:T(8,128)(2,1)} %gather_fusion.2, bf16[64,16,512]{2,1,0:T(8,128)(2,1)S(1)} %bitcast.67), kind=kLoop, calls=%fused_computation.9 | loop fusion | flops 4194304 | bytes 4194304 | tf_op jit(solution)/shard_map/concatenate | solution.py:215
  45.4 10.7 %all-to-all-start.1 = ((bf16[64,32,512]{2,1,0:T(8,128)(2,1)}), bf16[64,32,512]{2,1,0:T(8,128)(2,1)}, u32[]{:S(2)}, u32[]{:S(2)}) async-start(bf16[64,32,512]{2,1,0:T(8,128)(2,1)} %pad_maximum_fusion), calls=%async_computation.1 | async-start | bytes 4194304 | tf_op jit(solution)/shard_map/all_to_all | solution.py:216
  56.1 0.7 fusion.32
  60.7 1.4 pad_maximum_fusion.3
  65.0 3.9 %convolution_convert_fusion = bf16[1024,256]{1,0:T(8,128)(2,1)S(1)} fusion(bf16[1024,2048]{1,0:T(8,128)(2,1)} %copy-done.8, bf16[2048,256]{1,0:T(8,128)(2,1)} %param.16), kind=kOutput, calls=%fused_computation.17 | convolution fusion | flops 1074003968 | bytes 5767168 | tf_op jit(solution)/shard_map/dot_general | solution.py:261
  69.0 0.3 compare_and_fusion
  69.3 0.6 or_and_fusion
  70.0 1.3 add_select_fusion.bias_ref
  71.5 3.7 %fusion.33 = f32[1024,512]{1,0:T(8,128)} fusion(bf16[1024,2048]{1,0:T(8,128)(2,1)S(1)} %copy-done.9, bf16[2048,512]{1,0:T(8,128)(2,1)S(1)} %copy-done), kind=kOutput, calls=%fused_computation.108 | convolution fusion | flops 2147483648 | bytes 8388608 | tf_op jit(solution)/shard_map/dot_general | solution.py:246
  75.2 30.4 %all-to-all-done.1 = bf16[64,32,512]{2,1,0:T(8,128)(2,1)} async-done(((bf16[64,32,512]{2,1,0:T(8,128)(2,1)}), bf16[64,32,512]{2,1,0:T(8,128)(2,1)}, u32[]{:S(2)}, u32[]{:S(2)}) %all-to-all-start.1) | async-done | bytes 2097184 | tf_op jit(solution)/shard_map/all_to_all | solution.py:216
  105.5 1.7 fusion.29
  107.3 2.9 %select_reduce_fusion = f32[1024,16]{0,1:T(8,128)S(1)} fusion(pred[1024,64]{0,1:T(8,128)(4,1)S(1)} %iota_compare_fusion, bf16[64,16,512]{2,1,0:T(8,128)(2,1)S(1)} %get-tuple-element.15, bf16[1024,2048]{1,0:T(8,128)(2,1)} %copy-done.8, s32[]{:T(128)S(6)} %select_n.71), kind=kOutput, calls=%fused_computation.8 | convolution fusion | flops 1075822592 | bytes 2228228 | tf_op jit(solution)/shard_map/dot_general | solution.py:230
  110.2 1.7 collective-permute-start
  111.9 1.3 constant_dynamic-slice_fusion.res_ref
  113.2 1.7 collective-permute-done
  114.9 3.3 %collective-permute-start.1 = (f32[1024,16]{0,1:T(8,128)S(1)}, f32[1024,16]{0,1:T(8,128)S(1)}, u32[]{:S(2)}, u32[]{:S(2)}) collective-permute-start(f32[1024,16]{0,1:T(8,128)S(1)} %add.147), channel_id=1, source_target_pairs={{0,2},{1,3},{2,0},{3,1},{4,6},{5,7},{6,4},{7,5},{8,10},{9,11},{10,... | collective-permute-start | bytes 196616 | tf_op jit(solution)/shard_map/ppermute | solution.py:236
  118.2 0.3 pad_maximum_fusion.1
  118.6 2.1 %collective-permute-done.1 = f32[1024,16]{0,1:T(8,128)S(1)} collective-permute-done((f32[1024,16]{0,1:T(8,128)S(1)}, f32[1024,16]{0,1:T(8,128)S(1)}, u32[]{:S(2)}, u32[]{:S(2)}) %collective-permute-start.1) | collective-permute-done | bytes 65568 | tf_op jit(solution)/shard_map/ppermute | solution.py:236
  120.8 3.0 %convert_add_fusion.q_ref = f32[1024,512]{1,0:T(8,128)} fusion(f32[1024,512]{1,0:T(8,128)S(1)} %copy-done.17, pred[1024,64]{0,1:T(8,128)(4,1)S(1)} %iota_compare_fusion, bf16[64,16,512]{2,1,0:T(8,128)(2,1)S(1)} %get-tuple-element.16, bf16[1024,16]{0,1:T(8,128)(2,1)S(1)} %add_convert_fusion.1), kind=kOutput, calls=%fused_computation.12 | convolution fusion | flops 1076887552 | bytes 5341184 | tf_op jit(solution)/shard_map/dot_general | solution.py:242
  123.8 54.5 %shard_map.118 = bf16[1024,512]{1,0:T(8,128)(2,1)S(1)} custom-call(f32[1024,512]{1,0:T(8,128)} %convert_add_fusion.q_ref, f32[1024,128]{1,0:T(8,128)S(1)} %get-tuple-element.41.cs_ref, f32[1024,128]{1,0:T(8,128)S(1)} %get-tuple-element.42.sn_ref, bf16[1152,256]{1,0:T(8,128)(2,1)S(1)} %concatenate.98.k_ref, bf16[1152,256]{1,0:T(8,128)(2,1)S(1)} %concatenate.99.v_ref, ...), custom_call_target="tpu_custom_call" | custom-call | tf_op jit(solution)/shard_map/pallas_call | solution.py:161
  178.3 1.0 copy.51
  (76 shorter events, 1.4 us)
Async XLA Ops:
  0.0 71.4 %copy-start = (bf16[2048,512]{1,0:T(8,128)(2,1)S(1)}, bf16[2048,512]{1,0:T(8,128)(2,1)}, u32[]{:S(2)}) copy-start(bf16[2048,512]{1,0:T(8,128)(2,1)} %param.14) | copy-start | bytes 6291460
  0.0 23.3 %copy-start.15 = (f32[2048]{0:T(1024)S(1)}, f32[2048]{0:T(1024)}, u32[]{:S(2)}) copy-start(f32[2048]{0:T(1024)} %param.13) | copy-start | bytes 24580
  3.0 35.2 %all-to-all-start = ((s32[64,1,1]{2,1,0:T(1,128)}), s32[64,1,1]{2,1,0:T(1,128)S(1)}, u32[]{:S(2)}, u32[]{:S(2)}) async-start(s32[64,1,1]{2,1,0:T(1,128)} %copy.34), calls=%async_computation | async-start | bytes 65536 | tf_op jit(solution)/shard_map/all_to_all | solution.py:210
  16.0 7.4 %copy-start.3 = (bf16[1024,2048]{1,0:T(8,128)(2,1)S(1)}, bf16[1024,2048]{1,0:T(8,128)(2,1)}, u32[]{:S(2)}) copy-start(bf16[1024,2048]{1,0:T(8,128)(2,1)} %param.12) | copy-start | bytes 12582916
  23.4 1.2 copy-start.16
  24.6 1.9 %copy-start.8 = (bf16[1024,2048]{1,0:T(8,128)(2,1)}, bf16[1024,2048]{1,0:T(8,128)(2,1)S(1)}, u32[]{:S(2)}) copy-start(bf16[1024,2048]{1,0:T(8,128)(2,1)S(1)} %fusion.2) | copy-start | bytes 12582916
  27.6 10.5 %copy-start.13 = (s32[1,32]{1,0:T(1,128)S(1)}, s32[1,32]{1,0:T(1,128)}, u32[]{:S(2)}) copy-start(s32[1,32]{1,0:T(1,128)} %param.21) | copy-start | bytes 388
  27.6 11.9 %copy-start.2 = (bf16[16,512,16]{1,2,0:T(8,128)(2,1)S(1)}, bf16[16,512,16]{1,2,0:T(8,128)(2,1)}, u32[]{:S(2)}) copy-start(bf16[16,512,16]{1,2,0:T(8,128)(2,1)} %param.18) | copy-start | bytes 786436
  34.2 0.8 copy-start.4
  34.2 3.9 %copy-start.6 = (f32[1024,64]{1,0:T(8,128)}, f32[1024,64]{1,0:T(8,128)S(1)}, u32[]{:S(2)}) copy-start(f32[1024,64]{1,0:T(8,128)S(1)} %get-tuple-element.27) | copy-start | bytes 786436
  45.4 15.3 %copy-start.11 = (bf16[1024,2,64]{2,1,0:T(2,128)(2,1)S(1)}, bf16[1024,2,64]{2,1,0:T(2,128)(2,1)}, u32[]{:S(2)}) copy-start(bf16[1024,2,64]{2,1,0:T(2,128)(2,1)} %get-tuple-element.13) | copy-start | bytes 786436
  45.4 15.3 %copy-start.12 = (bf16[1024,2,64]{2,1,0:T(2,128)(2,1)S(1)}, bf16[1024,2,64]{2,1,0:T(2,128)(2,1)}, u32[]{:S(2)}) copy-start(bf16[1024,2,64]{2,1,0:T(2,128)(2,1)} %get-tuple-element.14) | copy-start | bytes 786436
  45.4 19.5 %copy-start.14 = (s32[8,128]{1,0:T(8,128)S(1)}, s32[8,128]{1,0:T(8,128)}, u32[]{:S(2)}) copy-start(s32[8,128]{1,0:T(8,128)} %constant.106.clone.1) | copy-start | bytes 12292
  45.4 60.1 %all-to-all-start.1 = ((bf16[64,32,512]{2,1,0:T(8,128)(2,1)}), bf16[64,32,512]{2,1,0:T(8,128)(2,1)}, u32[]{:S(2)}, u32[]{:S(2)}) async-start(bf16[64,32,512]{2,1,0:T(8,128)(2,1)} %pad_maximum_fusion), calls=%async_computation.1 | async-start | bytes 4194304 | tf_op jit(solution)/shard_map/all_to_all | solution.py:216
  65.0 6.5 %copy-start.9 = (bf16[1024,2048]{1,0:T(8,128)(2,1)S(1)}, bf16[1024,2048]{1,0:T(8,128)(2,1)}, u32[]{:S(2)}) copy-start(bf16[1024,2048]{1,0:T(8,128)(2,1)} %copy-done.8) | copy-start | bytes 12582916
  107.3 10.9 %copy-start.5 = (f32[1024,64]{1,0:T(8,128)S(1)}, f32[1024,64]{1,0:T(8,128)}, u32[]{:S(2)}) copy-start(f32[1024,64]{1,0:T(8,128)} %copy-done.4) | copy-start | bytes 786436
  107.3 10.9 %copy-start.7 = (f32[1024,64]{1,0:T(8,128)S(1)}, f32[1024,64]{1,0:T(8,128)}, u32[]{:S(2)}) copy-start(f32[1024,64]{1,0:T(8,128)} %copy-done.6) | copy-start | bytes 786436
  107.3 10.9 %copy-start.10 = (f32[1024,64]{1,0:T(8,128)S(1)}, f32[1024,64]{1,0:T(8,128)}, u32[]{:S(2)}) copy-start(f32[1024,64]{1,0:T(8,128)} %get-tuple-element.25) | copy-start | bytes 786436
  110.2 10.5 %copy-start.17 = (f32[1024,512]{1,0:T(8,128)S(1)}, f32[1024,512]{1,0:T(8,128)}, u32[]{:S(2)}) copy-start(f32[1024,512]{1,0:T(8,128)} %fusion.33) | copy-start | bytes 6291460
  110.2 4.6 %collective-permute-start = (f32[1024,16]{0,1:T(8,128)S(1)}, f32[1024,16]{0,1:T(8,128)S(1)}, u32[]{:S(2)}, u32[]{:S(2)}) collective-permute-start(f32[1024,16]{0,1:T(8,128)S(1)} %select_reduce_fusion), channel_id=1, source_target_pairs={{0,1},{1,0},{2,3},{3,2},{4,5},{5,4},{6,7},{7,6},{8,9},{9,8},{10,11... | collective-permute-start | bytes 196616 | tf_op jit(solution)/shard_map/ppermute | solution.py:236
  114.9 5.9 %collective-permute-start.1 = (f32[1024,16]{0,1:T(8,128)S(1)}, f32[1024,16]{0,1:T(8,128)S(1)}, u32[]{:S(2)}, u32[]{:S(2)}) collective-permute-start(f32[1024,16]{0,1:T(8,128)S(1)} %add.147), channel_id=1, source_target_pairs={{0,2},{1,3},{2,0},{3,1},{4,6},{5,7},{6,4},{7,5},{8,10},{9,11},{10,... | collective-permute-start | bytes 196616 | tf_op jit(solution)/shard_map/ppermute | solution.py:236
  120.8 3.0 %copy-start.1 = (f32[8,128,384]{2,1,0:T(8,128)S(1)}, f32[8,128,384]{2,1,0:T(8,128)}, u32[]{:S(2)}) copy-start(f32[8,128,384]{2,1,0:T(8,128)} %add_select_fusion.bias_ref) | copy-start | bytes 4718596

commit v7 on v6

--- a/solution.py
+++ b/solution.py
@@ -231,9 +231,12 @@
         normed_slice, down_in.T, preferred_element_type=jnp.float32
     ).reshape(tok_rows, req_count, rank_extent)
     partial_rank = jnp.sum(jnp.where(pick, wide_rank, jnp.float32(0.0)), 1)
-    for step in (1, 2):
-        pairs = [(i, i ^ step) for i in range(tp_count)]
-        partial_rank = partial_rank + lax.ppermute(partial_rank, "tp", pairs)
+    arrived = [
+        lax.ppermute(partial_rank, "tp", [(i, (i + k) % tp_count) for i in range(tp_count)])
+        for k in range(1, tp_count)
+    ]
+    for piece in arrived:
+        partial_rank = partial_rank + piece
     rank = partial_rank.astype(jnp.bfloat16)
     spread = jnp.where(pick, rank[:, None, :], jnp.zeros((), jnp.bfloat16)).reshape(
         tok_rows, req_count * rank_extent

time: 181 us -> 179 us (0.989)
  waiting for transfers between devices: 34.2 us -> 32.3 us
    ppermute x2 -> x3, starting transfers between devices: 4.93 us -> 5.91 us  [per_device(): lax.ppermute(partial_rank, 'tp', [(i, (i + k) % tp_count) for i in range(...]
    ppermute x2 -> x3, waiting for transfers between devices: 3.82 us -> 3.08 us  [per_device(): lax.ppermute(partial_rank, 'tp', [(i, (i + k) % tp_count) for i in range(...]
    unnamed x40 -> x48, local copies, waits for them, and re-layouts: 6.43 us -> 6.43 us
  transfers between devices with their start and end apart: 4 -> 5, of which waited for: 3 -> 3; matrix products, arithmetic and copies ran while one was open for 20% -> 20% of each run, Pallas kernels for 0% -> 0%
where the time goes in v7:
time: 179 us
  Pallas kernels  55.1 us (31%)
  waiting for transfers between devices  32.3 us (18%)
  starting transfers between devices  28.6 us (16%)
  other arithmetic  24 us (13%)
  local copies, waits for them, and re-layouts  18.1 us (10%)
  matrix products  14.7 us (8%)
  between operations  6.15 us (3%)
    pallas_call x1, Pallas kernels, attend_and_reduce(): pl.pallas_call(kernel, out_shape=jax.ShapeDtypeStruct((rows, piece), jnp....  55.1 us
    all_to_all x1, waiting for transfers between devices, per_device(): lax.all_to_all(maps_out, 'req', split_axis=0, concat_axis=0, tiled=True)  29.2 us
    all_to_all x1, starting transfers between devices, per_device(): lax.all_to_all(wanted.reshape(req_count, 1), 'req', split_axis=0, concat_...  12 us
    all_to_all x1, starting transfers between devices, per_device(): lax.all_to_all(maps_out, 'req', split_axis=0, concat_axis=0, tiled=True)  10.7 us
    unnamed x48, local copies, waits for them, and re-layouts  6.43 us
    ppermute x3, starting transfers between devices, per_device(): lax.ppermute(partial_rank, 'tp', [(i, (i + k) % tp_count) for i in range(...  5.91 us
    dot_general x1, matrix products, per_device(): jnp.dot(normalized_input, value_matrix, preferred_element_type=jnp.float32)  3.74 us
    dot_general x1, matrix products, per_device(): jnp.dot(normalized_input, query_matrix, preferred_element_type=jnp.float32)  3.67 us
  transfers between devices with their start and end apart: 5, of which 3 were waited for; matrix products, arithmetic and copies ran while one was open for 20% of the time, Pallas kernels for 0%

profile of v7, /device:TPU:2, one launch (start us, length us, event | category | flops | bytes accessed | tf_op | source)
XLA Modules:
  0.0 178.9 jit_solution(4633363656586811684)
XLA Ops:
  0.0 0.8 fusion.22
  0.8 1.4 gather_fusion
  2.3 0.7 copy.34
  3.0 12.0 %all-to-all-start = ((s32[64,1,1]{2,1,0:T(1,128)}), s32[64,1,1]{2,1,0:T(1,128)S(1)}, u32[]{:S(2)}, u32[]{:S(2)}) async-start(s32[64,1,1]{2,1,0:T(1,128)} %copy.34), calls=%async_computation | async-start | bytes 65536 | tf_op jit(solution)/shard_map/all_to_all | solution.py:210
  15.1 0.7 copy.33
  15.9 0.1 reduce
  16.0 0.9 select_bitcast_fusion
  16.9 0.9 select_bitcast_fusion.1
  17.9 0.9 select_reduce_fusion.5
  18.8 0.7 fusion.27
  19.5 0.8 select_reduce_fusion.1
  20.3 3.1 %fusion = f32[1024]{0:T(1024)S(1)} fusion(bf16[1024,2048]{1,0:T(8,128)(2,1)} %param.12), kind=kLoop, calls=%fused_computation.5 | loop fusion | flops 6290432 | bytes 4198400 | tf_op jit(solution)/shard_map/reduce_sum | solution.py:222
  23.4 1.0 fusion.2
  24.4 0.2 copy-done.20
  24.6 1.3 fusion.34
  25.9 0.6 copy-done.8
  26.5 1.0 fusion.30
  27.6 1.5 copy.41
  29.1 2.2 %copy.42 = f32[1024,2,64]{2,1,0:T(2,128)} copy(f32[1024,2,64]{0,2,1:T(8,128)} %get-tuple-element.17) | data formatting | bytes 1048576
  31.3 0.1 select_reduce_fusion.7
  31.4 3.0 %fusion.17 = (f32[1024,64]{1,0:T(8,128)}, f32[1024,64]{1,0:T(8,128)S(1)}, f32[1024,64]{1,0:T(8,128)S(1)}) fusion(f32[64]{0:T(128)S(1)} %negate_power_fusion, f32[1024]{0:T(1024)S(1)} %add_convert_fusion.2), kind=kLoop, calls=%fused_computation.35 | loop fusion | flops 131072 | bytes 790784 | tf_op jit(solution)/shard_map/neg | solution.py:258
  34.4 0.8 copy-done.4
  35.2 3.0 %subtract_convert_fusion = (bf16[1024,2,64]{2,1,0:T(2,128)(2,1)}, bf16[1024,2,64]{2,1,0:T(2,128)(2,1)}) fusion(f32[1024,2,64]{2,1,0:T(2,128)} %copy.42, f32[1024,2,64]{2,1,0:T(2,128)S(1)} %copy.41, f32[1024,64]{1,0:T(8,128)S(1)} %get-tuple-element.26, f32[1024,64]{1,0:T(8,128)S(1)} %get-tuple-element.27), kind=kLoop, calls=%fused_computation.22 | loop fusion | flops 1048576 | bytes 2097152 | tf_op jit(solution)/shard_map/convert
  38.3 1.2 reduce.1
  39.5 0.6 gather_fusion.1
  40.1 2.5 %gather_fusion.2 = bf16[64,16,512]{2,1,0:T(8,128)(2,1)} fusion(bf16[16,16,512]{2,1,0:T(8,128)(2,1)} %param.19, s32[1024]{0:T(1024)S(1)} %pad_clamp_fusion), kind=kCustom, calls=%fused_computation.2 | custom fusion | bytes 2097408 | tf_op jit(solution)/shard_map/gather | solution.py:214
  42.7 2.8 %pad_maximum_fusion = bf16[64,32,512]{2,1,0:T(8,128)(2,1)} fusion(bf16[64,16,512]{2,1,0:T(8,128)(2,1)} %gather_fusion.2, bf16[64,16,512]{2,1,0:T(8,128)(2,1)S(1)} %bitcast.67), kind=kLoop, calls=%fused_computation.9 | loop fusion | flops 4194304 | bytes 4194304 | tf_op jit(solution)/shard_map/concatenate | solution.py:215
  45.5 10.7 %all-to-all-start.1 = ((bf16[64,32,512]{2,1,0:T(8,128)(2,1)}), bf16[64,32,512]{2,1,0:T(8,128)(2,1)}, u32[]{:S(2)}, u32[]{:S(2)}) async-start(bf16[64,32,512]{2,1,0:T(8,128)(2,1)} %pad_maximum_fusion), calls=%async_computation.1 | async-start | bytes 4194304 | tf_op jit(solution)/shard_map/all_to_all | solution.py:216
  56.1 0.7 fusion.32
  60.6 1.4 pad_maximum_fusion.3
  64.8 3.7 %convolution_convert_fusion = bf16[1024,256]{1,0:T(8,128)(2,1)S(1)} fusion(bf16[1024,2048]{1,0:T(8,128)(2,1)} %copy-done.8, bf16[2048,256]{1,0:T(8,128)(2,1)} %param.16), kind=kOutput, calls=%fused_computation.17 | convolution fusion | flops 1074003968 | bytes 5767168 | tf_op jit(solution)/shard_map/dot_general | solution.py:264
  68.6 1.5 constant_dynamic-slice_fusion.res_ref
  70.2 0.3 compare_and_fusion
  70.5 0.6 or_and_fusion
  71.2 1.3 add_select_fusion.bias_ref
  72.7 3.7 %fusion.33 = f32[1024,512]{1,0:T(8,128)} fusion(bf16[1024,2048]{1,0:T(8,128)(2,1)S(1)} %copy-done.9, bf16[2048,512]{1,0:T(8,128)(2,1)S(1)} %copy-done), kind=kOutput, calls=%fused_computation.108 | convolution fusion | flops 2147483648 | bytes 8388608 | tf_op jit(solution)/shard_map/dot_general | solution.py:249
  76.3 29.2 %all-to-all-done.1 = bf16[64,32,512]{2,1,0:T(8,128)(2,1)} async-done(((bf16[64,32,512]{2,1,0:T(8,128)(2,1)}), bf16[64,32,512]{2,1,0:T(8,128)(2,1)}, u32[]{:S(2)}, u32[]{:S(2)}) %all-to-all-start.1) | async-done | bytes 2097184 | tf_op jit(solution)/shard_map/all_to_all | solution.py:216
  105.6 1.7 fusion.29
  107.3 3.0 %select_reduce_fusion = f32[1024,16]{0,1:T(8,128)S(1)} fusion(pred[1024,64]{0,1:T(8,128)(4,1)S(1)} %iota_compare_fusion, bf16[64,16,512]{2,1,0:T(8,128)(2,1)S(1)} %get-tuple-element.15, bf16[1024,2048]{1,0:T(8,128)(2,1)} %copy-done.8, s32[]{:T(128)S(6)} %select_n.71), kind=kOutput, calls=%fused_computation.8 | convolution fusion | flops 1075822592 | bytes 2228228 | tf_op jit(solution)/shard_map/dot_general | solution.py:230
  110.3 1.7 collective-permute-start
  112.0 2.9 %collective-permute-start.1 = (f32[1024,16]{0,1:T(8,128)S(1)}, f32[1024,16]{0,1:T(8,128)S(1)}, u32[]{:S(2)}, u32[]{:S(2)}) collective-permute-start(f32[1024,16]{0,1:T(8,128)S(1)} %select_reduce_fusion), channel_id=1, source_target_pairs={{0,2},{1,3},{2,0},{3,1},{4,6},{5,7},{6,4},{7,5},{8,10},{9,11},{10,... | collective-permute-start | bytes 196616 | tf_op jit(solution)/shard_map/ppermute | solution.py:235
  114.9 1.3 collective-permute-start.2
  116.2 0.3 pad_maximum_fusion.1
  116.7 2.1 %collective-permute-done.1 = f32[1024,16]{0,1:T(8,128)S(1)} collective-permute-done((f32[1024,16]{0,1:T(8,128)S(1)}, f32[1024,16]{0,1:T(8,128)S(1)}, u32[]{:S(2)}, u32[]{:S(2)}) %collective-permute-start.1) | collective-permute-done | bytes 65568 | tf_op jit(solution)/shard_map/ppermute | solution.py:235
  118.8 1.0 collective-permute-done.2
  119.8 3.0 %convert_add_fusion.q_ref = f32[1024,512]{1,0:T(8,128)} fusion(f32[1024,512]{1,0:T(8,128)S(1)} %copy-done.21, pred[1024,64]{0,1:T(8,128)(4,1)S(1)} %iota_compare_fusion, bf16[64,16,512]{2,1,0:T(8,128)(2,1)S(1)} %get-tuple-element.16, bf16[1024,16]{0,1:T(8,128)(2,1)S(1)} %add_convert_fusion.1), kind=kOutput, calls=%fused_computation.12 | convolution fusion | flops 1076887552 | bytes 5341184 | tf_op jit(solution)/shard_map/dot_general | solution.py:245
  122.8 55.1 %shard_map.118 = bf16[1024,512]{1,0:T(8,128)(2,1)S(1)} custom-call(f32[1024,512]{1,0:T(8,128)} %convert_add_fusion.q_ref, f32[1024,128]{1,0:T(8,128)S(1)} %get-tuple-element.41.cs_ref, f32[1024,128]{1,0:T(8,128)S(1)} %get-tuple-element.42.sn_ref, bf16[1152,256]{1,0:T(8,128)(2,1)S(1)} %concatenate.98.k_ref, bf16[1152,256]{1,0:T(8,128)(2,1)S(1)} %concatenate.99.v_ref, ...), custom_call_target="tpu_custom_call" | custom-call | tf_op jit(solution)/shard_map/pallas_call | solution.py:161
  177.9 1.0 copy.51
  (85 shorter events, 1.5 us)
Async XLA Ops:
  0.0 72.7 %copy-start = (bf16[2048,512]{1,0:T(8,128)(2,1)S(1)}, bf16[2048,512]{1,0:T(8,128)(2,1)}, u32[]{:S(2)}) copy-start(bf16[2048,512]{1,0:T(8,128)(2,1)} %param.14) | copy-start | bytes 6291460
  0.0 23.4 %copy-start.19 = (f32[2048]{0:T(1024)S(1)}, f32[2048]{0:T(1024)}, u32[]{:S(2)}) copy-start(f32[2048]{0:T(1024)} %param.13) | copy-start | bytes 24580
  3.0 35.2 %all-to-all-start = ((s32[64,1,1]{2,1,0:T(1,128)}), s32[64,1,1]{2,1,0:T(1,128)S(1)}, u32[]{:S(2)}, u32[]{:S(2)}) async-start(s32[64,1,1]{2,1,0:T(1,128)} %copy.34), calls=%async_computation | async-start | bytes 65536 | tf_op jit(solution)/shard_map/all_to_all | solution.py:210
  16.0 7.4 %copy-start.3 = (bf16[1024,2048]{1,0:T(8,128)(2,1)S(1)}, bf16[1024,2048]{1,0:T(8,128)(2,1)}, u32[]{:S(2)}) copy-start(bf16[1024,2048]{1,0:T(8,128)(2,1)} %param.12) | copy-start | bytes 12582916
  23.4 1.2 copy-start.20
  24.6 1.9 %copy-start.8 = (bf16[1024,2048]{1,0:T(8,128)(2,1)}, bf16[1024,2048]{1,0:T(8,128)(2,1)S(1)}, u32[]{:S(2)}) copy-start(bf16[1024,2048]{1,0:T(8,128)(2,1)S(1)} %fusion.2) | copy-start | bytes 12582916
  26.5 4.7 %copy-start.17 = (s32[1,32]{1,0:T(1,128)S(1)}, s32[1,32]{1,0:T(1,128)}, u32[]{:S(2)}) copy-start(s32[1,32]{1,0:T(1,128)} %param.21) | copy-start | bytes 388
  27.6 11.9 %copy-start.2 = (bf16[16,512,16]{1,2,0:T(8,128)(2,1)S(1)}, bf16[16,512,16]{1,2,0:T(8,128)(2,1)}, u32[]{:S(2)}) copy-start(bf16[16,512,16]{1,2,0:T(8,128)(2,1)} %param.18) | copy-start | bytes 786436
  34.4 0.8 copy-start.4
  34.4 3.9 %copy-start.6 = (f32[1024,64]{1,0:T(8,128)}, f32[1024,64]{1,0:T(8,128)S(1)}, u32[]{:S(2)}) copy-start(f32[1024,64]{1,0:T(8,128)S(1)} %get-tuple-element.27) | copy-start | bytes 786436
  45.5 15.1 %copy-start.13 = (bf16[1024,2,64]{2,1,0:T(2,128)(2,1)S(1)}, bf16[1024,2,64]{2,1,0:T(2,128)(2,1)}, u32[]{:S(2)}) copy-start(bf16[1024,2,64]{2,1,0:T(2,128)(2,1)} %get-tuple-element.13) | copy-start | bytes 786436
  45.5 15.1 %copy-start.14 = (bf16[1024,2,64]{2,1,0:T(2,128)(2,1)S(1)}, bf16[1024,2,64]{2,1,0:T(2,128)(2,1)}, u32[]{:S(2)}) copy-start(bf16[1024,2,64]{2,1,0:T(2,128)(2,1)} %get-tuple-element.14) | copy-start | bytes 786436
  45.5 19.2 %copy-start.18 = (s32[8,128]{1,0:T(8,128)S(1)}, s32[8,128]{1,0:T(8,128)}, u32[]{:S(2)}) copy-start(s32[8,128]{1,0:T(8,128)} %constant.106.clone.1) | copy-start | bytes 12292
  45.5 60.1 %all-to-all-start.1 = ((bf16[64,32,512]{2,1,0:T(8,128)(2,1)}), bf16[64,32,512]{2,1,0:T(8,128)(2,1)}, u32[]{:S(2)}, u32[]{:S(2)}) async-start(bf16[64,32,512]{2,1,0:T(8,128)(2,1)} %pad_maximum_fusion), calls=%async_computation.1 | async-start | bytes 4194304 | tf_op jit(solution)/shard_map/all_to_all | solution.py:216
  62.1 6.5 %copy-start.10 = (bf16[128,8,2,128]{3,1,2,0:T(8,128)(2,1)}, bf16[128,8,2,128]{3,1,2,0:T(8,128)(2,1)S(1)}, u32[]{:S(2)}) copy-start(bf16[128,8,2,128]{3,1,2,0:T(8,128)(2,1)S(1)} %copy.49) | copy-start | bytes 1572868
  68.5 4.0 %copy-start.15 = (bf16[1024,256]{1,0:T(8,128)(2,1)}, bf16[1024,256]{1,0:T(8,128)(2,1)S(1)}, u32[]{:S(2)}) copy-start(bf16[1024,256]{1,0:T(8,128)(2,1)S(1)} %convolution_convert_fusion) | copy-start | bytes 1572868
  68.6 4.1 %copy-start.9 = (bf16[1024,2048]{1,0:T(8,128)(2,1)S(1)}, bf16[1024,2048]{1,0:T(8,128)(2,1)}, u32[]{:S(2)}) copy-start(bf16[1024,2048]{1,0:T(8,128)(2,1)} %copy-done.8) | copy-start | bytes 12582916
  107.3 8.9 %copy-start.5 = (f32[1024,64]{1,0:T(8,128)S(1)}, f32[1024,64]{1,0:T(8,128)}, u32[]{:S(2)}) copy-start(f32[1024,64]{1,0:T(8,128)} %copy-done.4) | copy-start | bytes 786436
  107.3 8.9 %copy-start.7 = (f32[1024,64]{1,0:T(8,128)S(1)}, f32[1024,64]{1,0:T(8,128)}, u32[]{:S(2)}) copy-start(f32[1024,64]{1,0:T(8,128)} %copy-done.6) | copy-start | bytes 786436
  107.3 8.9 %copy-start.12 = (f32[1024,64]{1,0:T(8,128)S(1)}, f32[1024,64]{1,0:T(8,128)}, u32[]{:S(2)}) copy-start(f32[1024,64]{1,0:T(8,128)} %get-tuple-element.25) | copy-start | bytes 786436
  107.3 9.3 %copy-start.11 = (bf16[128,8,2,128]{3,1,2,0:T(8,128)(2,1)S(1)}, bf16[128,8,2,128]{3,1,2,0:T(8,128)(2,1)}, u32[]{:S(2)}) copy-start(bf16[128,8,2,128]{3,1,2,0:T(8,128)(2,1)} %copy-done.10) | copy-start | bytes 1572868
  107.3 9.3 %copy-start.16 = (bf16[1024,256]{1,0:T(8,128)(2,1)S(1)}, bf16[1024,256]{1,0:T(8,128)(2,1)}, u32[]{:S(2)}) copy-start(bf16[1024,256]{1,0:T(8,128)(2,1)} %copy-done.15) | copy-start | bytes 1572868
  110.3 9.5 %copy-start.21 = (f32[1024,512]{1,0:T(8,128)S(1)}, f32[1024,512]{1,0:T(8,128)}, u32[]{:S(2)}) copy-start(f32[1024,512]{1,0:T(8,128)} %fusion.33) | copy-start | bytes 6291460
  110.3 6.4 %collective-permute-start = (f32[1024,16]{0,1:T(8,128)S(1)}, f32[1024,16]{0,1:T(8,128)S(1)}, u32[]{:S(2)}, u32[]{:S(2)}) collective-permute-start(f32[1024,16]{0,1:T(8,128)S(1)} %select_reduce_fusion), channel_id=1, source_target_pairs={{0,1},{1,2},{2,3},{3,0},{4,5},{5,6},{6,7},{7,4},{8,9},{9,10},{10,1... | collective-permute-start | bytes 196616 | tf_op jit(solution)/shard_map/ppermute | solution.py:235
  112.0 6.8 %collective-permute-start.1 = (f32[1024,16]{0,1:T(8,128)S(1)}, f32[1024,16]{0,1:T(8,128)S(1)}, u32[]{:S(2)}, u32[]{:S(2)}) collective-permute-start(f32[1024,16]{0,1:T(8,128)S(1)} %select_reduce_fusion), channel_id=1, source_target_pairs={{0,2},{1,3},{2,0},{3,1},{4,6},{5,7},{6,4},{7,5},{8,10},{9,11},{10,... | collective-permute-start | bytes 196616 | tf_op jit(solution)/shard_map/ppermute | solution.py:235
  114.9 4.9 %collective-permute-start.2 = (f32[1024,16]{0,1:T(8,128)S(1)}, f32[1024,16]{0,1:T(8,128)S(1)}, u32[]{:S(2)}, u32[]{:S(2)}) collective-permute-start(f32[1024,16]{0,1:T(8,128)S(1)} %select_reduce_fusion), channel_id=1, source_target_pairs={{0,3},{1,0},{2,1},{3,2},{4,7},{5,4},{6,5},{7,6},{8,11},{9,8},{10,9... | collective-permute-start | bytes 196616 | tf_op jit(solution)/shard_map/ppermute | solution.py:235
  119.8 3.0 %copy-start.1 = (f32[8,128,384]{2,1,0:T(8,128)S(1)}, f32[8,128,384]{2,1,0:T(8,128)}, u32[]{:S(2)}) copy-start(f32[8,128,384]{2,1,0:T(8,128)} %add_select_fusion.bias_ref) | copy-start | bytes 4718596

commit v8 on v7

--- a/solution.py
+++ b/solution.py
@@ -60,32 +60,63 @@
 
 def attend_kernel(
     q_ref, cs_ref, sn_ref, k_ref, v_ref, kp_ref, vp_ref, bias_ref, wo_ref, res_ref, out_ref,
-    send_buf, recv_buf, send_sems, recv_sems, *, tp_count, heads, kv_heads, n_blocks
+    send_buf, relay_in, sum_buf, recv_buf, send_sems, recv_sems, *, tp_count, heads, kv_heads,
+    n_blocks
 ):
     me = lax.axis_index("tp")
     row_dev = lax.axis_index("req")
     piece = out_ref.shape[1]
+    half = piece // 2
+    up = lax.rem(me + 1, tp_count)
+    down = lax.rem(me + tp_count - 1, tp_count)
+    across = lax.rem(me + 2, tp_count)
     barrier = pltpu.get_barrier_semaphore()
-    for k in range(1, tp_count):
-        peer = lax.rem(me + k, tp_count)
+    for peer in (up, down):
         pl.semaphore_signal(
             barrier, inc=1, device_id=(row_dev, peer), device_id_type=pl.DeviceIdType.MESH
         )
-    pl.semaphore_wait(barrier, tp_count - 1)
+    pl.semaphore_wait(barrier, 2)
     rep = heads // kv_heads
 
-    def copy_of(b, k, source):
-        peer = lax.rem(me + k, tp_count)
-        col = pl.multiple_of(peer * piece, piece)
+    def raw_copy(b, side):
+        col = pl.multiple_of(across * piece + side * half, half)
+        return pltpu.make_async_remote_copy(
+            src_ref=send_buf.at[b, :, pl.ds(col, half)],
+            dst_ref=relay_in.at[b, side],
+            send_sem=send_sems.at[b * 4 + side],
+            recv_sem=recv_sems.at[b * 4 + side],
+            device_id=(row_dev, up if side == 0 else down),
+            device_id_type=pl.DeviceIdType.MESH,
+        )
+
+    def sum_copy(b, side):
         row = pl.multiple_of(b * BLOCK, BLOCK)
         return pltpu.make_async_remote_copy(
-            src_ref=send_buf.at[b, :, pl.ds(col, piece)],
-            dst_ref=recv_buf.at[source, pl.ds(row, BLOCK)],
-            send_sem=send_sems.at[b * tp_count + k],
-            recv_sem=recv_sems.at[source * n_blocks + b],
-            device_id=(row_dev, peer),
+            src_ref=sum_buf.at[b, side],
+            dst_ref=recv_buf.at[side, pl.ds(row, BLOCK)],
+            send_sem=send_sems.at[b * 4 + 2 + side],
+            recv_sem=recv_sems.at[b * 4 + 2 + side],
+            device_id=(row_dev, up if side == 0 else down),
             device_id_type=pl.DeviceIdType.MESH,
         )
+
+    def forward(b):
+        raw_copy(b, 0).wait_recv()
+        raw_copy(b, 1).wait_recv()
+        col_up = pl.multiple_of(up * piece, piece)
+        col_down = pl.multiple_of(down * piece, piece)
+        to_up = send_buf[b, :, pl.ds(col_up, piece)].astype(jnp.float32)
+        to_down = send_buf[b, :, pl.ds(col_down, piece)].astype(jnp.float32)
+        from_down = relay_in[b, 0].astype(jnp.float32)
+        from_up = relay_in[b, 1].astype(jnp.float32)
+        sum_buf[b, 0] = jnp.concatenate(
+            [to_up[:, :half] + from_down, to_up[:, half:]], 1
+        ).astype(sum_buf.dtype)
+        sum_buf[b, 1] = jnp.concatenate(
+            [to_down[:, :half], to_down[:, half:] + from_up], 1
+        ).astype(sum_buf.dtype)
+        sum_copy(b, 0).start()
+        sum_copy(b, 1).start()
 
     def block_body(b, carry):
         row = pl.multiple_of(b * BLOCK, BLOCK)
@@ -116,17 +147,23 @@
         att = jnp.concatenate(outs, 1)
         part = jnp.dot(att, wo_ref[...], preferred_element_type=jnp.float32)
         send_buf[b] = part.astype(jnp.bfloat16)
-        for k in range(1, tp_count):
-            copy_of(b, k, me).start()
+        raw_copy(b, 0).start()
+        raw_copy(b, 1).start()
+
+        @pl.when(b > 0)
+        def _():
+            forward(b - 1)
+
         return carry
 
     lax.fori_loop(0, n_blocks, block_body, 0)
+    forward(n_blocks - 1)
 
     def wait_body(b, carry):
-        for k in range(1, tp_count):
-            copy_of(b, k, me).wait_send()
-            source = lax.rem(me + tp_count - k, tp_count)
-            copy_of(b, k, source).wait_recv()
+        for side in (0, 1):
+            raw_copy(b, side).wait_send()
+            sum_copy(b, side).wait_send()
+            sum_copy(b, side).wait_recv()
         return carry
 
     lax.fori_loop(0, n_blocks, wait_body, 0)
@@ -136,9 +173,8 @@
         row = pl.multiple_of(b * BLOCK, BLOCK)
         total = res_ref[pl.ds(row, BLOCK), :].astype(jnp.float32)
         total = total + send_buf[b, :, pl.ds(own, piece)].astype(jnp.float32)
-        for k in range(1, tp_count):
-            source = lax.rem(me + tp_count - k, tp_count)
-            total = total + recv_buf[source, pl.ds(row, BLOCK), :].astype(jnp.float32)
+        for side in (0, 1):
+            total = total + recv_buf[side, pl.ds(row, BLOCK), :].astype(jnp.float32)
         out_ref[pl.ds(row, BLOCK), :] = total.astype(out_ref.dtype)
         return carry
 
@@ -165,9 +201,11 @@
         out_specs=pl.BlockSpec(memory_space=vmem),
         scratch_shapes=[
             pltpu.VMEM((n_blocks, BLOCK, width), jnp.bfloat16),
-            pltpu.VMEM((tp_count, rows, piece), jnp.bfloat16),
-            pltpu.SemaphoreType.DMA((n_blocks * tp_count,)),
-            pltpu.SemaphoreType.DMA((tp_count * n_blocks,)),
+            pltpu.VMEM((n_blocks, 2, BLOCK, piece // 2), jnp.bfloat16),
+            pltpu.VMEM((n_blocks, 2, BLOCK, piece), jnp.bfloat16),
+            pltpu.VMEM((2, rows, piece), jnp.bfloat16),
+            pltpu.SemaphoreType.DMA((n_blocks * 4,)),
+            pltpu.SemaphoreType.DMA((n_blocks * 4,)),
         ],
         compiler_params=pltpu.CompilerParams(
             collective_id=0, has_side_effects=True, vmem_limit_bytes=48 * 1024 * 1024

time: 179 us -> 169 us (0.944)
  Pallas kernels: 55.1 us -> 44.4 us
    pallas_call x1, Pallas kernels: 55.1 us -> 44.4 us  [attend_and_reduce(): pl.pallas_call(kernel, out_shape=jax.ShapeDtypeStruct((rows, piece), jnp....]
  transfers between devices with their start and end apart: 5 -> 5, of which waited for: 3 -> 3; matrix products, arithmetic and copies ran while one was open for 20% -> 22% of each run, Pallas kernels for 0% -> 0%
where the time goes in v8:
time: 169 us; the launch traced here: 168 us
  Pallas kernels  44.4 us (26%)
  waiting for transfers between devices  32.3 us (19%)
  starting transfers between devices  28.6 us (17%)
  other arithmetic  24 us (14%)
  local copies, waits for them, and re-layouts  18.1 us (11%)
  matrix products  14.7 us (9%)
  between operations  6.15 us (4%)
    pallas_call x1, Pallas kernels, attend_and_reduce(): pl.pallas_call(kernel, out_shape=jax.ShapeDtypeStruct((rows, piece), jnp....  44.4 us
    all_to_all x1, waiting for transfers between devices, per_device(): lax.all_to_all(maps_out, 'req', split_axis=0, concat_axis=0, tiled=True)  29.2 us
    all_to_all x1, starting transfers between devices, per_device(): lax.all_to_all(wanted.reshape(req_count, 1), 'req', split_axis=0, concat_...  12 us
    all_to_all x1, starting transfers between devices, per_device(): lax.all_to_all(maps_out, 'req', split_axis=0, concat_axis=0, tiled=True)  10.7 us
    unnamed x48, local copies, waits for them, and re-layouts  6.43 us
    ppermute x3, starting transfers between devices, per_device(): lax.ppermute(partial_rank, 'tp', [(i, (i + k) % tp_count) for i in range(...  5.91 us
    dot_general x1, matrix products, per_device(): jnp.dot(normalized_input, value_matrix, preferred_element_type=jnp.float32)  3.74 us
    dot_general x1, matrix products, per_device(): jnp.dot(normalized_input, query_matrix, preferred_element_type=jnp.float32)  3.67 us
  transfers between devices with their start and end apart: 5, of which 3 were waited for; matrix products, arithmetic and copies ran while one was open for 22% of the time, Pallas kernels for 0%

profile of v8, /device:TPU:2, one launch (start us, length us, event | category | flops | bytes accessed | tf_op | source)
XLA Modules:
  0.0 168.2 jit_solution(9730196766445575274)
XLA Ops:
  0.0 0.8 fusion.22
  0.8 1.4 gather_fusion
  2.3 0.7 copy.34
  3.0 12.0 %all-to-all-start = ((s32[64,1,1]{2,1,0:T(1,128)}), s32[64,1,1]{2,1,0:T(1,128)S(1)}, u32[]{:S(2)}, u32[]{:S(2)}) async-start(s32[64,1,1]{2,1,0:T(1,128)} %copy.34), calls=%async_computation | async-start | bytes 65536 | tf_op jit(solution)/shard_map/all_to_all | solution.py:248
  15.1 0.7 copy.33
  15.9 0.1 reduce
  16.0 0.9 select_bitcast_fusion
  16.9 0.9 select_bitcast_fusion.1
  17.9 0.9 select_reduce_fusion.5
  18.8 0.7 fusion.27
  19.5 0.8 select_reduce_fusion.1
  20.3 3.1 %fusion = f32[1024]{0:T(1024)S(1)} fusion(bf16[1024,2048]{1,0:T(8,128)(2,1)} %param.12), kind=kLoop, calls=%fused_computation.5 | loop fusion | flops 6290432 | bytes 4198400 | tf_op jit(solution)/shard_map/reduce_sum | solution.py:260
  23.4 1.0 fusion.2
  24.4 0.2 copy-done.20
  24.6 1.3 fusion.34
  25.9 0.6 copy-done.8
  26.5 1.0 fusion.30
  27.6 1.5 copy.41
  29.1 2.2 %copy.42 = f32[1024,2,64]{2,1,0:T(2,128)} copy(f32[1024,2,64]{0,2,1:T(8,128)} %get-tuple-element.17) | data formatting | bytes 1048576
  31.3 0.1 select_reduce_fusion.7
  31.4 3.0 %fusion.17 = (f32[1024,64]{1,0:T(8,128)}, f32[1024,64]{1,0:T(8,128)S(1)}, f32[1024,64]{1,0:T(8,128)S(1)}) fusion(f32[64]{0:T(128)S(1)} %negate_power_fusion, f32[1024]{0:T(1024)S(1)} %add_convert_fusion.2), kind=kLoop, calls=%fused_computation.35 | loop fusion | flops 131072 | bytes 790784 | tf_op jit(solution)/shard_map/neg | solution.py:296
  34.4 0.8 copy-done.4
  35.2 3.0 %subtract_convert_fusion = (bf16[1024,2,64]{2,1,0:T(2,128)(2,1)}, bf16[1024,2,64]{2,1,0:T(2,128)(2,1)}) fusion(f32[1024,2,64]{2,1,0:T(2,128)} %copy.42, f32[1024,2,64]{2,1,0:T(2,128)S(1)} %copy.41, f32[1024,64]{1,0:T(8,128)S(1)} %get-tuple-element.26, f32[1024,64]{1,0:T(8,128)S(1)} %get-tuple-element.27), kind=kLoop, calls=%fused_computation.22 | loop fusion | flops 1048576 | bytes 2097152 | tf_op jit(solution)/shard_map/convert
  38.3 1.2 reduce.1
  39.5 0.6 gather_fusion.1
  40.1 2.5 %gather_fusion.2 = bf16[64,16,512]{2,1,0:T(8,128)(2,1)} fusion(bf16[16,16,512]{2,1,0:T(8,128)(2,1)} %param.19, s32[1024]{0:T(1024)S(1)} %pad_clamp_fusion), kind=kCustom, calls=%fused_computation.2 | custom fusion | bytes 2097408 | tf_op jit(solution)/shard_map/gather | solution.py:252
  42.7 2.8 %pad_maximum_fusion = bf16[64,32,512]{2,1,0:T(8,128)(2,1)} fusion(bf16[64,16,512]{2,1,0:T(8,128)(2,1)} %gather_fusion.2, bf16[64,16,512]{2,1,0:T(8,128)(2,1)S(1)} %bitcast.67), kind=kLoop, calls=%fused_computation.9 | loop fusion | flops 4194304 | bytes 4194304 | tf_op jit(solution)/shard_map/concatenate | solution.py:253
  45.5 10.7 %all-to-all-start.1 = ((bf16[64,32,512]{2,1,0:T(8,128)(2,1)}), bf16[64,32,512]{2,1,0:T(8,128)(2,1)}, u32[]{:S(2)}, u32[]{:S(2)}) async-start(bf16[64,32,512]{2,1,0:T(8,128)(2,1)} %pad_maximum_fusion), calls=%async_computation.1 | async-start | bytes 4194304 | tf_op jit(solution)/shard_map/all_to_all | solution.py:254
  56.1 0.7 fusion.32
  60.6 1.4 pad_maximum_fusion.3
  64.8 3.7 %convolution_convert_fusion = bf16[1024,256]{1,0:T(8,128)(2,1)S(1)} fusion(bf16[1024,2048]{1,0:T(8,128)(2,1)} %copy-done.8, bf16[2048,256]{1,0:T(8,128)(2,1)} %param.16), kind=kOutput, calls=%fused_computation.17 | convolution fusion | flops 1074003968 | bytes 5767168 | tf_op jit(solution)/shard_map/dot_general | solution.py:302
  68.6 1.5 constant_dynamic-slice_fusion.res_ref
  70.2 0.3 compare_and_fusion
  70.5 0.6 or_and_fusion
  71.2 1.3 add_select_fusion.bias_ref
  72.7 3.7 %fusion.33 = f32[1024,512]{1,0:T(8,128)} fusion(bf16[1024,2048]{1,0:T(8,128)(2,1)S(1)} %copy-done.9, bf16[2048,512]{1,0:T(8,128)(2,1)S(1)} %copy-done), kind=kOutput, calls=%fused_computation.108 | convolution fusion | flops 2147483648 | bytes 8388608 | tf_op jit(solution)/shard_map/dot_general | solution.py:287
  76.3 29.2 %all-to-all-done.1 = bf16[64,32,512]{2,1,0:T(8,128)(2,1)} async-done(((bf16[64,32,512]{2,1,0:T(8,128)(2,1)}), bf16[64,32,512]{2,1,0:T(8,128)(2,1)}, u32[]{:S(2)}, u32[]{:S(2)}) %all-to-all-start.1) | async-done | bytes 2097184 | tf_op jit(solution)/shard_map/all_to_all | solution.py:254
  105.6 1.7 %fusion.29 = (bf16[64,16,512]{2,1,0:T(8,128)(2,1)S(1)}, bf16[64,16,512]{2,1,0:T(8,128)(2,1)S(1)}) fusion(bf16[64,32,512]{2,1,0:T(8,128)(2,1)} %all-to-all-done.1), kind=kLoop, calls=%fused_computation.104 | loop fusion | bytes 4194304 | tf_op jit(solution)/shard_map/slice | solution.py:255
  107.3 3.0 %select_reduce_fusion = f32[1024,16]{0,1:T(8,128)S(1)} fusion(pred[1024,64]{0,1:T(8,128)(4,1)S(1)} %iota_compare_fusion, bf16[64,16,512]{2,1,0:T(8,128)(2,1)S(1)} %get-tuple-element.15, bf16[1024,2048]{1,0:T(8,128)(2,1)} %copy-done.8, s32[]{:T(128)S(6)} %select_n.71), kind=kOutput, calls=%fused_computation.8 | convolution fusion | flops 1075822592 | bytes 2228228 | tf_op jit(solution)/shard_map/dot_general | solution.py:268
  110.3 1.7 collective-permute-start
  112.0 2.9 %collective-permute-start.1 = (f32[1024,16]{0,1:T(8,128)S(1)}, f32[1024,16]{0,1:T(8,128)S(1)}, u32[]{:S(2)}, u32[]{:S(2)}) collective-permute-start(f32[1024,16]{0,1:T(8,128)S(1)} %select_reduce_fusion), channel_id=1, source_target_pairs={{0,2},{1,3},{2,0},{3,1},{4,6},{5,7},{6,4},{7,5},{8,10},{9,11},{10,... | collective-permute-start | bytes 196616 | tf_op jit(solution)/shard_map/ppermute | solution.py:273
  114.9 1.3 collective-permute-start.2
  116.2 0.3 pad_maximum_fusion.1
  116.7 2.1 %collective-permute-done.1 = f32[1024,16]{0,1:T(8,128)S(1)} collective-permute-done((f32[1024,16]{0,1:T(8,128)S(1)}, f32[1024,16]{0,1:T(8,128)S(1)}, u32[]{:S(2)}, u32[]{:S(2)}) %collective-permute-start.1) | collective-permute-done | bytes 65568 | tf_op jit(solution)/shard_map/ppermute | solution.py:273
  118.8 1.0 collective-permute-done.2
  119.8 3.0 %convert_add_fusion.q_ref = f32[1024,512]{1,0:T(8,128)} fusion(f32[1024,512]{1,0:T(8,128)S(1)} %copy-done.21, pred[1024,64]{0,1:T(8,128)(4,1)S(1)} %iota_compare_fusion, bf16[64,16,512]{2,1,0:T(8,128)(2,1)S(1)} %get-tuple-element.16, bf16[1024,16]{0,1:T(8,128)(2,1)S(1)} %add_convert_fusion.1), kind=kOutput, calls=%fused_computation.12 | convolution fusion | flops 1076887552 | bytes 5341184 | tf_op jit(solution)/shard_map/dot_general | solution.py:283
  122.8 44.4 %shard_map.118 = bf16[1024,512]{1,0:T(8,128)(2,1)S(1)} custom-call(f32[1024,512]{1,0:T(8,128)} %convert_add_fusion.q_ref, f32[1024,128]{1,0:T(8,128)S(1)} %get-tuple-element.41.cs_ref, f32[1024,128]{1,0:T(8,128)S(1)} %get-tuple-element.42.sn_ref, bf16[1152,256]{1,0:T(8,128)(2,1)S(1)} %concatenate.98.k_ref, bf16[1152,256]{1,0:T(8,128)(2,1)S(1)} %concatenate.99.v_ref, ...), custom_call_target="tpu_custom_call" | custom-call | tf_op jit(solution)/shard_map/pallas_call | solution.py:197
  167.2 1.0 copy.51
  (85 shorter events, 1.5 us)
Async XLA Ops:
  0.0 72.7 %copy-start = (bf16[2048,512]{1,0:T(8,128)(2,1)S(1)}, bf16[2048,512]{1,0:T(8,128)(2,1)}, u32[]{:S(2)}) copy-start(bf16[2048,512]{1,0:T(8,128)(2,1)} %param.14) | copy-start | bytes 6291460
  0.0 23.4 %copy-start.19 = (f32[2048]{0:T(1024)S(1)}, f32[2048]{0:T(1024)}, u32[]{:S(2)}) copy-start(f32[2048]{0:T(1024)} %param.13) | copy-start | bytes 24580
  3.0 35.2 %all-to-all-start = ((s32[64,1,1]{2,1,0:T(1,128)}), s32[64,1,1]{2,1,0:T(1,128)S(1)}, u32[]{:S(2)}, u32[]{:S(2)}) async-start(s32[64,1,1]{2,1,0:T(1,128)} %copy.34), calls=%async_computation | async-start | bytes 65536 | tf_op jit(solution)/shard_map/all_to_all | solution.py:248
  16.0 7.4 %copy-start.3 = (bf16[1024,2048]{1,0:T(8,128)(2,1)S(1)}, bf16[1024,2048]{1,0:T(8,128)(2,1)}, u32[]{:S(2)}) copy-start(bf16[1024,2048]{1,0:T(8,128)(2,1)} %param.12) | copy-start | bytes 12582916
  23.4 1.2 copy-start.20
  24.6 1.9 %copy-start.8 = (bf16[1024,2048]{1,0:T(8,128)(2,1)}, bf16[1024,2048]{1,0:T(8,128)(2,1)S(1)}, u32[]{:S(2)}) copy-start(bf16[1024,2048]{1,0:T(8,128)(2,1)S(1)} %fusion.2) | copy-start | bytes 12582916
  26.5 4.7 %copy-start.17 = (s32[1,32]{1,0:T(1,128)S(1)}, s32[1,32]{1,0:T(1,128)}, u32[]{:S(2)}) copy-start(s32[1,32]{1,0:T(1,128)} %param.21) | copy-start | bytes 388
  27.6 11.9 %copy-start.2 = (bf16[16,512,16]{1,2,0:T(8,128)(2,1)S(1)}, bf16[16,512,16]{1,2,0:T(8,128)(2,1)}, u32[]{:S(2)}) copy-start(bf16[16,512,16]{1,2,0:T(8,128)(2,1)} %param.18) | copy-start | bytes 786436
  34.4 0.8 copy-start.4
  34.4 3.9 %copy-start.6 = (f32[1024,64]{1,0:T(8,128)}, f32[1024,64]{1,0:T(8,128)S(1)}, u32[]{:S(2)}) copy-start(f32[1024,64]{1,0:T(8,128)S(1)} %get-tuple-element.27) | copy-start | bytes 786436
  45.5 15.1 %copy-start.13 = (bf16[1024,2,64]{2,1,0:T(2,128)(2,1)S(1)}, bf16[1024,2,64]{2,1,0:T(2,128)(2,1)}, u32[]{:S(2)}) copy-start(bf16[1024,2,64]{2,1,0:T(2,128)(2,1)} %get-tuple-element.13) | copy-start | bytes 786436
  45.5 15.1 %copy-start.14 = (bf16[1024,2,64]{2,1,0:T(2,128)(2,1)S(1)}, bf16[1024,2,64]{2,1,0:T(2,128)(2,1)}, u32[]{:S(2)}) copy-start(bf16[1024,2,64]{2,1,0:T(2,128)(2,1)} %get-tuple-element.14) | copy-start | bytes 786436
  45.5 19.2 %copy-start.18 = (s32[8,128]{1,0:T(8,128)S(1)}, s32[8,128]{1,0:T(8,128)}, u32[]{:S(2)}) copy-start(s32[8,128]{1,0:T(8,128)} %constant.106.clone.1) | copy-start | bytes 12292
  45.5 60.1 %all-to-all-start.1 = ((bf16[64,32,512]{2,1,0:T(8,128)(2,1)}), bf16[64,32,512]{2,1,0:T(8,128)(2,1)}, u32[]{:S(2)}, u32[]{:S(2)}) async-start(bf16[64,32,512]{2,1,0:T(8,128)(2,1)} %pad_maximum_fusion), calls=%async_computation.1 | async-start | bytes 4194304 | tf_op jit(solution)/shard_map/all_to_all | solution.py:254
  62.1 6.5 %copy-start.10 = (bf16[128,8,2,128]{3,1,2,0:T(8,128)(2,1)}, bf16[128,8,2,128]{3,1,2,0:T(8,128)(2,1)S(1)}, u32[]{:S(2)}) copy-start(bf16[128,8,2,128]{3,1,2,0:T(8,128)(2,1)S(1)} %copy.49) | copy-start | bytes 1572868
  68.5 4.0 %copy-start.15 = (bf16[1024,256]{1,0:T(8,128)(2,1)}, bf16[1024,256]{1,0:T(8,128)(2,1)S(1)}, u32[]{:S(2)}) copy-start(bf16[1024,256]{1,0:T(8,128)(2,1)S(1)} %convolution_convert_fusion) | copy-start | bytes 1572868
  68.6 4.1 %copy-start.9 = (bf16[1024,2048]{1,0:T(8,128)(2,1)S(1)}, bf16[1024,2048]{1,0:T(8,128)(2,1)}, u32[]{:S(2)}) copy-start(bf16[1024,2048]{1,0:T(8,128)(2,1)} %copy-done.8) | copy-start | bytes 12582916
  107.3 8.9 %copy-start.5 = (f32[1024,64]{1,0:T(8,128)S(1)}, f32[1024,64]{1,0:T(8,128)}, u32[]{:S(2)}) copy-start(f32[1024,64]{1,0:T(8,128)} %copy-done.4) | copy-start | bytes 786436
  107.3 8.9 %copy-start.7 = (f32[1024,64]{1,0:T(8,128)S(1)}, f32[1024,64]{1,0:T(8,128)}, u32[]{:S(2)}) copy-start(f32[1024,64]{1,0:T(8,128)} %copy-done.6) | copy-start | bytes 786436
  107.3 8.9 %copy-start.12 = (f32[1024,64]{1,0:T(8,128)S(1)}, f32[1024,64]{1,0:T(8,128)}, u32[]{:S(2)}) copy-start(f32[1024,64]{1,0:T(8,128)} %get-tuple-element.25) | copy-start | bytes 786436
  107.3 9.3 %copy-start.11 = (bf16[128,8,2,128]{3,1,2,0:T(8,128)(2,1)S(1)}, bf16[128,8,2,128]{3,1,2,0:T(8,128)(2,1)}, u32[]{:S(2)}) copy-start(bf16[128,8,2,128]{3,1,2,0:T(8,128)(2,1)} %copy-done.10) | copy-start | bytes 1572868
  107.3 9.3 %copy-start.16 = (bf16[1024,256]{1,0:T(8,128)(2,1)S(1)}, bf16[1024,256]{1,0:T(8,128)(2,1)}, u32[]{:S(2)}) copy-start(bf16[1024,256]{1,0:T(8,128)(2,1)} %copy-done.15) | copy-start | bytes 1572868
  110.3 9.5 %copy-start.21 = (f32[1024,512]{1,0:T(8,128)S(1)}, f32[1024,512]{1,0:T(8,128)}, u32[]{:S(2)}) copy-start(f32[1024,512]{1,0:T(8,128)} %fusion.33) | copy-start | bytes 6291460
  110.3 6.4 %collective-permute-start = (f32[1024,16]{0,1:T(8,128)S(1)}, f32[1024,16]{0,1:T(8,128)S(1)}, u32[]{:S(2)}, u32[]{:S(2)}) collective-permute-start(f32[1024,16]{0,1:T(8,128)S(1)} %select_reduce_fusion), channel_id=1, source_target_pairs={{0,1},{1,2},{2,3},{3,0},{4,5},{5,6},{6,7},{7,4},{8,9},{9,10},{10,1... | collective-permute-start | bytes 196616 | tf_op jit(solution)/shard_map/ppermute | solution.py:273
  112.0 6.8 %collective-permute-start.1 = (f32[1024,16]{0,1:T(8,128)S(1)}, f32[1024,16]{0,1:T(8,128)S(1)}, u32[]{:S(2)}, u32[]{:S(2)}) collective-permute-start(f32[1024,16]{0,1:T(8,128)S(1)} %select_reduce_fusion), channel_id=1, source_target_pairs={{0,2},{1,3},{2,0},{3,1},{4,6},{5,7},{6,4},{7,5},{8,10},{9,11},{10,... | collective-permute-start | bytes 196616 | tf_op jit(solution)/shard_map/ppermute | solution.py:273
  114.9 4.9 %collective-permute-start.2 = (f32[1024,16]{0,1:T(8,128)S(1)}, f32[1024,16]{0,1:T(8,128)S(1)}, u32[]{:S(2)}, u32[]{:S(2)}) collective-permute-start(f32[1024,16]{0,1:T(8,128)S(1)} %select_reduce_fusion), channel_id=1, source_target_pairs={{0,3},{1,0},{2,1},{3,2},{4,7},{5,4},{6,5},{7,6},{8,11},{9,8},{10,9... | collective-permute-start | bytes 196616 | tf_op jit(solution)/shard_map/ppermute | solution.py:273
  119.8 3.0 %copy-start.1 = (f32[8,128,384]{2,1,0:T(8,128)S(1)}, f32[8,128,384]{2,1,0:T(8,128)}, u32[]{:S(2)}) copy-start(f32[8,128,384]{2,1,0:T(8,128)} %add_select_fusion.bias_ref) | copy-start | bytes 4718596

commit v9 on v8

--- a/solution.py
+++ b/solution.py
@@ -248,18 +248,18 @@
     wanted_in = lax.all_to_all(
         wanted.reshape(req_count, 1), "req", split_axis=0, concat_axis=0, tiled=True
     ).reshape(req_count)
-    down_sel = jnp.transpose(adapter_down_maps[wanted_in], (0, 2, 1))
-    up_sel = adapter_up_maps[wanted_in]
-    maps_out = jnp.concatenate([down_sel, up_sel], 1)
-    maps_in = lax.all_to_all(maps_out, "req", split_axis=0, concat_axis=0, tiled=True)
-    down_in = maps_in[:, :rank_extent, :].reshape(req_count * rank_extent, piece_width)
-    up_in = maps_in[:, rank_extent:, :].reshape(req_count * rank_extent, piece_width)
+    table = jnp.concatenate([jnp.transpose(adapter_down_maps, (0, 2, 1)), adapter_up_maps], 1)
     float_tok = tokens.astype(jnp.float32)
     normalized_input = (
         float_tok
         * lax.rsqrt(jnp.mean(float_tok * float_tok, -1, keepdims=True) + 1e-06)
         * input_norm_gain
     ).astype(jnp.bfloat16)
+    maps_out = table[wanted_in]
+    normalized_input, maps_out = lax.optimization_barrier((normalized_input, maps_out))
+    maps_in = lax.all_to_all(maps_out, "req", split_axis=0, concat_axis=0, tiled=True)
+    down_in = maps_in[:, :rank_extent, :].reshape(req_count * rank_extent, piece_width)
+    up_in = maps_in[:, rank_extent:, :].reshape(req_count * rank_extent, piece_width)
     normed_slice = lax.dynamic_slice_in_dim(
         normalized_input, tp_index * piece_width, piece_width, 1
     )

time: 169 us -> 161 us (0.953)
  waiting for transfers between devices: 32.3 us -> 26.2 us
  matrix products: 14.7 us -> 12.1 us
    all_to_all x1, waiting for transfers between devices: 29.2 us -> 22.9 us  [per_device(): lax.all_to_all(maps_out, 'req', split_axis=0, concat_axis=0, tiled=True)]
    convert_element_type x1, other arithmetic: 1.02 us -> 5.15 us  [per_device(): normalized_input = (float_tok * lax.rsqrt(jnp.mean(float_tok * float_tok,...]
    concatenate x1, other arithmetic: 2.78 us -> 0.04 us  [per_device(): jnp.concatenate([jnp.transpose(adapter_down_maps, (0, 2, 1)), adapter_up_...]
    dot_general x1, matrix products: 3.74 us -> 1.26 us  [per_device(): jnp.dot(normalized_input, value_matrix, preferred_element_type=jnp.float32)]
    unnamed x48 -> x42, local copies, waits for them, and re-layouts: 6.43 us -> 7.13 us
  transfers between devices with their start and end apart: 5 -> 5, of which waited for: 3 -> 3; matrix products, arithmetic and copies ran while one was open for 22% -> 24% of each run, Pallas kernels for 0% -> 0%
where the time goes in v9:
time: 161 us; the launch traced here: 160 us
  Pallas kernels  44.5 us (28%)
  starting transfers between devices  28.7 us (18%)
  waiting for transfers between devices  26.2 us (16%)
  other arithmetic  25.3 us (16%)
  local copies, waits for them, and re-layouts  17.3 us (11%)
  matrix products  12.1 us (8%)
  between operations  5.74 us (4%)
    pallas_call x1, Pallas kernels, attend_and_reduce(): pl.pallas_call(kernel, out_shape=jax.ShapeDtypeStruct((rows, piece), jnp....  44.5 us
    all_to_all x1, waiting for transfers between devices, per_device(): lax.all_to_all(maps_out, 'req', split_axis=0, concat_axis=0, tiled=True)  22.9 us
    all_to_all x1, starting transfers between devices, per_device(): lax.all_to_all(wanted.reshape(req_count, 1), 'req', split_axis=0, concat_...  12 us
    all_to_all x1, starting transfers between devices, per_device(): lax.all_to_all(maps_out, 'req', split_axis=0, concat_axis=0, tiled=True)  10.5 us
    unnamed x42, local copies, waits for them, and re-layouts  7.13 us
    ppermute x3, starting transfers between devices, per_device(): lax.ppermute(partial_rank, 'tp', [(i, (i + k) % tp_count) for i in range(...  6.13 us
    convert_element_type x1, other arithmetic, per_device(): normalized_input = (float_tok * lax.rsqrt(jnp.mean(float_tok * float_tok,...  5.15 us
    dot_general x1, matrix products, per_device(): jnp.dot(normalized_input, query_matrix, preferred_element_type=jnp.float32)  3.71 us
  transfers between devices with their start and end apart: 5, of which 3 were waited for; matrix products, arithmetic and copies ran while one was open for 24% of the time, Pallas kernels for 0%

profile of v9, /device:TPU:2, one launch (start us, length us, event | category | flops | bytes accessed | tf_op | source)
XLA Modules:
  0.0 160.0 jit_solution(2344980494698872853)
XLA Ops:
  0.0 0.8 fusion.22
  0.8 1.4 gather_fusion
  2.2 0.1 select_reduce_fusion.6
  2.3 0.7 copy.32
  3.0 12.0 %all-to-all-start = ((s32[64,1,1]{2,1,0:T(1,128)}), s32[64,1,1]{2,1,0:T(1,128)S(1)}, u32[]{:S(2)}, u32[]{:S(2)}) async-start(s32[64,1,1]{2,1,0:T(1,128)} %copy.32), calls=%async_computation | async-start | bytes 65536 | tf_op jit(solution)/shard_map/all_to_all | solution.py:248
  15.1 0.7 copy.33
  15.9 0.1 reduce.1
  16.0 0.8 select_bitcast_fusion
  16.8 0.7 select_bitcast_fusion.1
  17.4 0.1 convert_reduce_fusion
  17.6 0.9 select_reduce_fusion.5
  18.5 0.8 select_reduce_fusion.7
  19.3 0.6 fusion.32
  23.5 0.7 fusion.27
  24.1 0.8 select_reduce_fusion.1
  25.0 3.1 %fusion = f32[1024]{0:T(1024)S(1)} fusion(bf16[1024,2048]{1,0:T(8,128)(2,1)} %param.12), kind=kLoop, calls=%fused_computation.4 | loop fusion | flops 6290432 | bytes 4198400 | tf_op jit(solution)/shard_map/reduce_sum | solution.py:255
  28.6 5.1 %fusion.2 = bf16[1024,2048]{1,0:T(8,128)(2,1)} fusion(bf16[1024,2048]{1,0:T(8,128)(2,1)} %param.12, f32[2048]{0:T(1024)S(1)} %copy-done.15, f32[1024]{0:T(1024)S(1)} %add_rsqrt_fusion), kind=kLoop, calls=%fused_computation.6 | loop fusion | flops 8388608 | bytes 8400896 | tf_op jit(solution)/shard_map/convert_element_type | solution.py:257
  33.8 1.2 reduce
  35.1 2.0 %gather_fusion.1 = bf16[64,32,512]{2,1,0:T(8,128)(2,1)} fusion(bf16[16,32,512]{2,1,0:T(8,128)(2,1)S(1)} %pad_maximum_fusion, s32[1024]{0:T(1024)S(1)} %pad_clamp_fusion), kind=kCustom, calls=%fused_computation.1 | custom fusion | bytes 4194560 | tf_op jit(solution)/shard_map/gather | solution.py:258
  37.1 10.5 %all-to-all-start.1 = ((bf16[64,32,512]{2,1,0:T(8,128)(2,1)}), bf16[64,32,512]{2,1,0:T(8,128)(2,1)}, u32[]{:S(2)}, u32[]{:S(2)}) async-start(bf16[64,32,512]{2,1,0:T(8,128)(2,1)} %gather_fusion.1), calls=%async_computation.1 | async-start | bytes 4194304 | tf_op jit(solution)/shard_map/all_to_all | solution.py:260
  49.5 1.3 constant_dynamic-slice_fusion.res_ref
  50.9 1.9 %fusion.17 = (f32[1024,64]{1,0:T(8,128)S(1)}, f32[1024,64]{1,0:T(8,128)S(1)}, f32[1024,64]{1,0:T(8,128)S(1)}) fusion(f32[64]{0:T(128)S(1)} %negate_power_fusion, f32[1024]{0:T(1024)S(1)} %add_convert_fusion.2), kind=kLoop, calls=%fused_computation.34 | loop fusion | flops 131072 | bytes 790784 | tf_op jit(solution)/shard_map/neg | solution.py:296
  52.8 1.3 pad_maximum_fusion.1
  54.2 0.3 compare_and_fusion
  54.6 0.6 or_and_fusion
  55.2 1.3 add_select_fusion.bias_ref
  56.6 1.3 fusion.34
  57.9 1.0 fusion.30
  58.9 2.2 %copy.40 = f32[1024,2,64]{2,1,0:T(2,128)} copy(f32[1024,2,64]{0,2,1:T(8,128)} %get-tuple-element.22) | data formatting | bytes 1048576
  61.1 2.2 %copy.41 = f32[1024,2,64]{2,1,0:T(2,128)} copy(f32[1024,2,64]{0,2,1:T(8,128)} %get-tuple-element.21) | data formatting | bytes 1048576
  63.3 2.6 %subtract_convert_fusion = (bf16[1024,2,64]{2,1,0:T(2,128)(2,1)S(1)}, bf16[1024,2,64]{2,1,0:T(2,128)(2,1)S(1)}) fusion(f32[1024,2,64]{2,1,0:T(2,128)} %copy.41, f32[1024,2,64]{2,1,0:T(2,128)} %copy.40, f32[1024,64]{1,0:T(8,128)} %copy-done.4, f32[1024,64]{1,0:T(8,128)} %copy-done.5), kind=kLoop, calls=%fused_computation.20 | loop fusion | flops 1048576 | bytes 2097152 | tf_op jit(solution)/shard_map/convert
  65.9 1.4 pad_maximum_fusion.3
  67.5 0.8 copy-done.8
  68.3 1.3 convolution_convert_fusion
  69.6 0.8 copy-done.10
  70.4 3.7 %fusion.33 = f32[1024,512]{1,0:T(8,128)} fusion(bf16[1024,2048]{1,0:T(8,128)(2,1)S(1)} %copy-done.7, bf16[2048,512]{1,0:T(8,128)(2,1)S(1)} %copy-done), kind=kOutput, calls=%fused_computation.107 | convolution fusion | flops 2147483648 | bytes 8388608 | tf_op jit(solution)/shard_map/dot_general | solution.py:287
  74.2 22.9 %all-to-all-done.1 = bf16[64,32,512]{2,1,0:T(8,128)(2,1)} async-done(((bf16[64,32,512]{2,1,0:T(8,128)(2,1)}), bf16[64,32,512]{2,1,0:T(8,128)(2,1)}, u32[]{:S(2)}, u32[]{:S(2)}) %all-to-all-start.1) | async-done | bytes 2097184 | tf_op jit(solution)/shard_map/all_to_all | solution.py:260
  97.1 1.7 %fusion.29 = (bf16[64,16,512]{2,1,0:T(8,128)(2,1)S(1)}, bf16[64,16,512]{2,1,0:T(8,128)(2,1)S(1)}) fusion(bf16[64,32,512]{2,1,0:T(8,128)(2,1)} %all-to-all-done.1), kind=kLoop, calls=%fused_computation.103 | loop fusion | bytes 4194304 | tf_op jit(solution)/shard_map/slice | solution.py:261
  98.8 2.9 %select_reduce_fusion = f32[1024,16]{0,1:T(8,128)S(1)} fusion(pred[1024,64]{0,1:T(8,128)(4,1)S(1)} %iota_compare_fusion, bf16[64,16,512]{2,1,0:T(8,128)(2,1)S(1)} %get-tuple-element.19, bf16[1024,2048]{1,0:T(8,128)(2,1)} %fusion.2, s32[]{:T(128)S(6)} %select_n.72), kind=kOutput, calls=%fused_computation.7 | convolution fusion | flops 1075822592 | bytes 2228228 | tf_op jit(solution)/shard_map/dot_general | solution.py:268
  101.7 1.9 %collective-permute-start = (f32[1024,16]{0,1:T(8,128)S(1)}, f32[1024,16]{0,1:T(8,128)S(1)}, u32[]{:S(2)}, u32[]{:S(2)}) collective-permute-start(f32[1024,16]{0,1:T(8,128)S(1)} %select_reduce_fusion), channel_id=1, source_target_pairs={{0,1},{1,2},{2,3},{3,0},{4,5},{5,6},{6,7},{7,4},{8,9},{9,10},{10,1... | collective-permute-start | bytes 196616 | tf_op jit(solution)/shard_map/ppermute | solution.py:273
  103.6 2.9 %collective-permute-start.1 = (f32[1024,16]{0,1:T(8,128)S(1)}, f32[1024,16]{0,1:T(8,128)S(1)}, u32[]{:S(2)}, u32[]{:S(2)}) collective-permute-start(f32[1024,16]{0,1:T(8,128)S(1)} %select_reduce_fusion), channel_id=1, source_target_pairs={{0,2},{1,3},{2,0},{3,1},{4,6},{5,7},{6,4},{7,5},{8,10},{9,11},{10,... | collective-permute-start | bytes 196616 | tf_op jit(solution)/shard_map/ppermute | solution.py:273
  106.5 1.3 collective-permute-start.2
  107.9 0.1 maximum_maximum_fusion.1
  108.1 2.4 %collective-permute-done.1 = f32[1024,16]{0,1:T(8,128)S(1)} collective-permute-done((f32[1024,16]{0,1:T(8,128)S(1)}, f32[1024,16]{0,1:T(8,128)S(1)}, u32[]{:S(2)}, u32[]{:S(2)}) %collective-permute-start.1) | collective-permute-done | bytes 65568 | tf_op jit(solution)/shard_map/ppermute | solution.py:273
  110.4 1.0 collective-permute-done.2
  111.5 3.0 %convert_add_fusion.q_ref = f32[1024,512]{1,0:T(8,128)} fusion(f32[1024,512]{1,0:T(8,128)S(1)} %copy-done.18, pred[1024,64]{0,1:T(8,128)(4,1)S(1)} %iota_compare_fusion, bf16[64,16,512]{2,1,0:T(8,128)(2,1)S(1)} %get-tuple-element.20, bf16[1024,16]{0,1:T(8,128)(2,1)S(1)} %add_convert_fusion.1), kind=kOutput, calls=%fused_computation.10 | convolution fusion | flops 1076887552 | bytes 5341184 | tf_op jit(solution)/shard_map/dot_general | solution.py:283
  114.4 44.5 %shard_map.118 = bf16[1024,512]{1,0:T(8,128)(2,1)S(1)} custom-call(f32[1024,512]{1,0:T(8,128)} %convert_add_fusion.q_ref, f32[1024,128]{1,0:T(8,128)S(1)} %copy-done.2, f32[1024,128]{1,0:T(8,128)S(1)} %copy-done.3, bf16[1152,256]{1,0:T(8,128)(2,1)S(1)} %concatenate.98.k_ref, bf16[1152,256]{1,0:T(8,128)(2,1)S(1)} %concatenate.99.v_ref, ...), custom_call_target="tpu_custom_call" | custom-call | tf_op jit(solution)/shard_map/pallas_call | solution.py:197
  159.0 1.0 copy.50
  (78 shorter events, 1.3 us)
Async XLA Ops:
  0.0 70.4 %copy-start = (bf16[2048,512]{1,0:T(8,128)(2,1)S(1)}, bf16[2048,512]{1,0:T(8,128)(2,1)}, u32[]{:S(2)}) copy-start(bf16[2048,512]{1,0:T(8,128)(2,1)} %param.14) | copy-start | bytes 6291460
  3.0 30.8 %all-to-all-start = ((s32[64,1,1]{2,1,0:T(1,128)}), s32[64,1,1]{2,1,0:T(1,128)S(1)}, u32[]{:S(2)}, u32[]{:S(2)}) async-start(s32[64,1,1]{2,1,0:T(1,128)} %copy.32), calls=%async_computation | async-start | bytes 65536 | tf_op jit(solution)/shard_map/all_to_all | solution.py:248
  24.9 3.6 %copy-start.12 = (bf16[16,16,512]{2,1,0:T(8,128)(2,1)S(1)}, bf16[16,16,512]{2,1,0:T(8,128)(2,1)}, u32[]{:S(2)}) copy-start(bf16[16,16,512]{2,1,0:T(8,128)(2,1)} %param.19) | copy-start | bytes 786436
  24.9 3.6 %copy-start.13 = (bf16[16,512,16]{1,2,0:T(8,128)(2,1)S(1)}, bf16[16,512,16]{1,2,0:T(8,128)(2,1)}, u32[]{:S(2)}) copy-start(bf16[16,512,16]{1,2,0:T(8,128)(2,1)} %param.18) | copy-start | bytes 786436
  24.9 3.6 %copy-start.15 = (f32[2048]{0:T(1024)S(1)}, f32[2048]{0:T(1024)}, u32[]{:S(2)}) copy-start(f32[2048]{0:T(1024)} %param.13) | copy-start | bytes 24580
  28.6 5.2 %copy-start.14 = (s32[8,128]{1,0:T(8,128)S(1)}, s32[8,128]{1,0:T(8,128)}, u32[]{:S(2)}) copy-start(s32[8,128]{1,0:T(8,128)} %constant.106.clone.1) | copy-start | bytes 12292
  37.1 60.0 %all-to-all-start.1 = ((bf16[64,32,512]{2,1,0:T(8,128)(2,1)}), bf16[64,32,512]{2,1,0:T(8,128)(2,1)}, u32[]{:S(2)}, u32[]{:S(2)}) async-start(bf16[64,32,512]{2,1,0:T(8,128)(2,1)} %gather_fusion.1), calls=%async_computation.1 | async-start | bytes 4194304 | tf_op jit(solution)/shard_map/all_to_all | solution.py:260
  50.8 5.7 %copy-start.16 = (bf16[2048,256]{1,0:T(8,128)(2,1)S(1)}, bf16[2048,256]{1,0:T(8,128)(2,1)}, u32[]{:S(2)}) copy-start(bf16[2048,256]{1,0:T(8,128)(2,1)} %param.15) | copy-start | bytes 3145732
  52.8 3.8 %copy-start.4 = (f32[1024,64]{1,0:T(8,128)}, f32[1024,64]{1,0:T(8,128)S(1)}, u32[]{:S(2)}) copy-start(f32[1024,64]{1,0:T(8,128)S(1)} %get-tuple-element.30) | copy-start | bytes 786436
  52.8 3.7 %copy-start.5 = (f32[1024,64]{1,0:T(8,128)}, f32[1024,64]{1,0:T(8,128)S(1)}, u32[]{:S(2)}) copy-start(f32[1024,64]{1,0:T(8,128)S(1)} %get-tuple-element.31) | copy-start | bytes 786436
  52.8 3.8 %copy-start.6 = (bf16[1024,2048]{1,0:T(8,128)(2,1)S(1)}, bf16[1024,2048]{1,0:T(8,128)(2,1)}, u32[]{:S(2)}) copy-start(bf16[1024,2048]{1,0:T(8,128)(2,1)} %fusion.2) | copy-start | bytes 12582916
  63.3 5.0 %copy-start.7 = (bf16[1024,2048]{1,0:T(8,128)(2,1)S(1)}, bf16[1024,2048]{1,0:T(8,128)(2,1)}, u32[]{:S(2)}) copy-start(bf16[1024,2048]{1,0:T(8,128)(2,1)} %fusion.2) | copy-start | bytes 12582916
  65.9 2.4 %copy-start.17 = (bf16[2048,256]{1,0:T(8,128)(2,1)S(1)}, bf16[2048,256]{1,0:T(8,128)(2,1)}, u32[]{:S(2)}) copy-start(bf16[2048,256]{1,0:T(8,128)(2,1)} %param.16) | copy-start | bytes 3145732
  67.5 0.8 copy-start.8
  69.6 0.8 copy-start.10
  98.8 9.2 %copy-start.9 = (bf16[128,8,2,128]{3,1,2,0:T(8,128)(2,1)S(1)}, bf16[128,8,2,128]{3,1,2,0:T(8,128)(2,1)}, u32[]{:S(2)}) copy-start(bf16[128,8,2,128]{3,1,2,0:T(8,128)(2,1)} %copy-done.8) | copy-start | bytes 1572868
  98.8 9.2 %copy-start.11 = (bf16[1024,256]{1,0:T(8,128)(2,1)S(1)}, bf16[1024,256]{1,0:T(8,128)(2,1)}, u32[]{:S(2)}) copy-start(bf16[1024,256]{1,0:T(8,128)(2,1)} %copy-done.10) | copy-start | bytes 1572868
  101.7 9.7 %copy-start.18 = (f32[1024,512]{1,0:T(8,128)S(1)}, f32[1024,512]{1,0:T(8,128)}, u32[]{:S(2)}) copy-start(f32[1024,512]{1,0:T(8,128)} %fusion.33) | copy-start | bytes 6291460
  101.7 6.3 %collective-permute-start = (f32[1024,16]{0,1:T(8,128)S(1)}, f32[1024,16]{0,1:T(8,128)S(1)}, u32[]{:S(2)}, u32[]{:S(2)}) collective-permute-start(f32[1024,16]{0,1:T(8,128)S(1)} %select_reduce_fusion), channel_id=1, source_target_pairs={{0,1},{1,2},{2,3},{3,0},{4,5},{5,6},{6,7},{7,4},{8,9},{9,10},{10,1... | collective-permute-start | bytes 196616 | tf_op jit(solution)/shard_map/ppermute | solution.py:273
  103.6 6.8 %collective-permute-start.1 = (f32[1024,16]{0,1:T(8,128)S(1)}, f32[1024,16]{0,1:T(8,128)S(1)}, u32[]{:S(2)}, u32[]{:S(2)}) collective-permute-start(f32[1024,16]{0,1:T(8,128)S(1)} %select_reduce_fusion), channel_id=1, source_target_pairs={{0,2},{1,3},{2,0},{3,1},{4,6},{5,7},{6,4},{7,5},{8,10},{9,11},{10,... | collective-permute-start | bytes 196616 | tf_op jit(solution)/shard_map/ppermute | solution.py:273
  106.5 4.9 %collective-permute-start.2 = (f32[1024,16]{0,1:T(8,128)S(1)}, f32[1024,16]{0,1:T(8,128)S(1)}, u32[]{:S(2)}, u32[]{:S(2)}) collective-permute-start(f32[1024,16]{0,1:T(8,128)S(1)} %select_reduce_fusion), channel_id=1, source_target_pairs={{0,3},{1,0},{2,1},{3,2},{4,7},{5,4},{6,5},{7,6},{8,11},{9,8},{10,9... | collective-permute-start | bytes 196616 | tf_op jit(solution)/shard_map/ppermute | solution.py:273
  111.4 3.0 %copy-start.1 = (f32[8,128,384]{2,1,0:T(8,128)S(1)}, f32[8,128,384]{2,1,0:T(8,128)}, u32[]{:S(2)}) copy-start(f32[8,128,384]{2,1,0:T(8,128)} %add_select_fusion.bias_ref) | copy-start | bytes 4718596
  111.4 3.0 %copy-start.2 = (f32[1024,128]{1,0:T(8,128)S(1)}, f32[1024,128]{1,0:T(8,128)}, u32[]{:S(2)}) copy-start(f32[1024,128]{1,0:T(8,128)} %get-tuple-element.45.cs_ref) | copy-start | bytes 1572868
  111.4 3.0 %copy-start.3 = (f32[1024,128]{1,0:T(8,128)S(1)}, f32[1024,128]{1,0:T(8,128)}, u32[]{:S(2)}) copy-start(f32[1024,128]{1,0:T(8,128)} %get-tuple-element.46.sn_ref) | copy-start | bytes 1572868

commit v10 on v9

--- a/solution.py
+++ b/solution.py
@@ -211,6 +211,80 @@
             collective_id=0, has_side_effects=True, vmem_limit_bytes=48 * 1024 * 1024
         ),
     )(q, cs, sn, k_pad, v_pad, k_prompt, v_prompt, bias, wo, residual)
+
+
+def ids_kernel(wanted_ref, out_ref, landing, send_sems, recv_sems):
+    me = lax.axis_index("req")
+    col = lax.axis_index("tp")
+    count = lax.axis_size("req")
+    barrier = pltpu.get_barrier_semaphore()
+
+    def greet(k, carry):
+        peer = lax.rem(me + k, count)
+        pl.semaphore_signal(
+            barrier, inc=1, device_id=(peer, col), device_id_type=pl.DeviceIdType.MESH
+        )
+        return carry
+
+    lax.fori_loop(1, count, greet, 0)
+    pl.semaphore_wait(barrier, count - 1)
+
+    def copy_to(k):
+        dest = lax.rem(me + k, count)
+        return pltpu.make_async_remote_copy(
+            src_ref=wanted_ref.at[dest],
+            dst_ref=landing.at[me],
+            send_sem=send_sems.at[k],
+            recv_sem=recv_sems.at[k],
+            device_id=(dest, col),
+            device_id_type=pl.DeviceIdType.MESH,
+        )
+
+    def copy_from(k):
+        source = lax.rem(me + count - k, count)
+        return pltpu.make_async_remote_copy(
+            src_ref=wanted_ref.at[source],
+            dst_ref=landing.at[source],
+            send_sem=send_sems.at[k],
+            recv_sem=recv_sems.at[k],
+            device_id=(source, col),
+            device_id_type=pl.DeviceIdType.MESH,
+        )
+
+    def send(k, carry):
+        copy_to(k).start()
+        return carry
+
+    lax.fori_loop(1, count, send, 0)
+    out_ref[me] = wanted_ref[me]
+
+    def finish(k, carry):
+        copy_to(k).wait_send()
+        copy_from(k).wait_recv()
+        source = lax.rem(me + count - k, count)
+        out_ref[source] = landing[source]
+        return carry
+
+    lax.fori_loop(1, count, finish, 0)
+
+
+def exchange_ids(wanted):
+    count = wanted.shape[0]
+    tiles = jnp.broadcast_to(wanted[:, None, None], (count, 8, 128))
+    vmem = pltpu.MemorySpace.VMEM
+    got = pl.pallas_call(
+        ids_kernel,
+        out_shape=jax.ShapeDtypeStruct((count, 8, 128), jnp.int32),
+        in_specs=[pl.BlockSpec(memory_space=vmem)],
+        out_specs=pl.BlockSpec(memory_space=vmem),
+        scratch_shapes=[
+            pltpu.VMEM((count, 8, 128), jnp.int32),
+            pltpu.SemaphoreType.DMA((count,)),
+            pltpu.SemaphoreType.DMA((count,)),
+        ],
+        compiler_params=pltpu.CompilerParams(collective_id=1, has_side_effects=True),
+    )(tiles)
+    return got[:, 0, 0]
 
 
 def per_device(
@@ -245,9 +319,7 @@
     holder_ids = jnp.arange(req_count, dtype=jnp.int32)
     holder_hot = (holder[None, :] == holder_ids[:, None]).astype(jnp.int32)
     wanted = jnp.sum(holder_hot * local_slot[None, :], 1)
-    wanted_in = lax.all_to_all(
-        wanted.reshape(req_count, 1), "req", split_axis=0, concat_axis=0, tiled=True
-    ).reshape(req_count)
+    wanted_in = exchange_ids(wanted)
     table = jnp.concatenate([jnp.transpose(adapter_down_maps, (0, 2, 1)), adapter_up_maps], 1)
     float_tok = tokens.astype(jnp.float32)
     normalized_input = (

time: 161 us -> 158 us (0.981)
  Pallas kernels: 44.5 us -> 64 us
  starting transfers between devices: 28.7 us -> 15.6 us
  waiting for transfers between devices: 26.2 us -> 16.9 us
  matrix products: 12.1 us -> 17.1 us
  other arithmetic: 25.3 us -> 20.6 us
    pallas_call x0 -> x1, Pallas kernels: none -> 19.6 us  [exchange_ids(): pl.pallas_call(ids_kernel, out_shape=jax.ShapeDtypeStruct((count, 8, 128)...]
    all_to_all x1 -> x0, starting transfers between devices: 12 us -> none  [per_device(): lax.all_to_all(wanted.reshape(req_count, 1), 'req', split_axis=0, concat_...]
    all_to_all x1, waiting for transfers between devices: 22.9 us -> 13.8 us  [per_device(): lax.all_to_all(maps_out, 'req', split_axis=0, concat_axis=0, tiled=True)]
    dot_general x1, matrix products: 1.29 us -> 3.78 us  [per_device(): jnp.dot(normalized_input, key_matrix, preferred_element_type=jnp.float32)]
    dot_general x1, matrix products: 1.26 us -> 3.73 us  [per_device(): jnp.dot(normalized_input, value_matrix, preferred_element_type=jnp.float32)]
    unnamed x42 -> x44, local copies, waits for them, and re-layouts: 7.13 us -> 4.76 us
    slice x0 -> x1, local copies, waits for them, and re-layouts: none -> 2.22 us  [exchange_ids(): return got[:, 0, 0]]
  transfers between devices with their start and end apart: 5 -> 4, of which waited for: 3 -> 3; matrix products, arithmetic and copies ran while one was open for 24% -> 19% of each run, Pallas kernels for 0% -> 0%
where the time goes in v10:
time: 158 us; the launch traced here: 157 us
  Pallas kernels  64 us (41%)
  other arithmetic  20.6 us (13%)
  matrix products  17.1 us (11%)
  local copies, waits for them, and re-layouts  16.9 us (11%)
  waiting for transfers between devices  16.9 us (11%)
  starting transfers between devices  15.6 us (10%)
  between operations  6 us (4%)
    pallas_call x1, Pallas kernels, attend_and_reduce(): pl.pallas_call(kernel, out_shape=jax.ShapeDtypeStruct((rows, piece), jnp....  44.4 us
    pallas_call x1, Pallas kernels, exchange_ids(): pl.pallas_call(ids_kernel, out_shape=jax.ShapeDtypeStruct((count, 8, 128)...  19.6 us
    all_to_all x1, waiting for transfers between devices, per_device(): lax.all_to_all(maps_out, 'req', split_axis=0, concat_axis=0, tiled=True)  13.8 us
    all_to_all x1, starting transfers between devices, per_device(): lax.all_to_all(maps_out, 'req', split_axis=0, concat_axis=0, tiled=True)  9.69 us
    ppermute x3, starting transfers between devices, per_device(): lax.ppermute(partial_rank, 'tp', [(i, (i + k) % tp_count) for i in range(...  5.92 us
    convert_element_type x1, other arithmetic, per_device(): normalized_input = (float_tok * lax.rsqrt(jnp.mean(float_tok * float_tok,...  5.15 us
    unnamed x44, local copies, waits for them, and re-layouts  4.76 us
    dot_general x1, matrix products, per_device(): jnp.dot(normalized_input, key_matrix, preferred_element_type=jnp.float32)  3.78 us
  transfers between devices with their start and end apart: 4, of which 3 were waited for; matrix products, arithmetic and copies ran while one was open for 19% of the time, Pallas kernels for 0%

profile of v10, /device:TPU:2, one launch (start us, length us, event | category | flops | bytes accessed | tf_op | source)
XLA Modules:
  0.0 157.2 jit_solution(13334250741072954155)
XLA Ops:
  0.0 0.8 fusion.22
  0.8 1.4 gather_fusion
  2.2 0.1 select_reduce_fusion.6
  2.3 0.8 broadcast_in_dim.37.wanted_ref
  3.2 19.6 %shard_map.118 = s32[64,8,128]{2,1,0:T(8,128)} custom-call(s32[64,8,128]{2,1,0:T(8,128)} %broadcast_in_dim.37.wanted_ref), custom_call_target="tpu_custom_call" | custom-call | tf_op jit(solution)/shard_map/pallas_call | solution.py:275
  22.8 2.2 %slice_reduce_fusion = s32[64]{0:T(128)S(1)} fusion(s32[64,8,128]{2,1,0:T(8,128)} %shard_map.118), kind=kLoop, calls=%fused_computation.45 | loop fusion | bytes 512 | tf_op jit(solution)/shard_map/slice | solution.py:287
  25.0 3.1 %fusion = f32[1024]{0:T(1024)S(1)} fusion(bf16[1024,2048]{1,0:T(8,128)(2,1)} %param.12), kind=kLoop, calls=%fused_computation.4 | loop fusion | flops 6290432 | bytes 4198400 | tf_op jit(solution)/shard_map/reduce_sum | solution.py:327
  28.2 2.0 %gather_fusion.1 = bf16[64,32,512]{2,1,0:T(8,128)(2,1)} fusion(bf16[16,32,512]{2,1,0:T(8,128)(2,1)S(1)} %pad_maximum_fusion, s32[1024]{0:T(1024)S(1)} %pad_clamp_fusion), kind=kCustom, calls=%fused_computation.1 | custom fusion | bytes 4194560 | tf_op jit(solution)/shard_map/gather | solution.py:330
  30.2 5.2 %fusion.2 = bf16[1024,2048]{1,0:T(8,128)(2,1)} fusion(bf16[1024,2048]{1,0:T(8,128)(2,1)} %param.12, f32[2048]{0:T(1024)S(1)} %copy-done.17, f32[1024]{0:T(1024)S(1)} %add_rsqrt_fusion), kind=kLoop, calls=%fused_computation.6 | loop fusion | flops 8388608 | bytes 8400896 | tf_op jit(solution)/shard_map/convert_element_type | solution.py:329
  35.4 9.7 %all-to-all-start = ((bf16[64,32,512]{2,1,0:T(8,128)(2,1)}), bf16[64,32,512]{2,1,0:T(8,128)(2,1)}, u32[]{:S(2)}, u32[]{:S(2)}) async-start(bf16[64,32,512]{2,1,0:T(8,128)(2,1)} %gather_fusion.1), calls=%async_computation | async-start | bytes 4194304 | tf_op jit(solution)/shard_map/all_to_all | solution.py:332
  45.1 0.1 copy.25
  45.3 0.1 reduce.1
  45.5 0.1 convert_reduce_fusion
  45.6 0.2 select_reduce_fusion.5
  45.8 0.1 select_reduce_fusion.1
  45.9 3.8 %fusion.34 = f32[1024,256]{0,1:T(8,128)S(1)} fusion(bf16[1024,2048]{1,0:T(8,128)(2,1)} %fusion.2, bf16[2048,256]{1,0:T(8,128)(2,1)} %param.15), kind=kOutput, calls=%fused_computation.109 | convolution fusion | flops 1073741824 | bytes 6291456 | tf_op jit(solution)/shard_map/dot_general | solution.py:369
  49.7 1.0 fusion.30
  50.8 1.4 copy.32
  52.2 2.2 %copy.33 = f32[1024,2,64]{2,1,0:T(2,128)} copy(f32[1024,2,64]{0,2,1:T(8,128)} %get-tuple-element.21) | data formatting | bytes 1048576
  54.4 0.1 select_reduce_fusion.7
  54.5 3.0 %fusion.17 = (f32[1024,64]{1,0:T(8,128)}, f32[1024,64]{1,0:T(8,128)S(1)}, f32[1024,64]{1,0:T(8,128)S(1)}) fusion(f32[64]{0:T(128)S(1)} %negate_power_fusion, f32[1024]{0:T(1024)S(1)} %add_convert_fusion.2), kind=kLoop, calls=%fused_computation.34 | loop fusion | flops 131072 | bytes 790784 | tf_op jit(solution)/shard_map/neg | solution.py:368
  57.5 2.0 %subtract_convert_fusion = (bf16[1024,2,64]{2,1,0:T(2,128)(2,1)}, bf16[1024,2,64]{2,1,0:T(2,128)(2,1)}) fusion(f32[1024,2,64]{2,1,0:T(2,128)S(1)} %copy-done.7, f32[1024,2,64]{2,1,0:T(2,128)S(1)} %copy.32, f32[1024,64]{1,0:T(8,128)S(1)} %get-tuple-element.30, f32[1024,64]{1,0:T(8,128)S(1)} %get-tuple-element.31), kind=kLoop, calls=%fused_computation.20 | loop fusion | flops 1048576 | bytes 2097152 | tf_op jit(solution)/shard_map/convert
  59.5 0.6 fusion.32
  63.8 2.6 %pad_maximum_fusion.3 = bf16[1024,2,128]{2,1,0:T(2,128)(2,1)S(1)} fusion(bf16[1024,2,64]{2,1,0:T(2,128)(2,1)} %get-tuple-element.18, bf16[1024,2,64]{2,1,0:T(2,128)(2,1)} %get-tuple-element.17), kind=kLoop, calls=%fused_computation.31 | loop fusion | flops 1048576 | bytes 1048576 | tf_op jit(solution)/shard_map/concatenate | solution.py:23
  66.4 0.1 copy.40
  66.6 0.1 add.165
  66.7 0.1 reshape.382
  66.9 0.1 reshape.381
  67.0 0.1 reshape.380
  69.1 3.7 %convolution_convert_fusion = bf16[1024,256]{1,0:T(8,128)(2,1)S(1)} fusion(bf16[1024,2048]{1,0:T(8,128)(2,1)} %fusion.2, bf16[2048,256]{1,0:T(8,128)(2,1)} %param.16), kind=kOutput, calls=%fused_computation.15 | convolution fusion | flops 1074003968 | bytes 5767168 | tf_op jit(solution)/shard_map/dot_general | solution.py:374
  73.0 1.5 constant_dynamic-slice_fusion.res_ref
  74.5 0.3 compare_and_fusion
  74.9 0.6 or_and_fusion
  75.5 1.3 add_select_fusion.bias_ref
  76.9 0.1 maximum_maximum_fusion.1
  77.0 3.7 %fusion.33 = f32[1024,512]{1,0:T(8,128)} fusion(bf16[1024,2048]{1,0:T(8,128)(2,1)S(1)} %copy-done.6, bf16[2048,512]{1,0:T(8,128)(2,1)S(1)} %copy-done), kind=kOutput, calls=%fused_computation.108 | convolution fusion | flops 2147483648 | bytes 8388608 | tf_op jit(solution)/shard_map/dot_general | solution.py:359
  80.7 13.8 %all-to-all-done = bf16[64,32,512]{2,1,0:T(8,128)(2,1)} async-done(((bf16[64,32,512]{2,1,0:T(8,128)(2,1)}), bf16[64,32,512]{2,1,0:T(8,128)(2,1)}, u32[]{:S(2)}, u32[]{:S(2)}) %all-to-all-start) | async-done | bytes 2097184 | tf_op jit(solution)/shard_map/all_to_all | solution.py:332
  94.5 1.7 %fusion.29 = (bf16[64,16,512]{2,1,0:T(8,128)(2,1)S(1)}, bf16[64,16,512]{2,1,0:T(8,128)(2,1)S(1)}) fusion(bf16[64,32,512]{2,1,0:T(8,128)(2,1)} %all-to-all-done), kind=kLoop, calls=%fused_computation.104 | loop fusion | bytes 4194304 | tf_op jit(solution)/shard_map/slice | solution.py:333
  96.3 2.9 %select_reduce_fusion = f32[1024,16]{0,1:T(8,128)S(1)} fusion(pred[1024,64]{0,1:T(8,128)(4,1)S(1)} %iota_compare_fusion, bf16[64,16,512]{2,1,0:T(8,128)(2,1)S(1)} %get-tuple-element.19, bf16[1024,2048]{1,0:T(8,128)(2,1)} %fusion.2, s32[]{:T(128)S(6)} %select_n.72), kind=kOutput, calls=%fused_computation.7 | convolution fusion | flops 1075822592 | bytes 2228228 | tf_op jit(solution)/shard_map/dot_general | solution.py:340
  99.2 1.7 %collective-permute-start = (f32[1024,16]{0,1:T(8,128)S(1)}, f32[1024,16]{0,1:T(8,128)S(1)}, u32[]{:S(2)}, u32[]{:S(2)}) collective-permute-start(f32[1024,16]{0,1:T(8,128)S(1)} %select_reduce_fusion), channel_id=1, source_target_pairs={{0,1},{1,2},{2,3},{3,0},{4,5},{5,6},{6,7},{7,4},{8,9},{9,10},{10,1... | collective-permute-start | bytes 196616 | tf_op jit(solution)/shard_map/ppermute | solution.py:345
  100.9 2.9 %collective-permute-start.1 = (f32[1024,16]{0,1:T(8,128)S(1)}, f32[1024,16]{0,1:T(8,128)S(1)}, u32[]{:S(2)}, u32[]{:S(2)}) collective-permute-start(f32[1024,16]{0,1:T(8,128)S(1)} %select_reduce_fusion), channel_id=1, source_target_pairs={{0,2},{1,3},{2,0},{3,1},{4,6},{5,7},{6,4},{7,5},{8,10},{9,11},{10,... | collective-permute-start | bytes 196616 | tf_op jit(solution)/shard_map/ppermute | solution.py:345
  103.8 1.3 collective-permute-start.2
  105.2 0.3 pad_maximum_fusion.1
  105.7 2.1 %collective-permute-done.1 = f32[1024,16]{0,1:T(8,128)S(1)} collective-permute-done((f32[1024,16]{0,1:T(8,128)S(1)}, f32[1024,16]{0,1:T(8,128)S(1)}, u32[]{:S(2)}, u32[]{:S(2)}) %collective-permute-start.1) | collective-permute-done | bytes 65568 | tf_op jit(solution)/shard_map/ppermute | solution.py:345
  107.7 1.0 collective-permute-done.2
  108.8 3.0 %convert_add_fusion.q_ref = f32[1024,512]{1,0:T(8,128)} fusion(f32[1024,512]{1,0:T(8,128)S(1)} %copy-done.19, pred[1024,64]{0,1:T(8,128)(4,1)S(1)} %iota_compare_fusion, bf16[64,16,512]{2,1,0:T(8,128)(2,1)S(1)} %get-tuple-element.20, bf16[1024,16]{0,1:T(8,128)(2,1)S(1)} %add_convert_fusion.1), kind=kOutput, calls=%fused_computation.10 | convolution fusion | flops 1076887552 | bytes 5341184 | tf_op jit(solution)/shard_map/dot_general | solution.py:355
  111.7 44.4 %shard_map.119 = bf16[1024,512]{1,0:T(8,128)(2,1)S(1)} custom-call(f32[1024,512]{1,0:T(8,128)} %convert_add_fusion.q_ref, f32[1024,128]{1,0:T(8,128)S(1)} %get-tuple-element.45.cs_ref, f32[1024,128]{1,0:T(8,128)S(1)} %get-tuple-element.46.sn_ref, bf16[1152,256]{1,0:T(8,128)(2,1)S(1)} %concatenate.98.k_ref, bf16[1152,256]{1,0:T(8,128)(2,1)S(1)} %concatenate.99.v_ref, ...), custom_call_target="tpu_custom_call" | custom-call | tf_op jit(solution)/shard_map/pallas_call | solution.py:197
  156.2 1.0 copy.42
  (79 shorter events, 1.0 us)
Async XLA Ops:
  0.0 77.0 %copy-start = (bf16[2048,512]{1,0:T(8,128)(2,1)S(1)}, bf16[2048,512]{1,0:T(8,128)(2,1)}, u32[]{:S(2)}) copy-start(bf16[2048,512]{1,0:T(8,128)(2,1)} %param.14) | copy-start | bytes 6291460
  25.0 3.2 %copy-start.13 = (bf16[16,16,512]{2,1,0:T(8,128)(2,1)S(1)}, bf16[16,16,512]{2,1,0:T(8,128)(2,1)}, u32[]{:S(2)}) copy-start(bf16[16,16,512]{2,1,0:T(8,128)(2,1)} %param.19) | copy-start | bytes 786436
  25.0 3.2 %copy-start.14 = (bf16[16,512,16]{1,2,0:T(8,128)(2,1)S(1)}, bf16[16,512,16]{1,2,0:T(8,128)(2,1)}, u32[]{:S(2)}) copy-start(bf16[16,512,16]{1,2,0:T(8,128)(2,1)} %param.18) | copy-start | bytes 786436
  28.2 2.0 %copy-start.17 = (f32[2048]{0:T(1024)S(1)}, f32[2048]{0:T(1024)}, u32[]{:S(2)}) copy-start(f32[2048]{0:T(1024)} %param.13) | copy-start | bytes 24580
  35.4 9.7 %copy-start.18 = (s32[1,32]{1,0:T(1,128)S(1)}, s32[1,32]{1,0:T(1,128)}, u32[]{:S(2)}) copy-start(s32[1,32]{1,0:T(1,128)} %param.20) | copy-start | bytes 388
  35.4 10.0 %copy-start.15 = (s32[1,32]{1,0:T(1,128)S(1)}, s32[1,32]{1,0:T(1,128)}, u32[]{:S(2)}) copy-start(s32[1,32]{1,0:T(1,128)} %param.21) | copy-start | bytes 388
  35.4 59.1 %all-to-all-start = ((bf16[64,32,512]{2,1,0:T(8,128)(2,1)}), bf16[64,32,512]{2,1,0:T(8,128)(2,1)}, u32[]{:S(2)}, u32[]{:S(2)}) async-start(bf16[64,32,512]{2,1,0:T(8,128)(2,1)} %gather_fusion.1), calls=%async_computation | async-start | bytes 4194304 | tf_op jit(solution)/shard_map/all_to_all | solution.py:332
  54.4 3.1 %copy-start.7 = (f32[1024,2,64]{2,1,0:T(2,128)S(1)}, f32[1024,2,64]{2,1,0:T(2,128)}, u32[]{:S(2)}) copy-start(f32[1024,2,64]{2,1,0:T(2,128)} %copy.33) | copy-start | bytes 1572868
  57.5 2.0 %copy-start.2 = (f32[1024,64]{1,0:T(8,128)}, f32[1024,64]{1,0:T(8,128)S(1)}, u32[]{:S(2)}) copy-start(f32[1024,64]{1,0:T(8,128)S(1)} %get-tuple-element.30) | copy-start | bytes 786436
  57.5 2.0 %copy-start.4 = (f32[1024,64]{1,0:T(8,128)}, f32[1024,64]{1,0:T(8,128)S(1)}, u32[]{:S(2)}) copy-start(f32[1024,64]{1,0:T(8,128)S(1)} %get-tuple-element.31) | copy-start | bytes 786436
  59.5 9.6 %copy-start.16 = (s32[8,128]{1,0:T(8,128)S(1)}, s32[8,128]{1,0:T(8,128)}, u32[]{:S(2)}) copy-start(s32[8,128]{1,0:T(8,128)} %constant.106.clone.1) | copy-start | bytes 12292
  66.5 6.4 %copy-start.8 = (bf16[128,8,2,128]{3,1,2,0:T(8,128)(2,1)}, bf16[128,8,2,128]{3,1,2,0:T(8,128)(2,1)S(1)}, u32[]{:S(2)}) copy-start(bf16[128,8,2,128]{3,1,2,0:T(8,128)(2,1)S(1)} %copy.40) | copy-start | bytes 1572868
  72.9 3.9 %copy-start.11 = (bf16[1024,256]{1,0:T(8,128)(2,1)}, bf16[1024,256]{1,0:T(8,128)(2,1)S(1)}, u32[]{:S(2)}) copy-start(bf16[1024,256]{1,0:T(8,128)(2,1)S(1)} %convolution_convert_fusion) | copy-start | bytes 1572868
  72.9 4.0 %copy-start.6 = (bf16[1024,2048]{1,0:T(8,128)(2,1)S(1)}, bf16[1024,2048]{1,0:T(8,128)(2,1)}, u32[]{:S(2)}) copy-start(bf16[1024,2048]{1,0:T(8,128)(2,1)} %fusion.2) | copy-start | bytes 12582916
  96.3 8.9 %copy-start.3 = (f32[1024,64]{1,0:T(8,128)S(1)}, f32[1024,64]{1,0:T(8,128)}, u32[]{:S(2)}) copy-start(f32[1024,64]{1,0:T(8,128)} %copy-done.2) | copy-start | bytes 786436
  96.3 8.9 %copy-start.5 = (f32[1024,64]{1,0:T(8,128)S(1)}, f32[1024,64]{1,0:T(8,128)}, u32[]{:S(2)}) copy-start(f32[1024,64]{1,0:T(8,128)} %copy-done.4) | copy-start | bytes 786436
  96.3 8.9 %copy-start.10 = (f32[1024,64]{1,0:T(8,128)S(1)}, f32[1024,64]{1,0:T(8,128)}, u32[]{:S(2)}) copy-start(f32[1024,64]{1,0:T(8,128)} %get-tuple-element.29) | copy-start | bytes 786436
  99.2 6.3 %copy-start.9 = (bf16[128,8,2,128]{3,1,2,0:T(8,128)(2,1)S(1)}, bf16[128,8,2,128]{3,1,2,0:T(8,128)(2,1)}, u32[]{:S(2)}) copy-start(bf16[128,8,2,128]{3,1,2,0:T(8,128)(2,1)} %copy-done.8) | copy-start | bytes 1572868
  99.2 6.3 %copy-start.12 = (bf16[1024,256]{1,0:T(8,128)(2,1)S(1)}, bf16[1024,256]{1,0:T(8,128)(2,1)}, u32[]{:S(2)}) copy-start(bf16[1024,256]{1,0:T(8,128)(2,1)} %copy-done.11) | copy-start | bytes 1572868
  99.2 6.4 %collective-permute-start = (f32[1024,16]{0,1:T(8,128)S(1)}, f32[1024,16]{0,1:T(8,128)S(1)}, u32[]{:S(2)}, u32[]{:S(2)}) collective-permute-start(f32[1024,16]{0,1:T(8,128)S(1)} %select_reduce_fusion), channel_id=1, source_target_pairs={{0,1},{1,2},{2,3},{3,0},{4,5},{5,6},{6,7},{7,4},{8,9},{9,10},{10,1... | collective-permute-start | bytes 196616 | tf_op jit(solution)/shard_map/ppermute | solution.py:345
  100.9 6.8 %collective-permute-start.1 = (f32[1024,16]{0,1:T(8,128)S(1)}, f32[1024,16]{0,1:T(8,128)S(1)}, u32[]{:S(2)}, u32[]{:S(2)}) collective-permute-start(f32[1024,16]{0,1:T(8,128)S(1)} %select_reduce_fusion), channel_id=1, source_target_pairs={{0,2},{1,3},{2,0},{3,1},{4,6},{5,7},{6,4},{7,5},{8,10},{9,11},{10,... | collective-permute-start | bytes 196616 | tf_op jit(solution)/shard_map/ppermute | solution.py:345
  103.8 4.9 %collective-permute-start.2 = (f32[1024,16]{0,1:T(8,128)S(1)}, f32[1024,16]{0,1:T(8,128)S(1)}, u32[]{:S(2)}, u32[]{:S(2)}) collective-permute-start(f32[1024,16]{0,1:T(8,128)S(1)} %select_reduce_fusion), channel_id=1, source_target_pairs={{0,3},{1,0},{2,1},{3,2},{4,7},{5,4},{6,5},{7,6},{8,11},{9,8},{10,9... | collective-permute-start | bytes 196616 | tf_op jit(solution)/shard_map/ppermute | solution.py:345
  105.2 3.6 %copy-start.19 = (f32[1024,512]{1,0:T(8,128)S(1)}, f32[1024,512]{1,0:T(8,128)}, u32[]{:S(2)}) copy-start(f32[1024,512]{1,0:T(8,128)} %fusion.33) | copy-start | bytes 6291460
  108.8 3.0 %copy-start.1 = (f32[8,128,384]{2,1,0:T(8,128)S(1)}, f32[8,128,384]{2,1,0:T(8,128)}, u32[]{:S(2)}) copy-start(f32[8,128,384]{2,1,0:T(8,128)} %add_select_fusion.bias_ref) | copy-start | bytes 4718596

commit v11 on v10

--- a/solution.py
+++ b/solution.py
@@ -321,14 +321,14 @@
     wanted = jnp.sum(holder_hot * local_slot[None, :], 1)
     wanted_in = exchange_ids(wanted)
     table = jnp.concatenate([jnp.transpose(adapter_down_maps, (0, 2, 1)), adapter_up_maps], 1)
+    maps_out = table[wanted_in]
+    tokens, maps_out = lax.optimization_barrier((tokens, maps_out))
     float_tok = tokens.astype(jnp.float32)
     normalized_input = (
         float_tok
         * lax.rsqrt(jnp.mean(float_tok * float_tok, -1, keepdims=True) + 1e-06)
         * input_norm_gain
     ).astype(jnp.bfloat16)
-    maps_out = table[wanted_in]
-    normalized_input, maps_out = lax.optimization_barrier((normalized_input, maps_out))
     maps_in = lax.all_to_all(maps_out, "req", split_axis=0, concat_axis=0, tiled=True)
     down_in = maps_in[:, :rank_extent, :].reshape(req_count * rank_extent, piece_width)
     up_in = maps_in[:, rank_extent:, :].reshape(req_count * rank_extent, piece_width)

time: 158 us -> 150 us (0.949)
  waiting for transfers between devices: 16.9 us -> 13.9 us
  other arithmetic: 20.6 us -> 17.8 us
  matrix products: 17.1 us -> 14.7 us
    convert_element_type x1, other arithmetic: 5.15 us -> 1.03 us  [per_device(): normalized_input = (float_tok * lax.rsqrt(jnp.mean(float_tok * float_tok,...]
    all_to_all x1, waiting for transfers between devices: 13.8 us -> 10.9 us  [per_device(): lax.all_to_all(maps_out, 'req', split_axis=0, concat_axis=0, tiled=True)]
    dot_general x1, matrix products: 3.78 us -> 1.31 us  [per_device(): jnp.dot(normalized_input, key_matrix, preferred_element_type=jnp.float32)]
    unnamed x44 -> x46, local copies, waits for them, and re-layouts: 4.76 us -> 5.75 us
  transfers between devices with their start and end apart: 4 -> 4, of which waited for: 3 -> 3; matrix products, arithmetic and copies ran while one was open for 19% -> 21% of each run, Pallas kernels for 0% -> 0%
where the time goes in v11:
time: 150 us
  Pallas kernels  64 us (43%)
  local copies, waits for them, and re-layouts  17.9 us (12%)
  other arithmetic  17.8 us (12%)
  starting transfers between devices  15.6 us (10%)
  matrix products  14.7 us (10%)
  waiting for transfers between devices  13.9 us (9%)
  between operations  6 us (4%)
    pallas_call x1, Pallas kernels, attend_and_reduce(): pl.pallas_call(kernel, out_shape=jax.ShapeDtypeStruct((rows, piece), jnp....  44.5 us
    pallas_call x1, Pallas kernels, exchange_ids(): pl.pallas_call(ids_kernel, out_shape=jax.ShapeDtypeStruct((count, 8, 128)...  19.6 us
    all_to_all x1, waiting for transfers between devices, per_device(): lax.all_to_all(maps_out, 'req', split_axis=0, concat_axis=0, tiled=True)  10.9 us
    all_to_all x1, starting transfers between devices, per_device(): lax.all_to_all(maps_out, 'req', split_axis=0, concat_axis=0, tiled=True)  9.68 us
    ppermute x3, starting transfers between devices, per_device(): lax.ppermute(partial_rank, 'tp', [(i, (i + k) % tp_count) for i in range(...  5.89 us
    unnamed x46, local copies, waits for them, and re-layouts  5.75 us
    dot_general x1, matrix products, per_device(): jnp.dot(normalized_input, value_matrix, preferred_element_type=jnp.float32)  3.73 us
    dot_general x1, matrix products, per_device(): jnp.dot(normalized_input, query_matrix, preferred_element_type=jnp.float32)  3.7 us
  transfers between devices with their start and end apart: 4, of which 3 were waited for; matrix products, arithmetic and copies ran while one was open for 21% of the time, Pallas kernels for 0%

profile of v11, /device:TPU:2, one launch (start us, length us, event | category | flops | bytes accessed | tf_op | source)
XLA Modules:
  0.0 149.9 jit_solution(66237450724490772)
XLA Ops:
  0.0 0.8 fusion.22
  0.8 1.4 gather_fusion
  2.2 0.1 select_reduce_fusion.6
  2.3 0.8 broadcast_in_dim.37.wanted_ref
  3.2 19.6 %shard_map.118 = s32[64,8,128]{2,1,0:T(8,128)} custom-call(s32[64,8,128]{2,1,0:T(8,128)} %broadcast_in_dim.37.wanted_ref), custom_call_target="tpu_custom_call" | custom-call | tf_op jit(solution)/shard_map/pallas_call | solution.py:275
  22.7 2.2 %slice_reduce_fusion = s32[64]{0:T(128)S(1)} fusion(s32[64,8,128]{2,1,0:T(8,128)} %shard_map.118), kind=kLoop, calls=%fused_computation.45 | loop fusion | bytes 512 | tf_op jit(solution)/shard_map/slice | solution.py:287
  25.0 1.1 pad_maximum_fusion
  26.1 2.0 %gather_fusion.1 = bf16[64,32,512]{2,1,0:T(8,128)(2,1)} fusion(bf16[16,32,512]{2,1,0:T(8,128)(2,1)S(1)} %pad_maximum_fusion, s32[1024]{0:T(1024)S(1)} %pad_clamp_fusion), kind=kCustom, calls=%fused_computation.1 | custom fusion | bytes 4194560 | tf_op jit(solution)/shard_map/gather | solution.py:324
  28.1 9.7 %all-to-all-start = ((bf16[64,32,512]{2,1,0:T(8,128)(2,1)}), bf16[64,32,512]{2,1,0:T(8,128)(2,1)}, u32[]{:S(2)}, u32[]{:S(2)}) async-start(bf16[64,32,512]{2,1,0:T(8,128)(2,1)} %gather_fusion.1), calls=%async_computation | async-start | bytes 4194304 | tf_op jit(solution)/shard_map/all_to_all | solution.py:332
  37.8 0.1 copy.25
  37.9 0.1 reduce.1
  38.1 0.1 convert_reduce_fusion
  38.3 0.2 select_reduce_fusion.5
  38.4 0.1 select_reduce_fusion.1
  38.6 3.2 %fusion = f32[1024]{0:T(1024)S(1)} fusion(bf16[1024,2048]{1,0:T(8,128)(2,1)} %param.12), kind=kLoop, calls=%fused_computation.4 | loop fusion | flops 6290432 | bytes 4198400 | tf_op jit(solution)/shard_map/reduce_sum | solution.py:329
  41.9 0.2 copy-done.2
  42.1 1.0 fusion.2
  43.1 0.2 copy-done.19
  43.3 1.3 fusion.34
  44.6 0.6 copy-done.7
  45.2 1.0 fusion.30
  46.3 1.4 copy.32
  47.7 2.2 %copy.33 = f32[1024,2,64]{2,1,0:T(2,128)} copy(f32[1024,2,64]{0,2,1:T(8,128)} %get-tuple-element.21) | data formatting | bytes 1048576
  49.9 0.1 select_reduce_fusion.7
  50.0 3.0 %fusion.17 = (f32[1024,64]{1,0:T(8,128)}, f32[1024,64]{1,0:T(8,128)S(1)}, f32[1024,64]{1,0:T(8,128)S(1)}) fusion(f32[64]{0:T(128)S(1)} %negate_power_fusion, f32[1024]{0:T(1024)S(1)} %add_convert_fusion.2), kind=kLoop, calls=%fused_computation.34 | loop fusion | flops 131072 | bytes 790784 | tf_op jit(solution)/shard_map/neg | solution.py:368
  53.0 1.9 %subtract_convert_fusion = (bf16[1024,2,64]{2,1,0:T(2,128)(2,1)}, bf16[1024,2,64]{2,1,0:T(2,128)(2,1)}) fusion(f32[1024,2,64]{2,1,0:T(2,128)S(1)} %copy-done.9, f32[1024,2,64]{2,1,0:T(2,128)S(1)} %copy.32, f32[1024,64]{1,0:T(8,128)S(1)} %get-tuple-element.30, f32[1024,64]{1,0:T(8,128)S(1)} %get-tuple-element.31), kind=kLoop, calls=%fused_computation.20 | loop fusion | flops 1048576 | bytes 2097152 | tf_op jit(solution)/shard_map/convert
  55.0 0.6 fusion.32
  59.3 2.6 %pad_maximum_fusion.3 = bf16[1024,2,128]{2,1,0:T(2,128)(2,1)S(1)} fusion(bf16[1024,2,64]{2,1,0:T(2,128)(2,1)} %get-tuple-element.18, bf16[1024,2,64]{2,1,0:T(2,128)(2,1)} %get-tuple-element.17), kind=kLoop, calls=%fused_computation.31 | loop fusion | flops 1048576 | bytes 1048576 | tf_op jit(solution)/shard_map/concatenate | solution.py:23
  62.1 0.1 add.165
  64.6 3.7 %convolution_convert_fusion = bf16[1024,256]{1,0:T(8,128)(2,1)S(1)} fusion(bf16[1024,2048]{1,0:T(8,128)(2,1)} %copy-done.7, bf16[2048,256]{1,0:T(8,128)(2,1)} %param.16), kind=kOutput, calls=%fused_computation.15 | convolution fusion | flops 1074003968 | bytes 5767168 | tf_op jit(solution)/shard_map/dot_general | solution.py:374
  68.4 1.5 constant_dynamic-slice_fusion.res_ref
  70.0 0.3 compare_and_fusion
  70.4 0.8 or_and_fusion
  71.2 1.3 add_select_fusion.bias_ref
  72.5 0.1 maximum_maximum_fusion.1
  72.7 3.7 %fusion.33 = f32[1024,512]{1,0:T(8,128)} fusion(bf16[1024,2048]{1,0:T(8,128)(2,1)S(1)} %copy-done.8, bf16[2048,512]{1,0:T(8,128)(2,1)S(1)} %copy-done), kind=kOutput, calls=%fused_computation.108 | convolution fusion | flops 2147483648 | bytes 8388608 | tf_op jit(solution)/shard_map/dot_general | solution.py:359
  76.4 10.9 %all-to-all-done = bf16[64,32,512]{2,1,0:T(8,128)(2,1)} async-done(((bf16[64,32,512]{2,1,0:T(8,128)(2,1)}), bf16[64,32,512]{2,1,0:T(8,128)(2,1)}, u32[]{:S(2)}, u32[]{:S(2)}) %all-to-all-start) | async-done | bytes 2097184 | tf_op jit(solution)/shard_map/all_to_all | solution.py:332
  87.2 1.7 %fusion.29 = (bf16[64,16,512]{2,1,0:T(8,128)(2,1)S(1)}, bf16[64,16,512]{2,1,0:T(8,128)(2,1)S(1)}) fusion(bf16[64,32,512]{2,1,0:T(8,128)(2,1)} %all-to-all-done), kind=kLoop, calls=%fused_computation.104 | loop fusion | bytes 4194304 | tf_op jit(solution)/shard_map/slice | solution.py:333
  89.0 2.9 %select_reduce_fusion = f32[1024,16]{0,1:T(8,128)S(1)} fusion(pred[1024,64]{0,1:T(8,128)(4,1)S(1)} %iota_compare_fusion, bf16[64,16,512]{2,1,0:T(8,128)(2,1)S(1)} %get-tuple-element.19, bf16[1024,2048]{1,0:T(8,128)(2,1)} %copy-done.7, s32[]{:T(128)S(6)} %select_n.72), kind=kOutput, calls=%fused_computation.7 | convolution fusion | flops 1075822592 | bytes 2228228 | tf_op jit(solution)/shard_map/dot_general | solution.py:340
  92.0 1.6 %collective-permute-start = (f32[1024,16]{0,1:T(8,128)S(1)}, f32[1024,16]{0,1:T(8,128)S(1)}, u32[]{:S(2)}, u32[]{:S(2)}) collective-permute-start(f32[1024,16]{0,1:T(8,128)S(1)} %select_reduce_fusion), channel_id=1, source_target_pairs={{0,1},{1,2},{2,3},{3,0},{4,5},{5,6},{6,7},{7,4},{8,9},{9,10},{10,1... | collective-permute-start | bytes 196616 | tf_op jit(solution)/shard_map/ppermute | solution.py:345
  93.6 2.9 %collective-permute-start.1 = (f32[1024,16]{0,1:T(8,128)S(1)}, f32[1024,16]{0,1:T(8,128)S(1)}, u32[]{:S(2)}, u32[]{:S(2)}) collective-permute-start(f32[1024,16]{0,1:T(8,128)S(1)} %select_reduce_fusion), channel_id=1, source_target_pairs={{0,2},{1,3},{2,0},{3,1},{4,6},{5,7},{6,4},{7,5},{8,10},{9,11},{10,... | collective-permute-start | bytes 196616 | tf_op jit(solution)/shard_map/ppermute | solution.py:345
  96.5 1.3 collective-permute-start.2
  97.9 0.3 pad_maximum_fusion.1
  98.3 2.1 %collective-permute-done.1 = f32[1024,16]{0,1:T(8,128)S(1)} collective-permute-done((f32[1024,16]{0,1:T(8,128)S(1)}, f32[1024,16]{0,1:T(8,128)S(1)}, u32[]{:S(2)}, u32[]{:S(2)}) %collective-permute-start.1) | collective-permute-done | bytes 65568 | tf_op jit(solution)/shard_map/ppermute | solution.py:345
  100.4 1.0 collective-permute-done.2
  101.4 3.0 %convert_add_fusion.q_ref = f32[1024,512]{1,0:T(8,128)} fusion(f32[1024,512]{1,0:T(8,128)S(1)} %copy-done.20, pred[1024,64]{0,1:T(8,128)(4,1)S(1)} %iota_compare_fusion, bf16[64,16,512]{2,1,0:T(8,128)(2,1)S(1)} %get-tuple-element.20, bf16[1024,16]{0,1:T(8,128)(2,1)S(1)} %add_convert_fusion.1), kind=kOutput, calls=%fused_computation.10 | convolution fusion | flops 1076887552 | bytes 5341184 | tf_op jit(solution)/shard_map/dot_general | solution.py:355
  104.4 44.5 %shard_map.119 = bf16[1024,512]{1,0:T(8,128)(2,1)S(1)} custom-call(f32[1024,512]{1,0:T(8,128)} %convert_add_fusion.q_ref, f32[1024,128]{1,0:T(8,128)S(1)} %get-tuple-element.45.cs_ref, f32[1024,128]{1,0:T(8,128)S(1)} %get-tuple-element.46.sn_ref, bf16[1152,256]{1,0:T(8,128)(2,1)S(1)} %concatenate.98.k_ref, bf16[1152,256]{1,0:T(8,128)(2,1)S(1)} %concatenate.99.v_ref, ...), custom_call_target="tpu_custom_call" | custom-call | tf_op jit(solution)/shard_map/pallas_call | solution.py:197
  148.9 1.0 copy.42
  (81 shorter events, 1.3 us)
Async XLA Ops:
  0.0 72.6 %copy-start = (bf16[2048,512]{1,0:T(8,128)(2,1)S(1)}, bf16[2048,512]{1,0:T(8,128)(2,1)}, u32[]{:S(2)}) copy-start(bf16[2048,512]{1,0:T(8,128)(2,1)} %param.14) | copy-start | bytes 6291460
  28.1 9.7 %copy-start.18 = (s32[1,32]{1,0:T(1,128)S(1)}, s32[1,32]{1,0:T(1,128)}, u32[]{:S(2)}) copy-start(s32[1,32]{1,0:T(1,128)} %param.20) | copy-start | bytes 388
  28.1 10.0 %copy-start.15 = (s32[1,32]{1,0:T(1,128)S(1)}, s32[1,32]{1,0:T(1,128)}, u32[]{:S(2)}) copy-start(s32[1,32]{1,0:T(1,128)} %param.21) | copy-start | bytes 388
  28.1 59.1 %all-to-all-start = ((bf16[64,32,512]{2,1,0:T(8,128)(2,1)}), bf16[64,32,512]{2,1,0:T(8,128)(2,1)}, u32[]{:S(2)}, u32[]{:S(2)}) async-start(bf16[64,32,512]{2,1,0:T(8,128)(2,1)} %gather_fusion.1), calls=%async_computation | async-start | bytes 4194304 | tf_op jit(solution)/shard_map/all_to_all | solution.py:332
  38.6 3.5 %copy-start.2 = (bf16[1024,2048]{1,0:T(8,128)(2,1)S(1)}, bf16[1024,2048]{1,0:T(8,128)(2,1)}, u32[]{:S(2)}) copy-start(bf16[1024,2048]{1,0:T(8,128)(2,1)} %param.12) | copy-start | bytes 12582916
  38.6 3.4 %copy-start.17 = (f32[2048]{0:T(1024)S(1)}, f32[2048]{0:T(1024)}, u32[]{:S(2)}) copy-start(f32[2048]{0:T(1024)} %param.13) | copy-start | bytes 24580
  42.1 1.2 copy-start.19
  43.3 1.9 %copy-start.7 = (bf16[1024,2048]{1,0:T(8,128)(2,1)}, bf16[1024,2048]{1,0:T(8,128)(2,1)S(1)}, u32[]{:S(2)}) copy-start(bf16[1024,2048]{1,0:T(8,128)(2,1)S(1)} %fusion.2) | copy-start | bytes 12582916
  49.9 3.1 %copy-start.9 = (f32[1024,2,64]{2,1,0:T(2,128)S(1)}, f32[1024,2,64]{2,1,0:T(2,128)}, u32[]{:S(2)}) copy-start(f32[1024,2,64]{2,1,0:T(2,128)} %copy.33) | copy-start | bytes 1572868
  53.0 2.0 %copy-start.3 = (f32[1024,64]{1,0:T(8,128)}, f32[1024,64]{1,0:T(8,128)S(1)}, u32[]{:S(2)}) copy-start(f32[1024,64]{1,0:T(8,128)S(1)} %get-tuple-element.30) | copy-start | bytes 786436
  53.0 2.0 %copy-start.5 = (f32[1024,64]{1,0:T(8,128)}, f32[1024,64]{1,0:T(8,128)S(1)}, u32[]{:S(2)}) copy-start(f32[1024,64]{1,0:T(8,128)S(1)} %get-tuple-element.31) | copy-start | bytes 786436
  55.0 9.6 %copy-start.16 = (s32[8,128]{1,0:T(8,128)S(1)}, s32[8,128]{1,0:T(8,128)}, u32[]{:S(2)}) copy-start(s32[8,128]{1,0:T(8,128)} %constant.106.clone.1) | copy-start | bytes 12292
  62.0 6.4 %copy-start.10 = (bf16[128,8,2,128]{3,1,2,0:T(8,128)(2,1)}, bf16[128,8,2,128]{3,1,2,0:T(8,128)(2,1)S(1)}, u32[]{:S(2)}) copy-start(bf16[128,8,2,128]{3,1,2,0:T(8,128)(2,1)S(1)} %copy.40) | copy-start | bytes 1572868
  68.4 4.1 %copy-start.13 = (bf16[1024,256]{1,0:T(8,128)(2,1)}, bf16[1024,256]{1,0:T(8,128)(2,1)S(1)}, u32[]{:S(2)}) copy-start(bf16[1024,256]{1,0:T(8,128)(2,1)S(1)} %convolution_convert_fusion) | copy-start | bytes 1572868
  68.4 4.2 %copy-start.8 = (bf16[1024,2048]{1,0:T(8,128)(2,1)S(1)}, bf16[1024,2048]{1,0:T(8,128)(2,1)}, u32[]{:S(2)}) copy-start(bf16[1024,2048]{1,0:T(8,128)(2,1)} %copy-done.7) | copy-start | bytes 12582916
  89.0 8.9 %copy-start.4 = (f32[1024,64]{1,0:T(8,128)S(1)}, f32[1024,64]{1,0:T(8,128)}, u32[]{:S(2)}) copy-start(f32[1024,64]{1,0:T(8,128)} %copy-done.3) | copy-start | bytes 786436
  89.0 8.9 %copy-start.6 = (f32[1024,64]{1,0:T(8,128)S(1)}, f32[1024,64]{1,0:T(8,128)}, u32[]{:S(2)}) copy-start(f32[1024,64]{1,0:T(8,128)} %copy-done.5) | copy-start | bytes 786436
  89.0 8.9 %copy-start.12 = (f32[1024,64]{1,0:T(8,128)S(1)}, f32[1024,64]{1,0:T(8,128)}, u32[]{:S(2)}) copy-start(f32[1024,64]{1,0:T(8,128)} %get-tuple-element.29) | copy-start | bytes 786436
  91.9 6.3 %copy-start.11 = (bf16[128,8,2,128]{3,1,2,0:T(8,128)(2,1)S(1)}, bf16[128,8,2,128]{3,1,2,0:T(8,128)(2,1)}, u32[]{:S(2)}) copy-start(bf16[128,8,2,128]{3,1,2,0:T(8,128)(2,1)} %copy-done.10) | copy-start | bytes 1572868
  91.9 6.3 %copy-start.14 = (bf16[1024,256]{1,0:T(8,128)(2,1)S(1)}, bf16[1024,256]{1,0:T(8,128)(2,1)}, u32[]{:S(2)}) copy-start(bf16[1024,256]{1,0:T(8,128)(2,1)} %copy-done.13) | copy-start | bytes 1572868
  92.0 6.4 %collective-permute-start = (f32[1024,16]{0,1:T(8,128)S(1)}, f32[1024,16]{0,1:T(8,128)S(1)}, u32[]{:S(2)}, u32[]{:S(2)}) collective-permute-start(f32[1024,16]{0,1:T(8,128)S(1)} %select_reduce_fusion), channel_id=1, source_target_pairs={{0,1},{1,2},{2,3},{3,0},{4,5},{5,6},{6,7},{7,4},{8,9},{9,10},{10,1... | collective-permute-start | bytes 196616 | tf_op jit(solution)/shard_map/ppermute | solution.py:345
  93.6 6.8 %collective-permute-start.1 = (f32[1024,16]{0,1:T(8,128)S(1)}, f32[1024,16]{0,1:T(8,128)S(1)}, u32[]{:S(2)}, u32[]{:S(2)}) collective-permute-start(f32[1024,16]{0,1:T(8,128)S(1)} %select_reduce_fusion), channel_id=1, source_target_pairs={{0,2},{1,3},{2,0},{3,1},{4,6},{5,7},{6,4},{7,5},{8,10},{9,11},{10,... | collective-permute-start | bytes 196616 | tf_op jit(solution)/shard_map/ppermute | solution.py:345
  96.5 4.9 %collective-permute-start.2 = (f32[1024,16]{0,1:T(8,128)S(1)}, f32[1024,16]{0,1:T(8,128)S(1)}, u32[]{:S(2)}, u32[]{:S(2)}) collective-permute-start(f32[1024,16]{0,1:T(8,128)S(1)} %select_reduce_fusion), channel_id=1, source_target_pairs={{0,3},{1,0},{2,1},{3,2},{4,7},{5,4},{6,5},{7,6},{8,11},{9,8},{10,9... | collective-permute-start | bytes 196616 | tf_op jit(solution)/shard_map/ppermute | solution.py:345
  97.9 3.6 %copy-start.20 = (f32[1024,512]{1,0:T(8,128)S(1)}, f32[1024,512]{1,0:T(8,128)}, u32[]{:S(2)}) copy-start(f32[1024,512]{1,0:T(8,128)} %fusion.33) | copy-start | bytes 6291460
  101.4 3.0 %copy-start.1 = (f32[8,128,384]{2,1,0:T(8,128)S(1)}, f32[8,128,384]{2,1,0:T(8,128)}, u32[]{:S(2)}) copy-start(f32[8,128,384]{2,1,0:T(8,128)} %add_select_fusion.bias_ref) | copy-start | bytes 4718596

commit v12 on v11

--- a/solution.py
+++ b/solution.py
@@ -285,6 +285,56 @@
         compiler_params=pltpu.CompilerParams(collective_id=1, has_side_effects=True),
     )(tiles)
     return got[:, 0, 0]
+
+
+def rank_sum_kernel(part_ref, out_ref, landing, send_sems, recv_sems):
+    me = lax.axis_index("tp")
+    row_dev = lax.axis_index("req")
+    count = lax.axis_size("tp")
+    barrier = pltpu.get_barrier_semaphore()
+    for k in range(1, count):
+        pl.semaphore_signal(
+            barrier,
+            inc=1,
+            device_id=(row_dev, lax.rem(me + k, count)),
+            device_id_type=pl.DeviceIdType.MESH,
+        )
+    pl.semaphore_wait(barrier, count - 1)
+    copies = [
+        pltpu.make_async_remote_copy(
+            src_ref=part_ref,
+            dst_ref=landing.at[k - 1],
+            send_sem=send_sems.at[k - 1],
+            recv_sem=recv_sems.at[k - 1],
+            device_id=(row_dev, lax.rem(me + k, count)),
+            device_id_type=pl.DeviceIdType.MESH,
+        )
+        for k in range(1, count)
+    ]
+    for copy in copies:
+        copy.start()
+    total = part_ref[...]
+    for k, copy in enumerate(copies):
+        copy.wait()
+        total = total + landing[k]
+    out_ref[...] = total
+
+
+def rank_sum(part):
+    count = lax.axis_size("tp")
+    vmem = pltpu.MemorySpace.VMEM
+    return pl.pallas_call(
+        rank_sum_kernel,
+        out_shape=jax.ShapeDtypeStruct(part.shape, part.dtype),
+        in_specs=[pl.BlockSpec(memory_space=vmem)],
+        out_specs=pl.BlockSpec(memory_space=vmem),
+        scratch_shapes=[
+            pltpu.VMEM((count - 1,) + part.shape, part.dtype),
+            pltpu.SemaphoreType.DMA((count - 1,)),
+            pltpu.SemaphoreType.DMA((count - 1,)),
+        ],
+        compiler_params=pltpu.CompilerParams(collective_id=2, has_side_effects=True),
+    )(part)
 
 
 def per_device(
@@ -341,12 +391,7 @@
         normed_slice, down_in.T, preferred_element_type=jnp.float32
     ).reshape(tok_rows, req_count, rank_extent)
     partial_rank = jnp.sum(jnp.where(pick, wide_rank, jnp.float32(0.0)), 1)
-    arrived = [
-        lax.ppermute(partial_rank, "tp", [(i, (i + k) % tp_count) for i in range(tp_count)])
-        for k in range(1, tp_count)
-    ]
-    for piece in arrived:
-        partial_rank = partial_rank + piece
+    partial_rank = rank_sum(partial_rank.T).T
     rank = partial_rank.astype(jnp.bfloat16)
     spread = jnp.where(pick, rank[:, None, :], jnp.zeros((), jnp.bfloat16)).reshape(
         tok_rows, req_count * rank_extent

time: 150 us -> 158 us (1.053); the launches traced: 150 us -> 156 us
  Pallas kernels: 64 us -> 73.7 us
  starting transfers between devices: 15.6 us -> 9.69 us
  other arithmetic: 17.8 us -> 22.2 us
  local copies, waits for them, and re-layouts: 17.9 us -> 20.4 us
  waiting for transfers between devices: 13.9 us -> 11.5 us
  matrix products: 14.7 us -> 12.7 us
    pallas_call x0 -> x1, Pallas kernels: none -> 9.91 us  [rank_sum(): pl.pallas_call(rank_sum_kernel, out_shape=jax.ShapeDtypeStruct(part.shape...]
    ppermute x3 -> x0, starting transfers between devices: 5.89 us -> none  [per_device(): lax.ppermute(partial_rank, 'tp', [(i, (i + k) % tp_count) for i in range(...]
    ppermute x3 -> x0, waiting for transfers between devices: 3.07 us -> none  [per_device(): lax.ppermute(partial_rank, 'tp', [(i, (i + k) % tp_count) for i in range(...]
    dot_general x1, matrix products: 3.73 us -> 1.25 us  [per_device(): jnp.dot(normalized_input, value_matrix, preferred_element_type=jnp.float32)]
    convert_element_type x1, other arithmetic: 1.03 us -> 3.29 us  [per_device(): normalized_input = (float_tok * lax.rsqrt(jnp.mean(float_tok * float_tok,...]
    concatenate x1, other arithmetic: 0.34 us -> 2.35 us  [per_device(): cos_pair = jnp.concatenate([cosine, cosine], 1)]
    unnamed x46 -> x38, local copies, waits for them, and re-layouts: 5.75 us -> 5.95 us
  transfers between devices with their start and end apart: 4 -> 1, of which waited for: 3 -> 1; matrix products, arithmetic and copies ran while one was open for 21% -> 19% of each run, Pallas kernels for 0% -> 0%
where the time goes in v12:
time: 158 us; the launch traced here: 156 us
  Pallas kernels  73.7 us (47%)
  other arithmetic  22.2 us (14%)
  local copies, waits for them, and re-layouts  20.4 us (13%)
  matrix products  12.7 us (8%)
  waiting for transfers between devices  11.5 us (7%)
  starting transfers between devices  9.69 us (6%)
  between operations  5.99 us (4%)
    pallas_call x1, Pallas kernels, attend_and_reduce(): pl.pallas_call(kernel, out_shape=jax.ShapeDtypeStruct((rows, piece), jnp....  44.2 us
    pallas_call x1, Pallas kernels, exchange_ids(): pl.pallas_call(ids_kernel, out_shape=jax.ShapeDtypeStruct((count, 8, 128)...  19.6 us
    all_to_all x1, waiting for transfers between devices, per_device(): lax.all_to_all(maps_out, 'req', split_axis=0, concat_axis=0, tiled=True)  11.5 us
    pallas_call x1, Pallas kernels, rank_sum(): pl.pallas_call(rank_sum_kernel, out_shape=jax.ShapeDtypeStruct(part.shape...  9.91 us
    all_to_all x1, starting transfers between devices, per_device(): lax.all_to_all(maps_out, 'req', split_axis=0, concat_axis=0, tiled=True)  9.69 us
    unnamed x38, local copies, waits for them, and re-layouts  5.95 us
    dot_general x1, matrix products, per_device(): jnp.dot(normalized_input, query_matrix, preferred_element_type=jnp.float32)  3.68 us
    dot_general x1, matrix products, per_device(): jnp.dot(normed_slice, down_in.T, preferred_element_type=jnp.float32)  3.44 us
  transfers between devices with their start and end apart: 1, of which 1 were waited for; matrix products, arithmetic and copies ran while one was open for 19% of the time, Pallas kernels for 0%

profile of v12, /device:TPU:2, one launch (start us, length us, event | category | flops | bytes accessed | tf_op | source)
XLA Modules:
  0.0 156.2 jit_solution(2843991709729729455)
XLA Ops:
  0.0 0.8 fusion.20
  0.8 1.4 gather_fusion
  2.2 0.1 select_reduce_fusion.6
  2.3 0.8 broadcast_in_dim.37.wanted_ref
  3.2 19.6 %shard_map.118 = s32[64,8,128]{2,1,0:T(8,128)} custom-call(s32[64,8,128]{2,1,0:T(8,128)} %broadcast_in_dim.37.wanted_ref), custom_call_target="tpu_custom_call" | custom-call | tf_op jit(solution)/shard_map/pallas_call | solution.py:275
  22.8 2.2 %slice_reduce_fusion = s32[64]{0:T(128)S(1)} fusion(s32[64,8,128]{2,1,0:T(8,128)} %shard_map.118), kind=kLoop, calls=%fused_computation.45 | loop fusion | bytes 512 | tf_op jit(solution)/shard_map/slice | solution.py:287
  25.0 1.1 pad_maximum_fusion
  26.1 2.0 %gather_fusion.1 = bf16[64,32,512]{2,1,0:T(8,128)(2,1)} fusion(bf16[16,32,512]{2,1,0:T(8,128)(2,1)S(1)} %pad_maximum_fusion, s32[1024]{0:T(1024)S(1)} %pad_clamp_fusion), kind=kCustom, calls=%fused_computation.1 | custom fusion | bytes 4194560 | tf_op jit(solution)/shard_map/gather | solution.py:374
  28.1 9.7 %all-to-all-start = ((bf16[64,32,512]{2,1,0:T(8,128)(2,1)}), bf16[64,32,512]{2,1,0:T(8,128)(2,1)}, u32[]{:S(2)}, u32[]{:S(2)}) async-start(bf16[64,32,512]{2,1,0:T(8,128)(2,1)} %gather_fusion.1), calls=%async_computation | async-start | bytes 4194304 | tf_op jit(solution)/shard_map/all_to_all | solution.py:382
  37.8 0.1 copy.25
  38.0 0.1 reduce.1
  38.1 0.1 convert_reduce_fusion
  38.3 0.2 select_reduce_fusion.5
  38.5 0.1 select_reduce_fusion.7
  38.7 0.7 fusion.30
  43.0 3.1 %fusion = f32[1024]{0:T(1024)S(1)} fusion(bf16[1024,2048]{1,0:T(8,128)(2,1)} %param.12), kind=kLoop, calls=%fused_computation.4 | loop fusion | flops 6290432 | bytes 4198400 | tf_op jit(solution)/shard_map/reduce_sum | solution.py:379
  46.1 0.1 select_reduce_fusion.1
  46.3 3.3 %fusion.2 = bf16[1024,2048]{1,0:T(8,128)(2,1)S(1)} fusion(bf16[1024,2048]{1,0:T(8,128)(2,1)} %param.12, f32[2048]{0:T(1024)S(1)} %copy-done.13, f32[1024]{0:T(1024)S(1)} %add_rsqrt_fusion), kind=kLoop, calls=%fused_computation.6 | loop fusion | flops 8388608 | bytes 8400896 | tf_op jit(solution)/shard_map/convert_element_type | solution.py:381
  49.6 1.3 fusion.31
  50.9 0.6 copy-done.6
  51.5 0.1 fusion.28
  51.6 1.3 copy.33
  52.9 1.3 copy.32
  54.2 2.9 %fusion.15 = (f32[1024,64]{1,0:T(8,128)}, f32[1024,64]{1,0:T(8,128)S(1)}, f32[1024,64]{1,0:T(8,128)S(1)}) fusion(f32[64]{0:T(128)S(1)} %negate_power_fusion, f32[1024]{0:T(1024)S(1)} %add_convert_fusion.1), kind=kLoop, calls=%fused_computation.34 | loop fusion | flops 131072 | bytes 790784 | tf_op jit(solution)/shard_map/neg | solution.py:413
  57.2 2.5 %subtract_convert_fusion = (bf16[1024,2,64]{2,1,0:T(2,128)(2,1)S(1)}, bf16[1024,2,64]{2,1,0:T(2,128)(2,1)S(1)}) fusion(f32[1024,2,64]{2,1,0:T(2,128)} %copy.33, f32[1024,2,64]{2,1,0:T(2,128)} %copy.32, f32[1024,64]{1,0:T(8,128)S(1)} %get-tuple-element.30, f32[1024,64]{1,0:T(8,128)S(1)} %get-tuple-element.31), kind=kLoop, calls=%fused_computation.20 | loop fusion | flops 1048576 | bytes 2097152 | tf_op jit(solution)/shard_map/convert
  59.7 1.4 pad_maximum_fusion.3
  61.2 0.8 copy-done.9
  62.0 0.8 concatenate.98.k_ref
  62.9 1.3 convolution_convert_fusion
  64.1 0.8 copy-done.10
  64.9 0.9 concatenate.99.v_ref
  65.9 0.1 add.153
  68.4 0.9 constant_dynamic-slice_fusion.3
  69.3 2.3 %pad_maximum_fusion.1 = (f32[1024,128]{1,0:T(8,128)}, f32[1024,128]{1,0:T(8,128)}) fusion(f32[1024,64]{1,0:T(8,128)S(1)} %get-tuple-element.31, f32[1024,64]{1,0:T(8,128)S(1)} %get-tuple-element.30, f32[1024,64]{1,0:T(8,128)} %get-tuple-element.29), kind=kLoop, calls=%fused_computation.29 | loop fusion | flops 262144 | bytes 1835008 | tf_op jit(solution)/shard_map/concatenate | solution.py:412
  71.7 1.3 constant_dynamic-slice_fusion.res_ref
  73.0 0.3 compare_and_fusion
  73.4 0.8 or_and_fusion
  74.2 1.4 add_select_fusion.bias_ref
  75.7 0.1 maximum_maximum_fusion.1
  75.8 11.5 %all-to-all-done = bf16[64,32,512]{2,1,0:T(8,128)(2,1)} async-done(((bf16[64,32,512]{2,1,0:T(8,128)(2,1)}), bf16[64,32,512]{2,1,0:T(8,128)(2,1)}, u32[]{:S(2)}, u32[]{:S(2)}) %all-to-all-start) | async-done | bytes 2097184 | tf_op jit(solution)/shard_map/all_to_all | solution.py:382
  87.3 2.7 %fusion.27 = (bf16[64,16,512]{2,1,0:T(8,128)(2,1)S(1)}, bf16[64,16,512]{2,1,0:T(8,128)(2,1)}) fusion(bf16[64,32,512]{2,1,0:T(8,128)(2,1)} %all-to-all-done), kind=kLoop, calls=%fused_computation.104 | loop fusion | bytes 4194304 | tf_op jit(solution)/shard_map/slice | solution.py:383
  90.0 3.4 %select_reduce_fusion = f32[1024,16]{0,1:T(8,128)} fusion(pred[1024,64]{0,1:T(8,128)(4,1)S(1)} %iota_compare_fusion, bf16[64,16,512]{2,1,0:T(8,128)(2,1)S(1)} %get-tuple-element.19, bf16[1024,2048]{1,0:T(8,128)(2,1)} %copy-done.6, s32[]{:T(128)S(6)} %select_n.72), kind=kOutput, calls=%fused_computation.7 | convolution fusion | flops 1075822592 | bytes 2228228 | tf_op jit(solution)/shard_map/dot_general | solution.py:390
  93.4 9.9 %shard_map.119 = f32[16,1024]{1,0:T(8,128)} custom-call(f32[16,1024]{1,0:T(8,128)} %bitcast.77), custom_call_target="tpu_custom_call" | custom-call | tf_op jit(solution)/shard_map/pallas_call | solution.py:326
  103.3 0.8 convert_bitcast_fusion
  104.2 3.1 %fusion.3 = bf16[1024,512]{1,0:T(8,128)(2,1)S(1)} fusion(pred[1024,64]{0,1:T(8,128)(4,1)S(1)} %iota_compare_fusion, bf16[64,16,512]{2,1,0:T(8,128)(2,1)} %get-tuple-element.20, bf16[1024,16]{0,1:T(8,128)(2,1)S(1)} %convert_bitcast_fusion), kind=kOutput, calls=%fused_computation.9 | convolution fusion | flops 1075838976 | bytes 2195456 | tf_op jit(solution)/shard_map/dot_general | solution.py:400
  107.3 3.7 %convert_add_fusion.q_ref = f32[1024,512]{1,0:T(8,128)} fusion(bf16[1024,512]{1,0:T(8,128)(2,1)S(1)} %fusion.3, bf16[1024,2048]{1,0:T(8,128)(2,1)S(1)} %copy-done.8, bf16[2048,512]{1,0:T(8,128)(2,1)S(1)} %copy-done), kind=kOutput, calls=%fused_computation.10 | convolution fusion | flops 2148532224 | bytes 9437184 | tf_op jit(solution)/shard_map/dot_general | solution.py:404
  111.0 44.2 %shard_map.120 = bf16[1024,512]{1,0:T(8,128)(2,1)S(1)} custom-call(f32[1024,512]{1,0:T(8,128)} %convert_add_fusion.q_ref, f32[1024,128]{1,0:T(8,128)S(1)} %copy-done.4, f32[1024,128]{1,0:T(8,128)S(1)} %copy-done.5, bf16[1152,256]{1,0:T(8,128)(2,1)S(1)} %copy-done.2, bf16[1152,256]{1,0:T(8,128)(2,1)S(1)} %copy-done.3, ...), custom_call_target="tpu_custom_call" | custom-call | tf_op jit(solution)/shard_map/pallas_call | solution.py:197
  155.2 1.0 copy.42
  (67 shorter events, 1.1 us)
Async XLA Ops:
  0.0 107.2 %copy-start = (bf16[2048,512]{1,0:T(8,128)(2,1)S(1)}, bf16[2048,512]{1,0:T(8,128)(2,1)}, u32[]{:S(2)}) copy-start(bf16[2048,512]{1,0:T(8,128)(2,1)} %param.14) | copy-start | bytes 6291460
  26.1 11.8 %copy-start.14 = (s32[1,32]{1,0:T(1,128)S(1)}, s32[1,32]{1,0:T(1,128)}, u32[]{:S(2)}) copy-start(s32[1,32]{1,0:T(1,128)} %param.20) | copy-start | bytes 388
  26.1 12.1 %copy-start.11 = (s32[1,32]{1,0:T(1,128)S(1)}, s32[1,32]{1,0:T(1,128)}, u32[]{:S(2)}) copy-start(s32[1,32]{1,0:T(1,128)} %param.21) | copy-start | bytes 388
  28.1 18.1 %copy-start.13 = (f32[2048]{0:T(1024)S(1)}, f32[2048]{0:T(1024)}, u32[]{:S(2)}) copy-start(f32[2048]{0:T(1024)} %param.13) | copy-start | bytes 24580
  28.1 59.1 %all-to-all-start = ((bf16[64,32,512]{2,1,0:T(8,128)(2,1)}), bf16[64,32,512]{2,1,0:T(8,128)(2,1)}, u32[]{:S(2)}, u32[]{:S(2)}) async-start(bf16[64,32,512]{2,1,0:T(8,128)(2,1)} %gather_fusion.1), calls=%async_computation | async-start | bytes 4194304 | tf_op jit(solution)/shard_map/all_to_all | solution.py:382
  46.3 3.3 %copy-start.15 = (bf16[2048,256]{1,0:T(8,128)(2,1)S(1)}, bf16[2048,256]{1,0:T(8,128)(2,1)}, u32[]{:S(2)}) copy-start(bf16[2048,256]{1,0:T(8,128)(2,1)} %param.15) | copy-start | bytes 3145732
  49.6 1.9 %copy-start.6 = (bf16[1024,2048]{1,0:T(8,128)(2,1)}, bf16[1024,2048]{1,0:T(8,128)(2,1)S(1)}, u32[]{:S(2)}) copy-start(bf16[1024,2048]{1,0:T(8,128)(2,1)S(1)} %fusion.2) | copy-start | bytes 12582916
  57.2 5.7 %copy-start.7 = (bf16[1024,2048]{1,0:T(8,128)(2,1)S(1)}, bf16[1024,2048]{1,0:T(8,128)(2,1)}, u32[]{:S(2)}) copy-start(bf16[1024,2048]{1,0:T(8,128)(2,1)} %copy-done.6) | copy-start | bytes 12582916
  57.2 5.7 %copy-start.16 = (bf16[2048,256]{1,0:T(8,128)(2,1)S(1)}, bf16[2048,256]{1,0:T(8,128)(2,1)}, u32[]{:S(2)}) copy-start(bf16[2048,256]{1,0:T(8,128)(2,1)} %param.16) | copy-start | bytes 3145732
  61.2 0.8 copy-start.9
  62.9 5.5 %copy-start.12 = (s32[8,128]{1,0:T(8,128)S(1)}, s32[8,128]{1,0:T(8,128)}, u32[]{:S(2)}) copy-start(s32[8,128]{1,0:T(8,128)} %constant.106.clone.1) | copy-start | bytes 12292
  64.1 0.8 copy-start.10
  104.2 3.1 %copy-start.8 = (bf16[1024,2048]{1,0:T(8,128)(2,1)S(1)}, bf16[1024,2048]{1,0:T(8,128)(2,1)}, u32[]{:S(2)}) copy-start(bf16[1024,2048]{1,0:T(8,128)(2,1)} %copy-done.6) | copy-start | bytes 12582916
  107.3 3.7 %copy-start.1 = (f32[8,128,384]{2,1,0:T(8,128)S(1)}, f32[8,128,384]{2,1,0:T(8,128)}, u32[]{:S(2)}) copy-start(f32[8,128,384]{2,1,0:T(8,128)} %add_select_fusion.bias_ref) | copy-start | bytes 4718596
  107.3 3.7 %copy-start.2 = (bf16[1152,256]{1,0:T(8,128)(2,1)S(1)}, bf16[1152,256]{1,0:T(8,128)(2,1)}, u32[]{:S(2)}) copy-start(bf16[1152,256]{1,0:T(8,128)(2,1)} %concatenate.98.k_ref) | copy-start | bytes 1769476
  107.3 3.7 %copy-start.3 = (bf16[1152,256]{1,0:T(8,128)(2,1)S(1)}, bf16[1152,256]{1,0:T(8,128)(2,1)}, u32[]{:S(2)}) copy-start(bf16[1152,256]{1,0:T(8,128)(2,1)} %concatenate.99.v_ref) | copy-start | bytes 1769476
  107.3 3.7 %copy-start.4 = (f32[1024,128]{1,0:T(8,128)S(1)}, f32[1024,128]{1,0:T(8,128)}, u32[]{:S(2)}) copy-start(f32[1024,128]{1,0:T(8,128)} %get-tuple-element.45.cs_ref) | copy-start | bytes 1572868
  107.3 3.7 %copy-start.5 = (f32[1024,128]{1,0:T(8,128)S(1)}, f32[1024,128]{1,0:T(8,128)}, u32[]{:S(2)}) copy-start(f32[1024,128]{1,0:T(8,128)} %get-tuple-element.46.sn_ref) | copy-start | bytes 1572868

commit v13 on v11

--- a/solution.py
+++ b/solution.py
@@ -159,17 +159,13 @@
     lax.fori_loop(0, n_blocks, block_body, 0)
     forward(n_blocks - 1)
 
-    def wait_body(b, carry):
+    own = pl.multiple_of(me * piece, piece)
+
+    def finish_body(b, carry):
         for side in (0, 1):
             raw_copy(b, side).wait_send()
             sum_copy(b, side).wait_send()
             sum_copy(b, side).wait_recv()
-        return carry
-
-    lax.fori_loop(0, n_blocks, wait_body, 0)
-    own = pl.multiple_of(me * piece, piece)
-
-    def finish_body(b, carry):
         row = pl.multiple_of(b * BLOCK, BLOCK)
         total = res_ref[pl.ds(row, BLOCK), :].astype(jnp.float32)
         total = total + send_buf[b, :, pl.ds(own, piece)].astype(jnp.float32)

time: 150 us -> 150 us (level)
  transfers between devices with their start and end apart: 4 -> 4, of which waited for: 3 -> 3; matrix products, arithmetic and copies ran while one was open for 21% -> 22% of each run, Pallas kernels for 0% -> 0%
where the time goes in v13:
time: 150 us; the launch traced here: 149 us
  Pallas kernels  63.6 us (42%)
  local copies, waits for them, and re-layouts  17.9 us (12%)
  other arithmetic  17.8 us (12%)
  starting transfers between devices  15.6 us (10%)
  matrix products  14.7 us (10%)
  waiting for transfers between devices  13.9 us (9%)
  between operations  6 us (4%)
    pallas_call x1, Pallas kernels, attend_and_reduce(): pl.pallas_call(kernel, out_shape=jax.ShapeDtypeStruct((rows, piece), jnp....  44 us
    pallas_call x1, Pallas kernels, exchange_ids(): pl.pallas_call(ids_kernel, out_shape=jax.ShapeDtypeStruct((count, 8, 128)...  19.6 us
    all_to_all x1, waiting for transfers between devices, per_device(): lax.all_to_all(maps_out, 'req', split_axis=0, concat_axis=0, tiled=True)  10.9 us
    all_to_all x1, starting transfers between devices, per_device(): lax.all_to_all(maps_out, 'req', split_axis=0, concat_axis=0, tiled=True)  9.68 us
    ppermute x3, starting transfers between devices, per_device(): lax.ppermute(partial_rank, 'tp', [(i, (i + k) % tp_count) for i in range(...  5.89 us
    unnamed x46, local copies, waits for them, and re-layouts  5.75 us
    dot_general x1, matrix products, per_device(): jnp.dot(normalized_input, value_matrix, preferred_element_type=jnp.float32)  3.73 us
    dot_general x1, matrix products, per_device(): jnp.dot(normalized_input, query_matrix, preferred_element_type=jnp.float32)  3.7 us
  transfers between devices with their start and end apart: 4, of which 3 were waited for; matrix products, arithmetic and copies ran while one was open for 22% of the time, Pallas kernels for 0%

profile of v13, /device:TPU:2, one launch (start us, length us, event | category | flops | bytes accessed | tf_op | source)
XLA Modules:
  0.0 149.4 jit_solution(9352328349167207956)
XLA Ops:
  0.0 0.8 fusion.22
  0.8 1.4 gather_fusion
  2.2 0.1 select_reduce_fusion.6
  2.3 0.8 broadcast_in_dim.37.wanted_ref
  3.2 19.6 %shard_map.118 = s32[64,8,128]{2,1,0:T(8,128)} custom-call(s32[64,8,128]{2,1,0:T(8,128)} %broadcast_in_dim.37.wanted_ref), custom_call_target="tpu_custom_call" | custom-call | tf_op jit(solution)/shard_map/pallas_call | solution.py:271
  22.7 2.2 %slice_reduce_fusion = s32[64]{0:T(128)S(1)} fusion(s32[64,8,128]{2,1,0:T(8,128)} %shard_map.118), kind=kLoop, calls=%fused_computation.45 | loop fusion | bytes 512 | tf_op jit(solution)/shard_map/slice | solution.py:283
  25.0 1.1 pad_maximum_fusion
  26.1 2.0 %gather_fusion.1 = bf16[64,32,512]{2,1,0:T(8,128)(2,1)} fusion(bf16[16,32,512]{2,1,0:T(8,128)(2,1)S(1)} %pad_maximum_fusion, s32[1024]{0:T(1024)S(1)} %pad_clamp_fusion), kind=kCustom, calls=%fused_computation.1 | custom fusion | bytes 4194560 | tf_op jit(solution)/shard_map/gather | solution.py:320
  28.1 9.7 %all-to-all-start = ((bf16[64,32,512]{2,1,0:T(8,128)(2,1)}), bf16[64,32,512]{2,1,0:T(8,128)(2,1)}, u32[]{:S(2)}, u32[]{:S(2)}) async-start(bf16[64,32,512]{2,1,0:T(8,128)(2,1)} %gather_fusion.1), calls=%async_computation | async-start | bytes 4194304 | tf_op jit(solution)/shard_map/all_to_all | solution.py:328
  37.8 0.1 copy.25
  37.9 0.1 reduce.1
  38.1 0.1 convert_reduce_fusion
  38.3 0.2 select_reduce_fusion.5
  38.4 0.1 select_reduce_fusion.1
  38.6 3.2 %fusion = f32[1024]{0:T(1024)S(1)} fusion(bf16[1024,2048]{1,0:T(8,128)(2,1)} %param.12), kind=kLoop, calls=%fused_computation.4 | loop fusion | flops 6290432 | bytes 4198400 | tf_op jit(solution)/shard_map/reduce_sum | solution.py:325
  41.9 0.2 copy-done.2
  42.1 1.0 fusion.2
  43.1 0.2 copy-done.19
  43.3 1.3 fusion.34
  44.6 0.6 copy-done.7
  45.2 1.0 fusion.30
  46.3 1.4 copy.32
  47.7 2.2 %copy.33 = f32[1024,2,64]{2,1,0:T(2,128)} copy(f32[1024,2,64]{0,2,1:T(8,128)} %get-tuple-element.21) | data formatting | bytes 1048576
  49.9 0.1 select_reduce_fusion.7
  50.0 3.0 %fusion.17 = (f32[1024,64]{1,0:T(8,128)}, f32[1024,64]{1,0:T(8,128)S(1)}, f32[1024,64]{1,0:T(8,128)S(1)}) fusion(f32[64]{0:T(128)S(1)} %negate_power_fusion, f32[1024]{0:T(1024)S(1)} %add_convert_fusion.2), kind=kLoop, calls=%fused_computation.34 | loop fusion | flops 131072 | bytes 790784 | tf_op jit(solution)/shard_map/neg | solution.py:364
  53.0 1.9 %subtract_convert_fusion = (bf16[1024,2,64]{2,1,0:T(2,128)(2,1)}, bf16[1024,2,64]{2,1,0:T(2,128)(2,1)}) fusion(f32[1024,2,64]{2,1,0:T(2,128)S(1)} %copy-done.9, f32[1024,2,64]{2,1,0:T(2,128)S(1)} %copy.32, f32[1024,64]{1,0:T(8,128)S(1)} %get-tuple-element.30, f32[1024,64]{1,0:T(8,128)S(1)} %get-tuple-element.31), kind=kLoop, calls=%fused_computation.20 | loop fusion | flops 1048576 | bytes 2097152 | tf_op jit(solution)/shard_map/convert
  55.0 0.6 fusion.32
  59.3 2.6 %pad_maximum_fusion.3 = bf16[1024,2,128]{2,1,0:T(2,128)(2,1)S(1)} fusion(bf16[1024,2,64]{2,1,0:T(2,128)(2,1)} %get-tuple-element.18, bf16[1024,2,64]{2,1,0:T(2,128)(2,1)} %get-tuple-element.17), kind=kLoop, calls=%fused_computation.31 | loop fusion | flops 1048576 | bytes 1048576 | tf_op jit(solution)/shard_map/concatenate | solution.py:23
  62.1 0.1 add.165
  64.6 3.7 %convolution_convert_fusion = bf16[1024,256]{1,0:T(8,128)(2,1)S(1)} fusion(bf16[1024,2048]{1,0:T(8,128)(2,1)} %copy-done.7, bf16[2048,256]{1,0:T(8,128)(2,1)} %param.16), kind=kOutput, calls=%fused_computation.15 | convolution fusion | flops 1074003968 | bytes 5767168 | tf_op jit(solution)/shard_map/dot_general | solution.py:370
  68.4 1.5 constant_dynamic-slice_fusion.res_ref
  70.0 0.3 compare_and_fusion
  70.4 0.8 or_and_fusion
  71.2 1.3 add_select_fusion.bias_ref
  72.5 0.1 maximum_maximum_fusion.1
  72.7 3.7 %fusion.33 = f32[1024,512]{1,0:T(8,128)} fusion(bf16[1024,2048]{1,0:T(8,128)(2,1)S(1)} %copy-done.8, bf16[2048,512]{1,0:T(8,128)(2,1)S(1)} %copy-done), kind=kOutput, calls=%fused_computation.108 | convolution fusion | flops 2147483648 | bytes 8388608 | tf_op jit(solution)/shard_map/dot_general | solution.py:355
  76.4 10.9 %all-to-all-done = bf16[64,32,512]{2,1,0:T(8,128)(2,1)} async-done(((bf16[64,32,512]{2,1,0:T(8,128)(2,1)}), bf16[64,32,512]{2,1,0:T(8,128)(2,1)}, u32[]{:S(2)}, u32[]{:S(2)}) %all-to-all-start) | async-done | bytes 2097184 | tf_op jit(solution)/shard_map/all_to_all | solution.py:328
  87.2 1.7 %fusion.29 = (bf16[64,16,512]{2,1,0:T(8,128)(2,1)S(1)}, bf16[64,16,512]{2,1,0:T(8,128)(2,1)S(1)}) fusion(bf16[64,32,512]{2,1,0:T(8,128)(2,1)} %all-to-all-done), kind=kLoop, calls=%fused_computation.104 | loop fusion | bytes 4194304 | tf_op jit(solution)/shard_map/slice | solution.py:329
  89.0 2.9 %select_reduce_fusion = f32[1024,16]{0,1:T(8,128)S(1)} fusion(pred[1024,64]{0,1:T(8,128)(4,1)S(1)} %iota_compare_fusion, bf16[64,16,512]{2,1,0:T(8,128)(2,1)S(1)} %get-tuple-element.19, bf16[1024,2048]{1,0:T(8,128)(2,1)} %copy-done.7, s32[]{:T(128)S(6)} %select_n.72), kind=kOutput, calls=%fused_computation.7 | convolution fusion | flops 1075822592 | bytes 2228228 | tf_op jit(solution)/shard_map/dot_general | solution.py:336
  92.0 1.6 %collective-permute-start = (f32[1024,16]{0,1:T(8,128)S(1)}, f32[1024,16]{0,1:T(8,128)S(1)}, u32[]{:S(2)}, u32[]{:S(2)}) collective-permute-start(f32[1024,16]{0,1:T(8,128)S(1)} %select_reduce_fusion), channel_id=1, source_target_pairs={{0,1},{1,2},{2,3},{3,0},{4,5},{5,6},{6,7},{7,4},{8,9},{9,10},{10,1... | collective-permute-start | bytes 196616 | tf_op jit(solution)/shard_map/ppermute | solution.py:341
  93.6 2.9 %collective-permute-start.1 = (f32[1024,16]{0,1:T(8,128)S(1)}, f32[1024,16]{0,1:T(8,128)S(1)}, u32[]{:S(2)}, u32[]{:S(2)}) collective-permute-start(f32[1024,16]{0,1:T(8,128)S(1)} %select_reduce_fusion), channel_id=1, source_target_pairs={{0,2},{1,3},{2,0},{3,1},{4,6},{5,7},{6,4},{7,5},{8,10},{9,11},{10,... | collective-permute-start | bytes 196616 | tf_op jit(solution)/shard_map/ppermute | solution.py:341
  96.5 1.3 collective-permute-start.2
  97.9 0.3 pad_maximum_fusion.1
  98.3 2.1 %collective-permute-done.1 = f32[1024,16]{0,1:T(8,128)S(1)} collective-permute-done((f32[1024,16]{0,1:T(8,128)S(1)}, f32[1024,16]{0,1:T(8,128)S(1)}, u32[]{:S(2)}, u32[]{:S(2)}) %collective-permute-start.1) | collective-permute-done | bytes 65568 | tf_op jit(solution)/shard_map/ppermute | solution.py:341
  100.4 1.0 collective-permute-done.2
  101.4 3.0 %convert_add_fusion.q_ref = f32[1024,512]{1,0:T(8,128)} fusion(f32[1024,512]{1,0:T(8,128)S(1)} %copy-done.20, pred[1024,64]{0,1:T(8,128)(4,1)S(1)} %iota_compare_fusion, bf16[64,16,512]{2,1,0:T(8,128)(2,1)S(1)} %get-tuple-element.20, bf16[1024,16]{0,1:T(8,128)(2,1)S(1)} %add_convert_fusion.1), kind=kOutput, calls=%fused_computation.10 | convolution fusion | flops 1076887552 | bytes 5341184 | tf_op jit(solution)/shard_map/dot_general | solution.py:351
  104.4 44.0 %shard_map.119 = bf16[1024,512]{1,0:T(8,128)(2,1)S(1)} custom-call(f32[1024,512]{1,0:T(8,128)} %convert_add_fusion.q_ref, f32[1024,128]{1,0:T(8,128)S(1)} %get-tuple-element.45.cs_ref, f32[1024,128]{1,0:T(8,128)S(1)} %get-tuple-element.46.sn_ref, bf16[1152,256]{1,0:T(8,128)(2,1)S(1)} %concatenate.98.k_ref, bf16[1152,256]{1,0:T(8,128)(2,1)S(1)} %concatenate.99.v_ref, ...), custom_call_target="tpu_custom_call" | custom-call | tf_op jit(solution)/shard_map/pallas_call | solution.py:193
  148.4 1.0 copy.42
  (81 shorter events, 1.3 us)
Async XLA Ops:
  0.0 72.6 %copy-start = (bf16[2048,512]{1,0:T(8,128)(2,1)S(1)}, bf16[2048,512]{1,0:T(8,128)(2,1)}, u32[]{:S(2)}) copy-start(bf16[2048,512]{1,0:T(8,128)(2,1)} %param.14) | copy-start | bytes 6291460
  28.1 9.7 %copy-start.18 = (s32[1,32]{1,0:T(1,128)S(1)}, s32[1,32]{1,0:T(1,128)}, u32[]{:S(2)}) copy-start(s32[1,32]{1,0:T(1,128)} %param.20) | copy-start | bytes 388
  28.1 10.0 %copy-start.15 = (s32[1,32]{1,0:T(1,128)S(1)}, s32[1,32]{1,0:T(1,128)}, u32[]{:S(2)}) copy-start(s32[1,32]{1,0:T(1,128)} %param.21) | copy-start | bytes 388
  28.1 59.1 %all-to-all-start = ((bf16[64,32,512]{2,1,0:T(8,128)(2,1)}), bf16[64,32,512]{2,1,0:T(8,128)(2,1)}, u32[]{:S(2)}, u32[]{:S(2)}) async-start(bf16[64,32,512]{2,1,0:T(8,128)(2,1)} %gather_fusion.1), calls=%async_computation | async-start | bytes 4194304 | tf_op jit(solution)/shard_map/all_to_all | solution.py:328
  38.6 3.5 %copy-start.2 = (bf16[1024,2048]{1,0:T(8,128)(2,1)S(1)}, bf16[1024,2048]{1,0:T(8,128)(2,1)}, u32[]{:S(2)}) copy-start(bf16[1024,2048]{1,0:T(8,128)(2,1)} %param.12) | copy-start | bytes 12582916
  38.6 3.4 %copy-start.17 = (f32[2048]{0:T(1024)S(1)}, f32[2048]{0:T(1024)}, u32[]{:S(2)}) copy-start(f32[2048]{0:T(1024)} %param.13) | copy-start | bytes 24580
  42.1 1.2 copy-start.19
  43.3 1.9 %copy-start.7 = (bf16[1024,2048]{1,0:T(8,128)(2,1)}, bf16[1024,2048]{1,0:T(8,128)(2,1)S(1)}, u32[]{:S(2)}) copy-start(bf16[1024,2048]{1,0:T(8,128)(2,1)S(1)} %fusion.2) | copy-start | bytes 12582916
  49.9 3.1 %copy-start.9 = (f32[1024,2,64]{2,1,0:T(2,128)S(1)}, f32[1024,2,64]{2,1,0:T(2,128)}, u32[]{:S(2)}) copy-start(f32[1024,2,64]{2,1,0:T(2,128)} %copy.33) | copy-start | bytes 1572868
  53.0 2.0 %copy-start.3 = (f32[1024,64]{1,0:T(8,128)}, f32[1024,64]{1,0:T(8,128)S(1)}, u32[]{:S(2)}) copy-start(f32[1024,64]{1,0:T(8,128)S(1)} %get-tuple-element.30) | copy-start | bytes 786436
  53.0 2.0 %copy-start.5 = (f32[1024,64]{1,0:T(8,128)}, f32[1024,64]{1,0:T(8,128)S(1)}, u32[]{:S(2)}) copy-start(f32[1024,64]{1,0:T(8,128)S(1)} %get-tuple-element.31) | copy-start | bytes 786436
  55.0 9.6 %copy-start.16 = (s32[8,128]{1,0:T(8,128)S(1)}, s32[8,128]{1,0:T(8,128)}, u32[]{:S(2)}) copy-start(s32[8,128]{1,0:T(8,128)} %constant.106.clone.1) | copy-start | bytes 12292
  62.0 6.4 %copy-start.10 = (bf16[128,8,2,128]{3,1,2,0:T(8,128)(2,1)}, bf16[128,8,2,128]{3,1,2,0:T(8,128)(2,1)S(1)}, u32[]{:S(2)}) copy-start(bf16[128,8,2,128]{3,1,2,0:T(8,128)(2,1)S(1)} %copy.40) | copy-start | bytes 1572868
  68.4 4.1 %copy-start.13 = (bf16[1024,256]{1,0:T(8,128)(2,1)}, bf16[1024,256]{1,0:T(8,128)(2,1)S(1)}, u32[]{:S(2)}) copy-start(bf16[1024,256]{1,0:T(8,128)(2,1)S(1)} %convolution_convert_fusion) | copy-start | bytes 1572868
  68.4 4.2 %copy-start.8 = (bf16[1024,2048]{1,0:T(8,128)(2,1)S(1)}, bf16[1024,2048]{1,0:T(8,128)(2,1)}, u32[]{:S(2)}) copy-start(bf16[1024,2048]{1,0:T(8,128)(2,1)} %copy-done.7) | copy-start | bytes 12582916
  89.0 8.9 %copy-start.4 = (f32[1024,64]{1,0:T(8,128)S(1)}, f32[1024,64]{1,0:T(8,128)}, u32[]{:S(2)}) copy-start(f32[1024,64]{1,0:T(8,128)} %copy-done.3) | copy-start | bytes 786436
  89.0 8.9 %copy-start.6 = (f32[1024,64]{1,0:T(8,128)S(1)}, f32[1024,64]{1,0:T(8,128)}, u32[]{:S(2)}) copy-start(f32[1024,64]{1,0:T(8,128)} %copy-done.5) | copy-start | bytes 786436
  89.0 8.9 %copy-start.12 = (f32[1024,64]{1,0:T(8,128)S(1)}, f32[1024,64]{1,0:T(8,128)}, u32[]{:S(2)}) copy-start(f32[1024,64]{1,0:T(8,128)} %get-tuple-element.29) | copy-start | bytes 786436
  91.9 6.3 %copy-start.11 = (bf16[128,8,2,128]{3,1,2,0:T(8,128)(2,1)S(1)}, bf16[128,8,2,128]{3,1,2,0:T(8,128)(2,1)}, u32[]{:S(2)}) copy-start(bf16[128,8,2,128]{3,1,2,0:T(8,128)(2,1)} %copy-done.10) | copy-start | bytes 1572868
  91.9 6.3 %copy-start.14 = (bf16[1024,256]{1,0:T(8,128)(2,1)S(1)}, bf16[1024,256]{1,0:T(8,128)(2,1)}, u32[]{:S(2)}) copy-start(bf16[1024,256]{1,0:T(8,128)(2,1)} %copy-done.13) | copy-start | bytes 1572868
  92.0 6.4 %collective-permute-start = (f32[1024,16]{0,1:T(8,128)S(1)}, f32[1024,16]{0,1:T(8,128)S(1)}, u32[]{:S(2)}, u32[]{:S(2)}) collective-permute-start(f32[1024,16]{0,1:T(8,128)S(1)} %select_reduce_fusion), channel_id=1, source_target_pairs={{0,1},{1,2},{2,3},{3,0},{4,5},{5,6},{6,7},{7,4},{8,9},{9,10},{10,1... | collective-permute-start | bytes 196616 | tf_op jit(solution)/shard_map/ppermute | solution.py:341
  93.6 6.8 %collective-permute-start.1 = (f32[1024,16]{0,1:T(8,128)S(1)}, f32[1024,16]{0,1:T(8,128)S(1)}, u32[]{:S(2)}, u32[]{:S(2)}) collective-permute-start(f32[1024,16]{0,1:T(8,128)S(1)} %select_reduce_fusion), channel_id=1, source_target_pairs={{0,2},{1,3},{2,0},{3,1},{4,6},{5,7},{6,4},{7,5},{8,10},{9,11},{10,... | collective-permute-start | bytes 196616 | tf_op jit(solution)/shard_map/ppermute | solution.py:341
  96.5 4.9 %collective-permute-start.2 = (f32[1024,16]{0,1:T(8,128)S(1)}, f32[1024,16]{0,1:T(8,128)S(1)}, u32[]{:S(2)}, u32[]{:S(2)}) collective-permute-start(f32[1024,16]{0,1:T(8,128)S(1)} %select_reduce_fusion), channel_id=1, source_target_pairs={{0,3},{1,0},{2,1},{3,2},{4,7},{5,4},{6,5},{7,6},{8,11},{9,8},{10,9... | collective-permute-start | bytes 196616 | tf_op jit(solution)/shard_map/ppermute | solution.py:341
  97.9 3.6 %copy-start.20 = (f32[1024,512]{1,0:T(8,128)S(1)}, f32[1024,512]{1,0:T(8,128)}, u32[]{:S(2)}) copy-start(f32[1024,512]{1,0:T(8,128)} %fusion.33) | copy-start | bytes 6291460
  101.4 3.0 %copy-start.1 = (f32[8,128,384]{2,1,0:T(8,128)S(1)}, f32[8,128,384]{2,1,0:T(8,128)}, u32[]{:S(2)}) copy-start(f32[8,128,384]{2,1,0:T(8,128)} %add_select_fusion.bias_ref) | copy-start | bytes 4718596

commit v14 on v13

--- a/solution.py
+++ b/solution.py
@@ -55,7 +55,8 @@
     return (request_hot, starts, rows, token_positions, row_ids)
 
 
-BLOCK = 128
+BLOCK = 64
+PROMPT_ROWS = 128
 
 
 def attend_kernel(
@@ -381,7 +382,7 @@
     k_pad = jnp.concatenate([front, key_flat], 0)
     v_pad = jnp.concatenate([front, value_flat], 0)
     clamp_start = jnp.clip(prompt_start, 0, tok_rows - LMAX)
-    extra = BLOCK - group_count * LMAX
+    extra = PROMPT_ROWS - group_count * LMAX
     k_prompt = jnp.concatenate(
         [lax.dynamic_slice_in_dim(key_flat, clamp_start[g], LMAX, 0) for g in range(group_count)]
         + [jnp.zeros((extra, kv_width), jnp.bfloat16)],

time: 150 us -> 162 us (1.080)
  Pallas kernels: 63.6 us -> 74.4 us
    pallas_call x1, Pallas kernels: 44 us -> 54.9 us  [attend_and_reduce(): pl.pallas_call(kernel, out_shape=jax.ShapeDtypeStruct((rows, piece), jnp....]
    unnamed x46 -> x40, local copies, waits for them, and re-layouts: 5.75 us -> 5.4 us
  transfers between devices with their start and end apart: 4 -> 4, of which waited for: 3 -> 3; matrix products, arithmetic and copies ran while one was open for 22% -> 20% of each run, Pallas kernels for 0% -> 0%
where the time goes in v14:
time: 162 us; the launch traced here: 160 us
  Pallas kernels  74.4 us (46%)
  local copies, waits for them, and re-layouts  18.2 us (11%)
  other arithmetic  17.9 us (11%)
  starting transfers between devices  15.6 us (10%)
  matrix products  14.7 us (9%)
  waiting for transfers between devices  13.3 us (8%)
  between operations  6.24 us (4%)
    pallas_call x1, Pallas kernels, attend_and_reduce(): pl.pallas_call(kernel, out_shape=jax.ShapeDtypeStruct((rows, piece), jnp....  54.9 us
    pallas_call x1, Pallas kernels, exchange_ids(): pl.pallas_call(ids_kernel, out_shape=jax.ShapeDtypeStruct((count, 8, 128)...  19.6 us
    all_to_all x1, waiting for transfers between devices, per_device(): lax.all_to_all(maps_out, 'req', split_axis=0, concat_axis=0, tiled=True)  9.95 us
    all_to_all x1, starting transfers between devices, per_device(): lax.all_to_all(maps_out, 'req', split_axis=0, concat_axis=0, tiled=True)  9.68 us
    ppermute x3, starting transfers between devices, per_device(): lax.ppermute(partial_rank, 'tp', [(i, (i + k) % tp_count) for i in range(...  5.9 us
    unnamed x40, local copies, waits for them, and re-layouts  5.4 us
    dot_general x1, matrix products, per_device(): jnp.dot(normalized_input, value_matrix, preferred_element_type=jnp.float32)  3.74 us
    dot_general x1, matrix products, per_device(): jnp.dot(normalized_input, query_matrix, preferred_element_type=jnp.float32)  3.72 us
  transfers between devices with their start and end apart: 4, of which 3 were waited for; matrix products, arithmetic and copies ran while one was open for 20% of the time, Pallas kernels for 0%

profile of v14, /device:TPU:2, one launch (start us, length us, event | category | flops | bytes accessed | tf_op | source)
XLA Modules:
  0.0 160.4 jit_solution(189203915713706313)
XLA Ops:
  0.0 0.8 fusion.19
  0.8 1.4 gather_fusion
  2.2 0.1 select_reduce_fusion.6
  2.3 0.8 broadcast_in_dim.37.wanted_ref
  3.2 19.6 %shard_map.118 = s32[64,8,128]{2,1,0:T(8,128)} custom-call(s32[64,8,128]{2,1,0:T(8,128)} %broadcast_in_dim.37.wanted_ref), custom_call_target="tpu_custom_call" | custom-call | tf_op jit(solution)/shard_map/pallas_call | solution.py:272
  22.8 2.2 %slice_reduce_fusion = s32[64]{0:T(128)S(1)} fusion(s32[64,8,128]{2,1,0:T(8,128)} %shard_map.118), kind=kLoop, calls=%fused_computation.45 | loop fusion | bytes 512 | tf_op jit(solution)/shard_map/slice | solution.py:284
  25.0 1.1 pad_maximum_fusion
  26.1 2.0 %gather_fusion.1 = bf16[64,32,512]{2,1,0:T(8,128)(2,1)} fusion(bf16[16,32,512]{2,1,0:T(8,128)(2,1)S(1)} %pad_maximum_fusion, s32[1024]{0:T(1024)S(1)} %pad_clamp_fusion), kind=kCustom, calls=%fused_computation.1 | custom fusion | bytes 4194560 | tf_op jit(solution)/shard_map/gather | solution.py:321
  28.1 9.7 %all-to-all-start = ((bf16[64,32,512]{2,1,0:T(8,128)(2,1)}), bf16[64,32,512]{2,1,0:T(8,128)(2,1)}, u32[]{:S(2)}, u32[]{:S(2)}) async-start(bf16[64,32,512]{2,1,0:T(8,128)(2,1)} %gather_fusion.1), calls=%async_computation | async-start | bytes 4194304 | tf_op jit(solution)/shard_map/all_to_all | solution.py:329
  37.8 0.1 copy.25
  38.0 0.1 reduce.1
  38.2 0.1 convert_reduce_fusion
  38.3 0.2 select_reduce_fusion.5
  38.5 0.1 select_reduce_fusion.7
  38.6 0.7 fusion.29
  43.3 0.1 select_reduce_fusion.1
  43.4 3.2 %fusion = f32[1024]{0:T(1024)S(1)} fusion(bf16[1024,2048]{1,0:T(8,128)(2,1)} %param.12), kind=kLoop, calls=%fused_computation.4 | loop fusion | flops 6290432 | bytes 4198400 | tf_op jit(solution)/shard_map/reduce_sum | solution.py:326
  46.7 1.0 fusion.2
  47.7 0.2 copy-done.16
  47.9 1.3 fusion.31
  49.3 0.6 copy-done.4
  49.9 1.3 copy.32
  51.3 1.3 copy.33
  52.5 2.9 %fusion.17 = (f32[1024,64]{1,0:T(8,128)}, f32[1024,64]{1,0:T(8,128)S(1)}, f32[1024,64]{1,0:T(8,128)S(1)}) fusion(f32[64]{0:T(128)S(1)} %negate_power_fusion, f32[1024]{0:T(1024)S(1)} %add_convert_fusion.2), kind=kLoop, calls=%fused_computation.34 | loop fusion | flops 131072 | bytes 790784 | tf_op jit(solution)/shard_map/neg | solution.py:365
  55.5 2.3 %subtract_convert_fusion = (bf16[1024,2,64]{2,1,0:T(2,128)(2,1)S(1)}, bf16[1024,2,64]{2,1,0:T(2,128)(2,1)S(1)}) fusion(f32[1024,2,64]{2,1,0:T(2,128)} %copy.33, f32[1024,2,64]{2,1,0:T(2,128)} %copy.32, f32[1024,64]{1,0:T(8,128)S(1)} %get-tuple-element.32, f32[1024,64]{1,0:T(8,128)S(1)} %get-tuple-element.33), kind=kLoop, calls=%fused_computation.19 | loop fusion | flops 1048576 | bytes 2097152 | tf_op jit(solution)/shard_map/convert
  57.8 1.4 pad_maximum_fusion.3
  59.2 0.9 copy.40
  60.7 0.1 reshape.377
  63.6 0.8 constant_dynamic-slice_fusion.6
  64.4 3.7 %convolution_convert_fusion = bf16[1024,256]{1,0:T(8,128)(2,1)S(1)} fusion(bf16[1024,2048]{1,0:T(8,128)(2,1)} %copy-done.4, bf16[2048,256]{1,0:T(8,128)(2,1)} %param.16), kind=kOutput, calls=%fused_computation.14 | convolution fusion | flops 1074003968 | bytes 5767168 | tf_op jit(solution)/shard_map/dot_general | solution.py:371
  68.2 1.3 pad_maximum_fusion.1
  69.5 1.7 %constant_dynamic-slice_fusion.res_ref = bf16[1024,512]{1,0:T(8,128)(2,1)S(1)} fusion(bf16[1024,2048]{1,0:T(8,128)(2,1)} %param.12, s32[]{:T(128)S(6)} %select_n.72), kind=kLoop, calls=%fused_computation.69 | loop fusion | bytes 2097156 | tf_op jit(solution)/shard_map/dynamic_slice | solution.py:433
  71.4 0.7 iota_compare_fusion
  72.0 0.1 maximum_maximum_fusion.1
  72.1 1.5 or_and_fusion
  73.6 3.7 %fusion.30 = f32[1024,512]{1,0:T(8,128)} fusion(bf16[1024,2048]{1,0:T(8,128)(2,1)S(1)} %copy-done.5, bf16[2048,512]{1,0:T(8,128)(2,1)S(1)} %copy-done), kind=kOutput, calls=%fused_computation.105 | convolution fusion | flops 2147483648 | bytes 8388608 | tf_op jit(solution)/shard_map/dot_general | solution.py:356
  77.3 10.0 %all-to-all-done = bf16[64,32,512]{2,1,0:T(8,128)(2,1)} async-done(((bf16[64,32,512]{2,1,0:T(8,128)(2,1)}), bf16[64,32,512]{2,1,0:T(8,128)(2,1)}, u32[]{:S(2)}, u32[]{:S(2)}) %all-to-all-start) | async-done | bytes 2097184 | tf_op jit(solution)/shard_map/all_to_all | solution.py:329
  87.3 1.8 %fusion.26 = (bf16[64,16,512]{2,1,0:T(8,128)(2,1)S(1)}, bf16[64,16,512]{2,1,0:T(8,128)(2,1)S(1)}) fusion(bf16[64,32,512]{2,1,0:T(8,128)(2,1)} %all-to-all-done), kind=kLoop, calls=%fused_computation.101 | loop fusion | bytes 4194304 | tf_op jit(solution)/shard_map/slice | solution.py:330
  89.1 3.0 %select_reduce_fusion = f32[1024,16]{0,1:T(8,128)S(1)} fusion(pred[1024,64]{0,1:T(8,128)(4,1)S(1)} %copy-done.10, bf16[64,16,512]{2,1,0:T(8,128)(2,1)S(1)} %get-tuple-element.19, bf16[1024,2048]{1,0:T(8,128)(2,1)} %copy-done.4, s32[]{:T(128)S(6)} %select_n.72), kind=kOutput, calls=%fused_computation.7 | convolution fusion | flops 1075822592 | bytes 2228228 | tf_op jit(solution)/shard_map/dot_general | solution.py:337
  92.0 1.7 %collective-permute-start = (f32[1024,16]{0,1:T(8,128)S(1)}, f32[1024,16]{0,1:T(8,128)S(1)}, u32[]{:S(2)}, u32[]{:S(2)}) collective-permute-start(f32[1024,16]{0,1:T(8,128)S(1)} %select_reduce_fusion), channel_id=1, source_target_pairs={{0,1},{1,2},{2,3},{3,0},{4,5},{5,6},{6,7},{7,4},{8,9},{9,10},{10,1... | collective-permute-start | bytes 196616 | tf_op jit(solution)/shard_map/ppermute | solution.py:342
  93.7 2.9 %collective-permute-start.1 = (f32[1024,16]{0,1:T(8,128)S(1)}, f32[1024,16]{0,1:T(8,128)S(1)}, u32[]{:S(2)}, u32[]{:S(2)}) collective-permute-start(f32[1024,16]{0,1:T(8,128)S(1)} %select_reduce_fusion), channel_id=1, source_target_pairs={{0,2},{1,3},{2,0},{3,1},{4,6},{5,7},{6,4},{7,5},{8,10},{9,11},{10,... | collective-permute-start | bytes 196616 | tf_op jit(solution)/shard_map/ppermute | solution.py:342
  96.6 1.3 collective-permute-start.2
  97.9 0.1 add_select_fusion.bias_ref
  98.2 2.3 %collective-permute-done.1 = f32[1024,16]{0,1:T(8,128)S(1)} collective-permute-done((f32[1024,16]{0,1:T(8,128)S(1)}, f32[1024,16]{0,1:T(8,128)S(1)}, u32[]{:S(2)}, u32[]{:S(2)}) %collective-permute-start.1) | collective-permute-done | bytes 65568 | tf_op jit(solution)/shard_map/ppermute | solution.py:342
  100.5 1.0 collective-permute-done.2
  101.6 3.0 %convert_add_fusion.q_ref = f32[1024,512]{1,0:T(8,128)} fusion(f32[1024,512]{1,0:T(8,128)S(1)} %copy-done.17, pred[1024,64]{0,1:T(8,128)(4,1)S(1)} %copy-done.10, bf16[64,16,512]{2,1,0:T(8,128)(2,1)S(1)} %get-tuple-element.20, bf16[1024,16]{0,1:T(8,128)(2,1)S(1)} %add_convert_fusion.1), kind=kOutput, calls=%fused_computation.10 | convolution fusion | flops 1076887552 | bytes 5341184 | tf_op jit(solution)/shard_map/dot_general | solution.py:352
  104.6 54.9 %shard_map.119 = bf16[1024,512]{1,0:T(8,128)(2,1)S(1)} custom-call(f32[1024,512]{1,0:T(8,128)} %convert_add_fusion.q_ref, f32[1024,128]{1,0:T(8,128)S(1)} %copy-done.1, f32[1024,128]{1,0:T(8,128)S(1)} %copy-done.2, bf16[1088,256]{1,0:T(8,128)(2,1)S(1)} %concatenate.86.k_ref, bf16[1088,256]{1,0:T(8,128)(2,1)S(1)} %concatenate.87.v_ref, ...), custom_call_target="tpu_custom_call" | custom-call | tf_op jit(solution)/shard_map/pallas_call | solution.py:194
  159.4 1.0 copy.42
  (80 shorter events, 2.1 us)
Async XLA Ops:
  0.0 73.6 %copy-start = (bf16[2048,512]{1,0:T(8,128)(2,1)S(1)}, bf16[2048,512]{1,0:T(8,128)(2,1)}, u32[]{:S(2)}) copy-start(bf16[2048,512]{1,0:T(8,128)(2,1)} %param.14) | copy-start | bytes 6291460
  26.1 11.7 %copy-start.14 = (s32[1,32]{1,0:T(1,128)S(1)}, s32[1,32]{1,0:T(1,128)}, u32[]{:S(2)}) copy-start(s32[1,32]{1,0:T(1,128)} %param.20) | copy-start | bytes 388
  26.1 12.0 %copy-start.12 = (s32[1,32]{1,0:T(1,128)S(1)}, s32[1,32]{1,0:T(1,128)}, u32[]{:S(2)}) copy-start(s32[1,32]{1,0:T(1,128)} %param.21) | copy-start | bytes 388
  28.1 18.5 %copy-start.13 = (f32[2048]{0:T(1024)S(1)}, f32[2048]{0:T(1024)}, u32[]{:S(2)}) copy-start(f32[2048]{0:T(1024)} %param.13) | copy-start | bytes 24580
  28.1 59.1 %all-to-all-start = ((bf16[64,32,512]{2,1,0:T(8,128)(2,1)}), bf16[64,32,512]{2,1,0:T(8,128)(2,1)}, u32[]{:S(2)}, u32[]{:S(2)}) async-start(bf16[64,32,512]{2,1,0:T(8,128)(2,1)} %gather_fusion.1), calls=%async_computation | async-start | bytes 4194304 | tf_op jit(solution)/shard_map/all_to_all | solution.py:329
  43.3 3.4 %copy-start.3 = (bf16[1024,2048]{1,0:T(8,128)(2,1)S(1)}, bf16[1024,2048]{1,0:T(8,128)(2,1)}, u32[]{:S(2)}) copy-start(bf16[1024,2048]{1,0:T(8,128)(2,1)} %param.12) | copy-start | bytes 12582916
  46.7 1.2 copy-start.16
  47.9 1.9 %copy-start.4 = (bf16[1024,2048]{1,0:T(8,128)(2,1)}, bf16[1024,2048]{1,0:T(8,128)(2,1)S(1)}, u32[]{:S(2)}) copy-start(bf16[1024,2048]{1,0:T(8,128)(2,1)S(1)} %fusion.2) | copy-start | bytes 12582916
  52.5 10.8 %copy-start.11 = (s32[16,64]{1,0:T(8,128)S(1)}, s32[16,64]{1,0:T(8,128)}, u32[]{:S(2)}) copy-start(s32[16,64]{1,0:T(8,128)} %constant.102.clone.1) | copy-start | bytes 12292
  61.0 10.3 %copy-start.15 = (s32[128]{0:T(128)}, s32[128]{0:T(128)S(1)}, u32[]{:S(2)}) copy-start(s32[128]{0:T(128)S(1)} %concatenate.100) | copy-start | bytes 1540
  63.2 5.0 %copy-start.7 = (f32[1024,64]{1,0:T(8,128)S(1)}, f32[1024,64]{1,0:T(8,128)}, u32[]{:S(2)}) copy-start(f32[1024,64]{1,0:T(8,128)} %get-tuple-element.31) | copy-start | bytes 786436
  68.1 3.9 %copy-start.8 = (bf16[1024,256]{1,0:T(8,128)(2,1)}, bf16[1024,256]{1,0:T(8,128)(2,1)S(1)}, u32[]{:S(2)}) copy-start(bf16[1024,256]{1,0:T(8,128)(2,1)S(1)} %convolution_convert_fusion) | copy-start | bytes 1572868
  68.1 5.4 %copy-start.5 = (bf16[1024,2048]{1,0:T(8,128)(2,1)S(1)}, bf16[1024,2048]{1,0:T(8,128)(2,1)}, u32[]{:S(2)}) copy-start(bf16[1024,2048]{1,0:T(8,128)(2,1)} %copy-done.4) | copy-start | bytes 12582916
  87.3 1.8 %copy-start.10 = (pred[1024,64]{0,1:T(8,128)(4,1)S(1)}, pred[1024,64]{0,1:T(8,128)(4,1)}, u32[]{:S(2)}) copy-start(pred[1024,64]{0,1:T(8,128)(4,1)} %iota_compare_fusion) | copy-start | bytes 196612
  89.0 9.0 %copy-start.6 = (bf16[128,8,2,128]{3,1,2,0:T(8,128)(2,1)S(1)}, bf16[128,8,2,128]{3,1,2,0:T(8,128)(2,1)}, u32[]{:S(2)}) copy-start(bf16[128,8,2,128]{3,1,2,0:T(8,128)(2,1)} %copy.40) | copy-start | bytes 1572868
  89.0 9.1 %copy-start.9 = (bf16[1024,256]{1,0:T(8,128)(2,1)S(1)}, bf16[1024,256]{1,0:T(8,128)(2,1)}, u32[]{:S(2)}) copy-start(bf16[1024,256]{1,0:T(8,128)(2,1)} %copy-done.8) | copy-start | bytes 1572868
  89.1 12.5 %copy-start.17 = (f32[1024,512]{1,0:T(8,128)S(1)}, f32[1024,512]{1,0:T(8,128)}, u32[]{:S(2)}) copy-start(f32[1024,512]{1,0:T(8,128)} %fusion.30) | copy-start | bytes 6291460
  92.0 6.2 %collective-permute-start = (f32[1024,16]{0,1:T(8,128)S(1)}, f32[1024,16]{0,1:T(8,128)S(1)}, u32[]{:S(2)}, u32[]{:S(2)}) collective-permute-start(f32[1024,16]{0,1:T(8,128)S(1)} %select_reduce_fusion), channel_id=1, source_target_pairs={{0,1},{1,2},{2,3},{3,0},{4,5},{5,6},{6,7},{7,4},{8,9},{9,10},{10,1... | collective-permute-start | bytes 196616 | tf_op jit(solution)/shard_map/ppermute | solution.py:342
  93.7 6.8 %collective-permute-start.1 = (f32[1024,16]{0,1:T(8,128)S(1)}, f32[1024,16]{0,1:T(8,128)S(1)}, u32[]{:S(2)}, u32[]{:S(2)}) collective-permute-start(f32[1024,16]{0,1:T(8,128)S(1)} %select_reduce_fusion), channel_id=1, source_target_pairs={{0,2},{1,3},{2,0},{3,1},{4,6},{5,7},{6,4},{7,5},{8,10},{9,11},{10,... | collective-permute-start | bytes 196616 | tf_op jit(solution)/shard_map/ppermute | solution.py:342
  96.6 4.9 %collective-permute-start.2 = (f32[1024,16]{0,1:T(8,128)S(1)}, f32[1024,16]{0,1:T(8,128)S(1)}, u32[]{:S(2)}, u32[]{:S(2)}) collective-permute-start(f32[1024,16]{0,1:T(8,128)S(1)} %select_reduce_fusion), channel_id=1, source_target_pairs={{0,3},{1,0},{2,1},{3,2},{4,7},{5,4},{6,5},{7,6},{8,11},{9,8},{10,9... | collective-permute-start | bytes 196616 | tf_op jit(solution)/shard_map/ppermute | solution.py:342
  101.5 3.0 %copy-start.1 = (f32[1024,128]{1,0:T(8,128)S(1)}, f32[1024,128]{1,0:T(8,128)}, u32[]{:S(2)}) copy-start(f32[1024,128]{1,0:T(8,128)} %get-tuple-element.47.cs_ref) | copy-start | bytes 1572868
  101.5 3.0 %copy-start.2 = (f32[1024,128]{1,0:T(8,128)S(1)}, f32[1024,128]{1,0:T(8,128)}, u32[]{:S(2)}) copy-start(f32[1024,128]{1,0:T(8,128)} %get-tuple-element.48.sn_ref) | copy-start | bytes 1572868

commit v15 on v14

--- a/solution.py
+++ b/solution.py
@@ -55,7 +55,7 @@
     return (request_hot, starts, rows, token_positions, row_ids)
 
 
-BLOCK = 64
+BLOCK = 256
 PROMPT_ROWS = 128
 
 

time: 162 us -> 150 us (0.926)
  Pallas kernels: 74.4 us -> 63.8 us
    pallas_call x1, Pallas kernels: 54.9 us -> 44.2 us  [attend_and_reduce(): pl.pallas_call(kernel, out_shape=jax.ShapeDtypeStruct((rows, piece), jnp....]
    select_n x1, other arithmetic: 0.13 us -> 1.81 us  [per_device(): bias = jnp.where(vis, jnp.float32(0.0), jnp.float32(-1e+30))]
    unnamed x40 -> x42, local copies, waits for them, and re-layouts: 5.4 us -> 5.59 us
  transfers between devices with their start and end apart: 4 -> 4, of which waited for: 3 -> 3; matrix products, arithmetic and copies ran while one was open for 20% -> 22% of each run, Pallas kernels for 0% -> 0%
where the time goes in v15:
time: 150 us
  Pallas kernels  63.8 us (43%)
  other arithmetic  18.1 us (12%)
  local copies, waits for them, and re-layouts  17.8 us (12%)
  starting transfers between devices  15.6 us (10%)
  matrix products  14.6 us (10%)
  waiting for transfers between devices  13.6 us (9%)
  between operations  6.08 us (4%)
    pallas_call x1, Pallas kernels, attend_and_reduce(): pl.pallas_call(kernel, out_shape=jax.ShapeDtypeStruct((rows, piece), jnp....  44.2 us
    pallas_call x1, Pallas kernels, exchange_ids(): pl.pallas_call(ids_kernel, out_shape=jax.ShapeDtypeStruct((count, 8, 128)...  19.6 us
    all_to_all x1, waiting for transfers between devices, per_device(): lax.all_to_all(maps_out, 'req', split_axis=0, concat_axis=0, tiled=True)  10.6 us
    all_to_all x1, starting transfers between devices, per_device(): lax.all_to_all(maps_out, 'req', split_axis=0, concat_axis=0, tiled=True)  9.68 us
    ppermute x3, starting transfers between devices, per_device(): lax.ppermute(partial_rank, 'tp', [(i, (i + k) % tp_count) for i in range(...  5.89 us
    unnamed x42, local copies, waits for them, and re-layouts  5.59 us
    dot_general x1, matrix products, per_device(): jnp.dot(normalized_input, value_matrix, preferred_element_type=jnp.float32)  3.73 us
    dot_general x1, matrix products, per_device(): jnp.dot(normalized_input, query_matrix, preferred_element_type=jnp.float32)  3.67 us
  transfers between devices with their start and end apart: 4, of which 3 were waited for; matrix products, arithmetic and copies ran while one was open for 22% of the time, Pallas kernels for 0%

profile of v15, /device:TPU:2, one launch (start us, length us, event | category | flops | bytes accessed | tf_op | source)
XLA Modules:
  0.0 149.6 jit_solution(6427832278776695978)
XLA Ops:
  0.0 0.8 fusion.19
  0.8 1.4 gather_fusion
  2.2 0.1 select_reduce_fusion.6
  2.3 0.8 broadcast_in_dim.37.wanted_ref
  3.2 19.6 %shard_map.118 = s32[64,8,128]{2,1,0:T(8,128)} custom-call(s32[64,8,128]{2,1,0:T(8,128)} %broadcast_in_dim.37.wanted_ref), custom_call_target="tpu_custom_call" | custom-call | tf_op jit(solution)/shard_map/pallas_call | solution.py:272
  22.8 2.2 %slice_reduce_fusion = s32[64]{0:T(128)S(1)} fusion(s32[64,8,128]{2,1,0:T(8,128)} %shard_map.118), kind=kLoop, calls=%fused_computation.45 | loop fusion | bytes 512 | tf_op jit(solution)/shard_map/slice | solution.py:284
  25.0 1.1 pad_maximum_fusion
  26.1 2.1 %gather_fusion.1 = bf16[64,32,512]{2,1,0:T(8,128)(2,1)} fusion(bf16[16,32,512]{2,1,0:T(8,128)(2,1)S(1)} %pad_maximum_fusion, s32[1024]{0:T(1024)S(1)} %pad_clamp_fusion), kind=kCustom, calls=%fused_computation.1 | custom fusion | bytes 4194560 | tf_op jit(solution)/shard_map/gather | solution.py:321
  28.1 9.7 %all-to-all-start = ((bf16[64,32,512]{2,1,0:T(8,128)(2,1)}), bf16[64,32,512]{2,1,0:T(8,128)(2,1)}, u32[]{:S(2)}, u32[]{:S(2)}) async-start(bf16[64,32,512]{2,1,0:T(8,128)(2,1)} %gather_fusion.1), calls=%async_computation | async-start | bytes 4194304 | tf_op jit(solution)/shard_map/all_to_all | solution.py:329
  37.8 0.1 copy.25
  38.0 0.1 reduce.1
  38.2 0.1 convert_reduce_fusion
  38.3 0.2 select_reduce_fusion.5
  38.5 0.1 select_reduce_fusion.7
  38.6 0.7 fusion.29
  43.1 0.1 select_reduce_fusion.1
  43.2 3.2 %fusion = f32[1024]{0:T(1024)S(1)} fusion(bf16[1024,2048]{1,0:T(8,128)(2,1)} %param.12), kind=kLoop, calls=%fused_computation.4 | loop fusion | flops 6290432 | bytes 4198400 | tf_op jit(solution)/shard_map/reduce_sum | solution.py:326
  46.5 1.0 fusion.2
  47.5 0.2 copy-done.17
  47.7 1.3 fusion.31
  49.0 0.6 copy-done.6
  49.6 1.0 fusion.27
  50.7 1.4 copy.32
  52.1 2.2 %copy.33 = f32[1024,2,64]{2,1,0:T(2,128)} copy(f32[1024,2,64]{0,2,1:T(8,128)} %get-tuple-element.21) | data formatting | bytes 1048576
  54.3 2.9 %fusion.17 = (f32[1024,64]{1,0:T(8,128)}, f32[1024,64]{1,0:T(8,128)S(1)}, f32[1024,64]{1,0:T(8,128)S(1)}) fusion(f32[64]{0:T(128)S(1)} %negate_power_fusion, f32[1024]{0:T(1024)S(1)} %add_convert_fusion.2), kind=kLoop, calls=%fused_computation.34 | loop fusion | flops 131072 | bytes 790784 | tf_op jit(solution)/shard_map/neg | solution.py:365
  57.3 2.6 %subtract_convert_fusion = (bf16[1024,2,64]{2,1,0:T(2,128)(2,1)S(1)}, bf16[1024,2,64]{2,1,0:T(2,128)(2,1)S(1)}) fusion(f32[1024,2,64]{2,1,0:T(2,128)} %copy.33, f32[1024,2,64]{2,1,0:T(2,128)S(1)} %copy.32, f32[1024,64]{1,0:T(8,128)S(1)} %get-tuple-element.30, f32[1024,64]{1,0:T(8,128)S(1)} %get-tuple-element.31), kind=kLoop, calls=%fused_computation.21 | loop fusion | flops 1048576 | bytes 2097152 | tf_op jit(solution)/shard_map/convert
  59.9 1.4 pad_maximum_fusion.3
  61.6 0.1 add.165
  61.7 0.1 reshape.382
  64.2 3.7 %convolution_convert_fusion = bf16[1024,256]{1,0:T(8,128)(2,1)S(1)} fusion(bf16[1024,2048]{1,0:T(8,128)(2,1)} %copy-done.6, bf16[2048,256]{1,0:T(8,128)(2,1)} %param.16), kind=kOutput, calls=%fused_computation.16 | convolution fusion | flops 1074003968 | bytes 5767168 | tf_op jit(solution)/shard_map/dot_general | solution.py:371
  68.0 1.5 constant_dynamic-slice_fusion.res_ref
  69.5 0.3 compare_and_fusion
  69.8 1.2 or_and_fusion
  71.1 1.8 %add_select_fusion.bias_ref = f32[4,256,640]{2,1,0:T(8,128)} fusion(pred[4,256,128]{2,1,0:T(8,128)(4,1)S(1)} %compare_and_fusion, pred[4,256,512]{2,1,0:T(8,128)(4,1)S(1)} %or_and_fusion), kind=kLoop, calls=%fused_computation.8 | loop fusion | flops 1310720 | bytes 3276800 | tf_op jit(solution)/shard_map/jit(_where)/select_n | solution.py:432
  72.9 0.1 maximum_maximum_fusion.1
  73.0 3.7 %fusion.30 = f32[1024,512]{1,0:T(8,128)} fusion(bf16[1024,2048]{1,0:T(8,128)(2,1)S(1)} %copy-done.7, bf16[2048,512]{1,0:T(8,128)(2,1)S(1)} %copy-done), kind=kOutput, calls=%fused_computation.105 | convolution fusion | flops 2147483648 | bytes 8388608 | tf_op jit(solution)/shard_map/dot_general | solution.py:356
  76.7 10.6 %all-to-all-done = bf16[64,32,512]{2,1,0:T(8,128)(2,1)} async-done(((bf16[64,32,512]{2,1,0:T(8,128)(2,1)}), bf16[64,32,512]{2,1,0:T(8,128)(2,1)}, u32[]{:S(2)}, u32[]{:S(2)}) %all-to-all-start) | async-done | bytes 2097184 | tf_op jit(solution)/shard_map/all_to_all | solution.py:329
  87.3 1.7 %fusion.26 = (bf16[64,16,512]{2,1,0:T(8,128)(2,1)S(1)}, bf16[64,16,512]{2,1,0:T(8,128)(2,1)S(1)}) fusion(bf16[64,32,512]{2,1,0:T(8,128)(2,1)} %all-to-all-done), kind=kLoop, calls=%fused_computation.101 | loop fusion | bytes 4194304 | tf_op jit(solution)/shard_map/slice | solution.py:330
  89.0 2.9 %select_reduce_fusion = f32[1024,16]{0,1:T(8,128)S(1)} fusion(pred[1024,64]{0,1:T(8,128)(4,1)S(1)} %iota_compare_fusion, bf16[64,16,512]{2,1,0:T(8,128)(2,1)S(1)} %get-tuple-element.19, bf16[1024,2048]{1,0:T(8,128)(2,1)} %copy-done.6, s32[]{:T(128)S(6)} %select_n.72), kind=kOutput, calls=%fused_computation.7 | convolution fusion | flops 1075822592 | bytes 2228228 | tf_op jit(solution)/shard_map/dot_general | solution.py:337
  92.0 1.6 %collective-permute-start = (f32[1024,16]{0,1:T(8,128)S(1)}, f32[1024,16]{0,1:T(8,128)S(1)}, u32[]{:S(2)}, u32[]{:S(2)}) collective-permute-start(f32[1024,16]{0,1:T(8,128)S(1)} %select_reduce_fusion), channel_id=1, source_target_pairs={{0,1},{1,2},{2,3},{3,0},{4,5},{5,6},{6,7},{7,4},{8,9},{9,10},{10,1... | collective-permute-start | bytes 196616 | tf_op jit(solution)/shard_map/ppermute | solution.py:342
  93.6 2.9 %collective-permute-start.1 = (f32[1024,16]{0,1:T(8,128)S(1)}, f32[1024,16]{0,1:T(8,128)S(1)}, u32[]{:S(2)}, u32[]{:S(2)}) collective-permute-start(f32[1024,16]{0,1:T(8,128)S(1)} %select_reduce_fusion), channel_id=1, source_target_pairs={{0,2},{1,3},{2,0},{3,1},{4,6},{5,7},{6,4},{7,5},{8,10},{9,11},{10,... | collective-permute-start | bytes 196616 | tf_op jit(solution)/shard_map/ppermute | solution.py:342
  96.5 1.3 collective-permute-start.2
  97.9 0.3 pad_maximum_fusion.1
  98.4 2.1 %collective-permute-done.1 = f32[1024,16]{0,1:T(8,128)S(1)} collective-permute-done((f32[1024,16]{0,1:T(8,128)S(1)}, f32[1024,16]{0,1:T(8,128)S(1)}, u32[]{:S(2)}, u32[]{:S(2)}) %collective-permute-start.1) | collective-permute-done | bytes 65568 | tf_op jit(solution)/shard_map/ppermute | solution.py:342
  100.5 1.0 collective-permute-done.2
  101.5 3.0 %convert_add_fusion.q_ref = f32[1024,512]{1,0:T(8,128)} fusion(f32[1024,512]{1,0:T(8,128)S(1)} %copy-done.18, pred[1024,64]{0,1:T(8,128)(4,1)S(1)} %iota_compare_fusion, bf16[64,16,512]{2,1,0:T(8,128)(2,1)S(1)} %get-tuple-element.20, bf16[1024,16]{0,1:T(8,128)(2,1)S(1)} %add_convert_fusion.1), kind=kOutput, calls=%fused_computation.11 | convolution fusion | flops 1076887552 | bytes 5341184 | tf_op jit(solution)/shard_map/dot_general | solution.py:352
  104.5 44.2 %shard_map.119 = bf16[1024,512]{1,0:T(8,128)(2,1)S(1)} custom-call(f32[1024,512]{1,0:T(8,128)} %convert_add_fusion.q_ref, f32[1024,128]{1,0:T(8,128)S(1)} %get-tuple-element.45.cs_ref, f32[1024,128]{1,0:T(8,128)S(1)} %get-tuple-element.46.sn_ref, bf16[1280,256]{1,0:T(8,128)(2,1)S(1)} %concatenate.98.k_ref, bf16[1280,256]{1,0:T(8,128)(2,1)S(1)} %concatenate.99.v_ref, ...), custom_call_target="tpu_custom_call" | custom-call | tf_op jit(solution)/shard_map/pallas_call | solution.py:194
  148.7 1.0 copy.42
  (83 shorter events, 1.3 us)
Async XLA Ops:
  0.0 73.0 %copy-start = (bf16[2048,512]{1,0:T(8,128)(2,1)S(1)}, bf16[2048,512]{1,0:T(8,128)(2,1)}, u32[]{:S(2)}) copy-start(bf16[2048,512]{1,0:T(8,128)(2,1)} %param.14) | copy-start | bytes 6291460
  28.1 9.7 %copy-start.16 = (s32[1,32]{1,0:T(1,128)S(1)}, s32[1,32]{1,0:T(1,128)}, u32[]{:S(2)}) copy-start(s32[1,32]{1,0:T(1,128)} %param.20) | copy-start | bytes 388
  28.1 10.0 %copy-start.13 = (s32[1,32]{1,0:T(1,128)S(1)}, s32[1,32]{1,0:T(1,128)}, u32[]{:S(2)}) copy-start(s32[1,32]{1,0:T(1,128)} %param.21) | copy-start | bytes 388
  28.1 59.1 %all-to-all-start = ((bf16[64,32,512]{2,1,0:T(8,128)(2,1)}), bf16[64,32,512]{2,1,0:T(8,128)(2,1)}, u32[]{:S(2)}, u32[]{:S(2)}) async-start(bf16[64,32,512]{2,1,0:T(8,128)(2,1)} %gather_fusion.1), calls=%async_computation | async-start | bytes 4194304 | tf_op jit(solution)/shard_map/all_to_all | solution.py:329
  37.8 8.6 %copy-start.15 = (f32[2048]{0:T(1024)S(1)}, f32[2048]{0:T(1024)}, u32[]{:S(2)}) copy-start(f32[2048]{0:T(1024)} %param.13) | copy-start | bytes 24580
  43.0 3.5 %copy-start.1 = (bf16[1024,2048]{1,0:T(8,128)(2,1)S(1)}, bf16[1024,2048]{1,0:T(8,128)(2,1)}, u32[]{:S(2)}) copy-start(bf16[1024,2048]{1,0:T(8,128)(2,1)} %param.12) | copy-start | bytes 12582916
  46.5 1.2 copy-start.17
  47.7 1.9 %copy-start.6 = (bf16[1024,2048]{1,0:T(8,128)(2,1)}, bf16[1024,2048]{1,0:T(8,128)(2,1)S(1)}, u32[]{:S(2)}) copy-start(bf16[1024,2048]{1,0:T(8,128)(2,1)S(1)} %fusion.2) | copy-start | bytes 12582916
  57.2 4.1 %copy-start.2 = (f32[1024,64]{1,0:T(8,128)}, f32[1024,64]{1,0:T(8,128)S(1)}, u32[]{:S(2)}) copy-start(f32[1024,64]{1,0:T(8,128)S(1)} %get-tuple-element.30) | copy-start | bytes 786436
  57.3 4.1 %copy-start.4 = (f32[1024,64]{1,0:T(8,128)}, f32[1024,64]{1,0:T(8,128)S(1)}, u32[]{:S(2)}) copy-start(f32[1024,64]{1,0:T(8,128)S(1)} %get-tuple-element.31) | copy-start | bytes 786436
  57.3 6.8 %copy-start.14 = (s32[4,256]{1,0:T(4,128)S(1)}, s32[4,256]{1,0:T(4,128)}, u32[]{:S(2)}) copy-start(s32[4,256]{1,0:T(4,128)} %constant.106.clone.1) | copy-start | bytes 12292
  61.4 6.5 %copy-start.8 = (bf16[128,8,2,128]{3,1,2,0:T(8,128)(2,1)}, bf16[128,8,2,128]{3,1,2,0:T(8,128)(2,1)S(1)}, u32[]{:S(2)}) copy-start(bf16[128,8,2,128]{3,1,2,0:T(8,128)(2,1)S(1)} %copy.40) | copy-start | bytes 1572868
  67.9 5.0 %copy-start.11 = (bf16[1024,256]{1,0:T(8,128)(2,1)}, bf16[1024,256]{1,0:T(8,128)(2,1)S(1)}, u32[]{:S(2)}) copy-start(bf16[1024,256]{1,0:T(8,128)(2,1)S(1)} %convolution_convert_fusion) | copy-start | bytes 1572868
  69.4 3.6 %copy-start.7 = (bf16[1024,2048]{1,0:T(8,128)(2,1)S(1)}, bf16[1024,2048]{1,0:T(8,128)(2,1)}, u32[]{:S(2)}) copy-start(bf16[1024,2048]{1,0:T(8,128)(2,1)} %copy-done.6) | copy-start | bytes 12582916
  89.0 8.9 %copy-start.3 = (f32[1024,64]{1,0:T(8,128)S(1)}, f32[1024,64]{1,0:T(8,128)}, u32[]{:S(2)}) copy-start(f32[1024,64]{1,0:T(8,128)} %copy-done.2) | copy-start | bytes 786436
  89.0 8.9 %copy-start.5 = (f32[1024,64]{1,0:T(8,128)S(1)}, f32[1024,64]{1,0:T(8,128)}, u32[]{:S(2)}) copy-start(f32[1024,64]{1,0:T(8,128)} %copy-done.4) | copy-start | bytes 786436
  89.0 8.9 %copy-start.10 = (f32[1024,64]{1,0:T(8,128)S(1)}, f32[1024,64]{1,0:T(8,128)}, u32[]{:S(2)}) copy-start(f32[1024,64]{1,0:T(8,128)} %get-tuple-element.29) | copy-start | bytes 786436
  92.0 6.3 %copy-start.9 = (bf16[128,8,2,128]{3,1,2,0:T(8,128)(2,1)S(1)}, bf16[128,8,2,128]{3,1,2,0:T(8,128)(2,1)}, u32[]{:S(2)}) copy-start(bf16[128,8,2,128]{3,1,2,0:T(8,128)(2,1)} %copy-done.8) | copy-start | bytes 1572868
  92.0 6.3 %copy-start.12 = (bf16[1024,256]{1,0:T(8,128)(2,1)S(1)}, bf16[1024,256]{1,0:T(8,128)(2,1)}, u32[]{:S(2)}) copy-start(bf16[1024,256]{1,0:T(8,128)(2,1)} %copy-done.11) | copy-start | bytes 1572868
  92.0 6.4 %collective-permute-start = (f32[1024,16]{0,1:T(8,128)S(1)}, f32[1024,16]{0,1:T(8,128)S(1)}, u32[]{:S(2)}, u32[]{:S(2)}) collective-permute-start(f32[1024,16]{0,1:T(8,128)S(1)} %select_reduce_fusion), channel_id=1, source_target_pairs={{0,1},{1,2},{2,3},{3,0},{4,5},{5,6},{6,7},{7,4},{8,9},{9,10},{10,1... | collective-permute-start | bytes 196616 | tf_op jit(solution)/shard_map/ppermute | solution.py:342
  93.6 6.8 %collective-permute-start.1 = (f32[1024,16]{0,1:T(8,128)S(1)}, f32[1024,16]{0,1:T(8,128)S(1)}, u32[]{:S(2)}, u32[]{:S(2)}) collective-permute-start(f32[1024,16]{0,1:T(8,128)S(1)} %select_reduce_fusion), channel_id=1, source_target_pairs={{0,2},{1,3},{2,0},{3,1},{4,6},{5,7},{6,4},{7,5},{8,10},{9,11},{10,... | collective-permute-start | bytes 196616 | tf_op jit(solution)/shard_map/ppermute | solution.py:342
  96.5 4.9 %collective-permute-start.2 = (f32[1024,16]{0,1:T(8,128)S(1)}, f32[1024,16]{0,1:T(8,128)S(1)}, u32[]{:S(2)}, u32[]{:S(2)}) collective-permute-start(f32[1024,16]{0,1:T(8,128)S(1)} %select_reduce_fusion), channel_id=1, source_target_pairs={{0,3},{1,0},{2,1},{3,2},{4,7},{5,4},{6,5},{7,6},{8,11},{9,8},{10,9... | collective-permute-start | bytes 196616 | tf_op jit(solution)/shard_map/ppermute | solution.py:342
  97.9 3.6 %copy-start.18 = (f32[1024,512]{1,0:T(8,128)S(1)}, f32[1024,512]{1,0:T(8,128)}, u32[]{:S(2)}) copy-start(f32[1024,512]{1,0:T(8,128)} %fusion.30) | copy-start | bytes 6291460

commit v16 on v13

--- a/solution.py
+++ b/solution.py
@@ -213,17 +213,6 @@
     me = lax.axis_index("req")
     col = lax.axis_index("tp")
     count = lax.axis_size("req")
-    barrier = pltpu.get_barrier_semaphore()
-
-    def greet(k, carry):
-        peer = lax.rem(me + k, count)
-        pl.semaphore_signal(
-            barrier, inc=1, device_id=(peer, col), device_id_type=pl.DeviceIdType.MESH
-        )
-        return carry
-
-    lax.fori_loop(1, count, greet, 0)
-    pl.semaphore_wait(barrier, count - 1)
 
     def copy_to(k):
         dest = lax.rem(me + k, count)
@@ -278,7 +267,7 @@
             pltpu.SemaphoreType.DMA((count,)),
             pltpu.SemaphoreType.DMA((count,)),
         ],
-        compiler_params=pltpu.CompilerParams(collective_id=1, has_side_effects=True),
+        compiler_params=pltpu.CompilerParams(has_side_effects=True),
     )(tiles)
     return got[:, 0, 0]
 

time: 150 us -> 155 us (1.033)
  Pallas kernels: 63.6 us -> 72.6 us
  starting transfers between devices: 15.6 us -> 12 us
    pallas_call x1, Pallas kernels: 19.6 us -> 28.6 us  [exchange_ids(): pl.pallas_call(ids_kernel, out_shape=jax.ShapeDtypeStruct((count, 8, 128)...]
    all_to_all x1, starting transfers between devices: 9.68 us -> 6.08 us  [per_device(): lax.all_to_all(maps_out, 'req', split_axis=0, concat_axis=0, tiled=True)]
  transfers between devices with their start and end apart: 4 -> 4, of which waited for: 3 -> 3; matrix products, arithmetic and copies ran while one was open for 22% -> 21% of each run, Pallas kernels for 0% -> 0%
where the time goes in v16:
time: 155 us
  Pallas kernels  72.6 us (47%)
  local copies, waits for them, and re-layouts  17.9 us (12%)
  other arithmetic  17.8 us (11%)
  matrix products  14.6 us (9%)
  waiting for transfers between devices  13.9 us (9%)
  starting transfers between devices  12 us (8%)
  between operations  6 us (4%)
    pallas_call x1, Pallas kernels, attend_and_reduce(): pl.pallas_call(kernel, out_shape=jax.ShapeDtypeStruct((rows, piece), jnp....  44 us
    pallas_call x1, Pallas kernels, exchange_ids(): pl.pallas_call(ids_kernel, out_shape=jax.ShapeDtypeStruct((count, 8, 128)...  28.6 us
    all_to_all x1, waiting for transfers between devices, per_device(): lax.all_to_all(maps_out, 'req', split_axis=0, concat_axis=0, tiled=True)  10.9 us
    all_to_all x1, starting transfers between devices, per_device(): lax.all_to_all(maps_out, 'req', split_axis=0, concat_axis=0, tiled=True)  6.08 us
    ppermute x3, starting transfers between devices, per_device(): lax.ppermute(partial_rank, 'tp', [(i, (i + k) % tp_count) for i in range(...  5.94 us
    unnamed x46, local copies, waits for them, and re-layouts  5.75 us
    dot_general x1, matrix products, per_device(): jnp.dot(normalized_input, value_matrix, preferred_element_type=jnp.float32)  3.73 us
    dot_general x1, matrix products, per_device(): jnp.dot(normalized_input, query_matrix, preferred_element_type=jnp.float32)  3.7 us
  transfers between devices with their start and end apart: 4, of which 3 were waited for; matrix products, arithmetic and copies ran while one was open for 21% of the time, Pallas kernels for 0%

profile of v16, /device:TPU:2, one launch (start us, length us, event | category | flops | bytes accessed | tf_op | source)
XLA Modules:
  0.0 154.8 jit_solution(1395841916515177231)
XLA Ops:
  0.0 0.8 fusion.22
  0.8 1.4 gather_fusion
  2.2 0.1 select_reduce_fusion.6
  2.3 0.8 broadcast_in_dim.37.wanted_ref
  3.2 28.6 %shard_map.118 = s32[64,8,128]{2,1,0:T(8,128)} custom-call(s32[64,8,128]{2,1,0:T(8,128)} %broadcast_in_dim.37.wanted_ref), custom_call_target="tpu_custom_call" | custom-call | tf_op jit(solution)/shard_map/pallas_call | solution.py:260
  31.8 2.2 %slice_reduce_fusion = s32[64]{0:T(128)S(1)} fusion(s32[64,8,128]{2,1,0:T(8,128)} %shard_map.118), kind=kLoop, calls=%fused_computation.45 | loop fusion | bytes 512 | tf_op jit(solution)/shard_map/slice | solution.py:272
  34.0 1.1 pad_maximum_fusion
  35.1 2.0 %gather_fusion.1 = bf16[64,32,512]{2,1,0:T(8,128)(2,1)} fusion(bf16[16,32,512]{2,1,0:T(8,128)(2,1)S(1)} %pad_maximum_fusion, s32[1024]{0:T(1024)S(1)} %pad_clamp_fusion), kind=kCustom, calls=%fused_computation.1 | custom fusion | bytes 4194560 | tf_op jit(solution)/shard_map/gather | solution.py:309
  37.1 6.1 %all-to-all-start = ((bf16[64,32,512]{2,1,0:T(8,128)(2,1)}), bf16[64,32,512]{2,1,0:T(8,128)(2,1)}, u32[]{:S(2)}, u32[]{:S(2)}) async-start(bf16[64,32,512]{2,1,0:T(8,128)(2,1)} %gather_fusion.1), calls=%async_computation | async-start | bytes 4194304 | tf_op jit(solution)/shard_map/all_to_all | solution.py:317
  43.2 0.1 copy.25
  43.3 0.1 reduce.1
  43.6 0.1 convert_reduce_fusion
  43.7 0.2 select_reduce_fusion.5
  43.9 0.1 select_reduce_fusion.1
  44.0 3.2 %fusion = f32[1024]{0:T(1024)S(1)} fusion(bf16[1024,2048]{1,0:T(8,128)(2,1)} %param.12), kind=kLoop, calls=%fused_computation.4 | loop fusion | flops 6290432 | bytes 4198400 | tf_op jit(solution)/shard_map/reduce_sum | solution.py:314
  47.3 0.2 copy-done.2
  47.5 1.0 fusion.2
  48.5 0.2 copy-done.19
  48.7 1.3 fusion.34
  50.0 0.6 copy-done.7
  50.6 1.0 fusion.30
  51.7 1.4 copy.32
  53.1 2.2 %copy.33 = f32[1024,2,64]{2,1,0:T(2,128)} copy(f32[1024,2,64]{0,2,1:T(8,128)} %get-tuple-element.21) | data formatting | bytes 1048576
  55.3 0.1 select_reduce_fusion.7
  55.4 3.0 %fusion.17 = (f32[1024,64]{1,0:T(8,128)}, f32[1024,64]{1,0:T(8,128)S(1)}, f32[1024,64]{1,0:T(8,128)S(1)}) fusion(f32[64]{0:T(128)S(1)} %negate_power_fusion, f32[1024]{0:T(1024)S(1)} %add_convert_fusion.2), kind=kLoop, calls=%fused_computation.34 | loop fusion | flops 131072 | bytes 790784 | tf_op jit(solution)/shard_map/neg | solution.py:353
  58.4 1.9 %subtract_convert_fusion = (bf16[1024,2,64]{2,1,0:T(2,128)(2,1)}, bf16[1024,2,64]{2,1,0:T(2,128)(2,1)}) fusion(f32[1024,2,64]{2,1,0:T(2,128)S(1)} %copy-done.9, f32[1024,2,64]{2,1,0:T(2,128)S(1)} %copy.32, f32[1024,64]{1,0:T(8,128)S(1)} %get-tuple-element.30, f32[1024,64]{1,0:T(8,128)S(1)} %get-tuple-element.31), kind=kLoop, calls=%fused_computation.20 | loop fusion | flops 1048576 | bytes 2097152 | tf_op jit(solution)/shard_map/convert
  60.4 0.6 fusion.32
  64.7 2.6 %pad_maximum_fusion.3 = bf16[1024,2,128]{2,1,0:T(2,128)(2,1)S(1)} fusion(bf16[1024,2,64]{2,1,0:T(2,128)(2,1)} %get-tuple-element.18, bf16[1024,2,64]{2,1,0:T(2,128)(2,1)} %get-tuple-element.17), kind=kLoop, calls=%fused_computation.31 | loop fusion | flops 1048576 | bytes 1048576 | tf_op jit(solution)/shard_map/concatenate | solution.py:23
  67.5 0.1 add.165
  70.0 3.7 %convolution_convert_fusion = bf16[1024,256]{1,0:T(8,128)(2,1)S(1)} fusion(bf16[1024,2048]{1,0:T(8,128)(2,1)} %copy-done.7, bf16[2048,256]{1,0:T(8,128)(2,1)} %param.16), kind=kOutput, calls=%fused_computation.15 | convolution fusion | flops 1074003968 | bytes 5767168 | tf_op jit(solution)/shard_map/dot_general | solution.py:359
  73.9 1.5 constant_dynamic-slice_fusion.res_ref
  75.4 0.3 compare_and_fusion
  75.8 0.8 or_and_fusion
  76.6 1.3 add_select_fusion.bias_ref
  78.0 0.1 maximum_maximum_fusion.1
  78.1 3.7 %fusion.33 = f32[1024,512]{1,0:T(8,128)} fusion(bf16[1024,2048]{1,0:T(8,128)(2,1)S(1)} %copy-done.8, bf16[2048,512]{1,0:T(8,128)(2,1)S(1)} %copy-done), kind=kOutput, calls=%fused_computation.108 | convolution fusion | flops 2147483648 | bytes 8388608 | tf_op jit(solution)/shard_map/dot_general | solution.py:344
  81.8 10.9 %all-to-all-done = bf16[64,32,512]{2,1,0:T(8,128)(2,1)} async-done(((bf16[64,32,512]{2,1,0:T(8,128)(2,1)}), bf16[64,32,512]{2,1,0:T(8,128)(2,1)}, u32[]{:S(2)}, u32[]{:S(2)}) %all-to-all-start) | async-done | bytes 2097184 | tf_op jit(solution)/shard_map/all_to_all | solution.py:317
  92.6 1.7 %fusion.29 = (bf16[64,16,512]{2,1,0:T(8,128)(2,1)S(1)}, bf16[64,16,512]{2,1,0:T(8,128)(2,1)S(1)}) fusion(bf16[64,32,512]{2,1,0:T(8,128)(2,1)} %all-to-all-done), kind=kLoop, calls=%fused_computation.104 | loop fusion | bytes 4194304 | tf_op jit(solution)/shard_map/slice | solution.py:318
  94.4 2.9 %select_reduce_fusion = f32[1024,16]{0,1:T(8,128)S(1)} fusion(pred[1024,64]{0,1:T(8,128)(4,1)S(1)} %iota_compare_fusion, bf16[64,16,512]{2,1,0:T(8,128)(2,1)S(1)} %get-tuple-element.19, bf16[1024,2048]{1,0:T(8,128)(2,1)} %copy-done.7, s32[]{:T(128)S(6)} %select_n.72), kind=kOutput, calls=%fused_computation.7 | convolution fusion | flops 1075822592 | bytes 2228228 | tf_op jit(solution)/shard_map/dot_general | solution.py:325
  97.4 1.8 %collective-permute-start = (f32[1024,16]{0,1:T(8,128)S(1)}, f32[1024,16]{0,1:T(8,128)S(1)}, u32[]{:S(2)}, u32[]{:S(2)}) collective-permute-start(f32[1024,16]{0,1:T(8,128)S(1)} %select_reduce_fusion), channel_id=1, source_target_pairs={{0,1},{1,2},{2,3},{3,0},{4,5},{5,6},{6,7},{7,4},{8,9},{9,10},{10,1... | collective-permute-start | bytes 196616 | tf_op jit(solution)/shard_map/ppermute | solution.py:330
  99.1 2.8 %collective-permute-start.1 = (f32[1024,16]{0,1:T(8,128)S(1)}, f32[1024,16]{0,1:T(8,128)S(1)}, u32[]{:S(2)}, u32[]{:S(2)}) collective-permute-start(f32[1024,16]{0,1:T(8,128)S(1)} %select_reduce_fusion), channel_id=1, source_target_pairs={{0,2},{1,3},{2,0},{3,1},{4,6},{5,7},{6,4},{7,5},{8,10},{9,11},{10,... | collective-permute-start | bytes 196616 | tf_op jit(solution)/shard_map/ppermute | solution.py:330
  101.9 1.4 collective-permute-start.2
  103.3 0.3 pad_maximum_fusion.1
  103.8 2.0 %collective-permute-done.1 = f32[1024,16]{0,1:T(8,128)S(1)} collective-permute-done((f32[1024,16]{0,1:T(8,128)S(1)}, f32[1024,16]{0,1:T(8,128)S(1)}, u32[]{:S(2)}, u32[]{:S(2)}) %collective-permute-start.1) | collective-permute-done | bytes 65568 | tf_op jit(solution)/shard_map/ppermute | solution.py:330
  105.8 1.0 collective-permute-done.2
  106.8 3.0 %convert_add_fusion.q_ref = f32[1024,512]{1,0:T(8,128)} fusion(f32[1024,512]{1,0:T(8,128)S(1)} %copy-done.20, pred[1024,64]{0,1:T(8,128)(4,1)S(1)} %iota_compare_fusion, bf16[64,16,512]{2,1,0:T(8,128)(2,1)S(1)} %get-tuple-element.20, bf16[1024,16]{0,1:T(8,128)(2,1)S(1)} %add_convert_fusion.1), kind=kOutput, calls=%fused_computation.10 | convolution fusion | flops 1076887552 | bytes 5341184 | tf_op jit(solution)/shard_map/dot_general | solution.py:340
  109.8 44.0 %shard_map.119 = bf16[1024,512]{1,0:T(8,128)(2,1)S(1)} custom-call(f32[1024,512]{1,0:T(8,128)} %convert_add_fusion.q_ref, f32[1024,128]{1,0:T(8,128)S(1)} %get-tuple-element.45.cs_ref, f32[1024,128]{1,0:T(8,128)S(1)} %get-tuple-element.46.sn_ref, bf16[1152,256]{1,0:T(8,128)(2,1)S(1)} %concatenate.98.k_ref, bf16[1152,256]{1,0:T(8,128)(2,1)S(1)} %concatenate.99.v_ref, ...), custom_call_target="tpu_custom_call" | custom-call | tf_op jit(solution)/shard_map/pallas_call | solution.py:193
  153.8 1.0 copy.42
  (81 shorter events, 1.3 us)
Async XLA Ops:
  0.0 78.1 %copy-start = (bf16[2048,512]{1,0:T(8,128)(2,1)S(1)}, bf16[2048,512]{1,0:T(8,128)(2,1)}, u32[]{:S(2)}) copy-start(bf16[2048,512]{1,0:T(8,128)(2,1)} %param.14) | copy-start | bytes 6291460
  37.1 6.1 %copy-start.18 = (s32[1,32]{1,0:T(1,128)S(1)}, s32[1,32]{1,0:T(1,128)}, u32[]{:S(2)}) copy-start(s32[1,32]{1,0:T(1,128)} %param.20) | copy-start | bytes 388
  37.1 6.4 %copy-start.15 = (s32[1,32]{1,0:T(1,128)S(1)}, s32[1,32]{1,0:T(1,128)}, u32[]{:S(2)}) copy-start(s32[1,32]{1,0:T(1,128)} %param.21) | copy-start | bytes 388
  37.1 55.5 %all-to-all-start = ((bf16[64,32,512]{2,1,0:T(8,128)(2,1)}), bf16[64,32,512]{2,1,0:T(8,128)(2,1)}, u32[]{:S(2)}, u32[]{:S(2)}) async-start(bf16[64,32,512]{2,1,0:T(8,128)(2,1)} %gather_fusion.1), calls=%async_computation | async-start | bytes 4194304 | tf_op jit(solution)/shard_map/all_to_all | solution.py:317
  44.0 3.5 %copy-start.2 = (bf16[1024,2048]{1,0:T(8,128)(2,1)S(1)}, bf16[1024,2048]{1,0:T(8,128)(2,1)}, u32[]{:S(2)}) copy-start(bf16[1024,2048]{1,0:T(8,128)(2,1)} %param.12) | copy-start | bytes 12582916
  44.0 3.4 %copy-start.17 = (f32[2048]{0:T(1024)S(1)}, f32[2048]{0:T(1024)}, u32[]{:S(2)}) copy-start(f32[2048]{0:T(1024)} %param.13) | copy-start | bytes 24580
  47.5 1.2 copy-start.19
  48.7 1.9 %copy-start.7 = (bf16[1024,2048]{1,0:T(8,128)(2,1)}, bf16[1024,2048]{1,0:T(8,128)(2,1)S(1)}, u32[]{:S(2)}) copy-start(bf16[1024,2048]{1,0:T(8,128)(2,1)S(1)} %fusion.2) | copy-start | bytes 12582916
  55.3 3.1 %copy-start.9 = (f32[1024,2,64]{2,1,0:T(2,128)S(1)}, f32[1024,2,64]{2,1,0:T(2,128)}, u32[]{:S(2)}) copy-start(f32[1024,2,64]{2,1,0:T(2,128)} %copy.33) | copy-start | bytes 1572868
  58.4 2.0 %copy-start.3 = (f32[1024,64]{1,0:T(8,128)}, f32[1024,64]{1,0:T(8,128)S(1)}, u32[]{:S(2)}) copy-start(f32[1024,64]{1,0:T(8,128)S(1)} %get-tuple-element.30) | copy-start | bytes 786436
  58.4 2.0 %copy-start.5 = (f32[1024,64]{1,0:T(8,128)}, f32[1024,64]{1,0:T(8,128)S(1)}, u32[]{:S(2)}) copy-start(f32[1024,64]{1,0:T(8,128)S(1)} %get-tuple-element.31) | copy-start | bytes 786436
  60.4 9.6 %copy-start.16 = (s32[8,128]{1,0:T(8,128)S(1)}, s32[8,128]{1,0:T(8,128)}, u32[]{:S(2)}) copy-start(s32[8,128]{1,0:T(8,128)} %constant.106.clone.1) | copy-start | bytes 12292
  67.4 6.4 %copy-start.10 = (bf16[128,8,2,128]{3,1,2,0:T(8,128)(2,1)}, bf16[128,8,2,128]{3,1,2,0:T(8,128)(2,1)S(1)}, u32[]{:S(2)}) copy-start(bf16[128,8,2,128]{3,1,2,0:T(8,128)(2,1)S(1)} %copy.40) | copy-start | bytes 1572868
  73.8 4.1 %copy-start.13 = (bf16[1024,256]{1,0:T(8,128)(2,1)}, bf16[1024,256]{1,0:T(8,128)(2,1)S(1)}, u32[]{:S(2)}) copy-start(bf16[1024,256]{1,0:T(8,128)(2,1)S(1)} %convolution_convert_fusion) | copy-start | bytes 1572868
  73.8 4.2 %copy-start.8 = (bf16[1024,2048]{1,0:T(8,128)(2,1)S(1)}, bf16[1024,2048]{1,0:T(8,128)(2,1)}, u32[]{:S(2)}) copy-start(bf16[1024,2048]{1,0:T(8,128)(2,1)} %copy-done.7) | copy-start | bytes 12582916
  94.4 8.9 %copy-start.4 = (f32[1024,64]{1,0:T(8,128)S(1)}, f32[1024,64]{1,0:T(8,128)}, u32[]{:S(2)}) copy-start(f32[1024,64]{1,0:T(8,128)} %copy-done.3) | copy-start | bytes 786436
  94.4 8.9 %copy-start.6 = (f32[1024,64]{1,0:T(8,128)S(1)}, f32[1024,64]{1,0:T(8,128)}, u32[]{:S(2)}) copy-start(f32[1024,64]{1,0:T(8,128)} %copy-done.5) | copy-start | bytes 786436
  94.4 8.9 %copy-start.12 = (f32[1024,64]{1,0:T(8,128)S(1)}, f32[1024,64]{1,0:T(8,128)}, u32[]{:S(2)}) copy-start(f32[1024,64]{1,0:T(8,128)} %get-tuple-element.29) | copy-start | bytes 786436
  97.3 6.3 %copy-start.11 = (bf16[128,8,2,128]{3,1,2,0:T(8,128)(2,1)S(1)}, bf16[128,8,2,128]{3,1,2,0:T(8,128)(2,1)}, u32[]{:S(2)}) copy-start(bf16[128,8,2,128]{3,1,2,0:T(8,128)(2,1)} %copy-done.10) | copy-start | bytes 1572868
  97.3 6.4 %copy-start.14 = (bf16[1024,256]{1,0:T(8,128)(2,1)S(1)}, bf16[1024,256]{1,0:T(8,128)(2,1)}, u32[]{:S(2)}) copy-start(bf16[1024,256]{1,0:T(8,128)(2,1)} %copy-done.13) | copy-start | bytes 1572868
  97.4 6.4 %collective-permute-start = (f32[1024,16]{0,1:T(8,128)S(1)}, f32[1024,16]{0,1:T(8,128)S(1)}, u32[]{:S(2)}, u32[]{:S(2)}) collective-permute-start(f32[1024,16]{0,1:T(8,128)S(1)} %select_reduce_fusion), channel_id=1, source_target_pairs={{0,1},{1,2},{2,3},{3,0},{4,5},{5,6},{6,7},{7,4},{8,9},{9,10},{10,1... | collective-permute-start | bytes 196616 | tf_op jit(solution)/shard_map/ppermute | solution.py:330
  99.1 6.7 %collective-permute-start.1 = (f32[1024,16]{0,1:T(8,128)S(1)}, f32[1024,16]{0,1:T(8,128)S(1)}, u32[]{:S(2)}, u32[]{:S(2)}) collective-permute-start(f32[1024,16]{0,1:T(8,128)S(1)} %select_reduce_fusion), channel_id=1, source_target_pairs={{0,2},{1,3},{2,0},{3,1},{4,6},{5,7},{6,4},{7,5},{8,10},{9,11},{10,... | collective-permute-start | bytes 196616 | tf_op jit(solution)/shard_map/ppermute | solution.py:330
  101.9 4.9 %collective-permute-start.2 = (f32[1024,16]{0,1:T(8,128)S(1)}, f32[1024,16]{0,1:T(8,128)S(1)}, u32[]{:S(2)}, u32[]{:S(2)}) collective-permute-start(f32[1024,16]{0,1:T(8,128)S(1)} %select_reduce_fusion), channel_id=1, source_target_pairs={{0,3},{1,0},{2,1},{3,2},{4,7},{5,4},{6,5},{7,6},{8,11},{9,8},{10,9... | collective-permute-start | bytes 196616 | tf_op jit(solution)/shard_map/ppermute | solution.py:330
  103.3 3.5 %copy-start.20 = (f32[1024,512]{1,0:T(8,128)S(1)}, f32[1024,512]{1,0:T(8,128)}, u32[]{:S(2)}) copy-start(f32[1024,512]{1,0:T(8,128)} %fusion.33) | copy-start | bytes 6291460
  106.8 3.0 %copy-start.1 = (f32[8,128,384]{2,1,0:T(8,128)S(1)}, f32[8,128,384]{2,1,0:T(8,128)}, u32[]{:S(2)}) copy-start(f32[8,128,384]{2,1,0:T(8,128)} %add_select_fusion.bias_ref) | copy-start | bytes 4718596

commit v17 on v13

--- a/solution.py
+++ b/solution.py
@@ -280,7 +280,7 @@
         ],
         compiler_params=pltpu.CompilerParams(collective_id=1, has_side_effects=True),
     )(tiles)
-    return got[:, 0, 0]
+    return got
 
 
 def per_device(
@@ -317,7 +317,15 @@
     wanted = jnp.sum(holder_hot * local_slot[None, :], 1)
     wanted_in = exchange_ids(wanted)
     table = jnp.concatenate([jnp.transpose(adapter_down_maps, (0, 2, 1)), adapter_up_maps], 1)
-    maps_out = table[wanted_in]
+    slot_hot = (
+        wanted_in[:, 0, :adapters_per_part]
+        == jnp.arange(adapters_per_part, dtype=jnp.int32)[None, :]
+    ).astype(table.dtype)
+    maps_out = (
+        jnp.dot(slot_hot, table.reshape(adapters_per_part, -1), preferred_element_type=jnp.float32)
+        .astype(table.dtype)
+        .reshape((req_count,) + table.shape[1:])
+    )
     tokens, maps_out = lax.optimization_barrier((tokens, maps_out))
     float_tok = tokens.astype(jnp.float32)
     normalized_input = (

time: 150 us -> 150 us (level)
  other arithmetic: 17.8 us -> 20 us
  waiting for transfers between devices: 13.9 us -> 12.1 us
    unnamed x46, local copies, waits for them, and re-layouts: 5.75 us -> 8.79 us
    slice x1 -> x0, local copies, waits for them, and re-layouts: 2.22 us -> none  [exchange_ids(): return got[:, 0, 0]]
    gather x1 -> x0, local copies, waits for them, and re-layouts: 2.02 us -> none  [per_device(): maps_out = table[wanted_in]]
    all_to_all x1, waiting for transfers between devices: 10.9 us -> 9.06 us  [per_device(): lax.all_to_all(maps_out, 'req', split_axis=0, concat_axis=0, tiled=True)]
where the time goes in v17:
time: 150 us; the launch traced here: 149 us
  Pallas kernels  63.5 us (42%)
  other arithmetic  20 us (13%)
  local copies, waits for them, and re-layouts  16.8 us (11%)
  starting transfers between devices  15.6 us (10%)
  matrix products  15.4 us (10%)
  waiting for transfers between devices  12.1 us (8%)
  between operations  5.95 us (4%)
    pallas_call x1, Pallas kernels, attend_and_reduce(): pl.pallas_call(kernel, out_shape=jax.ShapeDtypeStruct((rows, piece), jnp....  43.9 us
    pallas_call x1, Pallas kernels, exchange_ids(): pl.pallas_call(ids_kernel, out_shape=jax.ShapeDtypeStruct((count, 8, 128)...  19.6 us
    all_to_all x1, starting transfers between devices, per_device(): lax.all_to_all(maps_out, 'req', split_axis=0, concat_axis=0, tiled=True)  9.69 us
    all_to_all x1, waiting for transfers between devices, per_device(): lax.all_to_all(maps_out, 'req', split_axis=0, concat_axis=0, tiled=True)  9.06 us
    unnamed x46, local copies, waits for them, and re-layouts  8.79 us
    ppermute x3, starting transfers between devices, per_device(): lax.ppermute(partial_rank, 'tp', [(i, (i + k) % tp_count) for i in range(...  5.9 us
    dot_general x1, matrix products, per_device(): jnp.dot(normalized_input, value_matrix, preferred_element_type=jnp.float32)  3.74 us
    dot_general x1, matrix products, per_device(): jnp.dot(normalized_input, query_matrix, preferred_element_type=jnp.float32)  3.68 us
  transfers between devices with their start and end apart: 4, of which 3 were waited for; matrix products, arithmetic and copies ran while one was open for 22% of the time, Pallas kernels for 0%

profile of v17, /device:TPU:2, one launch (start us, length us, event | category | flops | bytes accessed | tf_op | source)
XLA Modules:
  0.0 149.4 jit_solution(697101665086742328)
XLA Ops:
  0.0 0.8 fusion.23
  0.8 1.4 gather_fusion
  2.2 0.1 select_reduce_fusion.6
  2.3 0.8 broadcast_in_dim.37.wanted_ref
  3.2 19.6 %shard_map.118 = s32[64,8,128]{2,1,0:T(8,128)} custom-call(s32[64,8,128]{2,1,0:T(8,128)} %broadcast_in_dim.37.wanted_ref), custom_call_target="tpu_custom_call" | custom-call | tf_op jit(solution)/shard_map/pallas_call | solution.py:271
  22.8 1.0 iota_compare_fusion.3
  23.7 0.1 copy.28
  23.8 1.1 pad_maximum_fusion
  24.9 0.3 copy.38
  25.2 0.8 convolution_convert_fusion
  26.0 2.1 %copy.39 = bf16[8,8,32,512]{3,2,1,0:T(8,128)(2,1)} copy(bf16[8,8,32,512]{3,1,2,0:T(8,128)(2,1)S(1)} %bitcast.71) | data formatting | bytes 4194304
  28.1 9.7 %all-to-all-start = ((bf16[64,32,512]{2,1,0:T(8,128)(2,1)}), bf16[64,32,512]{2,1,0:T(8,128)(2,1)}, u32[]{:S(2)}, u32[]{:S(2)}) async-start(bf16[64,32,512]{2,1,0:T(8,128)(2,1)} %bitcast.70), calls=%async_computation | async-start | bytes 4194304 | tf_op jit(solution)/shard_map/all_to_all | solution.py:336
  38.0 0.1 reduce
  38.2 0.1 convert_reduce_fusion
  38.3 0.2 select_reduce_fusion.5
  38.5 0.1 select_reduce_fusion.1
  38.6 3.3 %fusion = f32[1024]{0:T(1024)S(1)} fusion(bf16[1024,2048]{1,0:T(8,128)(2,1)} %param.12), kind=kLoop, calls=%fused_computation.4 | loop fusion | flops 6290432 | bytes 4198400 | tf_op jit(solution)/shard_map/reduce_sum | solution.py:333
  42.0 1.0 fusion.2
  43.1 0.2 copy-done.18
  43.2 1.3 fusion.34
  44.6 0.6 copy-done.7
  45.2 1.0 fusion.30
  46.2 1.4 copy.36
  47.7 2.2 %copy.37 = f32[1024,2,64]{2,1,0:T(2,128)} copy(f32[1024,2,64]{0,2,1:T(8,128)} %get-tuple-element.21) | data formatting | bytes 1048576
  49.8 0.1 select_reduce_fusion.7
  50.0 3.0 %fusion.17 = (f32[1024,64]{1,0:T(8,128)}, f32[1024,64]{1,0:T(8,128)S(1)}, f32[1024,64]{1,0:T(8,128)S(1)}) fusion(f32[64]{0:T(128)S(1)} %negate_power_fusion, f32[1024]{0:T(1024)S(1)} %add_convert_fusion.2), kind=kLoop, calls=%fused_computation.34 | loop fusion | flops 131072 | bytes 790784 | tf_op jit(solution)/shard_map/neg | solution.py:372
  53.0 0.8 copy-done.3
  53.8 3.0 %subtract_convert_fusion = (bf16[1024,2,64]{2,1,0:T(2,128)(2,1)}, bf16[1024,2,64]{2,1,0:T(2,128)(2,1)}) fusion(f32[1024,2,64]{2,1,0:T(2,128)} %copy.37, f32[1024,2,64]{2,1,0:T(2,128)S(1)} %copy.36, f32[1024,64]{1,0:T(8,128)S(1)} %get-tuple-element.30, f32[1024,64]{1,0:T(8,128)S(1)} %get-tuple-element.31), kind=kLoop, calls=%fused_computation.20 | loop fusion | flops 1048576 | bytes 2097152 | tf_op jit(solution)/shard_map/convert
  56.8 0.6 fusion.32
  61.0 2.6 %pad_maximum_fusion.3 = bf16[1024,2,128]{2,1,0:T(2,128)(2,1)S(1)} fusion(bf16[1024,2,64]{2,1,0:T(2,128)(2,1)} %get-tuple-element.18, bf16[1024,2,64]{2,1,0:T(2,128)(2,1)} %get-tuple-element.17), kind=kLoop, calls=%fused_computation.31 | loop fusion | flops 1048576 | bytes 1048576 | tf_op jit(solution)/shard_map/concatenate | solution.py:23
  66.4 3.7 %convolution_convert_fusion.1 = bf16[1024,256]{1,0:T(8,128)(2,1)S(1)} fusion(bf16[1024,2048]{1,0:T(8,128)(2,1)} %copy-done.7, bf16[2048,256]{1,0:T(8,128)(2,1)} %param.16), kind=kOutput, calls=%fused_computation.15 | convolution fusion | flops 1074003968 | bytes 5767168 | tf_op jit(solution)/shard_map/dot_general | solution.py:378
  70.2 1.5 %constant_dynamic-slice_fusion.res_ref = bf16[1024,512]{1,0:T(8,128)(2,1)S(1)} fusion(bf16[1024,2048]{1,0:T(8,128)(2,1)} %param.12, s32[]{:T(128)S(6)} %select_n.61), kind=kLoop, calls=%fused_computation.71 | loop fusion | bytes 2097156 | tf_op jit(solution)/shard_map/dynamic_slice | solution.py:440
  71.8 0.3 compare_and_fusion
  72.2 0.8 or_and_fusion
  73.0 1.3 add_select_fusion.bias_ref
  74.5 3.7 %fusion.33 = f32[1024,512]{1,0:T(8,128)} fusion(bf16[1024,2048]{1,0:T(8,128)(2,1)S(1)} %copy-done.8, bf16[2048,512]{1,0:T(8,128)(2,1)S(1)} %copy-done), kind=kOutput, calls=%fused_computation.106 | convolution fusion | flops 2147483648 | bytes 8388608 | tf_op jit(solution)/shard_map/dot_general | solution.py:363
  78.2 9.1 %all-to-all-done = bf16[64,32,512]{2,1,0:T(8,128)(2,1)} async-done(((bf16[64,32,512]{2,1,0:T(8,128)(2,1)}), bf16[64,32,512]{2,1,0:T(8,128)(2,1)}, u32[]{:S(2)}, u32[]{:S(2)}) %all-to-all-start) | async-done | bytes 2097184 | tf_op jit(solution)/shard_map/all_to_all | solution.py:336
  87.2 1.7 %fusion.29 = (bf16[64,16,512]{2,1,0:T(8,128)(2,1)S(1)}, bf16[64,16,512]{2,1,0:T(8,128)(2,1)S(1)}) fusion(bf16[64,32,512]{2,1,0:T(8,128)(2,1)} %all-to-all-done), kind=kLoop, calls=%fused_computation.102 | loop fusion | bytes 4194304 | tf_op jit(solution)/shard_map/slice | solution.py:337
  89.0 3.0 %select_reduce_fusion = f32[1024,16]{0,1:T(8,128)S(1)} fusion(pred[1024,64]{0,1:T(8,128)(4,1)S(1)} %iota_compare_fusion, bf16[64,16,512]{2,1,0:T(8,128)(2,1)S(1)} %get-tuple-element.19, bf16[1024,2048]{1,0:T(8,128)(2,1)} %copy-done.7, s32[]{:T(128)S(6)} %select_n.61), kind=kOutput, calls=%fused_computation.7 | convolution fusion | flops 1075822592 | bytes 2228228 | tf_op jit(solution)/shard_map/dot_general | solution.py:344
  92.0 1.7 %collective-permute-start = (f32[1024,16]{0,1:T(8,128)S(1)}, f32[1024,16]{0,1:T(8,128)S(1)}, u32[]{:S(2)}, u32[]{:S(2)}) collective-permute-start(f32[1024,16]{0,1:T(8,128)S(1)} %select_reduce_fusion), channel_id=1, source_target_pairs={{0,1},{1,2},{2,3},{3,0},{4,5},{5,6},{6,7},{7,4},{8,9},{9,10},{10,1... | collective-permute-start | bytes 196616 | tf_op jit(solution)/shard_map/ppermute | solution.py:349
  93.7 2.9 %collective-permute-start.1 = (f32[1024,16]{0,1:T(8,128)S(1)}, f32[1024,16]{0,1:T(8,128)S(1)}, u32[]{:S(2)}, u32[]{:S(2)}) collective-permute-start(f32[1024,16]{0,1:T(8,128)S(1)} %select_reduce_fusion), channel_id=1, source_target_pairs={{0,2},{1,3},{2,0},{3,1},{4,6},{5,7},{6,4},{7,5},{8,10},{9,11},{10,... | collective-permute-start | bytes 196616 | tf_op jit(solution)/shard_map/ppermute | solution.py:349
  96.6 1.3 collective-permute-start.2
  97.9 0.3 pad_maximum_fusion.1
  98.4 2.1 %collective-permute-done.1 = f32[1024,16]{0,1:T(8,128)S(1)} collective-permute-done((f32[1024,16]{0,1:T(8,128)S(1)}, f32[1024,16]{0,1:T(8,128)S(1)}, u32[]{:S(2)}, u32[]{:S(2)}) %collective-permute-start.1) | collective-permute-done | bytes 65568 | tf_op jit(solution)/shard_map/ppermute | solution.py:349
  100.5 1.0 collective-permute-done.2
  101.5 3.0 %convert_add_fusion.q_ref = f32[1024,512]{1,0:T(8,128)} fusion(f32[1024,512]{1,0:T(8,128)S(1)} %copy-done.19, pred[1024,64]{0,1:T(8,128)(4,1)S(1)} %iota_compare_fusion, bf16[64,16,512]{2,1,0:T(8,128)(2,1)S(1)} %get-tuple-element.20, bf16[1024,16]{0,1:T(8,128)(2,1)S(1)} %add_convert_fusion.1), kind=kOutput, calls=%fused_computation.10 | convolution fusion | flops 1076887552 | bytes 5341184 | tf_op jit(solution)/shard_map/dot_general | solution.py:359
  104.5 43.9 %shard_map.119 = bf16[1024,512]{1,0:T(8,128)(2,1)S(1)} custom-call(f32[1024,512]{1,0:T(8,128)} %convert_add_fusion.q_ref, f32[1024,128]{1,0:T(8,128)S(1)} %get-tuple-element.45.cs_ref, f32[1024,128]{1,0:T(8,128)S(1)} %get-tuple-element.46.sn_ref, bf16[1152,256]{1,0:T(8,128)(2,1)S(1)} %concatenate.98.k_ref, bf16[1152,256]{1,0:T(8,128)(2,1)S(1)} %concatenate.99.v_ref, ...), custom_call_target="tpu_custom_call" | custom-call | tf_op jit(solution)/shard_map/pallas_call | solution.py:193
  148.4 1.0 copy.48
  (80 shorter events, 1.5 us)
Async XLA Ops:
  0.0 74.5 %copy-start = (bf16[2048,512]{1,0:T(8,128)(2,1)S(1)}, bf16[2048,512]{1,0:T(8,128)(2,1)}, u32[]{:S(2)}) copy-start(bf16[2048,512]{1,0:T(8,128)(2,1)} %param.14) | copy-start | bytes 6291460
  26.0 11.8 %copy-start.17 = (s32[1,32]{1,0:T(1,128)S(1)}, s32[1,32]{1,0:T(1,128)}, u32[]{:S(2)}) copy-start(s32[1,32]{1,0:T(1,128)} %param.20) | copy-start | bytes 388
  26.0 12.1 %copy-start.14 = (s32[1,32]{1,0:T(1,128)S(1)}, s32[1,32]{1,0:T(1,128)}, u32[]{:S(2)}) copy-start(s32[1,32]{1,0:T(1,128)} %param.21) | copy-start | bytes 388
  28.1 13.9 %copy-start.16 = (f32[2048]{0:T(1024)S(1)}, f32[2048]{0:T(1024)}, u32[]{:S(2)}) copy-start(f32[2048]{0:T(1024)} %param.13) | copy-start | bytes 24580
  28.1 59.1 %all-to-all-start = ((bf16[64,32,512]{2,1,0:T(8,128)(2,1)}), bf16[64,32,512]{2,1,0:T(8,128)(2,1)}, u32[]{:S(2)}, u32[]{:S(2)}) async-start(bf16[64,32,512]{2,1,0:T(8,128)(2,1)} %bitcast.70), calls=%async_computation | async-start | bytes 4194304 | tf_op jit(solution)/shard_map/all_to_all | solution.py:336
  38.1 3.9 %copy-start.2 = (bf16[1024,2048]{1,0:T(8,128)(2,1)S(1)}, bf16[1024,2048]{1,0:T(8,128)(2,1)}, u32[]{:S(2)}) copy-start(bf16[1024,2048]{1,0:T(8,128)(2,1)} %param.12) | copy-start | bytes 12582916
  42.0 1.2 copy-start.18
  43.2 1.9 %copy-start.7 = (bf16[1024,2048]{1,0:T(8,128)(2,1)}, bf16[1024,2048]{1,0:T(8,128)(2,1)S(1)}, u32[]{:S(2)}) copy-start(bf16[1024,2048]{1,0:T(8,128)(2,1)S(1)} %fusion.2) | copy-start | bytes 12582916
  50.0 16.3 %copy-start.15 = (s32[8,128]{1,0:T(8,128)S(1)}, s32[8,128]{1,0:T(8,128)}, u32[]{:S(2)}) copy-start(s32[8,128]{1,0:T(8,128)} %constant.104.clone.1) | copy-start | bytes 12292
  53.0 0.8 copy-start.3
  53.0 3.9 %copy-start.5 = (f32[1024,64]{1,0:T(8,128)}, f32[1024,64]{1,0:T(8,128)S(1)}, u32[]{:S(2)}) copy-start(f32[1024,64]{1,0:T(8,128)S(1)} %get-tuple-element.31) | copy-start | bytes 786436
  63.8 6.4 %copy-start.9 = (bf16[128,8,2,128]{3,1,2,0:T(8,128)(2,1)}, bf16[128,8,2,128]{3,1,2,0:T(8,128)(2,1)S(1)}, u32[]{:S(2)}) copy-start(bf16[128,8,2,128]{3,1,2,0:T(8,128)(2,1)S(1)} %copy.46) | copy-start | bytes 1572868
  70.2 4.2 %copy-start.12 = (bf16[1024,256]{1,0:T(8,128)(2,1)}, bf16[1024,256]{1,0:T(8,128)(2,1)S(1)}, u32[]{:S(2)}) copy-start(bf16[1024,256]{1,0:T(8,128)(2,1)S(1)} %convolution_convert_fusion.1) | copy-start | bytes 1572868
  70.2 4.3 %copy-start.8 = (bf16[1024,2048]{1,0:T(8,128)(2,1)S(1)}, bf16[1024,2048]{1,0:T(8,128)(2,1)}, u32[]{:S(2)}) copy-start(bf16[1024,2048]{1,0:T(8,128)(2,1)} %copy-done.7) | copy-start | bytes 12582916
  89.0 8.9 %copy-start.4 = (f32[1024,64]{1,0:T(8,128)S(1)}, f32[1024,64]{1,0:T(8,128)}, u32[]{:S(2)}) copy-start(f32[1024,64]{1,0:T(8,128)} %copy-done.3) | copy-start | bytes 786436
  89.0 8.9 %copy-start.6 = (f32[1024,64]{1,0:T(8,128)S(1)}, f32[1024,64]{1,0:T(8,128)}, u32[]{:S(2)}) copy-start(f32[1024,64]{1,0:T(8,128)} %copy-done.5) | copy-start | bytes 786436
  89.0 8.9 %copy-start.11 = (f32[1024,64]{1,0:T(8,128)S(1)}, f32[1024,64]{1,0:T(8,128)}, u32[]{:S(2)}) copy-start(f32[1024,64]{1,0:T(8,128)} %get-tuple-element.29) | copy-start | bytes 786436
  89.0 9.3 %copy-start.10 = (bf16[128,8,2,128]{3,1,2,0:T(8,128)(2,1)S(1)}, bf16[128,8,2,128]{3,1,2,0:T(8,128)(2,1)}, u32[]{:S(2)}) copy-start(bf16[128,8,2,128]{3,1,2,0:T(8,128)(2,1)} %copy-done.9) | copy-start | bytes 1572868
  89.0 9.3 %copy-start.13 = (bf16[1024,256]{1,0:T(8,128)(2,1)S(1)}, bf16[1024,256]{1,0:T(8,128)(2,1)}, u32[]{:S(2)}) copy-start(bf16[1024,256]{1,0:T(8,128)(2,1)} %copy-done.12) | copy-start | bytes 1572868
  92.0 9.5 %copy-start.19 = (f32[1024,512]{1,0:T(8,128)S(1)}, f32[1024,512]{1,0:T(8,128)}, u32[]{:S(2)}) copy-start(f32[1024,512]{1,0:T(8,128)} %fusion.33) | copy-start | bytes 6291460
  92.0 6.4 %collective-permute-start = (f32[1024,16]{0,1:T(8,128)S(1)}, f32[1024,16]{0,1:T(8,128)S(1)}, u32[]{:S(2)}, u32[]{:S(2)}) collective-permute-start(f32[1024,16]{0,1:T(8,128)S(1)} %select_reduce_fusion), channel_id=1, source_target_pairs={{0,1},{1,2},{2,3},{3,0},{4,5},{5,6},{6,7},{7,4},{8,9},{9,10},{10,1... | collective-permute-start | bytes 196616 | tf_op jit(solution)/shard_map/ppermute | solution.py:349
  93.7 6.8 %collective-permute-start.1 = (f32[1024,16]{0,1:T(8,128)S(1)}, f32[1024,16]{0,1:T(8,128)S(1)}, u32[]{:S(2)}, u32[]{:S(2)}) collective-permute-start(f32[1024,16]{0,1:T(8,128)S(1)} %select_reduce_fusion), channel_id=1, source_target_pairs={{0,2},{1,3},{2,0},{3,1},{4,6},{5,7},{6,4},{7,5},{8,10},{9,11},{10,... | collective-permute-start | bytes 196616 | tf_op jit(solution)/shard_map/ppermute | solution.py:349
  96.6 4.9 %collective-permute-start.2 = (f32[1024,16]{0,1:T(8,128)S(1)}, f32[1024,16]{0,1:T(8,128)S(1)}, u32[]{:S(2)}, u32[]{:S(2)}) collective-permute-start(f32[1024,16]{0,1:T(8,128)S(1)} %select_reduce_fusion), channel_id=1, source_target_pairs={{0,3},{1,0},{2,1},{3,2},{4,7},{5,4},{6,5},{7,6},{8,11},{9,8},{10,9... | collective-permute-start | bytes 196616 | tf_op jit(solution)/shard_map/ppermute | solution.py:349
  101.5 3.0 %copy-start.1 = (f32[8,128,384]{2,1,0:T(8,128)S(1)}, f32[8,128,384]{2,1,0:T(8,128)}, u32[]{:S(2)}) copy-start(f32[8,128,384]{2,1,0:T(8,128)} %add_select_fusion.bias_ref) | copy-start | bytes 4718596

commit v18 on v13

--- a/solution.py
+++ b/solution.py
@@ -59,7 +59,7 @@
 
 
 def attend_kernel(
-    q_ref, cs_ref, sn_ref, k_ref, v_ref, kp_ref, vp_ref, bias_ref, wo_ref, res_ref, out_ref,
+    q_ref, d_ref, cs_ref, sn_ref, k_ref, v_ref, kp_ref, vp_ref, bias_ref, wo_ref, res_ref, out_ref,
     send_buf, relay_in, sum_buf, recv_buf, send_sems, recv_sems, *, tp_count, heads, kv_heads,
     n_blocks
 ):
@@ -126,7 +126,9 @@
         outs = []
         for h in range(heads):
             g = h // rep
-            qf = q_ref[pl.ds(row, BLOCK), pl.ds(h * 128, 128)]
+            qf = q_ref[pl.ds(row, BLOCK), pl.ds(h * 128, 128)] + d_ref[
+                pl.ds(row, BLOCK), pl.ds(h * 128, 128)
+            ].astype(jnp.float32)
             qh = (qf * cs + pltpu.roll(qf, 64, 1) * sn).astype(jnp.bfloat16)
             kw = k_ref[pl.ds(row, 2 * BLOCK), pl.ds(g * 128, 128)]
             vw = v_ref[pl.ds(row, 2 * BLOCK), pl.ds(g * 128, 128)]
@@ -177,7 +179,7 @@
     lax.fori_loop(0, n_blocks, finish_body, 0)
 
 
-def attend_and_reduce(q, cs, sn, k_pad, v_pad, k_prompt, v_prompt, bias, wo, residual, tp_count):
+def attend_and_reduce(q, delta, cs, sn, k_pad, v_pad, k_prompt, v_prompt, bias, wo, residual, tp_count):
     rows, q_width = q.shape
     n_blocks = rows // BLOCK
     piece = residual.shape[1]
@@ -193,7 +195,7 @@
     return pl.pallas_call(
         kernel,
         out_shape=jax.ShapeDtypeStruct((rows, piece), jnp.bfloat16),
-        in_specs=[pl.BlockSpec(memory_space=vmem)] * 10,
+        in_specs=[pl.BlockSpec(memory_space=vmem)] * 11,
         out_specs=pl.BlockSpec(memory_space=vmem),
         scratch_shapes=[
             pltpu.VMEM((n_blocks, BLOCK, width), jnp.bfloat16),
@@ -206,7 +208,7 @@
         compiler_params=pltpu.CompilerParams(
             collective_id=0, has_side_effects=True, vmem_limit_bytes=48 * 1024 * 1024
         ),
-    )(q, cs, sn, k_pad, v_pad, k_prompt, v_prompt, bias, wo, residual)
+    )(q, delta, cs, sn, k_pad, v_pad, k_prompt, v_prompt, bias, wo, residual)
 
 
 def ids_kernel(wanted_ref, out_ref, landing, send_sems, recv_sems):
@@ -352,9 +354,7 @@
     ).astype(jnp.bfloat16)
     heads_local = query_matrix.shape[1] // HEAD_WIDTH
     kv_local = key_matrix.shape[1] // HEAD_WIDTH
-    query_full = jnp.dot(
-        normalized_input, query_matrix, preferred_element_type=jnp.float32
-    ) + query_delta.astype(jnp.float32)
+    query_full = jnp.dot(normalized_input, query_matrix, preferred_element_type=jnp.float32)
     half_dim = HEAD_WIDTH // 2
     inverse = 1000000.0 ** (-(jnp.arange(half_dim, dtype=jnp.float32) * 2.0 / HEAD_WIDTH))
     angles = token_positions[:, None] * inverse[None, :]
@@ -432,6 +432,7 @@
     residual = lax.dynamic_slice_in_dim(tokens, tp_index * piece_width, piece_width, 1)
     return attend_and_reduce(
         query_full,
+        query_delta,
         cos_pair,
         sin_pair,
         k_pad,

time: 150 us -> 149 us (level)
  waiting for transfers between devices: 13.9 us -> 11.7 us
    all_to_all x1, waiting for transfers between devices: 10.9 us -> 8.6 us  [per_device(): lax.all_to_all(maps_out, 'req', split_axis=0, concat_axis=0, tiled=True)]
    unnamed x46 -> x40, local copies, waits for them, and re-layouts: 5.75 us -> 6.38 us
where the time goes in v18:
time: 149 us
  Pallas kernels  64.1 us (43%)
  other arithmetic  19 us (13%)
  local copies, waits for them, and re-layouts  18.6 us (12%)
  starting transfers between devices  15.6 us (10%)
  matrix products  13.4 us (9%)
  waiting for transfers between devices  11.7 us (8%)
  between operations  6.32 us (4%)
    pallas_call x1, Pallas kernels, attend_and_reduce(): pl.pallas_call(kernel, out_shape=jax.ShapeDtypeStruct((rows, piece), jnp....  44.6 us
    pallas_call x1, Pallas kernels, exchange_ids(): pl.pallas_call(ids_kernel, out_shape=jax.ShapeDtypeStruct((count, 8, 128)...  19.6 us
    all_to_all x1, starting transfers between devices, per_device(): lax.all_to_all(maps_out, 'req', split_axis=0, concat_axis=0, tiled=True)  9.68 us
    all_to_all x1, waiting for transfers between devices, per_device(): lax.all_to_all(maps_out, 'req', split_axis=0, concat_axis=0, tiled=True)  8.6 us
    unnamed x40, local copies, waits for them, and re-layouts  6.38 us
    ppermute x3, starting transfers between devices, per_device(): lax.ppermute(partial_rank, 'tp', [(i, (i + k) % tp_count) for i in range(...  5.91 us
    dot_general x1, matrix products, per_device(): jnp.dot(normalized_input, value_matrix, preferred_element_type=jnp.float32)  3.73 us
    dot_general x1, matrix products, per_device(): jnp.dot(normalized_input, query_matrix, preferred_element_type=jnp.float32)  3.72 us
  transfers between devices with their start and end apart: 4, of which 3 were waited for; matrix products, arithmetic and copies ran while one was open for 22% of the time, Pallas kernels for 0%

profile of v18, /device:TPU:2, one launch (start us, length us, event | category | flops | bytes accessed | tf_op | source)
XLA Modules:
  0.0 148.7 jit_solution(9831729479104661524)
XLA Ops:
  0.0 0.8 fusion.20
  0.8 1.4 gather_fusion
  2.2 0.1 select_reduce_fusion.6
  2.3 0.8 broadcast_in_dim.37.wanted_ref
  3.2 19.6 %shard_map.118 = s32[64,8,128]{2,1,0:T(8,128)} custom-call(s32[64,8,128]{2,1,0:T(8,128)} %broadcast_in_dim.37.wanted_ref), custom_call_target="tpu_custom_call" | custom-call | tf_op jit(solution)/shard_map/pallas_call | solution.py:273
  22.8 2.2 %slice_reduce_fusion = s32[64]{0:T(128)S(1)} fusion(s32[64,8,128]{2,1,0:T(8,128)} %shard_map.118), kind=kLoop, calls=%fused_computation.44 | loop fusion | bytes 512 | tf_op jit(solution)/shard_map/slice | solution.py:285
  25.0 1.1 pad_maximum_fusion
  26.1 2.0 %gather_fusion.1 = bf16[64,32,512]{2,1,0:T(8,128)(2,1)} fusion(bf16[16,32,512]{2,1,0:T(8,128)(2,1)S(1)} %pad_maximum_fusion, s32[1024]{0:T(1024)S(1)} %pad_clamp_fusion), kind=kCustom, calls=%fused_computation.1 | custom fusion | bytes 4194560 | tf_op jit(solution)/shard_map/gather | solution.py:322
  28.1 9.7 %all-to-all-start = ((bf16[64,32,512]{2,1,0:T(8,128)(2,1)}), bf16[64,32,512]{2,1,0:T(8,128)(2,1)}, u32[]{:S(2)}, u32[]{:S(2)}) async-start(bf16[64,32,512]{2,1,0:T(8,128)(2,1)} %gather_fusion.1), calls=%async_computation | async-start | bytes 4194304 | tf_op jit(solution)/shard_map/all_to_all | solution.py:330
  37.8 0.1 copy.25
  38.0 0.1 reduce.1
  38.2 0.1 convert_reduce_fusion
  38.3 0.2 select_reduce_fusion.5
  38.5 0.1 select_reduce_fusion.1
  38.6 3.3 %fusion = f32[1024]{0:T(1024)S(1)} fusion(bf16[1024,2048]{1,0:T(8,128)(2,1)} %param.12), kind=kLoop, calls=%fused_computation.4 | loop fusion | flops 6290432 | bytes 4198400 | tf_op jit(solution)/shard_map/reduce_sum | solution.py:327
  42.0 1.0 fusion.2
  43.1 0.2 copy-done.17
  43.3 1.3 fusion.32
  44.6 0.6 copy-done.6
  45.2 1.0 fusion.28
  46.2 1.4 copy.32
  47.7 2.2 %copy.33 = f32[1024,2,64]{2,1,0:T(2,128)} copy(f32[1024,2,64]{0,2,1:T(8,128)} %get-tuple-element.21) | data formatting | bytes 1048576
  49.8 0.1 select_reduce_fusion.7
  50.0 3.0 %fusion.15 = (f32[1024,64]{1,0:T(8,128)}, f32[1024,64]{1,0:T(8,128)S(1)}, f32[1024,64]{1,0:T(8,128)S(1)}) fusion(f32[64]{0:T(128)S(1)} %negate_power_fusion, f32[1024]{0:T(1024)S(1)} %add_convert_fusion.2), kind=kLoop, calls=%fused_computation.33 | loop fusion | flops 131072 | bytes 790784 | tf_op jit(solution)/shard_map/neg | solution.py:364
  53.0 0.8 copy-done.2
  53.8 3.0 %subtract_convert_fusion = (bf16[1024,2,64]{2,1,0:T(2,128)(2,1)}, bf16[1024,2,64]{2,1,0:T(2,128)(2,1)}) fusion(f32[1024,2,64]{2,1,0:T(2,128)} %copy.33, f32[1024,2,64]{2,1,0:T(2,128)S(1)} %copy.32, f32[1024,64]{1,0:T(8,128)S(1)} %get-tuple-element.30, f32[1024,64]{1,0:T(8,128)S(1)} %get-tuple-element.31), kind=kLoop, calls=%fused_computation.19 | loop fusion | flops 1048576 | bytes 2097152 | tf_op jit(solution)/shard_map/convert
  56.9 0.7 fusion.30
  61.4 2.6 %pad_maximum_fusion.3 = bf16[1024,2,128]{2,1,0:T(2,128)(2,1)S(1)} fusion(bf16[1024,2,64]{2,1,0:T(2,128)(2,1)} %get-tuple-element.18, bf16[1024,2,64]{2,1,0:T(2,128)(2,1)} %get-tuple-element.17), kind=kLoop, calls=%fused_computation.30 | loop fusion | flops 1048576 | bytes 1048576 | tf_op jit(solution)/shard_map/concatenate | solution.py:23
  64.4 0.1 reshape.382
  66.9 3.7 %convolution_convert_fusion = bf16[1024,256]{1,0:T(8,128)(2,1)S(1)} fusion(bf16[1024,2048]{1,0:T(8,128)(2,1)} %copy-done.6, bf16[2048,256]{1,0:T(8,128)(2,1)} %param.16), kind=kOutput, calls=%fused_computation.14 | convolution fusion | flops 1074003968 | bytes 5767168 | tf_op jit(solution)/shard_map/dot_general | solution.py:370
  70.7 1.5 %constant_dynamic-slice_fusion.res_ref = bf16[1024,512]{1,0:T(8,128)(2,1)S(1)} fusion(bf16[1024,2048]{1,0:T(8,128)(2,1)} %param.12, s32[]{:T(128)S(6)} %select_n.72), kind=kLoop, calls=%fused_computation.71 | loop fusion | bytes 2097156 | tf_op jit(solution)/shard_map/dynamic_slice | solution.py:432
  72.3 0.3 compare_and_fusion
  72.6 0.8 or_and_fusion
  73.5 1.3 add_select_fusion.bias_ref
  74.8 0.1 maximum_maximum_fusion.1
  74.9 3.7 %fusion.31.q_ref = f32[1024,512]{1,0:T(8,128)} fusion(bf16[1024,2048]{1,0:T(8,128)(2,1)S(1)} %copy-done.7, bf16[2048,512]{1,0:T(8,128)(2,1)S(1)} %copy-done), kind=kOutput, calls=%fused_computation.107 | convolution fusion | flops 2147483648 | bytes 8388608 | tf_op jit(solution)/shard_map/dot_general | solution.py:357
  78.7 8.6 %all-to-all-done = bf16[64,32,512]{2,1,0:T(8,128)(2,1)} async-done(((bf16[64,32,512]{2,1,0:T(8,128)(2,1)}), bf16[64,32,512]{2,1,0:T(8,128)(2,1)}, u32[]{:S(2)}, u32[]{:S(2)}) %all-to-all-start) | async-done | bytes 2097184 | tf_op jit(solution)/shard_map/all_to_all | solution.py:330
  87.3 1.7 %fusion.27 = (bf16[64,16,512]{2,1,0:T(8,128)(2,1)S(1)}, bf16[64,16,512]{2,1,0:T(8,128)(2,1)S(1)}) fusion(bf16[64,32,512]{2,1,0:T(8,128)(2,1)} %all-to-all-done), kind=kLoop, calls=%fused_computation.103 | loop fusion | bytes 4194304 | tf_op jit(solution)/shard_map/slice | solution.py:331
  89.0 3.0 %select_reduce_fusion = f32[1024,16]{0,1:T(8,128)S(1)} fusion(pred[1024,64]{0,1:T(8,128)(4,1)S(1)} %iota_compare_fusion, bf16[64,16,512]{2,1,0:T(8,128)(2,1)S(1)} %get-tuple-element.19, bf16[1024,2048]{1,0:T(8,128)(2,1)} %copy-done.6, s32[]{:T(128)S(6)} %select_n.72), kind=kOutput, calls=%fused_computation.7 | convolution fusion | flops 1075822592 | bytes 2228228 | tf_op jit(solution)/shard_map/dot_general | solution.py:338
  92.0 1.7 %collective-permute-start = (f32[1024,16]{0,1:T(8,128)S(1)}, f32[1024,16]{0,1:T(8,128)S(1)}, u32[]{:S(2)}, u32[]{:S(2)}) collective-permute-start(f32[1024,16]{0,1:T(8,128)S(1)} %select_reduce_fusion), channel_id=1, source_target_pairs={{0,1},{1,2},{2,3},{3,0},{4,5},{5,6},{6,7},{7,4},{8,9},{9,10},{10,1... | collective-permute-start | bytes 196616 | tf_op jit(solution)/shard_map/ppermute | solution.py:343
  93.7 2.9 %collective-permute-start.1 = (f32[1024,16]{0,1:T(8,128)S(1)}, f32[1024,16]{0,1:T(8,128)S(1)}, u32[]{:S(2)}, u32[]{:S(2)}) collective-permute-start(f32[1024,16]{0,1:T(8,128)S(1)} %select_reduce_fusion), channel_id=1, source_target_pairs={{0,2},{1,3},{2,0},{3,1},{4,6},{5,7},{6,4},{7,5},{8,10},{9,11},{10,... | collective-permute-start | bytes 196616 | tf_op jit(solution)/shard_map/ppermute | solution.py:343
  96.6 1.3 collective-permute-start.2
  97.9 0.3 pad_maximum_fusion.1
  98.4 2.1 %collective-permute-done.1 = f32[1024,16]{0,1:T(8,128)S(1)} collective-permute-done((f32[1024,16]{0,1:T(8,128)S(1)}, f32[1024,16]{0,1:T(8,128)S(1)}, u32[]{:S(2)}, u32[]{:S(2)}) %collective-permute-start.1) | collective-permute-done | bytes 65568 | tf_op jit(solution)/shard_map/ppermute | solution.py:343
  100.5 1.0 collective-permute-done.2
  101.5 1.6 %fusion.3.d_ref = bf16[1024,512]{1,0:T(8,128)(2,1)S(1)} fusion(pred[1024,64]{0,1:T(8,128)(4,1)S(1)} %iota_compare_fusion, bf16[64,16,512]{2,1,0:T(8,128)(2,1)S(1)} %get-tuple-element.20, bf16[1024,16]{0,1:T(8,128)(2,1)S(1)} %add_convert_fusion.1), kind=kOutput, calls=%fused_computation.9 | convolution fusion | flops 1075838976 | bytes 2195456 | tf_op jit(solution)/shard_map/dot_general | solution.py:353
  103.2 44.6 %shard_map.119 = bf16[1024,512]{1,0:T(8,128)(2,1)S(1)} custom-call(f32[1024,512]{1,0:T(8,128)} %fusion.31.q_ref, bf16[1024,512]{1,0:T(8,128)(2,1)S(1)} %fusion.3.d_ref, f32[1024,128]{1,0:T(8,128)S(1)} %get-tuple-element.45.cs_ref, f32[1024,128]{1,0:T(8,128)S(1)} %get-tuple-element.46.sn_ref, bf16[1152,256]{1,0:T(8,128)(2,1)S(1)} %concatenate.98.k_ref, ...), custom_call_target="tpu_custom_call" | custom-call | tf_op jit(solution)/shard_map/pallas_call | solution.py:195
  147.7 1.0 copy.42
  (75 shorter events, 1.3 us)
Async XLA Ops:
  0.0 74.9 %copy-start = (bf16[2048,512]{1,0:T(8,128)(2,1)S(1)}, bf16[2048,512]{1,0:T(8,128)(2,1)}, u32[]{:S(2)}) copy-start(bf16[2048,512]{1,0:T(8,128)(2,1)} %param.14) | copy-start | bytes 6291460
  26.1 11.7 %copy-start.16 = (s32[1,32]{1,0:T(1,128)S(1)}, s32[1,32]{1,0:T(1,128)}, u32[]{:S(2)}) copy-start(s32[1,32]{1,0:T(1,128)} %param.20) | copy-start | bytes 388
  26.1 12.0 %copy-start.13 = (s32[1,32]{1,0:T(1,128)S(1)}, s32[1,32]{1,0:T(1,128)}, u32[]{:S(2)}) copy-start(s32[1,32]{1,0:T(1,128)} %param.21) | copy-start | bytes 388
  28.1 13.9 %copy-start.15 = (f32[2048]{0:T(1024)S(1)}, f32[2048]{0:T(1024)}, u32[]{:S(2)}) copy-start(f32[2048]{0:T(1024)} %param.13) | copy-start | bytes 24580
  28.1 59.1 %all-to-all-start = ((bf16[64,32,512]{2,1,0:T(8,128)(2,1)}), bf16[64,32,512]{2,1,0:T(8,128)(2,1)}, u32[]{:S(2)}, u32[]{:S(2)}) async-start(bf16[64,32,512]{2,1,0:T(8,128)(2,1)} %gather_fusion.1), calls=%async_computation | async-start | bytes 4194304 | tf_op jit(solution)/shard_map/all_to_all | solution.py:330
  38.1 3.9 %copy-start.1 = (bf16[1024,2048]{1,0:T(8,128)(2,1)S(1)}, bf16[1024,2048]{1,0:T(8,128)(2,1)}, u32[]{:S(2)}) copy-start(bf16[1024,2048]{1,0:T(8,128)(2,1)} %param.12) | copy-start | bytes 12582916
  42.0 1.2 copy-start.17
  43.3 1.9 %copy-start.6 = (bf16[1024,2048]{1,0:T(8,128)(2,1)}, bf16[1024,2048]{1,0:T(8,128)(2,1)S(1)}, u32[]{:S(2)}) copy-start(bf16[1024,2048]{1,0:T(8,128)(2,1)S(1)} %fusion.2) | copy-start | bytes 12582916
  50.0 16.8 %copy-start.14 = (s32[8,128]{1,0:T(8,128)S(1)}, s32[8,128]{1,0:T(8,128)}, u32[]{:S(2)}) copy-start(s32[8,128]{1,0:T(8,128)} %constant.106.clone.1) | copy-start | bytes 12292
  53.0 0.8 copy-start.2
  53.0 3.9 %copy-start.4 = (f32[1024,64]{1,0:T(8,128)}, f32[1024,64]{1,0:T(8,128)S(1)}, u32[]{:S(2)}) copy-start(f32[1024,64]{1,0:T(8,128)S(1)} %get-tuple-element.31) | copy-start | bytes 786436
  64.1 6.5 %copy-start.8 = (bf16[128,8,2,128]{3,1,2,0:T(8,128)(2,1)}, bf16[128,8,2,128]{3,1,2,0:T(8,128)(2,1)S(1)}, u32[]{:S(2)}) copy-start(bf16[128,8,2,128]{3,1,2,0:T(8,128)(2,1)S(1)} %copy.40) | copy-start | bytes 1572868
  70.6 4.2 %copy-start.11 = (bf16[1024,256]{1,0:T(8,128)(2,1)}, bf16[1024,256]{1,0:T(8,128)(2,1)S(1)}, u32[]{:S(2)}) copy-start(bf16[1024,256]{1,0:T(8,128)(2,1)S(1)} %convolution_convert_fusion) | copy-start | bytes 1572868
  70.6 4.3 %copy-start.7 = (bf16[1024,2048]{1,0:T(8,128)(2,1)S(1)}, bf16[1024,2048]{1,0:T(8,128)(2,1)}, u32[]{:S(2)}) copy-start(bf16[1024,2048]{1,0:T(8,128)(2,1)} %copy-done.6) | copy-start | bytes 12582916
  89.0 8.9 %copy-start.3 = (f32[1024,64]{1,0:T(8,128)S(1)}, f32[1024,64]{1,0:T(8,128)}, u32[]{:S(2)}) copy-start(f32[1024,64]{1,0:T(8,128)} %copy-done.2) | copy-start | bytes 786436
  89.0 8.9 %copy-start.5 = (f32[1024,64]{1,0:T(8,128)S(1)}, f32[1024,64]{1,0:T(8,128)}, u32[]{:S(2)}) copy-start(f32[1024,64]{1,0:T(8,128)} %copy-done.4) | copy-start | bytes 786436
  89.0 8.9 %copy-start.10 = (f32[1024,64]{1,0:T(8,128)S(1)}, f32[1024,64]{1,0:T(8,128)}, u32[]{:S(2)}) copy-start(f32[1024,64]{1,0:T(8,128)} %get-tuple-element.29) | copy-start | bytes 786436
  89.0 9.3 %copy-start.9 = (bf16[128,8,2,128]{3,1,2,0:T(8,128)(2,1)S(1)}, bf16[128,8,2,128]{3,1,2,0:T(8,128)(2,1)}, u32[]{:S(2)}) copy-start(bf16[128,8,2,128]{3,1,2,0:T(8,128)(2,1)} %copy-done.8) | copy-start | bytes 1572868
  89.0 9.3 %copy-start.12 = (bf16[1024,256]{1,0:T(8,128)(2,1)S(1)}, bf16[1024,256]{1,0:T(8,128)(2,1)}, u32[]{:S(2)}) copy-start(bf16[1024,256]{1,0:T(8,128)(2,1)} %copy-done.11) | copy-start | bytes 1572868
  92.0 6.4 %collective-permute-start = (f32[1024,16]{0,1:T(8,128)S(1)}, f32[1024,16]{0,1:T(8,128)S(1)}, u32[]{:S(2)}, u32[]{:S(2)}) collective-permute-start(f32[1024,16]{0,1:T(8,128)S(1)} %select_reduce_fusion), channel_id=1, source_target_pairs={{0,1},{1,2},{2,3},{3,0},{4,5},{5,6},{6,7},{7,4},{8,9},{9,10},{10,1... | collective-permute-start | bytes 196616 | tf_op jit(solution)/shard_map/ppermute | solution.py:343
  93.7 6.8 %collective-permute-start.1 = (f32[1024,16]{0,1:T(8,128)S(1)}, f32[1024,16]{0,1:T(8,128)S(1)}, u32[]{:S(2)}, u32[]{:S(2)}) collective-permute-start(f32[1024,16]{0,1:T(8,128)S(1)} %select_reduce_fusion), channel_id=1, source_target_pairs={{0,2},{1,3},{2,0},{3,1},{4,6},{5,7},{6,4},{7,5},{8,10},{9,11},{10,... | collective-permute-start | bytes 196616 | tf_op jit(solution)/shard_map/ppermute | solution.py:343
  96.6 4.9 %collective-permute-start.2 = (f32[1024,16]{0,1:T(8,128)S(1)}, f32[1024,16]{0,1:T(8,128)S(1)}, u32[]{:S(2)}, u32[]{:S(2)}) collective-permute-start(f32[1024,16]{0,1:T(8,128)S(1)} %select_reduce_fusion), channel_id=1, source_target_pairs={{0,3},{1,0},{2,1},{3,2},{4,7},{5,4},{6,5},{7,6},{8,11},{9,8},{10,9... | collective-permute-start | bytes 196616 | tf_op jit(solution)/shard_map/ppermute | solution.py:343
